TPU v7x, 128 devices: a whole 4x4x4 slice. The times are simulated.
128 devices in a mesh: section: 2 (over x_hi), dp: 8 (over y, core), tensor: 8 (over x_lo, z).
Axes of the slice: x: 4 (x_hi: 2, x_lo: 2; x = x_hi * 2 + x_lo), y: 4, z: 4, core: 2. Of those that a mesh axis runs over, the one named last changes fastest.
Arguments:
- inputs: float32 [2, 8, 768, 1024], P(None, 'dp', None, 'tensor'), may hold values from -6 to 6
- cotangent: float32 [2, 8, 768, 1024], P(None, 'dp', None, 'tensor'), may hold values from -6 to 6
- packed_weight: bfloat16 [2, 1024, 3, 1024], P('section', 'dp', None, 'tensor'), may hold values from -0.1875 to 0.1875
- bias_pair: bfloat16 [2, 2, 1024], P('section', None, ('tensor', 'dp')), may hold values from -3 to 3
- output_weight: bfloat16 [2, 1024, 1024], P('section', 'tensor', 'dp'), may hold values from -1 to 1
- output_bias: bfloat16 [2, 1024], P('section', ('tensor', 'dp')), may hold values from -3 to 3
- expand_weight: bfloat16 [2, 1024, 4096], P('section', 'dp', 'tensor'), may hold values from -0.1875 to 0.1875
- expand_bias: bfloat16 [2, 4096], P('section', ('tensor', 'dp')), may hold values from -3 to 3
- contract_weight: bfloat16 [2, 4096, 1024], P('section', 'tensor', 'dp'), may hold values from -0.09375 to 0.09375
- contract_bias: bfloat16 [2, 1024], P('section', ('tensor', 'dp')), may hold values from -3 to 3
- gain_first: bfloat16 [2, 1024], P('section', ('tensor', 'dp')), may hold values from 0.25 to 1.75
- shift_first: bfloat16 [2, 1024], P('section', ('tensor', 'dp')), may hold values from -3 to 3
- gain_second: bfloat16 [2, 1024], P('section', ('tensor', 'dp')), may hold values from 0.25 to 1.75
- shift_second: bfloat16 [2, 1024], P('section', ('tensor', 'dp')), may hold values from -3 to 3
Outputs:
- section_outputs: float32 [2, 2, 8, 768, 1024], P('section', None, 'dp', None, 'tensor')
- section_grads: float32 [2, 2, 8, 768, 1024], P('section', None, 'dp', None, 'tensor')
- packed_weight_grad: float32 [2, 1024, 3, 1024], P('section', 'dp', None, 'tensor')
- bias_pair_grad: float32 [2, 2, 1024], P('section', None, ('tensor', 'dp'))
- output_weight_grad: float32 [2, 1024, 1024], P('section', 'tensor', 'dp')
- output_bias_grad: float32 [2, 1024], P('section', ('tensor', 'dp'))
- expand_weight_grad: float32 [2, 1024, 4096], P('section', 'dp', 'tensor')
- expand_bias_grad: float32 [2, 4096], P('section', ('tensor', 'dp'))
- contract_weight_grad: float32 [2, 4096, 1024], P('section', 'tensor', 'dp')
- contract_bias_grad: float32 [2, 1024], P('section', ('tensor', 'dp'))
- gain_first_grad: float32 [2, 1024], P('section', ('tensor', 'dp'))
- shift_first_grad: float32 [2, 1024], P('section', ('tensor', 'dp'))
- gain_second_grad: float32 [2, 1024], P('section', ('tensor', 'dp'))
- shift_second_grad: float32 [2, 1024], P('section', ('tensor', 'dp'))
All inputs are finite; a program needn't handle non-finite values.
Results may differ from a plain program's by a relative error of at most 0.025.
Values may be sent and summed in bfloat16 or wider, within the bound.
No kernel may reach another device: no remote copies, remote signals or barrier semaphores. Data moves between devices by JAX's collectives and lax.ppermute only.
A program may use at most 192 MiB of HBM per device.

v0:
```python
import math

import jax
import jax.numpy as jnp
from jax import lax
from jax.sharding import PartitionSpec as P

HEAD_DIM = 64


epsilon = 1e-05
gelu_coef = math.sqrt(2.0 / math.pi)
masked_value = -1e30


def sent_to_all(array, axis):
    copies = jnp.broadcast_to(array, (lax.axis_size(axis), *array.shape))
    return lax.all_to_all(copies, axis, split_axis=0, concat_axis=0, tiled=True)


def taken_together(array, axis):
    return sent_to_all(array, axis).sum(axis=0)


def in_one(arrays, axis):
    ends = [0]
    for a in arrays:
        ends.append(ends[-1] + a.size)
    subtotal = taken_together(jnp.concatenate([a.ravel() for a in arrays]), axis)
    return tuple((subtotal[b:e].reshape(a.shape) for a, b, e in zip(arrays, ends, ends[1:])))


def joined_along(parts, dim):
    parts = jnp.moveaxis(parts, 0, dim)
    shape = parts.shape
    return parts.reshape(*shape[:dim], shape[dim] * shape[dim + 1], *shape[dim + 2 :])


def collect(array, axis, dim):
    parts = sent_to_all(array, axis)
    return joined_along(parts, dim)


def in_blocks(array, dim, peers):
    before, after = (array.shape[:dim], array.shape[dim + 1 :])
    return jnp.moveaxis(array.reshape(*before, peers, -1, *after), dim, 0)


def summed_on_arrival(array, axis, dim):
    parts = in_blocks(array, dim, lax.axis_size(axis))
    arrived = lax.all_to_all(parts, axis, split_axis=0, concat_axis=0, tiled=True)
    return arrived.astype(jnp.float32).sum(axis=0)


def side_by_side(arrays, axis, dim, along):
    both = jnp.concatenate(arrays, axis=along)
    result, at, gathered = (lax.psum_scatter(both, axis, scatter_dimension=dim, tiled=True), 0, [])
    for a in arrays:
        gathered.append(lax.slice_in_dim(result, at, at + a.shape[along], axis=along))
        at += a.shape[along]
    return tuple(gathered)


def in_one_piece(arrays, axis, dim, along):
    both = jnp.concatenate(arrays, axis=along)
    result, at, gathered = (lax.all_gather(both, axis, axis=dim, tiled=True), 0, [])
    for a in arrays:
        gathered.append(lax.slice_in_dim(result, at, at + a.shape[along], axis=along))
        at += a.shape[along]
    return tuple(gathered)


def from_behind(array, axis, by):
    peers = lax.axis_size(axis)
    pairs = [(i, i + by) for i in range(peers) if 0 <= i + by < peers]
    return lax.ppermute(array, axis, pairs)


def gelu_tanh(values):
    return (
        0.5 * values * (1.0 + jnp.tanh(gelu_coef * (values + 0.044715 * values * values * values)))
    )


def norm_forward(stream, gain, offset):
    width_all = stream.shape[1] * lax.axis_size("tensor")
    totals, squares = in_one((jnp.sum(stream, axis=1), jnp.sum(stream * stream, axis=1)), "tensor")
    mean_row = (totals / width_all)[:, None]
    var_row = (squares / width_all)[:, None] - mean_row * mean_row
    inv_scale = lax.rsqrt(var_row + epsilon)
    normal_part = (stream - mean_row) * inv_scale
    normed = (normal_part * gain + offset).astype(jnp.bfloat16)
    return (collect(normed, "tensor", 1), normal_part, inv_scale)


def norm_backward(partial_term, normal_part, inv_scale, gain):
    width_all = partial_term.shape[1]
    d_normed = summed_on_arrival(partial_term.astype(jnp.bfloat16), "tensor", 1)
    gain_grad = jnp.sum(d_normed * normal_part, axis=0)
    offset_grad = jnp.sum(d_normed, axis=0)
    scaled = d_normed * gain
    first_sum, second_sum = in_one(
        (jnp.sum(scaled, axis=1), jnp.sum(scaled * normal_part, axis=1)), "tensor"
    )
    stream_grad = inv_scale * (
        scaled - first_sum[:, None] / width_all - normal_part * second_sum[:, None] / width_all
    )
    return (stream_grad, gain_grad, offset_grad)


def branch_sum(partial_term):
    return summed_on_arrival(partial_term.astype(jnp.bfloat16), "tensor", 1)


def branch_grad(stream_grad):
    return collect(stream_grad.astype(jnp.bfloat16), "tensor", 1)


def causal_scores(queries, keys_in):
    length = queries.shape[0]
    scale_factor = queries.shape[2] ** (-0.5)
    scores = (
        jnp.einsum("qhe,khe->hqk", queries, keys_in, preferred_element_type=jnp.float32)
        * scale_factor
    )
    causal = lax.broadcasted_iota(jnp.int32, (length, length), 0) >= lax.broadcasted_iota(
        jnp.int32, (length, length), 1
    )
    return (jnp.where(causal[None], scores, masked_value), scale_factor)


def attend(operands):
    queries, keys_in, values_in = operands
    masked, scale_factor = causal_scores(queries, keys_in)
    highest = jnp.max(masked, axis=2, keepdims=True)
    logsum = highest + jnp.log(jnp.sum(jnp.exp(masked - highest), axis=2, keepdims=True))
    weights_low = jnp.exp(masked - logsum).astype(jnp.bfloat16)
    mixture = jnp.einsum("hqk,khe->qhe", weights_low, values_in, preferred_element_type=jnp.float32)
    return (mixture.astype(jnp.bfloat16), logsum[:, :, 0])


def attend_back(operands):
    queries, keys_in, values_in, logsum, mixed_grad = operands
    masked, scale_factor = causal_scores(queries, keys_in)
    probs_full = jnp.exp(masked - logsum[:, :, None])
    probs_grad = jnp.einsum(
        "qhe,khe->hqk", mixed_grad, values_in, preferred_element_type=jnp.float32
    )
    row_dot = jnp.sum(probs_full * probs_grad, axis=2, keepdims=True)
    score_grad = (probs_full * (probs_grad - row_dot)).astype(jnp.bfloat16)
    query_grad = (
        jnp.einsum("hqk,khe->qhe", score_grad, keys_in, preferred_element_type=jnp.float32)
        * scale_factor
    )
    key_grad = (
        jnp.einsum("hqk,qhe->khe", score_grad, queries, preferred_element_type=jnp.float32)
        * scale_factor
    )
    value_grad = jnp.einsum(
        "hqk,qhe->khe",
        probs_full.astype(jnp.bfloat16),
        mixed_grad,
        preferred_element_type=jnp.float32,
    )
    return (
        query_grad.astype(jnp.bfloat16),
        key_grad.astype(jnp.bfloat16),
        value_grad.astype(jnp.bfloat16),
    )


def attention_forward(normed_one, packed_weight, bias_pair, shape_heads, rows_count, width_part):
    packed = jnp.einsum(
        "nd,dcf->ncf", normed_one, packed_weight, preferred_element_type=jnp.float32
    )
    queries = (packed[:, 0] + bias_pair[0]).astype(jnp.bfloat16)
    keys_in = packed[:, 1].astype(jnp.bfloat16)
    values_in = (packed[:, 2] + bias_pair[1]).astype(jnp.bfloat16)
    mixture, logsum = lax.map(
        attend,
        (
            queries.reshape(shape_heads),
            keys_in.reshape(shape_heads),
            values_in.reshape(shape_heads),
        ),
    )
    return (queries, keys_in, values_in, logsum, mixture.reshape(rows_count, width_part))


def attention_backward(branch_one, kept_part, output_weight, shape_heads, rows_count, width_part):
    queries, keys_in, values_in, logsum, mixed_rows, normed_one = kept_part
    output_weight_grad = jnp.einsum(
        "nf,nd->fd", mixed_rows, branch_one, preferred_element_type=jnp.float32
    )
    mixed_grad = jnp.einsum(
        "nd,fd->nf", branch_one, output_weight, preferred_element_type=jnp.float32
    ).astype(jnp.bfloat16)
    query_grad, key_grad, value_grad = lax.map(
        attend_back,
        (
            queries.reshape(shape_heads),
            keys_in.reshape(shape_heads),
            values_in.reshape(shape_heads),
            logsum,
            mixed_grad.reshape(shape_heads),
        ),
    )
    query_rows = query_grad.reshape(rows_count, width_part)
    key_rows = key_grad.reshape(rows_count, width_part)
    value_rows = value_grad.reshape(rows_count, width_part)
    packed_grad = jnp.stack([query_rows, key_rows, value_rows], axis=1)
    bias_pair_grad = jnp.stack(
        [
            jnp.sum(query_rows.astype(jnp.float32), axis=0),
            jnp.sum(value_rows.astype(jnp.float32), axis=0),
        ]
    )
    packed_weight_grad = jnp.einsum(
        "nd,ncf->dcf", normed_one, packed_grad, preferred_element_type=jnp.float32
    )
    return (packed_grad, packed_weight_grad, bias_pair_grad, output_weight_grad)


def layer_forward(stream, weights):
    (
        packed_weight,
        bias_pair,
        output_weight,
        output_bias,
        expand_weight,
        expand_bias,
        contract_weight,
        contract_bias,
        gain_first,
        shift_first,
        gain_second,
        shift_second,
    ) = weights
    seq_count, length, width_part = stream.shape
    rows_count = seq_count * length
    shape_heads = (seq_count, length, width_part // HEAD_DIM, HEAD_DIM)
    stream_rows = stream.reshape(rows_count, width_part)
    normed_one, normal_one, inv_one = norm_forward(stream_rows, gain_first, shift_first)
    queries, keys_in, values_in, logsum, mixed_rows = attention_forward(
        normed_one, packed_weight, bias_pair, shape_heads, rows_count, width_part
    )
    residual = (
        stream_rows
        + branch_sum(jnp.dot(mixed_rows, output_weight, preferred_element_type=jnp.float32))
        + output_bias
    )
    normed_two, normal_two, inv_two = norm_forward(residual, gain_second, shift_second)
    hidden_pre = (
        jnp.dot(normed_two, expand_weight, preferred_element_type=jnp.float32) + expand_bias
    )
    hidden = gelu_tanh(hidden_pre).astype(jnp.bfloat16)
    result = (
        residual
        + branch_sum(jnp.dot(hidden, contract_weight, preferred_element_type=jnp.float32))
        + contract_bias
    )
    kept_values = (
        normed_one,
        normal_one,
        inv_one,
        queries,
        keys_in,
        values_in,
        logsum,
        mixed_rows,
        normed_two,
        normal_two,
        inv_two,
        hidden_pre,
        hidden,
    )
    return (result.reshape(stream.shape), kept_values)


def layer_backward(out_grad, kept_values, weights):
    (
        packed_weight,
        bias_pair,
        output_weight,
        output_bias,
        expand_weight,
        expand_bias,
        contract_weight,
        contract_bias,
        gain_first,
        shift_first,
        gain_second,
        shift_second,
    ) = weights
    (
        normed_one,
        normal_one,
        inv_one,
        queries,
        keys_in,
        values_in,
        logsum,
        mixed_rows,
        normed_two,
        normal_two,
        inv_two,
        hidden_pre,
        hidden,
    ) = kept_values
    seq_count, length, width_part = out_grad.shape
    rows_count = seq_count * length
    shape_heads = (seq_count, length, width_part // HEAD_DIM, HEAD_DIM)
    grad_rows = out_grad.reshape(rows_count, width_part)
    contract_bias_grad = jnp.sum(grad_rows, axis=0)
    branch_two = branch_grad(grad_rows)
    contract_weight_grad = jnp.einsum(
        "nf,nd->fd", hidden, branch_two, preferred_element_type=jnp.float32
    )
    hidden_grad = jnp.einsum(
        "nd,fd->nf", branch_two, contract_weight, preferred_element_type=jnp.float32
    )
    pre_grad = jax.vjp(gelu_tanh, hidden_pre)[1](hidden_grad)[0].astype(jnp.bfloat16)
    expand_bias_grad = jnp.sum(pre_grad.astype(jnp.float32), axis=0)
    expand_weight_grad = jnp.einsum(
        "nd,nf->df", normed_two, pre_grad, preferred_element_type=jnp.float32
    )
    second_grad, gain_second_grad, shift_second_grad = norm_backward(
        jnp.einsum("nf,df->nd", pre_grad, expand_weight, preferred_element_type=jnp.float32),
        normal_two,
        inv_two,
        gain_second,
    )
    residual_grad = grad_rows + second_grad
    output_bias_grad = jnp.sum(residual_grad, axis=0)
    branch_one = branch_grad(residual_grad)
    packed_grad, packed_weight_grad, bias_pair_grad, output_weight_grad = attention_backward(
        branch_one,
        (queries, keys_in, values_in, logsum, mixed_rows, normed_one),
        output_weight,
        shape_heads,
        rows_count,
        width_part,
    )
    first_grad, gain_first_grad, shift_first_grad = norm_backward(
        jnp.einsum("ncf,dcf->nd", packed_grad, packed_weight, preferred_element_type=jnp.float32),
        normal_one,
        inv_one,
        gain_first,
    )
    input_grad = (residual_grad + first_grad).reshape(out_grad.shape)
    return (
        input_grad,
        (
            packed_weight_grad,
            bias_pair_grad,
            output_weight_grad,
            output_bias_grad,
            expand_weight_grad,
            expand_bias_grad,
            contract_weight_grad,
            contract_bias_grad,
            gain_first_grad,
            shift_first_grad,
            gain_second_grad,
            shift_second_grad,
        ),
    )


def sum_at_end(grads):
    (
        part_packed,
        part_pair,
        part_outmat,
        part_outbias,
        part_expmat,
        part_expbias,
        part_conmat,
        part_conbias,
        part_gainone,
        part_shiftone,
        part_gaintwo,
        part_shifttwo,
    ) = grads
    return (
        lax.psum_scatter(
            part_packed[None].astype(jnp.bfloat16), "dp", scatter_dimension=1, tiled=True
        ).astype(jnp.float32),
        lax.psum_scatter(
            part_pair[None].astype(jnp.bfloat16), "dp", scatter_dimension=2, tiled=True
        ).astype(jnp.float32),
        lax.psum_scatter(
            part_outmat[None].astype(jnp.bfloat16), "dp", scatter_dimension=2, tiled=True
        ).astype(jnp.float32),
        lax.psum_scatter(
            part_outbias[None].astype(jnp.bfloat16), "dp", scatter_dimension=1, tiled=True
        ).astype(jnp.float32),
        lax.psum_scatter(
            part_expmat[None].astype(jnp.bfloat16), "dp", scatter_dimension=1, tiled=True
        ).astype(jnp.float32),
        lax.psum_scatter(
            part_expbias[None].astype(jnp.bfloat16), "dp", scatter_dimension=1, tiled=True
        ).astype(jnp.float32),
        lax.psum_scatter(
            part_conmat[None].astype(jnp.bfloat16), "dp", scatter_dimension=2, tiled=True
        ).astype(jnp.float32),
        *tuple(
            (
                part.astype(jnp.float32)
                for part in side_by_side(
                    (
                        part_conbias[None].astype(jnp.bfloat16),
                        part_gainone[None].astype(jnp.bfloat16),
                        part_shiftone[None].astype(jnp.bfloat16),
                        part_gaintwo[None].astype(jnp.bfloat16),
                        part_shifttwo[None].astype(jnp.bfloat16),
                    ),
                    "dp",
                    1,
                    0,
                )
            )
        ),
    )


def shards(
    inputs,
    cotangent,
    packed_weight,
    bias_pair,
    output_weight,
    output_bias,
    expand_weight,
    expand_bias,
    contract_weight,
    contract_bias,
    gain_first,
    shift_first,
    gain_second,
    shift_second,
):
    gathered = (
        lax.all_gather(packed_weight, "dp", axis=1, tiled=True),
        lax.all_gather(bias_pair, "dp", axis=2, tiled=True),
        lax.all_gather(output_weight, "dp", axis=2, tiled=True),
        lax.all_gather(output_bias, "dp", axis=1, tiled=True),
        lax.all_gather(expand_weight, "dp", axis=1, tiled=True),
        lax.all_gather(expand_bias, "dp", axis=1, tiled=True),
        lax.all_gather(contract_weight, "dp", axis=2, tiled=True),
        *in_one_piece(
            (contract_bias, gain_first, shift_first, gain_second, shift_second), "dp", 1, 0
        ),
    )
    weights = tuple((member[0] for member in gathered))
    is_first = lax.axis_index("section") == 0
    micro_count = inputs.shape[0]
    zero_block = jnp.zeros_like(inputs[0])
    received = zero_block
    returned = zero_block
    outputs_list = []
    kept_list = []
    backs_list = []
    grad_total = None
    for tick_index in range(micro_count + 2):
        if tick_index <= micro_count:
            own_input = inputs[tick_index] if tick_index < micro_count else zero_block
            stream = jnp.where(is_first, own_input, received)
            result, kept_values = layer_forward(stream, weights)
            outputs_list.append(result)
            kept_list.append(kept_values)
            if tick_index < micro_count:
                received = from_behind(result.astype(jnp.bfloat16), "section", 1).astype(
                    result.dtype
                )
        if tick_index >= 1:
            own_grad = cotangent[tick_index - 1] if tick_index - 1 < micro_count else zero_block
            out_grad = jnp.where(is_first, returned, own_grad)
            early_kept = kept_list[tick_index - 2] if tick_index >= 2 else kept_list[tick_index]
            late_kept = (
                kept_list[tick_index] if tick_index <= micro_count else kept_list[tick_index - 2]
            )
            chosen = jax.tree.map(
                lambda early_one, late_one: jnp.where(is_first, early_one, late_one),
                early_kept,
                late_kept,
            )
            input_grad, grads = layer_backward(out_grad, chosen, weights)
            backs_list.append(input_grad)
            if tick_index <= micro_count:
                returned = from_behind(input_grad.astype(jnp.bfloat16), "section", -1).astype(
                    input_grad.dtype
                )
            grad_total = grads if grad_total is None else jax.tree.map(jnp.add, grad_total, grads)
    reduced = sum_at_end(grad_total)
    section_outputs = jnp.stack(
        [
            jnp.where(is_first, outputs_list[slot_index], outputs_list[slot_index + 1])
            for slot_index in range(micro_count)
        ]
    )[None]
    section_grads = jnp.stack(
        [
            jnp.where(is_first, backs_list[slot_index + 1], backs_list[slot_index])
            for slot_index in range(micro_count)
        ]
    )[None]
    return (section_outputs, section_grads) + tuple(reduced)


def solution(mesh):
    in_specs = (
        P(None, "dp", None, "tensor"),
        P(None, "dp", None, "tensor"),
        P("section", "dp", None, "tensor"),
        P("section", None, ("tensor", "dp")),
        P("section", "tensor", "dp"),
        P("section", ("tensor", "dp")),
        P("section", "dp", "tensor"),
        P("section", ("tensor", "dp")),
        P("section", "tensor", "dp"),
        P("section", ("tensor", "dp")),
        P("section", ("tensor", "dp")),
        P("section", ("tensor", "dp")),
        P("section", ("tensor", "dp")),
        P("section", ("tensor", "dp")),
    )
    out_specs = (
        P("section", None, "dp", None, "tensor"),
        P("section", None, "dp", None, "tensor"),
        P("section", "dp", None, "tensor"),
        P("section", None, ("tensor", "dp")),
        P("section", "tensor", "dp"),
        P("section", ("tensor", "dp")),
        P("section", "dp", "tensor"),
        P("section", ("tensor", "dp")),
        P("section", "tensor", "dp"),
        P("section", ("tensor", "dp")),
        P("section", ("tensor", "dp")),
        P("section", ("tensor", "dp")),
        P("section", ("tensor", "dp")),
        P("section", ("tensor", "dp")),
    )
    return jax.shard_map(shards, mesh=mesh, in_specs=in_specs, out_specs=out_specs, check_vma=False)
```

profile of v0, /device:TPU:0, one launch (start us, length us, event | category | flops | bytes accessed | tf_op | source)
XLA Modules:
  0.0 1031.4 jit_solution(10585981143405735494)
XLA Ops:
  10.2 6.3 all-to-all-start
  17.3 12.1 %all-gather = bf16[8,16,5]{1,2,0:T(8,128)(2,1)S(1)} all-gather(bf16[1,16,5]{1,2,0:T(8,128)(2,1)S(1)} %bitcast.802), channel_id=1, replica_groups=mesh['section'=2,'dp'=8,'tensor'=8] {'dp'}, dimensions={0}, use_global_device_ids=true | all-gather | bytes 1440 | tf_op jit(solution)/shard_map/all_gather | solution.py:66
  32.3 5.8 all-to-all-start.1
  38.2 12.7 %all_gather.26 = bf16[1,2,128]{1,0,2:T(2,128)(2,1)S(1)} all-gather(bf16[1,2,16]{1,0,2:T(2,128)(2,1)S(1)} %copy.263), channel_id=1, replica_groups=mesh['section'=2,'dp'=8,'tensor'=8] {'dp'}, dimensions={2}, use_global_device_ids=true | all-gather | bytes 576 | tf_op jit(solution)/shard_map/all_gather | solution.py:445
  53.4 11.5 %all_gather.27 = bf16[1,128,1024]{2,1,0:T(8,128)(2,1)S(1)} all-gather(bf16[1,128,128]{2,1,0:T(8,128)(2,1)S(1)} %copy-done.125), channel_id=1, replica_groups=mesh['section'=2,'dp'=8,'tensor'=8] {'dp'}, dimensions={2}, use_global_device_ids=true | all-gather | bytes 294912 | tf_op jit(solution)/shard_map/all_gather | solution.py:446
  65.1 14.7 %all_gather.25 = bf16[1,1024,3,128]{1,3,2,0:T(8,128)(2,1)} all-gather(bf16[1,128,3,128]{1,3,2,0:T(8,128)(2,1)S(1)} %copy.262), channel_id=1, replica_groups=mesh['section'=2,'dp'=8,'tensor'=8] {'dp'}, dimensions={1}, use_global_device_ids=true | all-gather | bytes 884736 | tf_op jit(solution)/shard_map/all_gather | solution.py:444
  88.2 5.8 all-to-all-start.2
  97.2 14.0 %all-reduce.2 = (bf16[128]{0:T(256)(128)(2,1)S(1)}, bf16[512]{0:T(512)(128)(2,1)S(1)}) all-reduce(bf16[128]{0:T(256)(128)(2,1)S(1)} %dynamic-update-slice, bf16[512]{0:T(512)(128)(2,1)S(1)} %dynamic-update-slice.1), channel_id=1, replica_groups=mesh['section'=2,'dp'=8,'tensor'=8] {'dp'}, use_global_device_ids=true, to_apply=%add | all-reduce | flops 640 | bytes 2560
  122.2 5.6 all-to-all-done.3
  130.1 4.3 all-to-all-start.4
  134.5 19.5 %all-to-all-done.4 = bf16[8,768,128]{2,1,0:T(8,128)(2,1)} async-done(((bf16[8,768,128]{2,1,0:T(8,128)(2,1)}), bf16[8,768,128]{2,1,0:T(8,128)(2,1)}, u32[]{:S(2)}, u32[]{:S(2)}) %all-to-all-start.4) | async-done | bytes 1572896 | tf_op jit(solution)/shard_map/all_to_all | solution.py:18
  160.9 25.1 %all_to_all.192 = bf16[8,768,128]{2,1,0:T(8,128)(2,1)S(1)} all-to-all(bf16[8,768,128]{2,1,0:T(8,128)(2,1)S(1)} %bitcast.739), channel_id=1, replica_groups=mesh['section'=2,'dp'=8,'tensor'=8] {'tensor'}, dimensions={0} | all-to-all | bytes 3145728 | tf_op jit(solution)/shard_map/all_to_all | solution.py:51
  187.1 4.6 collective-permute-start
  195.3 8.7 all_to_all.193
  205.1 20.4 %all_to_all.194 = bf16[8,768,128]{2,1,0:T(8,128)(2,1)S(1)} all-to-all(bf16[8,768,128]{2,1,0:T(8,128)(2,1)S(1)} %broadcast_in_dim.290), channel_id=1, replica_groups=mesh['section'=2,'dp'=8,'tensor'=8] {'tensor'}, dimensions={0} | all-to-all | bytes 3145728 | tf_op jit(solution)/shard_map/all_to_all | solution.py:18
  232.6 19.8 %all_to_all.195 = bf16[8,768,128]{2,1,0:T(8,128)(2,1)S(1)} all-to-all(bf16[8,768,128]{2,1,0:T(8,128)(2,1)S(1)} %bitcast.740), channel_id=1, replica_groups=mesh['section'=2,'dp'=8,'tensor'=8] {'tensor'}, dimensions={0} | all-to-all | bytes 3145728 | tf_op jit(solution)/shard_map/all_to_all | solution.py:51
  253.0 8.8 all_to_all.196
  263.6 4.4 all-to-all-start.10
  268.2 13.7 %all-to-all-done.10 = bf16[8,768,128]{1,2,0:T(8,128)(2,1)} async-done(((bf16[8,768,128]{1,2,0:T(8,128)(2,1)}), bf16[8,768,128]{1,2,0:T(8,128)(2,1)}, u32[]{:S(2)}, u32[]{:S(2)}) %all-to-all-start.10) | async-done | bytes 1572896 | tf_op jit(solution)/shard_map/all_to_all | solution.py:18
  283.2 4.7 all-to-all-start.18
  291.8 12.4 %all-to-all-done.18 = bf16[8,768,128]{1,2,0:T(8,128)(2,1)} async-done(((bf16[8,768,128]{1,2,0:T(8,128)(2,1)}), bf16[8,768,128]{1,2,0:T(8,128)(2,1)}, u32[]{:S(2)}, u32[]{:S(2)}) %all-to-all-start.18) | async-done | bytes 1572896 | tf_op jit(solution)/shard_map/all_to_all | solution.py:18
  304.1 5.0 convert_reduce_fusion.20
  311.6 4.3 all-to-all-start.19
  320.2 14.9 %all-to-all-done.19 = bf16[8,768,128]{2,1,0:T(8,128)(2,1)} async-done(((bf16[8,768,128]{2,1,0:T(8,128)(2,1)}), bf16[8,768,128]{2,1,0:T(8,128)(2,1)}, u32[]{:S(2)}, u32[]{:S(2)}) %all-to-all-start.19) | async-done | bytes 1572896 | tf_op jit(solution)/shard_map/all_to_all | solution.py:51
  343.3 16.5 %all-to-all-done.11 = bf16[8,768,128]{2,1,0:T(8,128)(2,1)} async-done(((bf16[8,768,128]{2,1,0:T(8,128)(2,1)}), bf16[8,768,128]{2,1,0:T(8,128)(2,1)}, u32[]{:S(2)}, u32[]{:S(2)}) %all-to-all-start.11) | async-done | bytes 1572896 | tf_op jit(solution)/shard_map/all_to_all | solution.py:51
  367.5 6.5 collective-permute-start.1
  379.0 4.8 all-to-all-start.12
  385.0 5.1 all-to-all-done.12
  395.9 16.9 %all-to-all-done.21 = bf16[8,768,128]{1,2,0:T(8,128)(2,1)S(1)} async-done(((bf16[8,768,128]{1,2,0:T(8,128)(2,1)}), bf16[8,768,128]{1,2,0:T(8,128)(2,1)S(1)}, u32[]{:S(2)}, u32[]{:S(2)}) %all-to-all-start.21) | async-done | bytes 1572896 | tf_op jit(solution)/shard_map/all_to_all | solution.py:18
  414.4 4.5 all-to-all-start.13
  419.3 19.5 %all-to-all-done.13 = bf16[8,768,128]{2,1,0:T(8,128)(2,1)} async-done(((bf16[8,768,128]{2,1,0:T(8,128)(2,1)}), bf16[8,768,128]{2,1,0:T(8,128)(2,1)}, u32[]{:S(2)}, u32[]{:S(2)}) %all-to-all-start.13) | async-done | bytes 1572896 | tf_op jit(solution)/shard_map/all_to_all | solution.py:18
  454.0 4.3 all-to-all-start.14
  458.3 5.1 convert_reduce_fusion.25
  484.7 18.4 %all-to-all-done.22 = bf16[8,768,128]{2,1,0:T(8,128)(2,1)S(1)} async-done(((bf16[8,768,128]{2,1,0:T(8,128)(2,1)}), bf16[8,768,128]{2,1,0:T(8,128)(2,1)S(1)}, u32[]{:S(2)}, u32[]{:S(2)}) %all-to-all-start.22) | async-done | bytes 1572896 | tf_op jit(solution)/shard_map/all_to_all | solution.py:51
  518.4 5.8 all-to-all-done.23
  525.7 4.4 all-to-all-start.16
  534.2 20.1 %collective-permute-done.2 = bf16[1,768,128]{2,1,0:T(8,128)(2,1)S(1)} collective-permute-done((bf16[1,768,128]{2,1,0:T(8,128)(2,1)S(1)}, bf16[1,768,128]{2,1,0:T(8,128)(2,1)S(1)}, u32[]{:S(2)}, u32[]{:S(2)}) %collective-permute-start.2) | collective-permute-done | bytes 196640 | tf_op jit(solution)/shard_map/ppermute | solution.py:76
  555.8 4.9 all-to-all-start.24
  564.5 13.2 %all-to-all-done.24 = bf16[8,768,128]{1,2,0:T(8,128)(2,1)} async-done(((bf16[8,768,128]{1,2,0:T(8,128)(2,1)}), bf16[8,768,128]{1,2,0:T(8,128)(2,1)}, u32[]{:S(2)}, u32[]{:S(2)}) %all-to-all-start.24) | async-done | bytes 1572896 | tf_op jit(solution)/shard_map/all_to_all | solution.py:18
  577.7 5.1 convert_reduce_fusion.19
  584.2 24.2 %all_to_all.197 = bf16[8,768,128]{2,1,0:T(8,128)(2,1)S(1)} all-to-all(bf16[8,768,128]{2,1,0:T(8,128)(2,1)S(1)} %bitcast.741), channel_id=1, replica_groups=mesh['section'=2,'dp'=8,'tensor'=8] {'tensor'}, dimensions={0} | all-to-all | bytes 3145728 | tf_op jit(solution)/shard_map/all_to_all | solution.py:51
  611.1 8.9 all_to_all.198
  632.1 13.8 %all-to-all-done.27 = bf16[8,768,128]{1,2,0:T(8,128)(2,1)S(1)} async-done(((bf16[8,768,128]{1,2,0:T(8,128)(2,1)}), bf16[8,768,128]{1,2,0:T(8,128)(2,1)S(1)}, u32[]{:S(2)}, u32[]{:S(2)}) %all-to-all-start.27) | async-done | bytes 1572896 | tf_op jit(solution)/shard_map/all_to_all | solution.py:18
  646.3 5.1 convert_reduce_fusion.23
  658.8 24.9 %all_to_all.199 = bf16[8,768,128]{2,1,0:T(8,128)(2,1)S(1)} all-to-all(bf16[8,768,128]{2,1,0:T(8,128)(2,1)S(1)} %bitcast.742), channel_id=1, replica_groups=mesh['section'=2,'dp'=8,'tensor'=8] {'tensor'}, dimensions={0} | all-to-all | bytes 3145728 | tf_op jit(solution)/shard_map/all_to_all | solution.py:51
  687.3 8.7 all_to_all.200
  702.4 7.8 collective-permute-done.3
  710.5 20.5 %all_to_all.201 = bf16[8,768,128]{1,2,0:T(8,128)(2,1)S(1)} all-to-all(bf16[8,768,128]{1,2,0:T(8,128)(2,1)S(1)} %broadcast_in_dim.307), channel_id=1, replica_groups=mesh['section'=2,'dp'=8,'tensor'=8] {'tensor'}, dimensions={0} | all-to-all | bytes 3145728 | tf_op jit(solution)/shard_map/all_to_all | solution.py:18
  740.1 4.5 fusion.239
  744.6 4.7 fusion.127
  749.3 6.1 all-to-all-done.31
  764.5 5.4 all-to-all-done.32
  771.4 5.4 fusion.85
  776.7 6.0 copy.355
  791.6 4.4 all-to-all-start.33
  833.4 4.4 all-to-all-start.34
  852.5 5.4 all-to-all-done.34
  866.1 5.7 all-to-all-done.35
  883.7 4.6 fusion.86
  888.4 7.2 all-to-all-done.17
  903.1 23.7 %reduce-scatter.25.cloned.1.call-done = bf16[16,2]{1,0:T(8,128)(2,1)} async-done(((bf16[128,2]{1,0:T(8,128)(2,1)}), bf16[16,2]{1,0:T(8,128)(2,1)}) %reduce-scatter.25.cloned.1.call-update) | async-done | bytes 80
  928.2 30.4 %reduce-scatter.27.cloned.1.call-done = bf16[128,128]{1,0:T(8,128)(2,1)} async-done(((bf16[1024,128]{1,0:T(8,128)(2,1)}), bf16[128,128]{1,0:T(8,128)(2,1)}) %reduce-scatter.27.cloned.1.call-update) | async-done | bytes 32784
  961.1 29.0 %reduce-scatter.35.cloned.1.call-done = bf16[16,5]{1,0:T(8,128)(2,1)} async-done(((bf16[128,5]{1,0:T(8,128)(2,1)}), bf16[16,5]{1,0:T(8,128)(2,1)}) %reduce-scatter.35.cloned.1.call-update) | async-done | bytes 176
  994.0 28.6 %reduce-scatter.21.cloned.1.call-done = bf16[1,128,3,128]{3,1,2,0:T(8,128)(2,1)} async-done(((bf16[1,1024,3,128]{3,1,2,0:T(8,128)(2,1)}), bf16[1,128,3,128]{3,1,2,0:T(8,128)(2,1)}) %reduce-scatter.21.cloned.1.call-update) | async-done | bytes 98320 | tf_op jit(solution)/shard_map/reduce_scatter | solution.py:386
  (673 shorter events, 308.8 us)
Async XLA Ops:
  10.2 19.3 %all-to-all-start = ((f32[8,1,1536]{2,1,0:T(1,128)}), f32[8,1,1536]{2,1,0:T(1,128)S(1)}, u32[]{:S(2)}, u32[]{:S(2)}) async-start(f32[8,1,1536]{2,1,0:T(1,128)} %broadcast_in_dim.283), calls=%async_computation | async-start | bytes 98304 | tf_op jit(solution)/shard_map/all_to_all | solution.py:18
  29.5 232.4 %copy-start.130 = (f32[128]{0:T(128)}, f32[128]{0:T(128)S(1)}, u32[]{:S(2)}) copy-start(f32[128]{0:T(128)S(1)} %get-tuple-element.255) | copy-start | bytes 1540
  29.5 336.3 %copy-start.128 = (f32[128]{0:T(128)}, f32[128]{0:T(128)S(1)}, u32[]{:S(2)}) copy-start(f32[128]{0:T(128)S(1)} %get-tuple-element.254) | copy-start | bytes 1540
  29.5 354.3 %copy-start.93 = (f32[128]{0:T(128)}, f32[128]{0:T(128)S(1)}, u32[]{:S(2)}) copy-start(f32[128]{0:T(128)S(1)} %get-tuple-element.253) | copy-start | bytes 1540
  29.5 366.1 %copy-start.113 = (f32[128]{0:T(128)}, f32[128]{0:T(128)S(1)}, u32[]{:S(2)}) copy-start(f32[128]{0:T(128)S(1)} %get-tuple-element.257) | copy-start | bytes 1540
  32.3 47.5 %all-to-all-start.1 = ((bf16[8,768,128]{2,1,0:T(8,128)(2,1)}), bf16[8,768,128]{2,1,0:T(8,128)(2,1)S(1)}, u32[]{:S(2)}, u32[]{:S(2)}) async-start(bf16[8,768,128]{2,1,0:T(8,128)(2,1)} %broadcast_in_dim.284), calls=%async_computation.1 | async-start | bytes 3145728 | tf_op jit(solution)/shard_map/all_to_all | solution.py:18
  53.2 173.7 %copy-start.132 = (f32[2,64]{1,0:T(2,128)}, f32[2,64]{1,0:T(2,128)S(1)}, u32[]{:S(2)}) copy-start(f32[2,64]{1,0:T(2,128)S(1)} %reshape.1792) | copy-start | bytes 1540
  64.9 353.9 %copy-start.10 = (bf16[1,128,1024]{2,1,0:T(8,128)(2,1)}, bf16[1,128,1024]{2,1,0:T(8,128)(2,1)S(1)}, u32[]{:S(2)}) copy-start(bf16[1,128,1024]{2,1,0:T(8,128)(2,1)S(1)} %all_gather.27) | copy-start | bytes 786436
  88.2 26.9 %all-to-all-start.2 = ((bf16[8,768,128]{2,1,0:T(8,128)(2,1)}), bf16[8,768,128]{2,1,0:T(8,128)(2,1)}, u32[]{:S(2)}, u32[]{:S(2)}) async-start(bf16[8,768,128]{2,1,0:T(8,128)(2,1)} %bitcast.720), calls=%async_computation.2 | async-start | bytes 3145728 | tf_op jit(solution)/shard_map/all_to_all | solution.py:51
  94.1 22.7 %copy-start.13 = (f32[2,1,768,128]{3,2,1,0:T(8,128)S(1)}, f32[2,1,768,128]{3,2,1,0:T(8,128)}, u32[]{:S(2)}) copy-start(f32[2,1,768,128]{3,2,1,0:T(8,128)} %param.14) | copy-start | bytes 2359300
  94.1 40.4 %all-gather.4.cloned.1.call-start = ((), (), s32[]{:S(2)}) async-start(), calls=%async_computation.44 | async-start | bytes 1179648 | tf_op jit(solution)/shard_map/all_gather | solution.py:448
  111.2 254.6 %copy-start.109 = (f32[128]{0:T(128)}, f32[128]{0:T(128)S(1)}, u32[]{:S(2)}) copy-start(f32[128]{0:T(128)S(1)} %add.756) | copy-start | bytes 1540
  116.8 69.4 %copy-start.25 = (f32[768,128]{1,0:T(8,128)}, f32[768,128]{1,0:T(8,128)S(1)}, u32[]{:S(2)}) copy-start(f32[768,128]{1,0:T(8,128)S(1)} %convert_reduce_fusion.17) | copy-start | bytes 1179652
  117.9 9.9 all-to-all-start.3
  121.5 36.3 %all-gather.6.cloned.1.call-start = ((), (), s32[]{:S(2)}) async-start(), calls=%async_computation.45 | async-start | bytes 1179648 | tf_op jit(solution)/shard_map/all_gather | solution.py:450
  130.1 23.8 %all-to-all-start.4 = ((bf16[8,768,128]{2,1,0:T(8,128)(2,1)}), bf16[8,768,128]{2,1,0:T(8,128)(2,1)}, u32[]{:S(2)}, u32[]{:S(2)}) async-start(bf16[8,768,128]{2,1,0:T(8,128)(2,1)} %broadcast_in_dim.288), calls=%async_computation.4 | async-start | bytes 3145728 | tf_op jit(solution)/shard_map/all_to_all | solution.py:18
  134.4 153.4 %copy-start.149 = (f32[512]{0:T(512)}, f32[512]{0:T(512)S(1)}, u32[]{:S(2)}) copy-start(f32[512]{0:T(512)S(1)} %add.757) | copy-start | bytes 6148
  187.1 7.8 collective-permute-start
  252.6 113.2 %copy-start.15 = (f32[768,128]{1,0:T(8,128)}, f32[768,128]{1,0:T(8,128)S(1)}, u32[]{:S(2)}) copy-start(f32[768,128]{1,0:T(8,128)S(1)} %convert_reduce_fusion.15) | copy-start | bytes 1179652
  252.9 130.9 %copy-start.2 = (f32[768,128]{1,0:T(8,128)}, f32[768,128]{1,0:T(8,128)S(1)}, u32[]{:S(2)}) copy-start(f32[768,128]{1,0:T(8,128)S(1)} %get-tuple-element.206) | copy-start | bytes 1179652
  263.6 18.3 %all-to-all-start.10 = ((bf16[8,768,128]{1,2,0:T(8,128)(2,1)}), bf16[8,768,128]{1,2,0:T(8,128)(2,1)}, u32[]{:S(2)}, u32[]{:S(2)}) async-start(bf16[8,768,128]{1,2,0:T(8,128)(2,1)} %broadcast_in_dim.292), calls=%async_computation.10 | async-start | bytes 3145728 | tf_op jit(solution)/shard_map/all_to_all | solution.py:18
  283.2 21.0 %all-to-all-start.18 = ((bf16[8,768,128]{1,2,0:T(8,128)(2,1)}), bf16[8,768,128]{1,2,0:T(8,128)(2,1)}, u32[]{:S(2)}, u32[]{:S(2)}) async-start(bf16[8,768,128]{1,2,0:T(8,128)(2,1)} %broadcast_in_dim.299), calls=%async_computation.18 | async-start | bytes 3145728 | tf_op jit(solution)/shard_map/all_to_all | solution.py:18
  311.6 23.5 %all-to-all-start.19 = ((bf16[8,768,128]{2,1,0:T(8,128)(2,1)}), bf16[8,768,128]{2,1,0:T(8,128)(2,1)}, u32[]{:S(2)}, u32[]{:S(2)}) async-start(bf16[8,768,128]{2,1,0:T(8,128)(2,1)} %bitcast.738), calls=%async_computation.19 | async-start | bytes 3145728 | tf_op jit(solution)/shard_map/all_to_all | solution.py:51
  335.1 24.7 %all-to-all-start.11 = ((bf16[8,768,128]{2,1,0:T(8,128)(2,1)}), bf16[8,768,128]{2,1,0:T(8,128)(2,1)}, u32[]{:S(2)}, u32[]{:S(2)}) async-start(bf16[8,768,128]{2,1,0:T(8,128)(2,1)} %bitcast.735), calls=%async_computation.11 | async-start | bytes 3145728 | tf_op jit(solution)/shard_map/all_to_all | solution.py:51
  342.5 41.3 %copy-start.23 = (f32[768,128]{1,0:T(8,128)}, f32[768,128]{1,0:T(8,128)S(1)}, u32[]{:S(2)}) copy-start(f32[768,128]{1,0:T(8,128)S(1)} %get-tuple-element.116) | copy-start | bytes 1179652
  360.5 13.5 %all-to-all-start.20 = ((f32[8,1,1536]{2,1,0:T(1,128)}), f32[8,1,1536]{2,1,0:T(1,128)S(1)}, u32[]{:S(2)}, u32[]{:S(2)}) async-start(f32[8,1,1536]{2,1,0:T(1,128)} %broadcast_in_dim.300), calls=%async_computation.20 | async-start | bytes 98304 | tf_op jit(solution)/shard_map/all_to_all | solution.py:18
  367.5 10.5 %collective-permute-start.1 = (bf16[1,768,128]{2,1,0:T(8,128)(2,1)S(1)}, bf16[1,768,128]{2,1,0:T(8,128)(2,1)S(1)}, u32[]{:S(2)}, u32[]{:S(2)}) collective-permute-start(bf16[1,768,128]{2,1,0:T(8,128)(2,1)S(1)} %convert_element_type.629), channel_id=1, source_target_pairs={{0,64},{1,65},{2,66},{3,67},{4,68},{5,69},{6,70},{7,71},{8,72},{9,... | collective-permute-start | bytes 589832 | tf_op jit(solution)/shard_map/ppermute | solution.py:76
  379.0 11.1 %all-to-all-start.12 = ((f32[8,1,1536]{2,1,0:T(1,128)}), f32[8,1,1536]{2,1,0:T(1,128)S(1)}, u32[]{:S(2)}, u32[]{:S(2)}) async-start(f32[8,1,1536]{2,1,0:T(1,128)} %broadcast_in_dim.294), calls=%async_computation.12 | async-start | bytes 98304 | tf_op jit(solution)/shard_map/all_to_all | solution.py:18
  391.4 21.5 %all-to-all-start.21 = ((bf16[8,768,128]{1,2,0:T(8,128)(2,1)}), bf16[8,768,128]{1,2,0:T(8,128)(2,1)S(1)}, u32[]{:S(2)}, u32[]{:S(2)}) async-start(bf16[8,768,128]{1,2,0:T(8,128)(2,1)} %broadcast_in_dim.301), calls=%async_computation.21 | async-start | bytes 3145728 | tf_op jit(solution)/shard_map/all_to_all | solution.py:18
  414.4 24.4 %all-to-all-start.13 = ((bf16[8,768,128]{2,1,0:T(8,128)(2,1)}), bf16[8,768,128]{2,1,0:T(8,128)(2,1)}, u32[]{:S(2)}, u32[]{:S(2)}) async-start(bf16[8,768,128]{2,1,0:T(8,128)(2,1)} %broadcast_in_dim.295), calls=%async_computation.13 | async-start | bytes 3145728 | tf_op jit(solution)/shard_map/all_to_all | solution.py:18
  419.2 23.0 %copy-start.69 = (bf16[768,128]{0,1:T(8,128)(2,1)}, bf16[768,128]{0,1:T(8,128)(2,1)S(1)}, u32[]{:S(2)}) copy-start(bf16[768,128]{0,1:T(8,128)(2,1)S(1)} %convolution_convert_fusion.11) | copy-start | bytes 589828
  454.0 24.8 %all-to-all-start.14 = ((bf16[8,768,128]{2,1,0:T(8,128)(2,1)}), bf16[8,768,128]{2,1,0:T(8,128)(2,1)}, u32[]{:S(2)}, u32[]{:S(2)}) async-start(bf16[8,768,128]{2,1,0:T(8,128)(2,1)} %bitcast.734), calls=%async_computation.14 | async-start | bytes 3145728 | tf_op jit(solution)/shard_map/all_to_all | solution.py:51
  478.9 24.2 %all-to-all-start.22 = ((bf16[8,768,128]{2,1,0:T(8,128)(2,1)}), bf16[8,768,128]{2,1,0:T(8,128)(2,1)S(1)}, u32[]{:S(2)}, u32[]{:S(2)}) async-start(bf16[8,768,128]{2,1,0:T(8,128)(2,1)} %bitcast.736), calls=%async_computation.22 | async-start | bytes 3145728 | tf_op jit(solution)/shard_map/all_to_all | solution.py:51
  484.3 211.7 %copy-start.8 = (f32[768,128]{1,0:T(8,128)}, f32[768,128]{1,0:T(8,128)S(1)}, u32[]{:S(2)}) copy-start(f32[768,128]{1,0:T(8,128)S(1)} %convert_reduce_fusion.13) | copy-start | bytes 1179652
  484.4 25.5 %copy-start.87 = (f32[768]{0:T(1024)S(1)}, f32[768]{0:T(1024)}, u32[]{:S(2)}) copy-start(f32[768]{0:T(1024)} %copy-done.86) | copy-start | bytes 9220
  484.4 25.5 %copy-start.90 = (f32[768]{0:T(1024)S(1)}, f32[768]{0:T(1024)}, u32[]{:S(2)}) copy-start(f32[768]{0:T(1024)} %copy-done.89) | copy-start | bytes 9220
  484.4 25.5 %copy-start.114 = (f32[128]{0:T(128)S(1)}, f32[128]{0:T(128)}, u32[]{:S(2)}) copy-start(f32[128]{0:T(128)} %copy-done.113) | copy-start | bytes 1540
  484.7 33.4 %copy-start.96 = (f32[1536]{0:T(1024)S(1)}, f32[1536]{0:T(1024)}, u32[]{:S(2)}) copy-start(f32[1536]{0:T(1024)} %copy-done.95) | copy-start | bytes 18436
  503.7 10.1 all-to-all-start.15
  514.5 9.8 all-to-all-start.23
  518.1 102.0 %copy-start.122 = (f32[768]{0:T(1024)}, f32[768]{0:T(1024)S(1)}, u32[]{:S(2)}) copy-start(f32[768]{0:T(1024)S(1)} %get-tuple-element.231) | copy-start | bytes 9220
  525.7 28.8 %all-to-all-start.16 = ((bf16[8,768,128]{2,1,0:T(8,128)(2,1)}), bf16[8,768,128]{2,1,0:T(8,128)(2,1)}, u32[]{:S(2)}, u32[]{:S(2)}) async-start(bf16[8,768,128]{2,1,0:T(8,128)(2,1)} %broadcast_in_dim.297), calls=%async_computation.16 | async-start | bytes 3145728 | tf_op jit(solution)/shard_map/all_to_all | solution.py:18
  532.9 21.4 %collective-permute-start.2 = (bf16[1,768,128]{2,1,0:T(8,128)(2,1)S(1)}, bf16[1,768,128]{2,1,0:T(8,128)(2,1)S(1)}, u32[]{:S(2)}, u32[]{:S(2)}) collective-permute-start(bf16[1,768,128]{2,1,0:T(8,128)(2,1)S(1)} %get-tuple-element.202), channel_id=1, source_target_pairs={{64,0},{65,1},{66,2},{67,3},{68,4},{69,5},{70,6},{71,7},{72,8},{73... | collective-permute-start | bytes 589832 | tf_op jit(solution)/shard_map/ppermute | solution.py:76
  554.3 65.8 %copy-start.38 = (bf16[1,768,128]{2,1,0:T(8,128)(2,1)}, bf16[1,768,128]{2,1,0:T(8,128)(2,1)S(1)}, u32[]{:S(2)}) copy-start(bf16[1,768,128]{2,1,0:T(8,128)(2,1)S(1)} %collective-permute-done.2) | copy-start | bytes 589828
  555.8 22.0 %all-to-all-start.24 = ((bf16[8,768,128]{1,2,0:T(8,128)(2,1)}), bf16[8,768,128]{1,2,0:T(8,128)(2,1)}, u32[]{:S(2)}, u32[]{:S(2)}) async-start(bf16[8,768,128]{1,2,0:T(8,128)(2,1)} %broadcast_in_dim.303), calls=%async_computation.24 | async-start | bytes 3145728 | tf_op jit(solution)/shard_map/all_to_all | solution.py:18
  624.0 21.9 %all-to-all-start.27 = ((bf16[8,768,128]{1,2,0:T(8,128)(2,1)}), bf16[8,768,128]{1,2,0:T(8,128)(2,1)S(1)}, u32[]{:S(2)}, u32[]{:S(2)}) async-start(bf16[8,768,128]{1,2,0:T(8,128)(2,1)} %broadcast_in_dim.305), calls=%async_computation.27 | async-start | bytes 3145728 | tf_op jit(solution)/shard_map/all_to_all | solution.py:18
  701.1 9.1 collective-permute-start.3
  710.2 59.8 %copy-start.50 = (bf16[1,768,128]{2,1,0:T(8,128)(2,1)}, bf16[1,768,128]{2,1,0:T(8,128)(2,1)S(1)}, u32[]{:S(2)}) copy-start(bf16[1,768,128]{2,1,0:T(8,128)(2,1)S(1)} %collective-permute-done.3) | copy-start | bytes 589828
  735.7 19.7 %all-to-all-start.31 = ((bf16[8,768,128]{2,1,0:T(8,128)(2,1)}), bf16[8,768,128]{2,1,0:T(8,128)(2,1)}, u32[]{:S(2)}, u32[]{:S(2)}) async-start(bf16[8,768,128]{2,1,0:T(8,128)(2,1)} %bitcast.737), calls=%async_computation.31 | async-start | bytes 3145728 | tf_op jit(solution)/shard_map/all_to_all | solution.py:51
  760.0 9.9 all-to-all-start.32
  763.6 133.3 %reduce-scatter.31.cloned.1.call-start = ((), (), s32[]{:S(2)}) async-start(), calls=%async_computation.51 | async-start | bytes 147456
  764.5 133.7 %reduce-scatter.29.cloned.1.call-start = ((), (), s32[]{:S(2)}) async-start(), calls=%async_computation.50 | async-start | bytes 36864
  771.3 128.2 %reduce-scatter.33.cloned.1.call-start = ((), (), s32[]{:S(2)}) async-start(), calls=%async_computation.52 | async-start | bytes 1179648
  791.6 23.1 %all-to-all-start.33 = ((bf16[8,768,128]{1,2,0:T(8,128)(2,1)}), bf16[8,768,128]{1,2,0:T(8,128)(2,1)}, u32[]{:S(2)}, u32[]{:S(2)}) async-start(bf16[8,768,128]{1,2,0:T(8,128)(2,1)} %broadcast_in_dim.309), calls=%async_computation.33 | async-start | bytes 3145728 | tf_op jit(solution)/shard_map/all_to_all | solution.py:18
  796.1 105.4 %reduce-scatter.23.cloned.1.call-start = ((), (), s32[]{:S(2)}) async-start(), calls=%async_computation.47 | async-start | bytes 1179648 | tf_op jit(solution)/shard_map/reduce_scatter | solution.py:398
  833.4 24.4 %all-to-all-start.34 = ((bf16[8,768,128]{2,1,0:T(8,128)(2,1)}), bf16[8,768,128]{2,1,0:T(8,128)(2,1)}, u32[]{:S(2)}, u32[]{:S(2)}) async-start(bf16[8,768,128]{2,1,0:T(8,128)(2,1)} %bitcast.733), calls=%async_computation.34 | async-start | bytes 3145728 | tf_op jit(solution)/shard_map/all_to_all | solution.py:51
  837.9 89.0 %reduce-scatter.25.cloned.1.call-start = ((), (), s32[]{:S(2)}) async-start(), calls=%async_computation.48 | async-start | bytes 36864
  845.5 113.1 %reduce-scatter.27.cloned.1.call-start = ((), (), s32[]{:S(2)}) async-start(), calls=%async_computation.49 | async-start | bytes 294912
  861.9 9.9 all-to-all-start.35
  872.4 23.1 %all-to-all-start.17 = ((bf16[8,768,128]{2,1,0:T(8,128)(2,1)}), bf16[8,768,128]{2,1,0:T(8,128)(2,1)S(1)}, u32[]{:S(2)}, u32[]{:S(2)}) async-start(bf16[8,768,128]{2,1,0:T(8,128)(2,1)} %bitcast.710), calls=%async_computation.17 | async-start | bytes 3145728 | tf_op jit(solution)/shard_map/all_to_all | solution.py:51
  876.2 113.9 %reduce-scatter.35.cloned.1.call-start = ((), (), s32[]{:S(2)}) async-start(), calls=%async_computation.53 | async-start | bytes 36864
  883.7 138.9 %reduce-scatter.21.cloned.1.call-start = ((), (), s32[]{:S(2)}) async-start(), calls=%async_computation.46 | async-start | bytes 884736 | tf_op jit(solution)/shard_map/reduce_scatter | solution.py:386
  895.9 64.2 %copy-start.67 = (f32[1,1,768,128]{3,2,0,1:T(8,128)S(1)}, f32[1,1,768,128]{3,2,0,1:T(8,128)}, u32[]{:S(2)}) copy-start(f32[1,1,768,128]{3,2,0,1:T(8,128)} %get-tuple-element.221) | copy-start | bytes 1179652
  896.0 64.2 %copy-start.68 = (f32[1,1,768,128]{3,2,0,1:T(8,128)S(1)}, f32[1,1,768,128]{3,2,0,1:T(8,128)}, u32[]{:S(2)}) copy-start(f32[1,1,768,128]{3,2,0,1:T(8,128)} %get-tuple-element.197) | copy-start | bytes 1179652
  (152 other events, 832.8 us)
Sparse Core Ops, SparseCore 0:
  96.6 24.2 all-gather.3
  124.0 24.3 all-gather.5
  766.8 29.9 reduce-scatter.30
  799.1 29.3 reduce-scatter.28
  830.7 31.0 reduce-scatter.32
  864.1 30.6 reduce-scatter.22
  897.7 29.0 reduce-scatter.24
  929.3 29.2 reduce-scatter.26
  960.9 29.0 reduce-scatter.34
  992.4 30.1 reduce-scatter.20
where the time goes:
time: 1040 us; the launch traced here: 1030 us
  waiting for transfers between devices  365 us (35%)
  blocking collectives  235 us (23%)
  matrix products  138 us (13%)
  starting transfers between devices  128 us (12%)
  other arithmetic  75 us (7%)
  local copies, waits for them, and re-layouts  71.7 us (7%)
  between operations  18.7 us (2%)
    all_to_all x18, waiting for transfers between devices, sent_to_all(): return lax.all_to_all(copies, axis, split_axis=0, concat_axis=0, tiled=True)  143 us
    all_to_all x4, blocking collectives, summed_on_arrival(): lax.all_to_all(parts, axis, split_axis=0, concat_axis=0, tiled=True)  94.1 us
    unnamed x16, waiting for transfers between devices  84.4 us
    all_to_all x18, starting transfers between devices, sent_to_all(): return lax.all_to_all(copies, axis, split_axis=0, concat_axis=0, tiled=True)  78 us
    all_to_all x6, blocking collectives, sent_to_all(): return lax.all_to_all(copies, axis, split_axis=0, concat_axis=0, tiled=True)  76 us
    all_to_all x8, waiting for transfers between devices, summed_on_arrival(): lax.all_to_all(parts, axis, split_axis=0, concat_axis=0, tiled=True)  74.2 us
    all_to_all x8, starting transfers between devices, summed_on_arrival(): lax.all_to_all(parts, axis, split_axis=0, concat_axis=0, tiled=True)  35 us
    ppermute x4, waiting for transfers between devices, from_behind(): return lax.ppermute(array, axis, pairs)  35 us
  transfers between devices with their start and end apart: 40, of which 30 were waited for; matrix products, arithmetic and copies ran while one was open for 17% of the time, Pallas kernels for 0%

commit v1 on v0

--- a/solution.py
+++ b/solution.py
@@ -26,7 +26,7 @@
     ends = [0]
     for a in arrays:
         ends.append(ends[-1] + a.size)
-    subtotal = taken_together(jnp.concatenate([a.ravel() for a in arrays]), axis)
+    subtotal = lax.psum(jnp.concatenate([a.ravel() for a in arrays]), axis)
     return tuple((subtotal[b:e].reshape(a.shape) for a, b, e in zip(arrays, ends, ends[1:])))
 
 
@@ -37,8 +37,7 @@
 
 
 def collect(array, axis, dim):
-    parts = sent_to_all(array, axis)
-    return joined_along(parts, dim)
+    return lax.all_gather(array, axis, axis=dim, tiled=True)
 
 
 def in_blocks(array, dim, peers):
@@ -47,9 +46,7 @@
 
 
 def summed_on_arrival(array, axis, dim):
-    parts = in_blocks(array, dim, lax.axis_size(axis))
-    arrived = lax.all_to_all(parts, axis, split_axis=0, concat_axis=0, tiled=True)
-    return arrived.astype(jnp.float32).sum(axis=0)
+    return lax.psum_scatter(array, axis, scatter_dimension=dim, tiled=True).astype(jnp.float32)
 
 
 def side_by_side(arrays, axis, dim, along):

time: 1040 us -> 1630 us (1.57)
  waiting for transfers between devices: 365 us -> 1020 us
  starting transfers between devices: 128 us -> 15 us
  blocking collectives: 235 us -> 264 us
  other arithmetic: 75 us -> 56.6 us
    unnamed x16 -> x52, waiting for transfers between devices: 84.4 us -> 537 us
    all_gather x0 -> x12, waiting for transfers between devices: none -> 385 us  [collect(): return lax.all_gather(array, axis, axis=dim, tiled=True)]
    all_to_all x26 -> x0, waiting for transfers between devices: 217 us -> none  [the longest x18 143 us: sent_to_all(): return lax.all_to_all(copies, axis, split_axis=0, concat_axis=0, tiled=True)]
    psum x0 -> x10, blocking collectives: none -> 200 us  [in_one(): subtotal = lax.psum(jnp.concatenate([a.ravel() for a in arrays]), axis)]
    all_to_all x10 -> x0, blocking collectives: 170 us -> none  [the longest x4 94.1 us: summed_on_arrival(): lax.all_to_all(parts, axis, split_axis=0, concat_axis=0, tiled=True)]
    all_to_all x26 -> x0, starting transfers between devices: 113 us -> none  [the longest x18 78 us: sent_to_all(): return lax.all_to_all(copies, axis, split_axis=0, concat_axis=0, tiled=True)]
    unnamed x382 -> x384, local copies, waits for them, and re-layouts: 26.4 us -> 74.5 us
    reduce_scatter x1, waiting for transfers between devices: 0.01 us -> 27.1 us  [sum_at_end(): lax.psum_scatter(part_expmat[None].astype(jnp.bfloat16), 'dp', scatter_di...]
  transfers between devices with their start and end apart: 40 -> 38, of which waited for: 30 -> 32; matrix products, arithmetic and copies ran while one was open for 17% -> 10% of each run, Pallas kernels for 0% -> 0%
where the time goes in v1:
time: 1630 us; the launch traced here: 1620 us
  waiting for transfers between devices  1020 us (63%)
  blocking collectives  264 us (16%)
  matrix products  150 us (9%)
  local copies, waits for them, and re-layouts  87.6 us (5%)
  other arithmetic  56.6 us (3%)
  between operations  20 us (1%)
    unnamed x52, waiting for transfers between devices  537 us
    all_gather x12, waiting for transfers between devices, collect(): return lax.all_gather(array, axis, axis=dim, tiled=True)  385 us
    psum x10, blocking collectives, in_one(): subtotal = lax.psum(jnp.concatenate([a.ravel() for a in arrays]), axis)  200 us
    unnamed x384, local copies, waits for them, and re-layouts  74.5 us
  transfers between devices with their start and end apart: 38, of which 32 were waited for; matrix products, arithmetic and copies ran while one was open for 10% of the time, Pallas kernels for 0%

profile of v1, /device:TPU:0, one launch (start us, length us, event | category | flops | bytes accessed | tf_op | source)
XLA Modules:
  0.0 1617.4 jit_solution(12491692947367818068)
XLA Ops:
  10.5 21.3 %psum.84 = f32[1536]{0:T(1024)S(1)} all-reduce(f32[1536]{0:T(1024)S(1)} %pad_maximum_fusion.9), channel_id=1, replica_groups=mesh['section'=2,'dp'=8,'tensor'=8] {'tensor'}, use_global_device_ids=true, to_apply=%region_2.3 | all-reduce | flops 1536 | bytes 12288 | tf_op jit(solution)/shard_map/psum | solution.py:29
  32.6 12.1 all-gather
  47.0 12.7 all_gather.63
  62.2 11.5 all_gather.64
  73.9 13.5 all_gather.62
  99.6 13.8 all-reduce.4
  113.5 23.8 %reduce-scatter.61.cloned.1.call-done = bf16[128,768]{1,0:T(8,128)(2,1)} async-done(((bf16[1024,768]{1,0:T(8,128)(2,1)}), bf16[128,768]{1,0:T(8,128)(2,1)}) %reduce-scatter.61.cloned.1.call-update) | async-done | bytes 196624
  138.7 16.8 %psum.85 = f32[1536]{0:T(1024)S(1)} all-reduce(f32[1536]{0:T(1024)S(1)} %pad_maximum_fusion.10), channel_id=1, replica_groups=mesh['section'=2,'dp'=8,'tensor'=8] {'tensor'}, use_global_device_ids=true, to_apply=%region_8.9 | all-reduce | flops 1536 | bytes 12288 | tf_op jit(solution)/shard_map/psum | solution.py:29
  157.4 39.7 %all-gather.18.cloned.1.call-done = bf16[768,1024]{1,0:T(8,128)(2,1)} async-done(((bf16[768,128]{1,0:T(8,128)(2,1)}), bf16[768,1024]{1,0:T(8,128)(2,1)}) %all-gather.18.cloned.1.call-update) | async-done | bytes 1572880 | tf_op jit(solution)/shard_map/all_gather | solution.py:40
  197.1 3.8 convolution_add_fusion.2
  200.9 22.7 %all-gather.22.cloned.1.call-done = bf16[1,512,1024]{2,1,0:T(8,128)(2,1)} async-done(((bf16[1,512,128]{2,1,0:T(8,128)(2,1)}), bf16[1,512,1024]{2,1,0:T(8,128)(2,1)}) %all-gather.22.cloned.1.call-update) | async-done | bytes 1048592 | tf_op jit(solution)/shard_map/all_gather | solution.py:447
  223.6 4.0 convolution_convert_fusion.5
  230.3 42.2 %reduce-scatter.63.cloned.1.call-done = bf16[128,768]{1,0:T(8,128)(2,1)} async-done(((bf16[1024,768]{1,0:T(8,128)(2,1)}), bf16[128,768]{1,0:T(8,128)(2,1)}) %reduce-scatter.63.cloned.1.call-update) | async-done | bytes 196624
  273.6 4.7 collective-permute-start
  281.9 16.2 %psum.86 = f32[1536]{0:T(1024)S(1)} all-reduce(f32[1536]{0:T(1024)S(1)} %pad_maximum_fusion.11), channel_id=1, replica_groups=mesh['section'=2,'dp'=8,'tensor'=8] {'tensor'}, use_global_device_ids=true, to_apply=%region_12.13 | all-reduce | flops 1536 | bytes 12288 | tf_op jit(solution)/shard_map/psum | solution.py:29
  299.3 42.4 %all-gather.24.cloned.1.call-done = bf16[768,1024]{1,0:T(8,128)(2,1)} async-done(((bf16[768,128]{1,0:T(8,128)(2,1)}), bf16[768,1024]{1,0:T(8,128)(2,1)}) %all-gather.24.cloned.1.call-update) | async-done | bytes 1572880 | tf_op jit(solution)/shard_map/all_gather | solution.py:40
  353.4 42.9 %reduce-scatter.65.cloned.1.call-done = bf16[128,768]{1,0:T(8,128)(2,1)} async-done(((bf16[1024,768]{1,0:T(8,128)(2,1)}), bf16[128,768]{1,0:T(8,128)(2,1)}) %reduce-scatter.65.cloned.1.call-update) | async-done | bytes 196624
  399.3 16.8 %psum.87 = f32[1536]{0:T(1024)S(1)} all-reduce(f32[1536]{0:T(1024)S(1)} %pad_maximum_fusion.12), channel_id=1, replica_groups=mesh['section'=2,'dp'=8,'tensor'=8] {'tensor'}, use_global_device_ids=true, to_apply=%region_18.19 | all-reduce | flops 1536 | bytes 12288 | tf_op jit(solution)/shard_map/psum | solution.py:29
  418.4 39.3 %all-gather.26.cloned.1.call-done = bf16[768,1024]{1,0:T(8,128)(2,1)} async-done(((bf16[768,128]{1,0:T(8,128)(2,1)}), bf16[768,1024]{1,0:T(8,128)(2,1)}) %all-gather.26.cloned.1.call-update) | async-done | bytes 1572880 | tf_op jit(solution)/shard_map/all_gather | solution.py:40
  457.7 3.8 convolution_add_fusion.1
  461.5 40.7 %all-gather.32.cloned.1.call-done = bf16[768,1024]{1,0:T(8,128)(2,1)} async-done(((bf16[768,128]{1,0:T(8,128)(2,1)}), bf16[768,1024]{1,0:T(8,128)(2,1)}) %all-gather.32.cloned.1.call-update) | async-done | bytes 1572880 | tf_op jit(solution)/shard_map/all_gather | solution.py:40
  502.2 5.0 convert_reduce_fusion.2
  513.0 3.9 convolution_convert_fusion.4
  519.7 36.3 %reduce-scatter.73.cloned.1.call-done = bf16[128,768]{1,0:T(8,128)(2,1)} async-done(((bf16[1024,768]{1,0:T(8,128)(2,1)}), bf16[128,768]{1,0:T(8,128)(2,1)}) %reduce-scatter.73.cloned.1.call-update) | async-done | bytes 196624
  557.0 41.0 %reduce-scatter.67.cloned.1.call-done = bf16[128,768]{1,0:T(8,128)(2,1)} async-done(((bf16[1024,768]{1,0:T(8,128)(2,1)}), bf16[128,768]{1,0:T(8,128)(2,1)}) %reduce-scatter.67.cloned.1.call-update) | async-done | bytes 196624
  600.7 4.6 collective-permute-start.1
  608.7 30.6 %all-reduce.3 = (f32[1536]{0:T(1024)S(1)}, f32[1536]{0:T(1024)S(1)}) all-reduce(f32[1536]{0:T(1024)S(1)} %pad_maximum_fusion.13, f32[1536]{0:T(1024)S(1)} %pad_maximum_fusion.15), channel_id=1, replica_groups=mesh['section'=2,'dp'=8,'tensor'=8] {'tensor'}, use_global_device_ids=true, to_apply=%region_22.23 | all-reduce | flops 3072 | bytes 24576 | tf_op jit(solution)/shard_map/psum | solution.py:29
  643.1 39.4 %all-gather.28.cloned.1.call-done = bf16[768,1024]{1,0:T(8,128)(2,1)} async-done(((bf16[768,128]{1,0:T(8,128)(2,1)}), bf16[768,1024]{1,0:T(8,128)(2,1)}) %all-gather.28.cloned.1.call-update) | async-done | bytes 1572880 | tf_op jit(solution)/shard_map/all_gather | solution.py:40
  689.0 38.5 %all-gather.34.cloned.1.call-done = bf16[768,1024]{1,0:T(8,128)(2,1)} async-done(((bf16[768,128]{1,0:T(8,128)(2,1)}), bf16[768,1024]{1,0:T(8,128)(2,1)}) %all-gather.34.cloned.1.call-update) | async-done | bytes 1572880 | tf_op jit(solution)/shard_map/all_gather | solution.py:40
  729.6 5.1 multiply_reduce_fusion.2
  745.6 5.1 convert_reduce_fusion.13
  764.6 23.9 %reduce-scatter.69.cloned.1.call-done = bf16[128,768]{1,0:T(8,128)(2,1)} async-done(((bf16[1024,768]{1,0:T(8,128)(2,1)}), bf16[128,768]{1,0:T(8,128)(2,1)}) %reduce-scatter.69.cloned.1.call-update) | async-done | bytes 196624
  789.6 41.1 %reduce-scatter.75.cloned.1.call-done = bf16[128,768]{1,0:T(8,128)(2,1)} async-done(((bf16[1024,768]{1,0:T(8,128)(2,1)}), bf16[128,768]{1,0:T(8,128)(2,1)}) %reduce-scatter.75.cloned.1.call-update) | async-done | bytes 196624
  832.9 31.1 %all-reduce.2 = (f32[1536]{0:T(1024)S(1)}, f32[1536]{0:T(1024)S(1)}) all-reduce(f32[1536]{0:T(1024)S(1)} %pad_maximum_fusion.14, f32[1536]{0:T(1024)S(1)} %pad_maximum_fusion.16), channel_id=1, replica_groups=mesh['section'=2,'dp'=8,'tensor'=8] {'tensor'}, use_global_device_ids=true, to_apply=%region_28.29 | all-reduce | flops 3072 | bytes 24576 | tf_op jit(solution)/shard_map/psum | solution.py:29
  867.7 7.6 collective-permute-done.2
  876.1 28.6 %all-gather.30.cloned.1.call-done = bf16[768,1024]{1,0:T(8,128)(2,1)} async-done(((bf16[768,128]{1,0:T(8,128)(2,1)}), bf16[768,1024]{1,0:T(8,128)(2,1)}) %all-gather.30.cloned.1.call-update) | async-done | bytes 1572880 | tf_op jit(solution)/shard_map/all_gather | solution.py:40
  913.6 40.8 %all-gather.36.cloned.1.call-done = bf16[768,1024]{1,0:T(8,128)(2,1)} async-done(((bf16[768,128]{1,0:T(8,128)(2,1)}), bf16[768,1024]{1,0:T(8,128)(2,1)}) %all-gather.36.cloned.1.call-update) | async-done | bytes 1572880 | tf_op jit(solution)/shard_map/all_gather | solution.py:40
  954.5 4.5 convert_reduce_fusion.1
  966.6 41.2 %reduce-scatter.77.cloned.1.call-done = bf16[128,768]{1,0:T(8,128)(2,1)} async-done(((bf16[1024,768]{1,0:T(8,128)(2,1)}), bf16[128,768]{1,0:T(8,128)(2,1)}) %reduce-scatter.77.cloned.1.call-update) | async-done | bytes 196624
  1011.6 16.9 %psum.92 = f32[1536]{0:T(1024)S(1)} all-reduce(f32[1536]{0:T(1024)S(1)} %pad_maximum_fusion.17), channel_id=1, replica_groups=mesh['section'=2,'dp'=8,'tensor'=8] {'tensor'}, use_global_device_ids=true, to_apply=%region_42.43 | all-reduce | flops 1536 | bytes 12288 | tf_op jit(solution)/shard_map/psum | solution.py:29
  1035.5 37.1 %all-gather.38.cloned.1.call-done = bf16[768,1024]{1,0:T(8,128)(2,1)} async-done(((bf16[768,128]{1,0:T(8,128)(2,1)}), bf16[768,1024]{1,0:T(8,128)(2,1)}) %all-gather.38.cloned.1.call-update) | async-done | bytes 1572880 | tf_op jit(solution)/shard_map/all_gather | solution.py:40
  1074.7 5.1 convert_reduce_fusion.11
  1087.2 3.4 bitcast_convert_fusion.1
  1093.3 42.5 %reduce-scatter.79.cloned.1.call-done = bf16[128,768]{1,0:T(8,128)(2,1)} async-done(((bf16[1024,768]{1,0:T(8,128)(2,1)}), bf16[128,768]{1,0:T(8,128)(2,1)}) %reduce-scatter.79.cloned.1.call-update) | async-done | bytes 196624
  1140.3 16.9 %psum.93 = f32[1536]{0:T(1024)S(1)} all-reduce(f32[1536]{0:T(1024)S(1)} %pad_maximum_fusion.18), channel_id=1, replica_groups=mesh['section'=2,'dp'=8,'tensor'=8] {'tensor'}, use_global_device_ids=true, to_apply=%region_47.48 | all-reduce | flops 1536 | bytes 12288 | tf_op jit(solution)/shard_map/psum | solution.py:29
  1160.9 7.8 collective-permute-done.3
  1170.8 38.4 %all-gather.40.cloned.1.call-done = bf16[768,1024]{1,0:T(8,128)(2,1)} async-done(((bf16[768,128]{1,0:T(8,128)(2,1)}), bf16[768,1024]{1,0:T(8,128)(2,1)}) %all-gather.40.cloned.1.call-update) | async-done | bytes 1572880 | tf_op jit(solution)/shard_map/all_gather | solution.py:40
  1209.2 4.4 convert_reduce_fusion
  1219.5 41.9 %reduce-scatter.81.cloned.1.call-done = bf16[128,768]{1,0:T(8,128)(2,1)} async-done(((bf16[1024,768]{1,0:T(8,128)(2,1)}), bf16[128,768]{1,0:T(8,128)(2,1)}) %reduce-scatter.81.cloned.1.call-update) | async-done | bytes 196624
  1263.4 16.9 %psum.94 = f32[1536]{0:T(1024)S(1)} all-reduce(f32[1536]{0:T(1024)S(1)} %pad_maximum_fusion.19), channel_id=1, replica_groups=mesh['section'=2,'dp'=8,'tensor'=8] {'tensor'}, use_global_device_ids=true, to_apply=%region_51.52 | all-reduce | flops 1536 | bytes 12288 | tf_op jit(solution)/shard_map/psum | solution.py:29
  1283.1 4.5 fusion.222
  1291.5 5.2 fusion.52
  1296.7 5.9 copy.214
  1320.8 3.4 fusion.37
  1327.1 4.6 convert_reduce_fusion.9
  1331.7 4.2 multiply_reduce_fusion
  1360.8 27.1 %reduce-scatter.59.cloned.1.call-done = bf16[1,128,512]{2,1,0:T(8,128)(2,1)} async-done(((bf16[1,1024,512]{2,1,0:T(8,128)(2,1)}), bf16[1,128,512]{2,1,0:T(8,128)(2,1)}) %reduce-scatter.59.cloned.1.call-update) | async-done | bytes 131088 | tf_op jit(solution)/shard_map/reduce_scatter | solution.py:395
  1389.5 29.7 %reduce-scatter.89.cloned.1.call-done = bf16[16,1]{1,0:T(8,128)(2,1)} async-done(((bf16[128,1]{1,0:T(8,128)(2,1)}), bf16[16,1]{1,0:T(8,128)(2,1)}) %reduce-scatter.89.cloned.1.call-update) | async-done | bytes 48
  1420.5 30.6 %reduce-scatter.85.cloned.1.call-done = bf16[16,2]{1,0:T(8,128)(2,1)} async-done(((bf16[128,2]{1,0:T(8,128)(2,1)}), bf16[16,2]{1,0:T(8,128)(2,1)}) %reduce-scatter.85.cloned.1.call-update) | async-done | bytes 80
  1452.4 30.2 %reduce-scatter.87.cloned.1.call-done = bf16[128,128]{1,0:T(8,128)(2,1)} async-done(((bf16[1024,128]{1,0:T(8,128)(2,1)}), bf16[128,128]{1,0:T(8,128)(2,1)}) %reduce-scatter.87.cloned.1.call-update) | async-done | bytes 32784
  1484.2 31.0 %reduce-scatter.57.cloned.1.call-done = bf16[1,128,3,128]{3,1,2,0:T(8,128)(2,1)} async-done(((bf16[1,1024,3,128]{3,1,2,0:T(8,128)(2,1)}), bf16[1,128,3,128]{3,1,2,0:T(8,128)(2,1)}) %reduce-scatter.57.cloned.1.call-update) | async-done | bytes 98320 | tf_op jit(solution)/shard_map/reduce_scatter | solution.py:383
  1516.8 40.4 %reduce-scatter.83.cloned.1.call-done = bf16[128,768]{1,0:T(8,128)(2,1)} async-done(((bf16[1024,768]{1,0:T(8,128)(2,1)}), bf16[128,768]{1,0:T(8,128)(2,1)}) %reduce-scatter.83.cloned.1.call-update) | async-done | bytes 196624
  1558.6 16.8 %psum.95 = f32[1536]{0:T(1024)S(1)} all-reduce(f32[1536]{0:T(1024)S(1)} %pad_maximum_fusion.20), channel_id=1, replica_groups=mesh['section'=2,'dp'=8,'tensor'=8] {'tensor'}, use_global_device_ids=true, to_apply=%region_56.57 | all-reduce | flops 1536 | bytes 12288 | tf_op jit(solution)/shard_map/psum | solution.py:29
  1577.6 28.0 %reduce-scatter.95.cloned.1.call-done = bf16[16,5]{1,0:T(8,128)(2,1)} async-done(((bf16[128,5]{1,0:T(8,128)(2,1)}), bf16[16,5]{1,0:T(8,128)(2,1)}) %reduce-scatter.95.cloned.1.call-update) | async-done | bytes 176
  (630 shorter events, 231.6 us)
Async XLA Ops:
  8.0 79.3 %all-gather.16.cloned.1.call-start = ((), (), s32[]{:S(2)}) async-start(), calls=%async_computation.20 | async-start | bytes 1769472 | tf_op jit(solution)/shard_map/all_gather | solution.py:40
  44.8 110.7 %copy-start.78 = (f32[128]{0:T(128)}, f32[128]{0:T(128)S(1)}, u32[]{:S(2)}) copy-start(f32[128]{0:T(128)S(1)} %get-tuple-element.311) | copy-start | bytes 1540
  44.8 110.7 %copy-start.107 = (f32[128]{0:T(128)}, f32[128]{0:T(128)S(1)}, u32[]{:S(2)}) copy-start(f32[128]{0:T(128)S(1)} %get-tuple-element.313) | copy-start | bytes 1540
  44.8 228.7 %copy-start.110 = (f32[128]{0:T(128)}, f32[128]{0:T(128)S(1)}, u32[]{:S(2)}) copy-start(f32[128]{0:T(128)S(1)} %get-tuple-element.312) | copy-start | bytes 1540
  44.8 253.3 %copy-start.81 = (f32[128]{0:T(128)}, f32[128]{0:T(128)S(1)}, u32[]{:S(2)}) copy-start(f32[128]{0:T(128)S(1)} %get-tuple-element.315) | copy-start | bytes 1540
  44.8 253.3 %copy-start.105 = (f32[128]{0:T(128)}, f32[128]{0:T(128)S(1)}, u32[]{:S(2)}) copy-start(f32[128]{0:T(128)S(1)} %get-tuple-element.314) | copy-start | bytes 1540
  46.8 90.4 %reduce-scatter.61.cloned.1.call-start = ((), (), s32[]{:S(2)}) async-start(), calls=%async_computation.36 | async-start | bytes 1769472
  61.9 282.3 %copy-start.113 = (f32[2,64]{1,0:T(2,128)}, f32[2,64]{1,0:T(2,128)S(1)}, u32[]{:S(2)}) copy-start(f32[2,64]{1,0:T(2,128)S(1)} %reshape.660) | copy-start | bytes 1540
  62.0 282.0 %copy-start.103 = (f32[2,64]{1,0:T(2,128)}, f32[2,64]{1,0:T(2,128)S(1)}, u32[]{:S(2)}) copy-start(f32[2,64]{1,0:T(2,128)S(1)} %reshape.661) | copy-start | bytes 1540
  73.7 653.7 %copy-start.4 = (bf16[1,128,1024]{2,1,0:T(8,128)(2,1)}, bf16[1,128,1024]{2,1,0:T(8,128)(2,1)S(1)}, u32[]{:S(2)}) copy-start(bf16[1,128,1024]{2,1,0:T(8,128)(2,1)S(1)} %all_gather.64) | copy-start | bytes 786436
  96.6 60.8 %all-gather.20.cloned.1.call-start = ((), (), s32[]{:S(2)}) async-start(), calls=%async_computation.22 | async-start | bytes 1179648 | tf_op jit(solution)/shard_map/all_gather | solution.py:445
  97.2 99.9 %all-gather.18.cloned.1.call-start = ((), (), s32[]{:S(2)}) async-start(), calls=%async_computation.21 | async-start | bytes 1769472 | tf_op jit(solution)/shard_map/all_gather | solution.py:40
  113.5 284.6 %copy-start.101 = (f32[128]{0:T(128)}, f32[128]{0:T(128)S(1)}, u32[]{:S(2)}) copy-start(f32[128]{0:T(128)S(1)} %add.680) | copy-start | bytes 1540
  138.6 460.5 %copy-start.7 = (f32[768,128]{1,0:T(8,128)}, f32[768,128]{1,0:T(8,128)S(1)}, u32[]{:S(2)}) copy-start(f32[768,128]{1,0:T(8,128)S(1)} %get-tuple-element.262) | copy-start | bytes 1179652
  156.5 67.1 %all-gather.22.cloned.1.call-start = ((), (), s32[]{:S(2)}) async-start(), calls=%async_computation.23 | async-start | bytes 1179648 | tf_op jit(solution)/shard_map/all_gather | solution.py:447
  157.1 115.4 %reduce-scatter.63.cloned.1.call-start = ((), (), s32[]{:S(2)}) async-start(), calls=%async_computation.37 | async-start | bytes 1769472
  230.2 111.5 %all-gather.24.cloned.1.call-start = ((), (), s32[]{:S(2)}) async-start(), calls=%async_computation.24 | async-start | bytes 1769472 | tf_op jit(solution)/shard_map/all_gather | solution.py:40
  273.6 7.9 collective-permute-start
  299.3 97.0 %reduce-scatter.65.cloned.1.call-start = ((), (), s32[]{:S(2)}) async-start(), calls=%async_computation.38 | async-start | bytes 1769472
  353.4 104.3 %copy-start.128 = (f32[512]{0:T(512)S(1)}, f32[512]{0:T(512)}, u32[]{:S(2)}) copy-start(f32[512]{0:T(512)} %copy-done.127) | copy-start | bytes 6148
  353.4 104.3 %all-gather.26.cloned.1.call-start = ((), (), s32[]{:S(2)}) async-start(), calls=%async_computation.25 | async-start | bytes 1769472 | tf_op jit(solution)/shard_map/all_gather | solution.py:40
  417.1 85.2 %all-gather.32.cloned.1.call-start = ((), (), s32[]{:S(2)}) async-start(), calls=%async_computation.28 | async-start | bytes 1769472 | tf_op jit(solution)/shard_map/all_gather | solution.py:40
  417.9 138.0 %reduce-scatter.73.cloned.1.call-start = ((), (), s32[]{:S(2)}) async-start(), calls=%async_computation.42 | async-start | bytes 1769472
  513.0 85.1 %reduce-scatter.67.cloned.1.call-start = ((), (), s32[]{:S(2)}) async-start(), calls=%async_computation.39 | async-start | bytes 1769472
  519.6 162.9 %all-gather.28.cloned.1.call-start = ((), (), s32[]{:S(2)}) async-start(), calls=%async_computation.26 | async-start | bytes 1769472 | tf_op jit(solution)/shard_map/all_gather | solution.py:40
  555.9 83.5 %copy-start.73 = (f32[1536]{0:T(1024)S(1)}, f32[1536]{0:T(1024)}, u32[]{:S(2)}) copy-start(f32[1536]{0:T(1024)} %copy-done.72) | copy-start | bytes 18436
  555.9 84.1 %copy-start.82 = (f32[128]{0:T(128)S(1)}, f32[128]{0:T(128)}, u32[]{:S(2)}) copy-start(f32[128]{0:T(128)} %copy-done.81) | copy-start | bytes 1540
  555.9 84.1 %copy-start.106 = (f32[128]{0:T(128)S(1)}, f32[128]{0:T(128)}, u32[]{:S(2)}) copy-start(f32[128]{0:T(128)} %copy-done.105) | copy-start | bytes 1540
  600.7 7.7 collective-permute-start.1
  641.0 86.5 %all-gather.34.cloned.1.call-start = ((), (), s32[]{:S(2)}) async-start(), calls=%async_computation.29 | async-start | bytes 1769472 | tf_op jit(solution)/shard_map/all_gather | solution.py:40
  642.8 145.6 %reduce-scatter.69.cloned.1.call-start = ((), (), s32[]{:S(2)}) async-start(), calls=%async_computation.40 | async-start | bytes 1769472
  745.5 85.1 %reduce-scatter.75.cloned.1.call-start = ((), (), s32[]{:S(2)}) async-start(), calls=%async_computation.43 | async-start | bytes 1769472
  764.4 99.5 %copy-start.71 = (f32[1536]{0:T(1024)S(1)}, f32[1536]{0:T(1024)}, u32[]{:S(2)}) copy-start(f32[1536]{0:T(1024)} %copy-done.70) | copy-start | bytes 18436
  764.4 99.6 %copy-start.80 = (f32[128]{0:T(128)S(1)}, f32[128]{0:T(128)}, u32[]{:S(2)}) copy-start(f32[128]{0:T(128)} %copy-done.78) | copy-start | bytes 1540
  764.5 99.6 %copy-start.109 = (f32[128]{0:T(128)S(1)}, f32[128]{0:T(128)}, u32[]{:S(2)}) copy-start(f32[128]{0:T(128)} %copy-done.107) | copy-start | bytes 1540
  764.5 100.6 %copy-start.13 = (f32[768,128]{1,0:T(8,128)S(1)}, f32[768,128]{1,0:T(8,128)}, u32[]{:S(2)}) copy-start(f32[768,128]{1,0:T(8,128)} %copy-done.12) | copy-start | bytes 1179652
  764.5 100.6 %copy-start.75 = (f32[768]{0:T(1024)S(1)}, f32[768]{0:T(1024)}, u32[]{:S(2)}) copy-start(f32[768]{0:T(1024)} %copy-done.74) | copy-start | bytes 9220
  764.5 140.2 %all-gather.30.cloned.1.call-start = ((), (), s32[]{:S(2)}) async-start(), calls=%async_computation.27 | async-start | bytes 1769472 | tf_op jit(solution)/shard_map/all_gather | solution.py:40
  865.0 89.5 %all-gather.36.cloned.1.call-start = ((), (), s32[]{:S(2)}) async-start(), calls=%async_computation.30 | async-start | bytes 1769472 | tf_op jit(solution)/shard_map/all_gather | solution.py:40
  866.2 9.1 collective-permute-start.2
  876.0 88.7 %reduce-scatter.71.cloned.1.call-start = ((), (), s32[]{:S(2)}) async-start(), calls=%async_computation.41 | async-start | bytes 1769472
  913.6 94.1 %reduce-scatter.77.cloned.1.call-start = ((), (), s32[]{:S(2)}) async-start(), calls=%async_computation.44 | async-start | bytes 1769472
  964.7 107.9 %all-gather.38.cloned.1.call-start = ((), (), s32[]{:S(2)}) async-start(), calls=%async_computation.31 | async-start | bytes 1769472 | tf_op jit(solution)/shard_map/all_gather | solution.py:40
  1032.0 103.8 %reduce-scatter.79.cloned.1.call-start = ((), (), s32[]{:S(2)}) async-start(), calls=%async_computation.45 | async-start | bytes 1769472
  1093.2 116.0 %all-gather.40.cloned.1.call-start = ((), (), s32[]{:S(2)}) async-start(), calls=%async_computation.32 | async-start | bytes 1769472 | tf_op jit(solution)/shard_map/all_gather | solution.py:40
  1159.6 9.1 collective-permute-start.3
  1170.6 90.8 %reduce-scatter.81.cloned.1.call-start = ((), (), s32[]{:S(2)}) async-start(), calls=%async_computation.46 | async-start | bytes 1769472
  1219.4 105.6 %all-gather.42.cloned.1.call-start = ((), (), s32[]{:S(2)}) async-start(), calls=%async_computation.33 | async-start | bytes 1769472 | tf_op jit(solution)/shard_map/all_gather | solution.py:40
  1283.0 74.4 %reduce-scatter.91.cloned.1.call-start = ((), (), s32[]{:S(2)}) async-start(), calls=%async_computation.51 | async-start | bytes 147456
  1291.4 67.4 %reduce-scatter.93.cloned.1.call-start = ((), (), s32[]{:S(2)}) async-start(), calls=%async_computation.52 | async-start | bytes 1179648
  1305.6 82.3 %reduce-scatter.59.cloned.1.call-start = ((), (), s32[]{:S(2)}) async-start(), calls=%async_computation.35 | async-start | bytes 1179648 | tf_op jit(solution)/shard_map/reduce_scatter | solution.py:395
  1312.2 107.0 %reduce-scatter.89.cloned.1.call-start = ((), (), s32[]{:S(2)}) async-start(), calls=%async_computation.50 | async-start | bytes 36864
  1324.9 126.1 %reduce-scatter.85.cloned.1.call-start = ((), (), s32[]{:S(2)}) async-start(), calls=%async_computation.48 | async-start | bytes 36864
  1341.0 141.6 %reduce-scatter.87.cloned.1.call-start = ((), (), s32[]{:S(2)}) async-start(), calls=%async_computation.49 | async-start | bytes 294912
  1344.6 170.5 %reduce-scatter.57.cloned.1.call-start = ((), (), s32[]{:S(2)}) async-start(), calls=%async_computation.34 | async-start | bytes 884736 | tf_op jit(solution)/shard_map/reduce_scatter | solution.py:383
  1349.3 207.9 %reduce-scatter.83.cloned.1.call-start = ((), (), s32[]{:S(2)}) async-start(), calls=%async_computation.47 | async-start | bytes 1769472
  1355.2 250.4 %reduce-scatter.95.cloned.1.call-start = ((), (), s32[]{:S(2)}) async-start(), calls=%async_computation.53 | async-start | bytes 36864
  1357.4 200.9 %copy-start.84 = (f32[128]{0:T(128)S(1)}, f32[128]{0:T(128)}, u32[]{:S(2)}) copy-start(f32[128]{0:T(128)} %copy-done.81) | copy-start | bytes 1540
  1358.7 216.7 %copy-start.124 = (f32[128]{0:T(128)S(1)}, f32[128]{0:T(128)}, u32[]{:S(2)}) copy-start(f32[128]{0:T(128)} %get-tuple-element.211) | copy-start | bytes 1540
  1358.8 216.7 %copy-start.125 = (f32[128]{0:T(128)S(1)}, f32[128]{0:T(128)}, u32[]{:S(2)}) copy-start(f32[128]{0:T(128)} %get-tuple-element.234) | copy-start | bytes 1540
  1358.8 216.7 %copy-start.130 = (f32[128]{0:T(128)S(1)}, f32[128]{0:T(128)}, u32[]{:S(2)}) copy-start(f32[128]{0:T(128)} %get-tuple-element.213) | copy-start | bytes 1540
  1358.8 216.7 %copy-start.131 = (f32[128]{0:T(128)S(1)}, f32[128]{0:T(128)}, u32[]{:S(2)}) copy-start(f32[128]{0:T(128)} %get-tuple-element.235) | copy-start | bytes 1540
  1359.8 216.5 %copy-start.76 = (f32[768]{0:T(1024)S(1)}, f32[768]{0:T(1024)}, u32[]{:S(2)}) copy-start(f32[768]{0:T(1024)} %copy-done.74) | copy-start | bytes 9220
  1484.2 92.5 %copy-start.46 = (f32[1,1,768,128]{3,2,1,0:T(8,128)S(1)}, f32[1,1,768,128]{3,2,1,0:T(8,128)}, u32[]{:S(2)}) copy-start(f32[1,1,768,128]{3,2,1,0:T(8,128)} %get-tuple-element.251) | copy-start | bytes 1179652
  (139 other events, 2553.6 us)
Sparse Core Ops, SparseCore 0:
  46.9 38.8 all-gather.15
  96.7 40.4 reduce-scatter.60
  230.3 42.0 reduce-scatter.62
  353.5 42.7 reduce-scatter.64
  513.1 42.7 reduce-scatter.72
  558.2 39.8 reduce-scatter.66
  745.7 42.7 reduce-scatter.68
  790.9 39.7 reduce-scatter.74
  913.7 45.7 reduce-scatter.70
  964.8 42.9 reduce-scatter.76
  1170.7 38.4 all-gather.39
  1283.1 40.4 all-gather.41
Sparse Core Ops, SparseCore 1:
  98.8 22.7 all-gather.19
  156.6 40.4 all-gather.17
  198.6 25.0 all-gather.21
  299.4 42.3 all-gather.23
  417.2 40.5 all-gather.25
  459.3 42.9 all-gather.31
  641.1 41.3 all-gather.27
  684.5 42.9 all-gather.33
  865.1 39.5 all-gather.29
  906.8 47.6 all-gather.35
  1032.0 40.4 all-gather.37
  1093.3 42.4 reduce-scatter.78
  1219.5 41.8 reduce-scatter.80
  1291.5 29.7 reduce-scatter.90
  1323.8 30.8 reduce-scatter.92
  1357.2 30.6 reduce-scatter.58
  1390.3 28.8 reduce-scatter.88
  1422.1 28.8 reduce-scatter.84
  1453.4 29.2 reduce-scatter.86
  1485.0 30.1 reduce-scatter.56
  1517.6 39.5 reduce-scatter.82
  1576.4 29.2 reduce-scatter.94

commit v2 on v0

--- a/solution.py
+++ b/solution.py
@@ -367,61 +367,47 @@
     )
 
 
-def sum_at_end(grads):
-    (
-        part_packed,
-        part_pair,
-        part_outmat,
-        part_outbias,
-        part_expmat,
-        part_expbias,
-        part_conmat,
-        part_conbias,
-        part_gainone,
-        part_shiftone,
-        part_gaintwo,
-        part_shifttwo,
-    ) = grads
-    return (
-        lax.psum_scatter(
-            part_packed[None].astype(jnp.bfloat16), "dp", scatter_dimension=1, tiled=True
-        ).astype(jnp.float32),
-        lax.psum_scatter(
-            part_pair[None].astype(jnp.bfloat16), "dp", scatter_dimension=2, tiled=True
-        ).astype(jnp.float32),
-        lax.psum_scatter(
-            part_outmat[None].astype(jnp.bfloat16), "dp", scatter_dimension=2, tiled=True
-        ).astype(jnp.float32),
-        lax.psum_scatter(
-            part_outbias[None].astype(jnp.bfloat16), "dp", scatter_dimension=1, tiled=True
-        ).astype(jnp.float32),
-        lax.psum_scatter(
-            part_expmat[None].astype(jnp.bfloat16), "dp", scatter_dimension=1, tiled=True
-        ).astype(jnp.float32),
-        lax.psum_scatter(
-            part_expbias[None].astype(jnp.bfloat16), "dp", scatter_dimension=1, tiled=True
-        ).astype(jnp.float32),
-        lax.psum_scatter(
-            part_conmat[None].astype(jnp.bfloat16), "dp", scatter_dimension=2, tiled=True
-        ).astype(jnp.float32),
-        *tuple(
-            (
-                part.astype(jnp.float32)
-                for part in side_by_side(
-                    (
-                        part_conbias[None].astype(jnp.bfloat16),
-                        part_gainone[None].astype(jnp.bfloat16),
-                        part_shiftone[None].astype(jnp.bfloat16),
-                        part_gaintwo[None].astype(jnp.bfloat16),
-                        part_shifttwo[None].astype(jnp.bfloat16),
-                    ),
-                    "dp",
-                    1,
-                    0,
-                )
-            )
-        ),
-    )
+def as_blocks(array, dim, peers):
+    before, after = (array.shape[:dim], array.shape[dim + 1 :])
+    split = array.reshape(*before, peers, array.shape[dim] // peers, *after)
+    return jnp.moveaxis(split, dim, 0).reshape(peers, -1)
+
+
+def from_blocks(flat, shape, dim, peers):
+    block_shape = (*shape[:dim], shape[dim] // peers, *shape[dim + 1 :])
+    return flat.reshape(block_shape)
+
+
+def sum_at_end(grads, dims):
+    peers = lax.axis_size("dp")
+    pieces = [as_blocks(g.astype(jnp.bfloat16), d, peers) for g, d in zip(grads, dims)]
+    widths = [p.shape[1] for p in pieces]
+    spare = -sum(widths) % 1024
+    pieces.append(jnp.zeros((peers, spare), jnp.bfloat16))
+    total = lax.psum_scatter(
+        jnp.concatenate(pieces, axis=1).reshape(1, -1, 128), "dp", scatter_dimension=1, tiled=True
+    ).reshape(1, -1)
+    reduced, at = ([], 0)
+    for g, d, w in zip(grads, dims, widths):
+        piece = total[0, at : at + w].astype(jnp.float32)
+        reduced.append(from_blocks(piece, g.shape, d, peers)[None])
+        at += w
+    return tuple(reduced)
+
+
+def gather_all(weights, dims):
+    peers = lax.axis_size("dp")
+    size = sum(w.size for w in weights)
+    flat = jnp.concatenate([w.reshape(-1) for w in weights] + [jnp.zeros((-size % 1024,), jnp.bfloat16)])
+    every = lax.all_gather(flat[None], "dp", axis=0, tiled=True)
+    gathered, at = ([], 0)
+    for w, d in zip(weights, dims):
+        part = every[:, at : at + w.size].reshape(peers, *w.shape)
+        part = jnp.moveaxis(part, 0, d)
+        shape = part.shape
+        gathered.append(part.reshape(*shape[:d], shape[d] * shape[d + 1], *shape[d + 2 :]))
+        at += w.size
+    return tuple(gathered)
 
 
 def shards(
@@ -440,19 +426,24 @@
     gain_second,
     shift_second,
 ):
-    gathered = (
-        lax.all_gather(packed_weight, "dp", axis=1, tiled=True),
-        lax.all_gather(bias_pair, "dp", axis=2, tiled=True),
-        lax.all_gather(output_weight, "dp", axis=2, tiled=True),
-        lax.all_gather(output_bias, "dp", axis=1, tiled=True),
-        lax.all_gather(expand_weight, "dp", axis=1, tiled=True),
-        lax.all_gather(expand_bias, "dp", axis=1, tiled=True),
-        lax.all_gather(contract_weight, "dp", axis=2, tiled=True),
-        *in_one_piece(
-            (contract_bias, gain_first, shift_first, gain_second, shift_second), "dp", 1, 0
+    gathered = gather_all(
+        (
+            packed_weight[0],
+            bias_pair[0],
+            output_weight[0],
+            output_bias[0],
+            expand_weight[0],
+            expand_bias[0],
+            contract_weight[0],
+            contract_bias[0],
+            gain_first[0],
+            shift_first[0],
+            gain_second[0],
+            shift_second[0],
         ),
-    )
-    weights = tuple((member[0] for member in gathered))
+        (0, 1, 1, 0, 0, 0, 1, 0, 0, 0, 0, 0),
+    )
+    weights = gathered
     is_first = lax.axis_index("section") == 0
     micro_count = inputs.shape[0]
     zero_block = jnp.zeros_like(inputs[0])
@@ -492,7 +483,7 @@
                     input_grad.dtype
                 )
             grad_total = grads if grad_total is None else jax.tree.map(jnp.add, grad_total, grads)
-    reduced = sum_at_end(grad_total)
+    reduced = sum_at_end(grad_total, (0, 1, 1, 0, 0, 0, 1, 0, 0, 0, 0, 0))
     section_outputs = jnp.stack(
         [
             jnp.where(is_first, outputs_list[slot_index], outputs_list[slot_index + 1])

time: 1040 us -> 1000 us (0.962)
  local copies, waits for them, and re-layouts: 71.7 us -> 164 us
  blocking collectives: 235 us -> 163 us
  waiting for transfers between devices: 365 us -> 306 us
    unnamed x16 -> x3, waiting for transfers between devices: 84.4 us -> 7.97 us
    all_gather x4 -> x0, blocking collectives: 51 us -> none  [the longest x1 14.7 us: shards(): lax.all_gather(packed_weight, 'dp', axis=1, tiled=True)]
    reduce_scatter x2 -> x0, waiting for transfers between devices: 28.6 us -> none  [the longest x1 28.6 us: sum_at_end(): lax.psum_scatter(part_packed[None].astype(jnp.bfloat16), 'dp', scatter_di...]
    unnamed x382 -> x395, local copies, waits for them, and re-layouts: 26.4 us -> 50.7 us
    all_to_all x8, waiting for transfers between devices: 74.2 us -> 94 us  [summed_on_arrival(): lax.all_to_all(parts, axis, split_axis=0, concat_axis=0, tiled=True)]
    concatenate x2, local copies, waits for them, and re-layouts: 1.48 us -> 20 us  [the longest x1 18.6 us: gather_all(): jnp.concatenate([w.reshape(-1) for w in weights] + [jnp.zeros((-size % 10...]
    transpose x0 -> x9, local copies, waits for them, and re-layouts: none -> 18.3 us  [the longest x6 15.8 us: joined_along(): parts = jnp.moveaxis(parts, 0, dim)]
    all_gather x2 -> x1, waiting for transfers between devices: 0.02 us -> 17.5 us  [gather_all(): every = lax.all_gather(flat[None], 'dp', axis=0, tiled=True)]
  transfers between devices with their start and end apart: 40 -> 32, of which waited for: 30 -> 27; matrix products, arithmetic and copies ran while one was open for 17% -> 17% of each run, Pallas kernels for 0% -> 0%
where the time goes in v2:
time: 1000 us; the launch traced here: 988 us
  waiting for transfers between devices  306 us (31%)
  local copies, waits for them, and re-layouts  164 us (16%)
  blocking collectives  163 us (16%)
  matrix products  139 us (14%)
  starting transfers between devices  131 us (13%)
  other arithmetic  68.5 us (7%)
  between operations  17.3 us (2%)
    all_to_all x18, waiting for transfers between devices, sent_to_all(): return lax.all_to_all(copies, axis, split_axis=0, concat_axis=0, tiled=True)  153 us
    all_to_all x8, waiting for transfers between devices, summed_on_arrival(): lax.all_to_all(parts, axis, split_axis=0, concat_axis=0, tiled=True)  94 us
    all_to_all x4, blocking collectives, summed_on_arrival(): lax.all_to_all(parts, axis, split_axis=0, concat_axis=0, tiled=True)  91.6 us
    all_to_all x18, starting transfers between devices, sent_to_all(): return lax.all_to_all(copies, axis, split_axis=0, concat_axis=0, tiled=True)  82.4 us
    all_to_all x6, blocking collectives, sent_to_all(): return lax.all_to_all(copies, axis, split_axis=0, concat_axis=0, tiled=True)  70.9 us
    unnamed x395, local copies, waits for them, and re-layouts  50.7 us
    all_to_all x8, starting transfers between devices, summed_on_arrival(): lax.all_to_all(parts, axis, split_axis=0, concat_axis=0, tiled=True)  35.4 us
    ppermute x4, waiting for transfers between devices, from_behind(): return lax.ppermute(array, axis, pairs)  33.9 us
  transfers between devices with their start and end apart: 32, of which 27 were waited for; matrix products, arithmetic and copies ran while one was open for 17% of the time, Pallas kernels for 0%

profile of v2, /device:TPU:0, one launch (start us, length us, event | category | flops | bytes accessed | tf_op | source)
XLA Modules:
  0.0 988.0 jit_solution(12209835081111356285)
XLA Ops:
  10.1 18.6 %concatenate.46 = bf16[197632]{0:T(1024)(128)(2,1)} concatenate(bf16[49152]{0:T(1024)(128)(2,1)S(1)} %reshape_squeeze.15, bf16[32]{0:T(256)(128)(2,1)S(1)} %reshape_squeeze.16, bf16[16384]{0:T(1024)(128)(2,1)} %bitcast.837, bf16[16]{0:T(256)(128)(2,1)} %bitcast.839, bf16[65536]{0:T(1024)(128)(2,1)S(1)} %bitcast.819, bf16[64]{0:T(256)(128)(2,1)} %bitcast.840, ...), dimensions={0} | concatenate | bytes 790528 | tf_op jit(solution)/shard_map/concatenate | solution.py:401
  29.1 12.4 %all_to_all.192 = f32[8,1,1536]{2,1,0:T(1,128)S(1)} all-to-all(f32[8,1,1536]{2,1,0:T(1,128)S(1)} %broadcast_in_dim.287), channel_id=1, replica_groups=mesh['section'=2,'dp'=8,'tensor'=8] {'tensor'}, dimensions={0} | all-to-all | bytes 98304 | tf_op jit(solution)/shard_map/all_to_all | solution.py:18
  41.6 17.5 %all-gather.3.cloned.1.call-done = bf16[1581056]{0:T(1024)(128)(2,1)} async-done(((bf16[197632]{0:T(1024)(128)(2,1)}), bf16[1581056]{0:T(1024)(128)(2,1)}) %all-gather.3.cloned.1.call-update) | async-done | bytes 3162128 | tf_op jit(solution)/shard_map/all_gather | solution.py:402
  59.2 4.9 reshape.1723
  66.8 5.3 all-to-all-start.1
  77.9 15.2 %all-to-all-done.1 = bf16[8,768,128]{2,1,0:T(8,128)(2,1)} async-done(((bf16[8,768,128]{2,1,0:T(8,128)(2,1)}), bf16[8,768,128]{2,1,0:T(8,128)(2,1)}, u32[]{:S(2)}, u32[]{:S(2)}) %all-to-all-start.1) | async-done | bytes 1572896 | tf_op jit(solution)/shard_map/all_to_all | solution.py:18
  105.7 20.5 %all-to-all-done.2 = bf16[8,768,128]{2,1,0:T(8,128)(2,1)} async-done(((bf16[8,768,128]{2,1,0:T(8,128)(2,1)}), bf16[8,768,128]{2,1,0:T(8,128)(2,1)}, u32[]{:S(2)}, u32[]{:S(2)}) %all-to-all-start.2) | async-done | bytes 1572896 | tf_op jit(solution)/shard_map/all_to_all | solution.py:51
  132.7 6.1 all-to-all-done.3
  141.1 4.5 all-to-all-start.4
  156.7 8.4 all-to-all-done.4
  174.8 20.4 %all-to-all-done.5 = bf16[8,768,128]{2,1,0:T(8,128)(2,1)} async-done(((bf16[8,768,128]{2,1,0:T(8,128)(2,1)}), bf16[8,768,128]{2,1,0:T(8,128)(2,1)}, u32[]{:S(2)}, u32[]{:S(2)}) %all-to-all-start.5) | async-done | bytes 1572896 | tf_op jit(solution)/shard_map/all_to_all | solution.py:51
  197.7 4.6 collective-permute-start
  206.7 9.4 all_to_all.193
  217.3 22.0 %all_to_all.194 = bf16[8,768,128]{2,1,0:T(8,128)(2,1)S(1)} all-to-all(bf16[8,768,128]{2,1,0:T(8,128)(2,1)S(1)} %broadcast_in_dim.296), channel_id=1, replica_groups=mesh['section'=2,'dp'=8,'tensor'=8] {'tensor'}, dimensions={0} | all-to-all | bytes 3145728 | tf_op jit(solution)/shard_map/all_to_all | solution.py:18
  246.5 21.3 %all_to_all.195 = bf16[8,768,128]{2,1,0:T(8,128)(2,1)S(1)} all-to-all(bf16[8,768,128]{2,1,0:T(8,128)(2,1)S(1)} %bitcast.758), channel_id=1, replica_groups=mesh['section'=2,'dp'=8,'tensor'=8] {'tensor'}, dimensions={0} | all-to-all | bytes 3145728 | tf_op jit(solution)/shard_map/all_to_all | solution.py:51
  268.4 8.8 all_to_all.196
  278.9 4.4 all-to-all-start.10
  283.4 15.2 %all-to-all-done.10 = bf16[8,768,128]{1,2,0:T(8,128)(2,1)} async-done(((bf16[8,768,128]{1,2,0:T(8,128)(2,1)}), bf16[8,768,128]{1,2,0:T(8,128)(2,1)}, u32[]{:S(2)}, u32[]{:S(2)}) %all-to-all-start.10) | async-done | bytes 1572896 | tf_op jit(solution)/shard_map/all_to_all | solution.py:18
  300.0 4.5 all-to-all-start.18
  308.4 15.4 %all-to-all-done.18 = bf16[8,768,128]{2,1,0:T(8,128)(2,1)} async-done(((bf16[8,768,128]{2,1,0:T(8,128)(2,1)}), bf16[8,768,128]{2,1,0:T(8,128)(2,1)}, u32[]{:S(2)}, u32[]{:S(2)}) %all-to-all-start.18) | async-done | bytes 1572896 | tf_op jit(solution)/shard_map/all_to_all | solution.py:18
  323.8 5.0 convert_reduce_fusion.20
  339.8 16.2 %all-to-all-done.19 = bf16[8,768,128]{2,1,0:T(8,128)(2,1)} async-done(((bf16[8,768,128]{2,1,0:T(8,128)(2,1)}), bf16[8,768,128]{2,1,0:T(8,128)(2,1)}, u32[]{:S(2)}, u32[]{:S(2)}) %all-to-all-start.19) | async-done | bytes 1572896 | tf_op jit(solution)/shard_map/all_to_all | solution.py:51
  364.1 16.7 %all-to-all-done.11 = bf16[8,768,128]{2,1,0:T(8,128)(2,1)} async-done(((bf16[8,768,128]{2,1,0:T(8,128)(2,1)}), bf16[8,768,128]{2,1,0:T(8,128)(2,1)}, u32[]{:S(2)}, u32[]{:S(2)}) %all-to-all-start.11) | async-done | bytes 1572896 | tf_op jit(solution)/shard_map/all_to_all | solution.py:51
  389.4 5.5 collective-permute-start.1
  399.9 4.8 all-to-all-start.12
  405.8 5.3 all-to-all-done.12
  417.0 16.9 %all-to-all-done.21 = bf16[8,768,128]{2,1,0:T(8,128)(2,1)S(1)} async-done(((bf16[8,768,128]{2,1,0:T(8,128)(2,1)}), bf16[8,768,128]{2,1,0:T(8,128)(2,1)S(1)}, u32[]{:S(2)}, u32[]{:S(2)}) %all-to-all-start.21) | async-done | bytes 1572896 | tf_op jit(solution)/shard_map/all_to_all | solution.py:18
  435.5 4.8 all-to-all-start.13
  441.0 19.2 %all-to-all-done.13 = bf16[8,768,128]{2,1,0:T(8,128)(2,1)} async-done(((bf16[8,768,128]{2,1,0:T(8,128)(2,1)}), bf16[8,768,128]{2,1,0:T(8,128)(2,1)}, u32[]{:S(2)}, u32[]{:S(2)}) %all-to-all-start.13) | async-done | bytes 1572896 | tf_op jit(solution)/shard_map/all_to_all | solution.py:18
  480.2 5.1 convert_reduce_fusion.25
  506.5 18.4 %all-to-all-done.22 = bf16[8,768,128]{2,1,0:T(8,128)(2,1)S(1)} async-done(((bf16[8,768,128]{2,1,0:T(8,128)(2,1)}), bf16[8,768,128]{2,1,0:T(8,128)(2,1)S(1)}, u32[]{:S(2)}, u32[]{:S(2)}) %all-to-all-start.22) | async-done | bytes 1572896 | tf_op jit(solution)/shard_map/all_to_all | solution.py:51
  540.8 5.3 all-to-all-done.23
  548.1 4.4 all-to-all-start.16
  558.6 18.2 %collective-permute-done.2 = bf16[1,768,128]{2,1,0:T(8,128)(2,1)S(1)} collective-permute-done((bf16[1,768,128]{2,1,0:T(8,128)(2,1)S(1)}, bf16[1,768,128]{2,1,0:T(8,128)(2,1)S(1)}, u32[]{:S(2)}, u32[]{:S(2)}) %collective-permute-start.2) | collective-permute-done | bytes 196640 | tf_op jit(solution)/shard_map/ppermute | solution.py:76
  578.2 4.8 all-to-all-start.24
  586.8 13.2 %all-to-all-done.24 = bf16[8,768,128]{2,1,0:T(8,128)(2,1)} async-done(((bf16[8,768,128]{2,1,0:T(8,128)(2,1)}), bf16[8,768,128]{2,1,0:T(8,128)(2,1)}, u32[]{:S(2)}, u32[]{:S(2)}) %all-to-all-start.24) | async-done | bytes 1572896 | tf_op jit(solution)/shard_map/all_to_all | solution.py:18
  600.0 5.0 convert_reduce_fusion.19
  606.3 24.2 %all_to_all.197 = bf16[8,768,128]{2,1,0:T(8,128)(2,1)S(1)} all-to-all(bf16[8,768,128]{2,1,0:T(8,128)(2,1)S(1)} %bitcast.759), channel_id=1, replica_groups=mesh['section'=2,'dp'=8,'tensor'=8] {'tensor'}, dimensions={0} | all-to-all | bytes 3145728 | tf_op jit(solution)/shard_map/all_to_all | solution.py:51
  634.1 8.9 all_to_all.198
  646.4 4.6 all-to-all-start.27
  654.1 15.0 %all-to-all-done.27 = bf16[8,768,128]{2,1,0:T(8,128)(2,1)} async-done(((bf16[8,768,128]{2,1,0:T(8,128)(2,1)}), bf16[8,768,128]{2,1,0:T(8,128)(2,1)}, u32[]{:S(2)}, u32[]{:S(2)}) %all-to-all-start.27) | async-done | bytes 1572896 | tf_op jit(solution)/shard_map/all_to_all | solution.py:18
  671.2 5.2 convert_reduce_fusion.23
  686.3 24.9 %all_to_all.199 = bf16[8,768,128]{2,1,0:T(8,128)(2,1)S(1)} all-to-all(bf16[8,768,128]{2,1,0:T(8,128)(2,1)S(1)} %bitcast.760), channel_id=1, replica_groups=mesh['section'=2,'dp'=8,'tensor'=8] {'tensor'}, dimensions={0} | all-to-all | bytes 3145728 | tf_op jit(solution)/shard_map/all_to_all | solution.py:51
  714.7 9.4 all_to_all.200
  732.7 7.8 collective-permute-done.3
  741.8 4.7 all-to-all-start.30
  763.2 5.0 convert_reduce_fusion.18
  770.7 5.5 all-to-all-start.31
  776.2 4.5 fusion.39
  783.2 5.5 fusion.113
  804.4 5.9 all-to-all-start.32
  810.3 4.6 add_convert_fusion.1
  823.1 5.7 all-to-all-start.33
  828.8 4.4 fusion.93
  837.3 8.4 all-to-all-done.33
  847.8 5.1 convert_reduce_fusion.21
  863.4 4.7 all-to-all-start.34
  887.5 7.1 dynamic-update-slice.4
  896.0 6.8 dynamic-update-slice.6
  906.8 5.7 all-to-all-start.35
  912.7 6.0 all-to-all-done.35
  928.5 5.0 reshape.1707
  937.6 21.2 %all_to_all.201 = bf16[8,768,128]{2,1,0:T(8,128)(2,1)S(1)} all-to-all(bf16[8,768,128]{2,1,0:T(8,128)(2,1)S(1)} %bitcast.762), channel_id=1, replica_groups=mesh['section'=2,'dp'=8,'tensor'=8] {'tensor'}, dimensions={0} | all-to-all | bytes 3145728 | tf_op jit(solution)/shard_map/all_to_all | solution.py:51
  961.8 7.9 reduce-scatter.5.cloned.1.call-done
  (690 shorter events, 338.6 us)
Async XLA Ops:
  7.2 21.5 %copy-start.5 = (f32[2,1,768,128]{3,2,1,0:T(8,128)S(1)}, f32[2,1,768,128]{3,2,1,0:T(8,128)}, u32[]{:S(2)}) copy-start(f32[2,1,768,128]{3,2,1,0:T(8,128)} %param.14) | copy-start | bytes 2359300
  7.2 52.0 %all-gather.3.cloned.1.call-start = ((), (), s32[]{:S(2)}) async-start(), calls=%async_computation.37 | async-start | bytes 3557376 | tf_op jit(solution)/shard_map/all_gather | solution.py:402
  41.6 23.6 %copy-start.113 = (f32[768]{0:T(1024)}, f32[768]{0:T(1024)S(1)}, u32[]{:S(2)}) copy-start(f32[768]{0:T(1024)S(1)} %get-tuple-element.312) | copy-start | bytes 9220
  41.6 23.5 %copy-start.115 = (f32[768]{0:T(1024)}, f32[768]{0:T(1024)S(1)}, u32[]{:S(2)}) copy-start(f32[768]{0:T(1024)S(1)} %get-tuple-element.313) | copy-start | bytes 9220
  65.1 351.6 %copy-start.122 = (f32[128]{0:T(128)}, f32[128]{0:T(128)S(1)}, u32[]{:S(2)}) copy-start(f32[128]{0:T(128)S(1)} %reshape.1709) | copy-start | bytes 1540
  66.8 26.3 %all-to-all-start.1 = ((bf16[8,768,128]{2,1,0:T(8,128)(2,1)}), bf16[8,768,128]{2,1,0:T(8,128)(2,1)}, u32[]{:S(2)}, u32[]{:S(2)}) async-start(bf16[8,768,128]{2,1,0:T(8,128)(2,1)} %broadcast_in_dim.290), calls=%async_computation.1 | async-start | bytes 3145728 | tf_op jit(solution)/shard_map/all_to_all | solution.py:18
  73.0 167.8 %copy-start.142 = (f32[2,64]{1,0:T(2,128)}, f32[2,64]{1,0:T(2,128)S(1)}, u32[]{:S(2)}) copy-start(f32[2,64]{1,0:T(2,128)S(1)} %reshape.1711) | copy-start | bytes 1540
  73.1 167.6 %copy-start.136 = (f32[2,64]{1,0:T(2,128)}, f32[2,64]{1,0:T(2,128)S(1)}, u32[]{:S(2)}) copy-start(f32[2,64]{1,0:T(2,128)S(1)} %reshape.1712) | copy-start | bytes 1540
  74.4 171.2 %copy-start.16 = (bf16[128,8,128]{0,2,1:T(8,128)(2,1)}, bf16[128,8,128]{0,2,1:T(8,128)(2,1)S(1)}, u32[]{:S(2)}) copy-start(bf16[128,8,128]{0,2,1:T(8,128)(2,1)S(1)} %copy.232) | copy-start | bytes 786436
  77.9 17.4 %copy-start.66 = (bf16[1024,3,128]{0,2,1:T(8,128)(2,1)}, bf16[1024,3,128]{0,2,1:T(8,128)(2,1)S(1)}, u32[]{:S(2)}) copy-start(bf16[1024,3,128]{0,2,1:T(8,128)(2,1)S(1)} %copy.229) | copy-start | bytes 2359300
  101.3 24.9 %all-to-all-start.2 = ((bf16[8,768,128]{2,1,0:T(8,128)(2,1)}), bf16[8,768,128]{2,1,0:T(8,128)(2,1)}, u32[]{:S(2)}, u32[]{:S(2)}) async-start(bf16[8,768,128]{2,1,0:T(8,128)(2,1)} %bitcast.756), calls=%async_computation.2 | async-start | bytes 3145728 | tf_op jit(solution)/shard_map/all_to_all | solution.py:51
  105.7 281.1 %copy-start.101 = (f32[128]{0:T(128)}, f32[128]{0:T(128)S(1)}, u32[]{:S(2)}) copy-start(f32[128]{0:T(128)S(1)} %reshape.1713) | copy-start | bytes 1540
  127.8 69.0 %copy-start.14 = (f32[768,128]{1,0:T(8,128)}, f32[768,128]{1,0:T(8,128)S(1)}, u32[]{:S(2)}) copy-start(f32[768,128]{1,0:T(8,128)S(1)} %convert_reduce_fusion.17) | copy-start | bytes 1179652
  128.9 9.9 %all-to-all-start.3 = ((f32[8,1,1536]{2,1,0:T(1,128)}), f32[8,1,1536]{2,1,0:T(1,128)S(1)}, u32[]{:S(2)}, u32[]{:S(2)}) async-start(f32[8,1,1536]{2,1,0:T(1,128)} %broadcast_in_dim.293), calls=%async_computation.3 | async-start | bytes 98304 | tf_op jit(solution)/shard_map/all_to_all | solution.py:18
  132.6 272.2 %copy-start.93 = (f32[128]{0:T(128)}, f32[128]{0:T(128)S(1)}, u32[]{:S(2)}) copy-start(f32[128]{0:T(128)S(1)} %reshape.1714) | copy-start | bytes 1540
  132.7 144.5 %copy-start.147 = (f32[128]{0:T(128)}, f32[128]{0:T(128)S(1)}, u32[]{:S(2)}) copy-start(f32[128]{0:T(128)S(1)} %reshape.1715) | copy-start | bytes 1540
  141.1 23.9 %all-to-all-start.4 = ((bf16[8,768,128]{2,1,0:T(8,128)(2,1)}), bf16[8,768,128]{2,1,0:T(8,128)(2,1)}, u32[]{:S(2)}, u32[]{:S(2)}) async-start(bf16[8,768,128]{2,1,0:T(8,128)(2,1)} %broadcast_in_dim.294), calls=%async_computation.4 | async-start | bytes 3145728 | tf_op jit(solution)/shard_map/all_to_all | solution.py:18
  149.4 155.1 %copy-start.170 = (f32[512]{0:T(512)}, f32[512]{0:T(512)S(1)}, u32[]{:S(2)}) copy-start(f32[512]{0:T(512)S(1)} %reshape.1716) | copy-start | bytes 6148
  170.4 24.8 %all-to-all-start.5 = ((bf16[8,768,128]{2,1,0:T(8,128)(2,1)}), bf16[8,768,128]{2,1,0:T(8,128)(2,1)}, u32[]{:S(2)}, u32[]{:S(2)}) async-start(bf16[8,768,128]{2,1,0:T(8,128)(2,1)} %bitcast.754), calls=%async_computation.5 | async-start | bytes 3145728 | tf_op jit(solution)/shard_map/all_to_all | solution.py:51
  174.8 212.0 %copy-start.145 = (f32[128]{0:T(128)}, f32[128]{0:T(128)S(1)}, u32[]{:S(2)}) copy-start(f32[128]{0:T(128)S(1)} %reshape.1717) | copy-start | bytes 1540
  197.7 8.6 collective-permute-start
  217.3 22.0 %copy-start.67 = (bf16[1024,3,128]{0,2,1:T(8,128)(2,1)S(1)}, bf16[1024,3,128]{0,2,1:T(8,128)(2,1)}, u32[]{:S(2)}) copy-start(bf16[1024,3,128]{0,2,1:T(8,128)(2,1)} %copy-done.66) | copy-start | bytes 2359300
  240.9 223.4 %copy-start.34 = (bf16[768,2,64]{0,2,1:T(8,128)(2,1)}, bf16[768,2,64]{0,2,1:T(8,128)(2,1)S(1)}, u32[]{:S(2)}) copy-start(bf16[768,2,64]{0,2,1:T(8,128)(2,1)S(1)} %add_convert_fusion.9) | copy-start | bytes 589828
  268.0 118.7 %copy-start.7 = (f32[768,128]{1,0:T(8,128)}, f32[768,128]{1,0:T(8,128)S(1)}, u32[]{:S(2)}) copy-start(f32[768,128]{1,0:T(8,128)S(1)} %convert_reduce_fusion.15) | copy-start | bytes 1179652
  268.3 136.4 %copy-start.2 = (f32[768,128]{1,0:T(8,128)}, f32[768,128]{1,0:T(8,128)S(1)}, u32[]{:S(2)}) copy-start(f32[768,128]{1,0:T(8,128)S(1)} %get-tuple-element.258) | copy-start | bytes 1179652
  278.9 19.7 %all-to-all-start.10 = ((bf16[8,768,128]{1,2,0:T(8,128)(2,1)}), bf16[8,768,128]{1,2,0:T(8,128)(2,1)}, u32[]{:S(2)}, u32[]{:S(2)}) async-start(bf16[8,768,128]{1,2,0:T(8,128)(2,1)} %broadcast_in_dim.298), calls=%async_computation.10 | async-start | bytes 3145728 | tf_op jit(solution)/shard_map/all_to_all | solution.py:18
  300.0 23.8 %all-to-all-start.18 = ((bf16[8,768,128]{2,1,0:T(8,128)(2,1)}), bf16[8,768,128]{2,1,0:T(8,128)(2,1)}, u32[]{:S(2)}, u32[]{:S(2)}) async-start(bf16[8,768,128]{2,1,0:T(8,128)(2,1)} %broadcast_in_dim.305), calls=%async_computation.18 | async-start | bytes 3145728 | tf_op jit(solution)/shard_map/all_to_all | solution.py:18
  331.2 24.8 %all-to-all-start.19 = ((bf16[8,768,128]{2,1,0:T(8,128)(2,1)}), bf16[8,768,128]{2,1,0:T(8,128)(2,1)}, u32[]{:S(2)}, u32[]{:S(2)}) async-start(bf16[8,768,128]{2,1,0:T(8,128)(2,1)} %bitcast.755), calls=%async_computation.19 | async-start | bytes 3145728 | tf_op jit(solution)/shard_map/all_to_all | solution.py:51
  356.0 24.8 %all-to-all-start.11 = ((bf16[8,768,128]{2,1,0:T(8,128)(2,1)}), bf16[8,768,128]{2,1,0:T(8,128)(2,1)}, u32[]{:S(2)}, u32[]{:S(2)}) async-start(bf16[8,768,128]{2,1,0:T(8,128)(2,1)} %bitcast.752), calls=%async_computation.11 | async-start | bytes 3145728 | tf_op jit(solution)/shard_map/all_to_all | solution.py:51
  363.3 41.4 %copy-start.12 = (f32[768,128]{1,0:T(8,128)}, f32[768,128]{1,0:T(8,128)S(1)}, u32[]{:S(2)}) copy-start(f32[768,128]{1,0:T(8,128)S(1)} %get-tuple-element.208) | copy-start | bytes 1179652
  381.5 13.5 %all-to-all-start.20 = ((f32[8,1,1536]{2,1,0:T(1,128)}), f32[8,1,1536]{2,1,0:T(1,128)S(1)}, u32[]{:S(2)}, u32[]{:S(2)}) async-start(f32[8,1,1536]{2,1,0:T(1,128)} %broadcast_in_dim.306), calls=%async_computation.20 | async-start | bytes 98304 | tf_op jit(solution)/shard_map/all_to_all | solution.py:18
  389.4 9.6 collective-permute-start.1
  395.0 17.4 %copy-start.130 = (f32[768]{0:T(1024)}, f32[768]{0:T(1024)S(1)}, u32[]{:S(2)}) copy-start(f32[768]{0:T(1024)S(1)} %get-tuple-element.304) | copy-start | bytes 9220
  395.0 17.4 %copy-start.131 = (f32[768]{0:T(1024)}, f32[768]{0:T(1024)S(1)}, u32[]{:S(2)}) copy-start(f32[768]{0:T(1024)S(1)} %get-tuple-element.305) | copy-start | bytes 9220
  399.9 11.1 %all-to-all-start.12 = ((f32[8,1,1536]{2,1,0:T(1,128)}), f32[8,1,1536]{2,1,0:T(1,128)S(1)}, u32[]{:S(2)}, u32[]{:S(2)}) async-start(f32[8,1,1536]{2,1,0:T(1,128)} %broadcast_in_dim.300), calls=%async_computation.12 | async-start | bytes 98304 | tf_op jit(solution)/shard_map/all_to_all | solution.py:18
  412.4 21.5 %all-to-all-start.21 = ((bf16[8,768,128]{2,1,0:T(8,128)(2,1)}), bf16[8,768,128]{2,1,0:T(8,128)(2,1)S(1)}, u32[]{:S(2)}, u32[]{:S(2)}) async-start(bf16[8,768,128]{2,1,0:T(8,128)(2,1)} %broadcast_in_dim.307), calls=%async_computation.21 | async-start | bytes 3145728 | tf_op jit(solution)/shard_map/all_to_all | solution.py:18
  416.7 18.8 %copy-start.105 = (f32[768]{0:T(1024)}, f32[768]{0:T(1024)S(1)}, u32[]{:S(2)}) copy-start(f32[768]{0:T(1024)S(1)} %get-tuple-element.293) | copy-start | bytes 9220
  416.7 18.8 %copy-start.107 = (f32[768]{0:T(1024)}, f32[768]{0:T(1024)S(1)}, u32[]{:S(2)}) copy-start(f32[768]{0:T(1024)S(1)} %get-tuple-element.294) | copy-start | bytes 9220
  435.5 24.7 %all-to-all-start.13 = ((bf16[8,768,128]{2,1,0:T(8,128)(2,1)}), bf16[8,768,128]{2,1,0:T(8,128)(2,1)}, u32[]{:S(2)}, u32[]{:S(2)}) async-start(bf16[8,768,128]{2,1,0:T(8,128)(2,1)} %broadcast_in_dim.301), calls=%async_computation.13 | async-start | bytes 3145728 | tf_op jit(solution)/shard_map/all_to_all | solution.py:18
  441.0 23.3 %copy-start.70 = (bf16[768,128]{0,1:T(8,128)(2,1)}, bf16[768,128]{0,1:T(8,128)(2,1)S(1)}, u32[]{:S(2)}) copy-start(bf16[768,128]{0,1:T(8,128)(2,1)S(1)} %fusion.98) | copy-start | bytes 589828
  475.9 24.8 %all-to-all-start.14 = ((bf16[8,768,128]{2,1,0:T(8,128)(2,1)}), bf16[8,768,128]{2,1,0:T(8,128)(2,1)}, u32[]{:S(2)}, u32[]{:S(2)}) async-start(bf16[8,768,128]{2,1,0:T(8,128)(2,1)} %bitcast.751), calls=%async_computation.14 | async-start | bytes 3145728 | tf_op jit(solution)/shard_map/all_to_all | solution.py:51
  500.7 24.2 %all-to-all-start.22 = ((bf16[8,768,128]{2,1,0:T(8,128)(2,1)}), bf16[8,768,128]{2,1,0:T(8,128)(2,1)S(1)}, u32[]{:S(2)}, u32[]{:S(2)}) async-start(bf16[8,768,128]{2,1,0:T(8,128)(2,1)} %bitcast.753), calls=%async_computation.22 | async-start | bytes 3145728 | tf_op jit(solution)/shard_map/all_to_all | solution.py:51
  506.2 25.8 %copy-start.88 = (f32[768]{0:T(1024)S(1)}, f32[768]{0:T(1024)}, u32[]{:S(2)}) copy-start(f32[768]{0:T(1024)} %copy-done.87) | copy-start | bytes 9220
  506.2 25.8 %copy-start.91 = (f32[768]{0:T(1024)S(1)}, f32[768]{0:T(1024)}, u32[]{:S(2)}) copy-start(f32[768]{0:T(1024)} %copy-done.90) | copy-start | bytes 9220
  506.2 25.7 %copy-start.123 = (f32[128]{0:T(128)S(1)}, f32[128]{0:T(128)}, u32[]{:S(2)}) copy-start(f32[128]{0:T(128)} %copy-done.122) | copy-start | bytes 1540
  506.5 33.4 %copy-start.100 = (f32[1536]{0:T(1024)S(1)}, f32[1536]{0:T(1024)}, u32[]{:S(2)}) copy-start(f32[1536]{0:T(1024)} %copy-done.99) | copy-start | bytes 18436
  525.6 10.2 %all-to-all-start.15 = ((f32[8,1,1536]{2,1,0:T(1,128)}), f32[8,1,1536]{2,1,0:T(1,128)S(1)}, u32[]{:S(2)}, u32[]{:S(2)}) async-start(f32[8,1,1536]{2,1,0:T(1,128)} %broadcast_in_dim.302), calls=%async_computation.15 | async-start | bytes 98304 | tf_op jit(solution)/shard_map/all_to_all | solution.py:18
  536.5 9.6 all-to-all-start.23
  548.1 28.7 %all-to-all-start.16 = ((bf16[8,768,128]{2,1,0:T(8,128)(2,1)}), bf16[8,768,128]{2,1,0:T(8,128)(2,1)}, u32[]{:S(2)}, u32[]{:S(2)}) async-start(bf16[8,768,128]{2,1,0:T(8,128)(2,1)} %broadcast_in_dim.303), calls=%async_computation.16 | async-start | bytes 3145728 | tf_op jit(solution)/shard_map/all_to_all | solution.py:18
  557.3 19.5 %collective-permute-start.2 = (bf16[1,768,128]{2,1,0:T(8,128)(2,1)S(1)}, bf16[1,768,128]{2,1,0:T(8,128)(2,1)S(1)}, u32[]{:S(2)}, u32[]{:S(2)}) collective-permute-start(bf16[1,768,128]{2,1,0:T(8,128)(2,1)S(1)} %get-tuple-element.254), channel_id=1, source_target_pairs={{64,0},{65,1},{66,2},{67,3},{68,4},{69,5},{70,6},{71,7},{72,8},{73... | collective-permute-start | bytes 589832 | tf_op jit(solution)/shard_map/ppermute | solution.py:76
  578.2 21.9 %all-to-all-start.24 = ((bf16[8,768,128]{2,1,0:T(8,128)(2,1)}), bf16[8,768,128]{2,1,0:T(8,128)(2,1)}, u32[]{:S(2)}, u32[]{:S(2)}) async-start(bf16[8,768,128]{2,1,0:T(8,128)(2,1)} %broadcast_in_dim.309), calls=%async_computation.24 | async-start | bytes 3145728 | tf_op jit(solution)/shard_map/all_to_all | solution.py:18
  646.4 22.6 %all-to-all-start.27 = ((bf16[8,768,128]{2,1,0:T(8,128)(2,1)}), bf16[8,768,128]{2,1,0:T(8,128)(2,1)}, u32[]{:S(2)}, u32[]{:S(2)}) async-start(bf16[8,768,128]{2,1,0:T(8,128)(2,1)} %broadcast_in_dim.311), calls=%async_computation.27 | async-start | bytes 3145728 | tf_op jit(solution)/shard_map/all_to_all | solution.py:18
  731.4 9.1 collective-permute-start.3
  741.8 21.4 %all-to-all-start.30 = ((bf16[8,768,128]{2,1,0:T(8,128)(2,1)}), bf16[8,768,128]{2,1,0:T(8,128)(2,1)}, u32[]{:S(2)}, u32[]{:S(2)}) async-start(bf16[8,768,128]{2,1,0:T(8,128)(2,1)} %broadcast_in_dim.313), calls=%async_computation.30 | async-start | bytes 3145728 | tf_op jit(solution)/shard_map/all_to_all | solution.py:18
  770.7 29.2 %all-to-all-start.31 = ((bf16[8,768,128]{2,1,0:T(8,128)(2,1)}), bf16[8,768,128]{2,1,0:T(8,128)(2,1)}, u32[]{:S(2)}, u32[]{:S(2)}) async-start(bf16[8,768,128]{2,1,0:T(8,128)(2,1)} %bitcast.750), calls=%async_computation.31 | async-start | bytes 3145728 | tf_op jit(solution)/shard_map/all_to_all | solution.py:51
  804.4 15.9 %all-to-all-start.32 = ((f32[8,1,1536]{2,1,0:T(1,128)}), f32[8,1,1536]{2,1,0:T(1,128)}, u32[]{:S(2)}, u32[]{:S(2)}) async-start(f32[8,1,1536]{2,1,0:T(1,128)} %broadcast_in_dim.314), calls=%async_computation.32 | async-start | bytes 98304 | tf_op jit(solution)/shard_map/all_to_all | solution.py:18
  823.1 22.7 %all-to-all-start.33 = ((bf16[8,768,128]{2,1,0:T(8,128)(2,1)}), bf16[8,768,128]{2,1,0:T(8,128)(2,1)}, u32[]{:S(2)}, u32[]{:S(2)}) async-start(bf16[8,768,128]{2,1,0:T(8,128)(2,1)} %broadcast_in_dim.315), calls=%async_computation.33 | async-start | bytes 3145728 | tf_op jit(solution)/shard_map/all_to_all | solution.py:18
  863.4 39.5 %all-to-all-start.34 = ((bf16[8,768,128]{2,1,0:T(8,128)(2,1)}), bf16[8,768,128]{2,1,0:T(8,128)(2,1)}, u32[]{:S(2)}, u32[]{:S(2)}) async-start(bf16[8,768,128]{2,1,0:T(8,128)(2,1)} %bitcast.749), calls=%async_computation.34 | async-start | bytes 3145728 | tf_op jit(solution)/shard_map/all_to_all | solution.py:51
  902.9 16.0 %copy-start.25 = (f32[1,768,128]{2,1,0:T(8,128)S(1)}, f32[1,768,128]{2,1,0:T(8,128)}, u32[]{:S(2)}) copy-start(f32[1,768,128]{2,1,0:T(8,128)} %copy-done.24) | copy-start | bytes 1179652
  902.9 16.0 %copy-start.44 = (bf16[1,768,128]{2,1,0:T(8,128)(2,1)S(1)}, bf16[1,768,128]{2,1,0:T(8,128)(2,1)}, u32[]{:S(2)}) copy-start(bf16[1,768,128]{2,1,0:T(8,128)(2,1)} %copy-done.42) | copy-start | bytes 589828
  906.1 18.2 %copy-start.150 = (bf16[8,16]{1,0:T(8,128)(2,1)S(1)}, bf16[8,16]{1,0:T(8,128)(2,1)}, u32[]{:S(2)}) copy-start(bf16[8,16]{1,0:T(8,128)(2,1)} %convert_element_type.778) | copy-start | bytes 772
  906.1 19.6 %copy-start.149 = (bf16[8,16]{1,0:T(8,128)(2,1)S(1)}, bf16[8,16]{1,0:T(8,128)(2,1)}, u32[]{:S(2)}) copy-start(bf16[8,16]{1,0:T(8,128)(2,1)} %convert_element_type.780) | copy-start | bytes 772
  906.8 12.0 %all-to-all-start.35 = ((f32[8,1,1536]{2,1,0:T(1,128)}), f32[8,1,1536]{2,1,0:T(1,128)S(1)}, u32[]{:S(2)}, u32[]{:S(2)}) async-start(f32[8,1,1536]{2,1,0:T(1,128)} %broadcast_in_dim.316), calls=%async_computation.35 | async-start | bytes 98304 | tf_op jit(solution)/shard_map/all_to_all | solution.py:18
  912.4 57.3 %reduce-scatter.5.cloned.1.call-start = ((), (), s32[]{:S(2)}) async-start(), calls=%async_computation.38 | async-start | bytes 3557376
  (157 other events, 624.0 us)
Sparse Core Ops, SparseCore 0:
  28.8 30.2 all-gather.2
  933.7 35.9 reduce-scatter.4

commit v3 on v2

--- a/solution.py
+++ b/solution.py
@@ -378,17 +378,25 @@
     return flat.reshape(block_shape)
 
 
-def sum_at_end(grads, dims):
+def sum_at_end(grads_zero, grads_last, dims):
     peers = lax.axis_size("dp")
-    pieces = [as_blocks(g.astype(jnp.bfloat16), d, peers) for g, d in zip(grads, dims)]
+    pieces = [
+        jnp.concatenate(
+            [as_blocks(g0.astype(jnp.bfloat16), d, peers), as_blocks(g1.astype(jnp.bfloat16), d, peers)]
+        )
+        for g0, g1, d in zip(grads_zero, grads_last, dims)
+    ]
     widths = [p.shape[1] for p in pieces]
     spare = -sum(widths) % 1024
-    pieces.append(jnp.zeros((peers, spare), jnp.bfloat16))
+    pieces.append(jnp.zeros((2 * peers, spare), jnp.bfloat16))
     total = lax.psum_scatter(
-        jnp.concatenate(pieces, axis=1).reshape(1, -1, 128), "dp", scatter_dimension=1, tiled=True
+        jnp.concatenate(pieces, axis=1).reshape(1, -1, 128),
+        ("section", "dp"),
+        scatter_dimension=1,
+        tiled=True,
     ).reshape(1, -1)
     reduced, at = ([], 0)
-    for g, d, w in zip(grads, dims, widths):
+    for g, d, w in zip(grads_zero, dims, widths):
         piece = total[0, at : at + w].astype(jnp.float32)
         reduced.append(from_blocks(piece, g.shape, d, peers)[None])
         at += w
@@ -399,15 +407,19 @@
     peers = lax.axis_size("dp")
     size = sum(w.size for w in weights)
     flat = jnp.concatenate([w.reshape(-1) for w in weights] + [jnp.zeros((-size % 1024,), jnp.bfloat16)])
-    every = lax.all_gather(flat[None], "dp", axis=0, tiled=True)
-    gathered, at = ([], 0)
-    for w, d in zip(weights, dims):
-        part = every[:, at : at + w.size].reshape(peers, *w.shape)
-        part = jnp.moveaxis(part, 0, d)
-        shape = part.shape
-        gathered.append(part.reshape(*shape[:d], shape[d] * shape[d + 1], *shape[d + 2 :]))
-        at += w.size
-    return tuple(gathered)
+    every = lax.all_gather(flat[None], ("section", "dp"), axis=0, tiled=True)
+    layers = []
+    for layer_index in range(every.shape[0] // peers):
+        rows = every[layer_index * peers : (layer_index + 1) * peers]
+        gathered, at = ([], 0)
+        for w, d in zip(weights, dims):
+            part = rows[:, at : at + w.size].reshape(peers, *w.shape)
+            part = jnp.moveaxis(part, 0, d)
+            shape = part.shape
+            gathered.append(part.reshape(*shape[:d], shape[d] * shape[d + 1], *shape[d + 2 :]))
+            at += w.size
+        layers.append(tuple(gathered))
+    return layers
 
 
 def shards(
@@ -426,7 +438,8 @@
     gain_second,
     shift_second,
 ):
-    gathered = gather_all(
+    dims = (0, 1, 1, 0, 0, 0, 1, 0, 0, 0, 0, 0)
+    weights_zero, weights_last = gather_all(
         (
             packed_weight[0],
             bias_pair[0],
@@ -441,60 +454,25 @@
             gain_second[0],
             shift_second[0],
         ),
-        (0, 1, 1, 0, 0, 0, 1, 0, 0, 0, 0, 0),
-    )
-    weights = gathered
-    is_first = lax.axis_index("section") == 0
-    micro_count = inputs.shape[0]
-    zero_block = jnp.zeros_like(inputs[0])
-    received = zero_block
-    returned = zero_block
-    outputs_list = []
-    kept_list = []
-    backs_list = []
-    grad_total = None
-    for tick_index in range(micro_count + 2):
-        if tick_index <= micro_count:
-            own_input = inputs[tick_index] if tick_index < micro_count else zero_block
-            stream = jnp.where(is_first, own_input, received)
-            result, kept_values = layer_forward(stream, weights)
-            outputs_list.append(result)
-            kept_list.append(kept_values)
-            if tick_index < micro_count:
-                received = from_behind(result.astype(jnp.bfloat16), "section", 1).astype(
-                    result.dtype
-                )
-        if tick_index >= 1:
-            own_grad = cotangent[tick_index - 1] if tick_index - 1 < micro_count else zero_block
-            out_grad = jnp.where(is_first, returned, own_grad)
-            early_kept = kept_list[tick_index - 2] if tick_index >= 2 else kept_list[tick_index]
-            late_kept = (
-                kept_list[tick_index] if tick_index <= micro_count else kept_list[tick_index - 2]
-            )
-            chosen = jax.tree.map(
-                lambda early_one, late_one: jnp.where(is_first, early_one, late_one),
-                early_kept,
-                late_kept,
-            )
-            input_grad, grads = layer_backward(out_grad, chosen, weights)
-            backs_list.append(input_grad)
-            if tick_index <= micro_count:
-                returned = from_behind(input_grad.astype(jnp.bfloat16), "section", -1).astype(
-                    input_grad.dtype
-                )
-            grad_total = grads if grad_total is None else jax.tree.map(jnp.add, grad_total, grads)
-    reduced = sum_at_end(grad_total, (0, 1, 1, 0, 0, 0, 1, 0, 0, 0, 0, 0))
-    section_outputs = jnp.stack(
-        [
-            jnp.where(is_first, outputs_list[slot_index], outputs_list[slot_index + 1])
-            for slot_index in range(micro_count)
-        ]
+        dims,
+    )
+    section_index = lax.axis_index("section")
+    is_first = section_index == 0
+    stream = lax.dynamic_index_in_dim(inputs, section_index, axis=0, keepdims=False)
+    out_grad = lax.dynamic_index_in_dim(cotangent, section_index, axis=0, keepdims=False)
+    middle, kept_zero = layer_forward(stream, weights_zero)
+    final, kept_last = layer_forward(middle, weights_last)
+    swap = [(0, 1), (1, 0)]
+    other_out = lax.ppermute(jnp.where(is_first, final, middle), "section", swap)
+    middle_grad, grads_last = layer_backward(out_grad, kept_last, weights_last)
+    input_grad, grads_zero = layer_backward(middle_grad, kept_zero, weights_zero)
+    other_grad = lax.ppermute(jnp.where(is_first, middle_grad, input_grad), "section", swap)
+    reduced = sum_at_end(grads_zero, grads_last, dims)
+    section_outputs = jnp.where(
+        is_first, jnp.stack([middle, other_out]), jnp.stack([other_out, final])
     )[None]
-    section_grads = jnp.stack(
-        [
-            jnp.where(is_first, backs_list[slot_index + 1], backs_list[slot_index])
-            for slot_index in range(micro_count)
-        ]
+    section_grads = jnp.where(
+        is_first, jnp.stack([input_grad, other_grad]), jnp.stack([other_grad, middle_grad])
     )[None]
     return (section_outputs, section_grads) + tuple(reduced)
 

time: 1000 us -> 822 us (0.82)
  blocking collectives: 163 us -> 76.9 us
  matrix products: 139 us -> 73.7 us
  starting transfers between devices: 131 us -> 89.5 us
  waiting for transfers between devices: 306 us -> 322 us
  other arithmetic: 68.5 us -> 52.9 us
  local copies, waits for them, and re-layouts: 164 us -> 177 us
    all_to_all x4 -> x2, blocking collectives: 91.6 us -> 46.4 us  [summed_on_arrival(): lax.all_to_all(parts, axis, split_axis=0, concat_axis=0, tiled=True)]
    all_to_all x6 -> x2, blocking collectives: 70.9 us -> 30.5 us  [sent_to_all(): return lax.all_to_all(copies, axis, split_axis=0, concat_axis=0, tiled=True)]
    all_to_all x18 -> x14, waiting for transfers between devices: 153 us -> 115 us  [sent_to_all(): return lax.all_to_all(copies, axis, split_axis=0, concat_axis=0, tiled=True)]
    all_gather x1, waiting for transfers between devices: 17.5 us -> 53 us  [gather_all(): every = lax.all_gather(flat[None], ('section', 'dp'), axis=0, tiled=True)]
    unnamed x3, waiting for transfers between devices: 7.97 us -> 42.3 us
    all_to_all x18 -> x14, starting transfers between devices: 82.4 us -> 59.1 us  [sent_to_all(): return lax.all_to_all(copies, axis, split_axis=0, concat_axis=0, tiled=True)]
    unnamed x395 -> x228, local copies, waits for them, and re-layouts: 50.7 us -> 62.8 us
    ppermute x4 -> x2, waiting for transfers between devices: 33.9 us -> 21.8 us  [the longest x1 12.3 us: shards(): lax.ppermute(jnp.where(is_first, middle_grad, input_grad), 'section', swap)]
  transfers between devices with their start and end apart: 32 -> 24, of which waited for: 27 -> 22; matrix products, arithmetic and copies ran while one was open for 17% -> 17% of each run, Pallas kernels for 0% -> 0%
where the time goes in v3:
time: 822 us; the launch traced here: 809 us
  waiting for transfers between devices  322 us (39%)
  local copies, waits for them, and re-layouts  177 us (22%)
  starting transfers between devices  89.5 us (11%)
  blocking collectives  76.9 us (9%)
  matrix products  73.7 us (9%)
  other arithmetic  52.9 us (6%)
  between operations  16.1 us (2%)
    all_to_all x14, waiting for transfers between devices, sent_to_all(): return lax.all_to_all(copies, axis, split_axis=0, concat_axis=0, tiled=True)  115 us
    all_to_all x6, waiting for transfers between devices, summed_on_arrival(): lax.all_to_all(parts, axis, split_axis=0, concat_axis=0, tiled=True)  90.3 us
    unnamed x228, local copies, waits for them, and re-layouts  62.8 us
    all_to_all x14, starting transfers between devices, sent_to_all(): return lax.all_to_all(copies, axis, split_axis=0, concat_axis=0, tiled=True)  59.1 us
    all_gather x1, waiting for transfers between devices, gather_all(): every = lax.all_gather(flat[None], ('section', 'dp'), axis=0, tiled=True)  53 us
    all_to_all x2, blocking collectives, summed_on_arrival(): lax.all_to_all(parts, axis, split_axis=0, concat_axis=0, tiled=True)  46.4 us
    unnamed x3, waiting for transfers between devices  42.3 us
    all_to_all x2, blocking collectives, sent_to_all(): return lax.all_to_all(copies, axis, split_axis=0, concat_axis=0, tiled=True)  30.5 us
  transfers between devices with their start and end apart: 24, of which 22 were waited for; matrix products, arithmetic and copies ran while one was open for 17% of the time, Pallas kernels for 0%

profile of v3, /device:TPU:0, one launch (start us, length us, event | category | flops | bytes accessed | tf_op | source)
XLA Modules:
  0.0 809.0 jit_solution(17597425664250880801)
XLA Ops:
  10.1 18.6 %concatenate.107 = bf16[197632]{0:T(1024)(128)(2,1)} concatenate(bf16[49152]{0:T(1024)(128)(2,1)S(1)} %reshape_squeeze.15, bf16[32]{0:T(256)(128)(2,1)S(1)} %reshape_squeeze.16, bf16[16384]{0:T(1024)(128)(2,1)} %bitcast.625, bf16[16]{0:T(256)(128)(2,1)} %bitcast.628, bf16[65536]{0:T(1024)(128)(2,1)S(1)} %bitcast.612, bf16[64]{0:T(256)(128)(2,1)} %bitcast.629, ...), dimensions={0} | concatenate | bytes 790528 | tf_op jit(solution)/shard_map/concatenate | solution.py:409
  29.8 6.3 all-to-all-start
  36.3 6.1 all-to-all-done
  42.5 53.0 %all-gather.3.cloned.1.call-done = bf16[3162112]{0:T(1024)(128)(2,1)} async-done(((bf16[197632]{0:T(1024)(128)(2,1)}), bf16[3162112]{0:T(1024)(128)(2,1)}) %all-gather.3.cloned.1.call-update) | async-done | bytes 6324240 | tf_op jit(solution)/shard_map/all_gather | solution.py:410
  95.4 6.2 reshape.1987
  105.0 4.4 all-to-all-start.1
  118.0 12.4 %all-to-all-done.1 = bf16[8,768,128]{2,1,0:T(8,128)(2,1)} async-done(((bf16[8,768,128]{2,1,0:T(8,128)(2,1)}), bf16[8,768,128]{2,1,0:T(8,128)(2,1)}, u32[]{:S(2)}, u32[]{:S(2)}) %all-to-all-start.1) | async-done | bytes 1572896 | tf_op jit(solution)/shard_map/all_to_all | solution.py:18
  139.8 3.6 all-to-all-start.2
  143.5 20.5 %all-to-all-done.2 = bf16[8,768,128]{2,1,0:T(8,128)(2,1)S(1)} async-done(((bf16[8,768,128]{2,1,0:T(8,128)(2,1)}), bf16[8,768,128]{2,1,0:T(8,128)(2,1)S(1)}, u32[]{:S(2)}, u32[]{:S(2)}) %all-to-all-start.2) | async-done | bytes 1572896 | tf_op jit(solution)/shard_map/all_to_all | solution.py:51
  165.2 3.9 all-to-all-start.3
  169.2 6.1 all-to-all-done.3
  177.1 4.3 all-to-all-start.4
  181.4 4.7 fusion.142
  192.4 8.6 %all-to-all-done.4 = bf16[8,768,128]{1,2,0:T(8,128)(2,1)} async-done(((bf16[8,768,128]{1,2,0:T(8,128)(2,1)}), bf16[8,768,128]{1,2,0:T(8,128)(2,1)}, u32[]{:S(2)}, u32[]{:S(2)}) %all-to-all-start.4) | async-done | bytes 1572896 | tf_op jit(solution)/shard_map/all_to_all | solution.py:18
  206.1 3.6 all-to-all-start.5
  209.8 20.5 %all-to-all-done.5 = bf16[8,768,128]{2,1,0:T(8,128)(2,1)S(1)} async-done(((bf16[8,768,128]{2,1,0:T(8,128)(2,1)}), bf16[8,768,128]{2,1,0:T(8,128)(2,1)S(1)}, u32[]{:S(2)}, u32[]{:S(2)}) %all-to-all-start.5) | async-done | bytes 1572896 | tf_op jit(solution)/shard_map/all_to_all | solution.py:51
  231.6 3.6 all-to-all-start.6
  235.4 6.1 all-to-all-done.6
  243.3 4.7 all-to-all-start.7
  250.9 16.7 %all-to-all-done.7 = bf16[8,768,128]{2,1,0:T(8,128)(2,1)} async-done(((bf16[8,768,128]{2,1,0:T(8,128)(2,1)}), bf16[8,768,128]{2,1,0:T(8,128)(2,1)}, u32[]{:S(2)}, u32[]{:S(2)}) %all-to-all-start.7) | async-done | bytes 1572896 | tf_op jit(solution)/shard_map/all_to_all | solution.py:18
  276.7 3.6 all-to-all-start.8
  280.3 20.5 %all-to-all-done.8 = bf16[8,768,128]{2,1,0:T(8,128)(2,1)S(1)} async-done(((bf16[8,768,128]{2,1,0:T(8,128)(2,1)}), bf16[8,768,128]{2,1,0:T(8,128)(2,1)S(1)}, u32[]{:S(2)}, u32[]{:S(2)}) %all-to-all-start.8) | async-done | bytes 1572896 | tf_op jit(solution)/shard_map/all_to_all | solution.py:51
  302.2 3.6 all-to-all-start.9
  305.9 6.1 all-to-all-done.9
  313.9 4.3 all-to-all-start.10
  319.2 18.5 %all-to-all-done.10 = bf16[8,768,128]{1,2,0:T(8,128)(2,1)} async-done(((bf16[8,768,128]{1,2,0:T(8,128)(2,1)}), bf16[8,768,128]{1,2,0:T(8,128)(2,1)}, u32[]{:S(2)}, u32[]{:S(2)}) %all-to-all-start.10) | async-done | bytes 1572896 | tf_op jit(solution)/shard_map/all_to_all | solution.py:18
  339.0 4.1 all-to-all-start.12
  345.9 3.9 convolution_add_fusion
  349.8 13.9 %all-to-all-done.12 = bf16[8,768,128]{2,1,0:T(8,128)(2,1)S(1)} async-done(((bf16[8,768,128]{2,1,0:T(8,128)(2,1)}), bf16[8,768,128]{2,1,0:T(8,128)(2,1)S(1)}, u32[]{:S(2)}, u32[]{:S(2)}) %all-to-all-start.12) | async-done | bytes 1572896 | tf_op jit(solution)/shard_map/all_to_all | solution.py:18
  363.7 5.0 fusion.147
  370.1 25.2 %all_to_all.128 = bf16[8,768,128]{2,1,0:T(8,128)(2,1)S(1)} all-to-all(bf16[8,768,128]{2,1,0:T(8,128)(2,1)S(1)} %bitcast.563), channel_id=1, replica_groups=mesh['section'=2,'dp'=8,'tensor'=8] {'tensor'}, dimensions={0} | all-to-all | bytes 3145728 | tf_op jit(solution)/shard_map/all_to_all | solution.py:51
  397.1 8.7 %all_to_all.129 = f32[8,1,1536]{2,1,0:T(1,128)S(1)} all-to-all(f32[8,1,1536]{2,1,0:T(1,128)S(1)} %broadcast_in_dim.205), channel_id=1, replica_groups=mesh['section'=2,'dp'=8,'tensor'=8] {'tensor'}, dimensions={0} | all-to-all | bytes 98304 | tf_op jit(solution)/shard_map/all_to_all | solution.py:18
  410.1 21.8 %all_to_all.130 = bf16[8,768,128]{2,1,0:T(8,128)(2,1)S(1)} all-to-all(bf16[8,768,128]{2,1,0:T(8,128)(2,1)S(1)} %broadcast_in_dim.206), channel_id=1, replica_groups=mesh['section'=2,'dp'=8,'tensor'=8] {'tensor'}, dimensions={0} | all-to-all | bytes 3145728 | tf_op jit(solution)/shard_map/all_to_all | solution.py:18
  447.1 21.3 %all_to_all.131 = bf16[8,768,128]{2,1,0:T(8,128)(2,1)S(1)} all-to-all(bf16[8,768,128]{2,1,0:T(8,128)(2,1)S(1)} %bitcast.564), channel_id=1, replica_groups=mesh['section'=2,'dp'=8,'tensor'=8] {'tensor'}, dimensions={0} | all-to-all | bytes 3145728 | tf_op jit(solution)/shard_map/all_to_all | solution.py:51
  471.7 3.3 all-to-all-start.17
  485.5 4.5 all-to-all-start.18
  490.1 3.6 convolution_convert_fusion.8
  496.3 3.1 fusion.43
  510.1 2.8 reshape_reshape.29
  515.2 4.3 fusion.148
  519.5 3.5 convolution_convert_fusion.9
  528.1 5.7 all-to-all-start.19
  533.8 3.0 pad_maximum_fusion.1
  539.4 8.9 %all-to-all-done.19 = bf16[8,768,128]{2,1,0:T(8,128)(2,1)S(1)} async-done(((bf16[8,768,128]{2,1,0:T(8,128)(2,1)}), bf16[8,768,128]{2,1,0:T(8,128)(2,1)S(1)}, u32[]{:S(2)}, u32[]{:S(2)}) %all-to-all-start.19) | async-done | bytes 1572896 | tf_op jit(solution)/shard_map/all_to_all | solution.py:51
  549.7 4.1 all-to-all-start.20
  553.8 3.1 fusion.42
  562.9 4.3 all-to-all-start.21
  567.3 3.0 pad_maximum_fusion
  571.5 13.8 %all-to-all-done.21 = bf16[8,768,128]{2,1,0:T(8,128)(2,1)} async-done(((bf16[8,768,128]{2,1,0:T(8,128)(2,1)}), bf16[8,768,128]{2,1,0:T(8,128)(2,1)}, u32[]{:S(2)}, u32[]{:S(2)}) %all-to-all-start.21) | async-done | bytes 1572896 | tf_op jit(solution)/shard_map/all_to_all | solution.py:18
  587.4 4.0 bitcast_reduce_fusion
  591.4 4.2 multiply_reduce_fusion
  604.7 3.6 all-to-all-start.22
  619.4 4.9 dynamic-update-slice.2
  625.8 13.0 %dynamic-update-slice.4 = bf16[16,197632]{1,0:T(8,128)(2,1)} dynamic-update-slice(bf16[16,197632]{1,0:T(8,128)(2,1)} %dynamic-update-slice.3, bf16[16,65536]{1,0:T(8,128)(2,1)} %pad_maximum_fusion.1, s32[]{} %constant.165, s32[]{} %constant.173) | dynamic-update-slice | bytes 4194308
  640.2 12.8 %dynamic-update-slice.6 = bf16[16,197632]{1,0:T(8,128)(2,1)} dynamic-update-slice(bf16[16,197632]{1,0:T(8,128)(2,1)} %dynamic-update-slice.5, bf16[16,65536]{1,0:T(8,128)(2,1)} %pad_maximum_fusion, s32[]{} %constant.165, s32[]{} %constant.177) | dynamic-update-slice | bytes 4194308
  664.5 6.5 reshape.1962
  676.8 5.8 all-to-all-start.11
  682.8 19.8 %all-to-all-done.11 = bf16[8,768,128]{2,1,0:T(8,128)(2,1)} async-done(((bf16[8,768,128]{2,1,0:T(8,128)(2,1)}), bf16[8,768,128]{2,1,0:T(8,128)(2,1)}, u32[]{:S(2)}, u32[]{:S(2)}) %all-to-all-start.11) | async-done | bytes 1572896 | tf_op jit(solution)/shard_map/all_to_all | solution.py:51
  705.7 3.6 all-to-all-start.23
  715.9 3.6 fusion.56
  723.9 9.5 %collective-permute-done = f32[1,768,128]{2,1,0:T(8,128)} collective-permute-done((f32[1,768,128]{2,1,0:T(8,128)}, f32[1,768,128]{2,1,0:T(8,128)}, u32[]{:S(2)}, u32[]{:S(2)}) %collective-permute-start) | collective-permute-done | bytes 393248 | tf_op jit(solution)/shard_map/ppermute | solution.py:466
  735.5 12.3 %collective-permute-done.1 = f32[1,768,128]{2,1,0:T(8,128)S(1)} collective-permute-done((f32[1,768,128]{2,1,0:T(8,128)S(1)}, f32[1,768,128]{2,1,0:T(8,128)S(1)}, u32[]{:S(2)}, u32[]{:S(2)}) %collective-permute-start.1) | collective-permute-done | bytes 393248 | tf_op jit(solution)/shard_map/ppermute | solution.py:469
  748.7 42.2 %reduce-scatter.5.cloned.1.call-done = bf16[1,1544,128]{2,1,0:T(8,128)(2,1)} async-done(((bf16[1,24704,128]{2,1,0:T(8,128)(2,1)}), bf16[1,1544,128]{2,1,0:T(8,128)(2,1)}) %reduce-scatter.5.cloned.1.call-update) | async-done | bytes 395280
  791.0 4.2 copy.343
  (466 shorter events, 197.6 us)
Async XLA Ops:
  7.2 21.5 %copy-start.4 = (f32[2,1,768,128]{3,2,1,0:T(8,128)S(1)}, f32[2,1,768,128]{3,2,1,0:T(8,128)}, u32[]{:S(2)}) copy-start(f32[2,1,768,128]{3,2,1,0:T(8,128)} %param.14) | copy-start | bytes 2359300
  7.2 88.2 %all-gather.3.cloned.1.call-start = ((), (), s32[]{:S(2)}) async-start(), calls=%async_computation.25 | async-start | bytes 6719488 | tf_op jit(solution)/shard_map/all_gather | solution.py:410
  29.8 12.6 %all-to-all-start = ((f32[8,1,1536]{2,1,0:T(1,128)}), f32[8,1,1536]{2,1,0:T(1,128)S(1)}, u32[]{:S(2)}, u32[]{:S(2)}) async-start(f32[8,1,1536]{2,1,0:T(1,128)} %broadcast_in_dim.192), calls=%async_computation | async-start | bytes 98304 | tf_op jit(solution)/shard_map/all_to_all | solution.py:18
  105.0 25.4 %all-to-all-start.1 = ((bf16[8,768,128]{2,1,0:T(8,128)(2,1)}), bf16[8,768,128]{2,1,0:T(8,128)(2,1)}, u32[]{:S(2)}, u32[]{:S(2)}) async-start(bf16[8,768,128]{2,1,0:T(8,128)(2,1)} %broadcast_in_dim.195), calls=%async_computation.1 | async-start | bytes 3145728 | tf_op jit(solution)/shard_map/all_to_all | solution.py:18
  113.2 19.8 %copy-start.81 = (f32[2,64]{1,0:T(2,128)}, f32[2,64]{1,0:T(2,128)S(1)}, u32[]{:S(2)}) copy-start(f32[2,64]{1,0:T(2,128)S(1)} %reshape.1967) | copy-start | bytes 1540
  113.3 22.0 %copy-start.89 = (f32[2,64]{1,0:T(2,128)}, f32[2,64]{1,0:T(2,128)S(1)}, u32[]{:S(2)}) copy-start(f32[2,64]{1,0:T(2,128)S(1)} %reshape.1966) | copy-start | bytes 1540
  139.8 24.2 %all-to-all-start.2 = ((bf16[8,768,128]{2,1,0:T(8,128)(2,1)}), bf16[8,768,128]{2,1,0:T(8,128)(2,1)S(1)}, u32[]{:S(2)}, u32[]{:S(2)}) async-start(bf16[8,768,128]{2,1,0:T(8,128)(2,1)} %bitcast.551), calls=%async_computation.2 | async-start | bytes 3145728 | tf_op jit(solution)/shard_map/all_to_all | solution.py:51
  143.5 21.0 %copy-start.75 = (f32[128]{0:T(128)}, f32[128]{0:T(128)S(1)}, u32[]{:S(2)}) copy-start(f32[128]{0:T(128)S(1)} %reshape.1968) | copy-start | bytes 1540
  164.2 12.9 %copy-start.8 = (f32[768,128]{1,0:T(8,128)}, f32[768,128]{1,0:T(8,128)S(1)}, u32[]{:S(2)}) copy-start(f32[768,128]{1,0:T(8,128)S(1)} %convert_reduce_fusion.7) | copy-start | bytes 1179652
  165.2 10.1 %all-to-all-start.3 = ((f32[8,1,1536]{2,1,0:T(1,128)}), f32[8,1,1536]{2,1,0:T(1,128)S(1)}, u32[]{:S(2)}, u32[]{:S(2)}) async-start(f32[8,1,1536]{2,1,0:T(1,128)} %broadcast_in_dim.198), calls=%async_computation.3 | async-start | bytes 98304 | tf_op jit(solution)/shard_map/all_to_all | solution.py:18
  169.2 8.0 copy-start.67
  177.1 23.8 %all-to-all-start.4 = ((bf16[8,768,128]{1,2,0:T(8,128)(2,1)}), bf16[8,768,128]{1,2,0:T(8,128)(2,1)}, u32[]{:S(2)}, u32[]{:S(2)}) async-start(bf16[8,768,128]{1,2,0:T(8,128)(2,1)} %broadcast_in_dim.199), calls=%async_computation.4 | async-start | bytes 3145728 | tf_op jit(solution)/shard_map/all_to_all | solution.py:18
  191.0 9.9 %copy-start.43 = (bf16[1024,512]{1,0:T(8,128)(2,1)S(1)}, bf16[1024,512]{1,0:T(8,128)(2,1)}, u32[]{:S(2)}) copy-start(bf16[1024,512]{1,0:T(8,128)(2,1)} %reshape_reshape.25) | copy-start | bytes 3145732
  206.1 24.2 %all-to-all-start.5 = ((bf16[8,768,128]{2,1,0:T(8,128)(2,1)}), bf16[8,768,128]{2,1,0:T(8,128)(2,1)S(1)}, u32[]{:S(2)}, u32[]{:S(2)}) async-start(bf16[8,768,128]{2,1,0:T(8,128)(2,1)} %bitcast.549), calls=%async_computation.5 | async-start | bytes 3145728 | tf_op jit(solution)/shard_map/all_to_all | solution.py:51
  209.8 21.0 %copy-start.77 = (f32[128]{0:T(128)}, f32[128]{0:T(128)S(1)}, u32[]{:S(2)}) copy-start(f32[128]{0:T(128)S(1)} %reshape.1972) | copy-start | bytes 1540
  230.6 12.7 %copy-start.10 = (f32[768,128]{1,0:T(8,128)}, f32[768,128]{1,0:T(8,128)S(1)}, u32[]{:S(2)}) copy-start(f32[768,128]{1,0:T(8,128)S(1)} %convert_reduce_fusion.6) | copy-start | bytes 1179652
  230.9 70.2 %copy-start.6 = (f32[768,128]{1,0:T(8,128)}, f32[768,128]{1,0:T(8,128)S(1)}, u32[]{:S(2)}) copy-start(f32[768,128]{1,0:T(8,128)S(1)} %get-tuple-element.188) | copy-start | bytes 1179652
  231.6 9.9 %all-to-all-start.6 = ((f32[8,1,1536]{2,1,0:T(1,128)}), f32[8,1,1536]{2,1,0:T(1,128)S(1)}, u32[]{:S(2)}, u32[]{:S(2)}) async-start(f32[8,1,1536]{2,1,0:T(1,128)} %broadcast_in_dim.200), calls=%async_computation.6 | async-start | bytes 98304 | tf_op jit(solution)/shard_map/all_to_all | solution.py:18
  235.4 8.0 copy-start.69
  243.3 5.8 copy-start.34
  243.3 24.2 %all-to-all-start.7 = ((bf16[8,768,128]{2,1,0:T(8,128)(2,1)}), bf16[8,768,128]{2,1,0:T(8,128)(2,1)}, u32[]{:S(2)}, u32[]{:S(2)}) async-start(bf16[8,768,128]{2,1,0:T(8,128)(2,1)} %broadcast_in_dim.201), calls=%async_computation.7 | async-start | bytes 3145728 | tf_op jit(solution)/shard_map/all_to_all | solution.py:18
  248.2 21.7 %copy-start.83 = (f32[2,64]{1,0:T(2,128)}, f32[2,64]{1,0:T(2,128)S(1)}, u32[]{:S(2)}) copy-start(f32[2,64]{1,0:T(2,128)S(1)} %reshape.1976) | copy-start | bytes 1540
  248.3 23.9 %copy-start.91 = (f32[2,64]{1,0:T(2,128)}, f32[2,64]{1,0:T(2,128)S(1)}, u32[]{:S(2)}) copy-start(f32[2,64]{1,0:T(2,128)S(1)} %reshape.1975) | copy-start | bytes 1540
  250.9 18.9 %copy-start.55 = (bf16[1024,3,128]{0,2,1:T(8,128)(2,1)}, bf16[1024,3,128]{0,2,1:T(8,128)(2,1)S(1)}, u32[]{:S(2)}) copy-start(bf16[1024,3,128]{0,2,1:T(8,128)(2,1)S(1)} %copy.196) | copy-start | bytes 2359300
  276.7 24.2 %all-to-all-start.8 = ((bf16[8,768,128]{2,1,0:T(8,128)(2,1)}), bf16[8,768,128]{2,1,0:T(8,128)(2,1)S(1)}, u32[]{:S(2)}, u32[]{:S(2)}) async-start(bf16[8,768,128]{2,1,0:T(8,128)(2,1)} %bitcast.547), calls=%async_computation.8 | async-start | bytes 3145728 | tf_op jit(solution)/shard_map/all_to_all | solution.py:51
  280.3 21.0 %copy-start.72 = (f32[128]{0:T(128)}, f32[128]{0:T(128)S(1)}, u32[]{:S(2)}) copy-start(f32[128]{0:T(128)S(1)} %reshape.1977) | copy-start | bytes 1540
  301.4 12.5 %copy-start.20 = (f32[768,128]{1,0:T(8,128)}, f32[768,128]{1,0:T(8,128)S(1)}, u32[]{:S(2)}) copy-start(f32[768,128]{1,0:T(8,128)S(1)} %get-tuple-element.187) | copy-start | bytes 1179652
  302.2 9.9 %all-to-all-start.9 = ((f32[8,1,1536]{2,1,0:T(1,128)}), f32[8,1,1536]{2,1,0:T(1,128)S(1)}, u32[]{:S(2)}, u32[]{:S(2)}) async-start(f32[8,1,1536]{2,1,0:T(1,128)} %broadcast_in_dim.202), calls=%async_computation.9 | async-start | bytes 98304 | tf_op jit(solution)/shard_map/all_to_all | solution.py:18
  305.9 89.6 %copy-start.65 = (f32[128]{0:T(128)}, f32[128]{0:T(128)S(1)}, u32[]{:S(2)}) copy-start(f32[128]{0:T(128)S(1)} %reshape.1978) | copy-start | bytes 1540
  313.9 23.8 %all-to-all-start.10 = ((bf16[8,768,128]{1,2,0:T(8,128)(2,1)}), bf16[8,768,128]{1,2,0:T(8,128)(2,1)}, u32[]{:S(2)}, u32[]{:S(2)}) async-start(bf16[8,768,128]{1,2,0:T(8,128)(2,1)} %broadcast_in_dim.203), calls=%async_computation.10 | async-start | bytes 3145728 | tf_op jit(solution)/shard_map/all_to_all | solution.py:18
  339.0 24.7 %all-to-all-start.12 = ((bf16[8,768,128]{2,1,0:T(8,128)(2,1)}), bf16[8,768,128]{2,1,0:T(8,128)(2,1)S(1)}, u32[]{:S(2)}, u32[]{:S(2)}) async-start(bf16[8,768,128]{2,1,0:T(8,128)(2,1)} %broadcast_in_dim.204), calls=%async_computation.12 | async-start | bytes 3145728 | tf_op jit(solution)/shard_map/all_to_all | solution.py:18
  363.7 5.0 copy-start.45
  370.1 63.6 %slice-start.2 = ((s8[4718592]{0:T(1024)(128)(4,1)}), s8[524288]{0:T(1024)(128)(4,1)S(1)}, s32[]{:S(2)}) async-start(s8[4718592]{0:T(1024)(128)(4,1)} %bitcast.557), calls=%async_computation.29 | async-start | bytes 1048576
  407.2 26.5 %slice-start.3 = ((s8[4718592]{0:T(1024)(128)(4,1)}), s8[4194304]{0:T(1024)(128)(4,1)S(1)}, s32[]{:S(2)}) async-start(s8[4718592]{0:T(1024)(128)(4,1)} %bitcast.557), calls=%async_computation.30 | async-start | bytes 8388608
  410.1 23.0 %copy-start.52 = (bf16[1,8,128,128]{3,1,2,0:T(8,128)(2,1)S(1)}, bf16[1,8,128,128]{3,1,2,0:T(8,128)(2,1)}, u32[]{:S(2)}) copy-start(bf16[1,8,128,128]{3,1,2,0:T(8,128)(2,1)} %copy-done.51) | copy-start | bytes 786436
  471.7 9.6 %all-to-all-start.17 = ((f32[8,1,1536]{2,1,0:T(1,128)}), f32[8,1,1536]{2,1,0:T(1,128)S(1)}, u32[]{:S(2)}, u32[]{:S(2)}) async-start(f32[8,1,1536]{2,1,0:T(1,128)} %broadcast_in_dim.207), calls=%async_computation.17 | async-start | bytes 98304 | tf_op jit(solution)/shard_map/all_to_all | solution.py:18
  485.5 29.6 %all-to-all-start.18 = ((bf16[8,768,128]{2,1,0:T(8,128)(2,1)}), bf16[8,768,128]{2,1,0:T(8,128)(2,1)}, u32[]{:S(2)}, u32[]{:S(2)}) async-start(bf16[8,768,128]{2,1,0:T(8,128)(2,1)} %broadcast_in_dim.208), calls=%async_computation.18 | async-start | bytes 3145728 | tf_op jit(solution)/shard_map/all_to_all | solution.py:18
  528.1 20.2 %all-to-all-start.19 = ((bf16[8,768,128]{2,1,0:T(8,128)(2,1)}), bf16[8,768,128]{2,1,0:T(8,128)(2,1)S(1)}, u32[]{:S(2)}, u32[]{:S(2)}) async-start(bf16[8,768,128]{2,1,0:T(8,128)(2,1)} %bitcast.562), calls=%async_computation.19 | async-start | bytes 3145728 | tf_op jit(solution)/shard_map/all_to_all | solution.py:51
  539.4 9.1 %copy-start.68 = (f32[128]{0:T(128)S(1)}, f32[128]{0:T(128)}, u32[]{:S(2)}) copy-start(f32[128]{0:T(128)} %copy-done.67) | copy-start | bytes 1540
  548.5 11.6 %copy-start.16 = (f32[768,128]{1,0:T(8,128)}, f32[768,128]{1,0:T(8,128)S(1)}, u32[]{:S(2)}) copy-start(f32[768,128]{1,0:T(8,128)S(1)} %convert_reduce_fusion.1) | copy-start | bytes 1179652
  549.7 10.3 %all-to-all-start.20 = ((f32[8,1,1536]{2,1,0:T(1,128)}), f32[8,1,1536]{2,1,0:T(1,128)S(1)}, u32[]{:S(2)}, u32[]{:S(2)}) async-start(f32[8,1,1536]{2,1,0:T(1,128)} %broadcast_in_dim.209), calls=%async_computation.20 | async-start | bytes 98304 | tf_op jit(solution)/shard_map/all_to_all | solution.py:18
  562.9 22.3 %all-to-all-start.21 = ((bf16[8,768,128]{2,1,0:T(8,128)(2,1)}), bf16[8,768,128]{2,1,0:T(8,128)(2,1)}, u32[]{:S(2)}, u32[]{:S(2)}) async-start(bf16[8,768,128]{2,1,0:T(8,128)(2,1)} %broadcast_in_dim.210), calls=%async_computation.21 | async-start | bytes 3145728 | tf_op jit(solution)/shard_map/all_to_all | solution.py:18
  570.3 15.0 %copy-start.50 = (bf16[1,8,128,128]{3,1,2,0:T(8,128)(2,1)S(1)}, bf16[1,8,128,128]{3,1,2,0:T(8,128)(2,1)}, u32[]{:S(2)}) copy-start(bf16[1,8,128,128]{3,1,2,0:T(8,128)(2,1)} %copy-done.49) | copy-start | bytes 786436
  570.4 17.0 %copy-start.62 = (f32[2,768]{1,0:T(2,128)S(1)}, f32[2,768]{1,0:T(2,128)}, u32[]{:S(2)}) copy-start(f32[2,768]{1,0:T(2,128)} %copy-done.61) | copy-start | bytes 18436
  587.3 8.2 %slice-start = ((s8[4718592]{0:T(1024)(128)(4,1)}), s8[4194304]{0:T(1024)(128)(4,1)S(1)}, s32[]{:S(2)}) async-start(s8[4718592]{0:T(1024)(128)(4,1)} %bitcast.555), calls=%async_computation.27 | async-start | bytes 8388608
  604.7 49.8 %all-to-all-start.22 = ((bf16[8,768,128]{2,1,0:T(8,128)(2,1)}), bf16[8,768,128]{2,1,0:T(8,128)(2,1)S(1)}, u32[]{:S(2)}, u32[]{:S(2)}) async-start(bf16[8,768,128]{2,1,0:T(8,128)(2,1)} %bitcast.561), calls=%async_computation.22 | async-start | bytes 3145728 | tf_op jit(solution)/shard_map/all_to_all | solution.py:51
  608.3 182.7 %reduce-scatter.5.cloned.1.call-start = ((), (), s32[]{:S(2)}) async-start(), calls=%async_computation.26 | async-start | bytes 6719488
  655.6 15.4 %copy-start.22 = (f32[768,128]{1,0:T(8,128)}, f32[768,128]{1,0:T(8,128)S(1)}, u32[]{:S(2)}) copy-start(f32[768,128]{1,0:T(8,128)S(1)} %convert_reduce_fusion) | copy-start | bytes 1179652
  676.8 5.9 copy-start.74
  676.8 25.8 %all-to-all-start.11 = ((bf16[8,768,128]{2,1,0:T(8,128)(2,1)}), bf16[8,768,128]{2,1,0:T(8,128)(2,1)}, u32[]{:S(2)}, u32[]{:S(2)}) async-start(bf16[8,768,128]{2,1,0:T(8,128)(2,1)} %bitcast.545), calls=%async_computation.11 | async-start | bytes 3145728 | tf_op jit(solution)/shard_map/all_to_all | solution.py:51
  682.6 26.7 %copy-start.5 = (f32[2,1,768,128]{3,2,1,0:T(8,128)S(1)}, f32[2,1,768,128]{3,2,1,0:T(8,128)}, u32[]{:S(2)}) copy-start(f32[2,1,768,128]{3,2,1,0:T(8,128)} %param.14) | copy-start | bytes 2359300
  682.6 26.7 %copy-start.9 = (f32[768,128]{1,0:T(8,128)S(1)}, f32[768,128]{1,0:T(8,128)}, u32[]{:S(2)}) copy-start(f32[768,128]{1,0:T(8,128)} %copy-done.8) | copy-start | bytes 1179652
  682.6 26.7 %copy-start.11 = (f32[768,128]{1,0:T(8,128)S(1)}, f32[768,128]{1,0:T(8,128)}, u32[]{:S(2)}) copy-start(f32[768,128]{1,0:T(8,128)} %copy-done.10) | copy-start | bytes 1179652
  682.6 26.7 %copy-start.73 = (f32[128]{0:T(128)S(1)}, f32[128]{0:T(128)}, u32[]{:S(2)}) copy-start(f32[128]{0:T(128)} %copy-done.72) | copy-start | bytes 1540
  682.6 26.7 %copy-start.76 = (f32[128]{0:T(128)S(1)}, f32[128]{0:T(128)}, u32[]{:S(2)}) copy-start(f32[128]{0:T(128)} %copy-done.75) | copy-start | bytes 1540
  682.6 26.7 %copy-start.78 = (f32[128]{0:T(128)S(1)}, f32[128]{0:T(128)}, u32[]{:S(2)}) copy-start(f32[128]{0:T(128)} %copy-done.77) | copy-start | bytes 1540
  705.0 10.8 %copy-start.13 = (f32[768,128]{1,0:T(8,128)S(1)}, f32[768,128]{1,0:T(8,128)}, u32[]{:S(2)}) copy-start(f32[768,128]{1,0:T(8,128)} %copy-done.12) | copy-start | bytes 1179652
  705.0 10.8 %copy-start.15 = (f32[768,128]{1,0:T(8,128)S(1)}, f32[768,128]{1,0:T(8,128)}, u32[]{:S(2)}) copy-start(f32[768,128]{1,0:T(8,128)} %copy-done.14) | copy-start | bytes 1179652
  705.0 10.8 %copy-start.17 = (f32[768,128]{1,0:T(8,128)S(1)}, f32[768,128]{1,0:T(8,128)}, u32[]{:S(2)}) copy-start(f32[768,128]{1,0:T(8,128)} %copy-done.16) | copy-start | bytes 1179652
  705.0 10.8 %copy-start.66 = (f32[128]{0:T(128)S(1)}, f32[128]{0:T(128)}, u32[]{:S(2)}) copy-start(f32[128]{0:T(128)} %copy-done.65) | copy-start | bytes 1540
  705.0 10.8 %copy-start.71 = (f32[128]{0:T(128)S(1)}, f32[128]{0:T(128)}, u32[]{:S(2)}) copy-start(f32[128]{0:T(128)} %copy-done.69) | copy-start | bytes 1540
  705.7 10.1 %all-to-all-start.23 = ((f32[8,1,1536]{2,1,0:T(1,128)}), f32[8,1,1536]{2,1,0:T(1,128)S(1)}, u32[]{:S(2)}, u32[]{:S(2)}) async-start(f32[8,1,1536]{2,1,0:T(1,128)} %broadcast_in_dim.211), calls=%async_computation.23 | async-start | bytes 98304 | tf_op jit(solution)/shard_map/all_to_all | solution.py:18
  711.2 22.2 %collective-permute-start = (f32[1,768,128]{2,1,0:T(8,128)}, f32[1,768,128]{2,1,0:T(8,128)}, u32[]{:S(2)}, u32[]{:S(2)}) collective-permute-start(f32[1,768,128]{2,1,0:T(8,128)} %fusion.90), channel_id=1, source_target_pairs={{0,64},{64,0},{1,65},{65,1},{2,66},{66,2},{3,67},{67,3},{4,68},{68... | collective-permute-start | bytes 1179656 | tf_op jit(solution)/shard_map/ppermute | solution.py:466
  721.6 26.2 %collective-permute-start.1 = (f32[1,768,128]{2,1,0:T(8,128)S(1)}, f32[1,768,128]{2,1,0:T(8,128)S(1)}, u32[]{:S(2)}, u32[]{:S(2)}) collective-permute-start(f32[1,768,128]{2,1,0:T(8,128)S(1)} %fusion.56), channel_id=1, source_target_pairs={{0,64},{64,0},{1,65},{65,1},{2,66},{66,2},{3,67},{67,3},{4,68},{68... | collective-permute-start | bytes 1179656 | tf_op jit(solution)/shard_map/ppermute | solution.py:469
  (64 other events, 138.9 us)
Sparse Core Ops, SparseCore 0:
  28.8 66.5 all-gather.2
  671.1 119.8 reduce-scatter.4

commit v4 on v3

--- a/solution.py
+++ b/solution.py
@@ -11,6 +11,7 @@
 epsilon = 1e-05
 gelu_coef = math.sqrt(2.0 / math.pi)
 masked_value = -1e30
+ROW_CHUNKS = 2
 
 
 def sent_to_all(array, axis):
@@ -219,6 +220,15 @@
         "nd,ncf->dcf", normed_one, packed_grad, preferred_element_type=jnp.float32
     )
     return (packed_grad, packed_weight_grad, bias_pair_grad, output_weight_grad)
+
+
+def split_rows(array, parts):
+    cut = array.shape[0] // parts
+    return [array[i * cut : (i + 1) * cut] for i in range(parts)]
+
+
+def joined(arrays):
+    return jnp.concatenate(arrays, axis=0)
 
 
 def layer_forward(stream, weights):
@@ -239,42 +249,53 @@
     seq_count, length, width_part = stream.shape
     rows_count = seq_count * length
     shape_heads = (seq_count, length, width_part // HEAD_DIM, HEAD_DIM)
-    stream_rows = stream.reshape(rows_count, width_part)
-    normed_one, normal_one, inv_one = norm_forward(stream_rows, gain_first, shift_first)
-    queries, keys_in, values_in, logsum, mixed_rows = attention_forward(
-        normed_one, packed_weight, bias_pair, shape_heads, rows_count, width_part
-    )
-    residual = (
-        stream_rows
-        + branch_sum(jnp.dot(mixed_rows, output_weight, preferred_element_type=jnp.float32))
-        + output_bias
-    )
-    normed_two, normal_two, inv_two = norm_forward(residual, gain_second, shift_second)
-    hidden_pre = (
-        jnp.dot(normed_two, expand_weight, preferred_element_type=jnp.float32) + expand_bias
-    )
-    hidden = gelu_tanh(hidden_pre).astype(jnp.bfloat16)
-    result = (
-        residual
-        + branch_sum(jnp.dot(hidden, contract_weight, preferred_element_type=jnp.float32))
-        + contract_bias
-    )
+    pieces = split_rows(stream.reshape(rows_count, width_part), ROW_CHUNKS)
+    firsts = [norm_forward(piece, gain_first, shift_first) for piece in pieces]
+    packs = [
+        jnp.einsum("nd,dcf->ncf", first[0], packed_weight, preferred_element_type=jnp.float32)
+        for first in firsts
+    ]
+    queries = joined([(pack[:, 0] + bias_pair[0]).astype(jnp.bfloat16) for pack in packs])
+    keys_in = joined([pack[:, 1].astype(jnp.bfloat16) for pack in packs])
+    values_in = joined([(pack[:, 2] + bias_pair[1]).astype(jnp.bfloat16) for pack in packs])
+    mixture, logsum = lax.map(
+        attend,
+        (
+            queries.reshape(shape_heads),
+            keys_in.reshape(shape_heads),
+            values_in.reshape(shape_heads),
+        ),
+    )
+    mixed_rows = mixture.reshape(rows_count, width_part)
+    results, seconds = ([], [])
+    for piece, mixed in zip(pieces, split_rows(mixed_rows, ROW_CHUNKS)):
+        residual = (
+            piece
+            + branch_sum(jnp.dot(mixed, output_weight, preferred_element_type=jnp.float32))
+            + output_bias
+        )
+        normed_two, normal_two, inv_two = norm_forward(residual, gain_second, shift_second)
+        hidden_pre = (
+            jnp.dot(normed_two, expand_weight, preferred_element_type=jnp.float32) + expand_bias
+        )
+        hidden = gelu_tanh(hidden_pre).astype(jnp.bfloat16)
+        results.append(
+            residual
+            + branch_sum(jnp.dot(hidden, contract_weight, preferred_element_type=jnp.float32))
+            + contract_bias
+        )
+        seconds.append((normed_two, normal_two, inv_two, hidden_pre, hidden))
     kept_values = (
-        normed_one,
-        normal_one,
-        inv_one,
+        joined([first[0] for first in firsts]),
+        joined([first[1] for first in firsts]),
+        joined([first[2] for first in firsts]),
         queries,
         keys_in,
         values_in,
         logsum,
         mixed_rows,
-        normed_two,
-        normal_two,
-        inv_two,
-        hidden_pre,
-        hidden,
-    )
-    return (result.reshape(stream.shape), kept_values)
+    ) + tuple(joined([second[i] for second in seconds]) for i in range(5))
+    return (joined(results).reshape(stream.shape), kept_values)
 
 
 def layer_backward(out_grad, kept_values, weights):
@@ -312,42 +333,90 @@
     shape_heads = (seq_count, length, width_part // HEAD_DIM, HEAD_DIM)
     grad_rows = out_grad.reshape(rows_count, width_part)
     contract_bias_grad = jnp.sum(grad_rows, axis=0)
-    branch_two = branch_grad(grad_rows)
+    parts = [split_rows(a, ROW_CHUNKS) for a in (grad_rows, hidden_pre, normal_two, inv_two)]
+    branch_twos, pre_grads, residual_grads, branch_ones, mixed_grads = ([], [], [], [], [])
+    gain_second_grad, shift_second_grad = (0.0, 0.0)
+    for grad_part, pre_part, normal_part, inv_part in zip(*parts):
+        branch_two = branch_grad(grad_part)
+        hidden_grad = jnp.einsum(
+            "nd,fd->nf", branch_two, contract_weight, preferred_element_type=jnp.float32
+        )
+        pre_grad = jax.vjp(gelu_tanh, pre_part)[1](hidden_grad)[0].astype(jnp.bfloat16)
+        second_grad, gain_part, shift_part = norm_backward(
+            jnp.einsum("nf,df->nd", pre_grad, expand_weight, preferred_element_type=jnp.float32),
+            normal_part,
+            inv_part,
+            gain_second,
+        )
+        residual_grad = grad_part + second_grad
+        branch_one = branch_grad(residual_grad)
+        mixed_grads.append(
+            jnp.einsum(
+                "nd,fd->nf", branch_one, output_weight, preferred_element_type=jnp.float32
+            ).astype(jnp.bfloat16)
+        )
+        branch_twos.append(branch_two)
+        pre_grads.append(pre_grad)
+        residual_grads.append(residual_grad)
+        branch_ones.append(branch_one)
+        gain_second_grad = gain_second_grad + gain_part
+        shift_second_grad = shift_second_grad + shift_part
     contract_weight_grad = jnp.einsum(
-        "nf,nd->fd", hidden, branch_two, preferred_element_type=jnp.float32
-    )
-    hidden_grad = jnp.einsum(
-        "nd,fd->nf", branch_two, contract_weight, preferred_element_type=jnp.float32
-    )
-    pre_grad = jax.vjp(gelu_tanh, hidden_pre)[1](hidden_grad)[0].astype(jnp.bfloat16)
+        "nf,nd->fd", hidden, joined(branch_twos), preferred_element_type=jnp.float32
+    )
+    pre_grad = joined(pre_grads)
     expand_bias_grad = jnp.sum(pre_grad.astype(jnp.float32), axis=0)
     expand_weight_grad = jnp.einsum(
         "nd,nf->df", normed_two, pre_grad, preferred_element_type=jnp.float32
     )
-    second_grad, gain_second_grad, shift_second_grad = norm_backward(
-        jnp.einsum("nf,df->nd", pre_grad, expand_weight, preferred_element_type=jnp.float32),
-        normal_two,
-        inv_two,
-        gain_second,
-    )
-    residual_grad = grad_rows + second_grad
-    output_bias_grad = jnp.sum(residual_grad, axis=0)
-    branch_one = branch_grad(residual_grad)
-    packed_grad, packed_weight_grad, bias_pair_grad, output_weight_grad = attention_backward(
-        branch_one,
-        (queries, keys_in, values_in, logsum, mixed_rows, normed_one),
-        output_weight,
-        shape_heads,
-        rows_count,
-        width_part,
-    )
-    first_grad, gain_first_grad, shift_first_grad = norm_backward(
-        jnp.einsum("ncf,dcf->nd", packed_grad, packed_weight, preferred_element_type=jnp.float32),
-        normal_one,
-        inv_one,
-        gain_first,
-    )
-    input_grad = (residual_grad + first_grad).reshape(out_grad.shape)
+    output_bias_grad = jnp.sum(joined(residual_grads), axis=0)
+    output_weight_grad = jnp.einsum(
+        "nf,nd->fd", mixed_rows, joined(branch_ones), preferred_element_type=jnp.float32
+    )
+    mixed_grad = joined(mixed_grads)
+    query_grad, key_grad, value_grad = lax.map(
+        attend_back,
+        (
+            queries.reshape(shape_heads),
+            keys_in.reshape(shape_heads),
+            values_in.reshape(shape_heads),
+            logsum,
+            mixed_grad.reshape(shape_heads),
+        ),
+    )
+    query_rows = query_grad.reshape(rows_count, width_part)
+    key_rows = key_grad.reshape(rows_count, width_part)
+    value_rows = value_grad.reshape(rows_count, width_part)
+    packed_grad = jnp.stack([query_rows, key_rows, value_rows], axis=1)
+    bias_pair_grad = jnp.stack(
+        [
+            jnp.sum(query_rows.astype(jnp.float32), axis=0),
+            jnp.sum(value_rows.astype(jnp.float32), axis=0),
+        ]
+    )
+    packed_weight_grad = jnp.einsum(
+        "nd,ncf->dcf", normed_one, packed_grad, preferred_element_type=jnp.float32
+    )
+    input_grads = []
+    gain_first_grad, shift_first_grad = (0.0, 0.0)
+    for packed_part, normal_part, inv_part, residual_grad in zip(
+        split_rows(packed_grad, ROW_CHUNKS),
+        split_rows(normal_one, ROW_CHUNKS),
+        split_rows(inv_one, ROW_CHUNKS),
+        residual_grads,
+    ):
+        first_grad, gain_part, shift_part = norm_backward(
+            jnp.einsum(
+                "ncf,dcf->nd", packed_part, packed_weight, preferred_element_type=jnp.float32
+            ),
+            normal_part,
+            inv_part,
+            gain_first,
+        )
+        input_grads.append(residual_grad + first_grad)
+        gain_first_grad = gain_first_grad + gain_part
+        shift_first_grad = shift_first_grad + shift_part
+    input_grad = joined(input_grads).reshape(out_grad.shape)
     return (
         input_grad,
         (

time: 822 us -> 1010 us (1.23)
  starting transfers between devices: 89.5 us -> 208 us
  blocking collectives: 76.9 us -> 0 us
  local copies, waits for them, and re-layouts: 177 us -> 224 us
  waiting for transfers between devices: 322 us -> 367 us
  matrix products: 73.7 us -> 99.6 us
  other arithmetic: 52.9 us -> 77.5 us
    all_to_all x4 -> x0, blocking collectives: 76.9 us -> none  [the longest x2 46.4 us: summed_on_arrival(): lax.all_to_all(parts, axis, split_axis=0, concat_axis=0, tiled=True)]
    all_to_all x14 -> x32, starting transfers between devices: 59.1 us -> 134 us  [sent_to_all(): return lax.all_to_all(copies, axis, split_axis=0, concat_axis=0, tiled=True)]
    all_to_all x14 -> x32, waiting for transfers between devices: 115 us -> 167 us  [sent_to_all(): return lax.all_to_all(copies, axis, split_axis=0, concat_axis=0, tiled=True)]
    all_to_all x6 -> x16, starting transfers between devices: 25.9 us -> 68.9 us  [summed_on_arrival(): lax.all_to_all(parts, axis, split_axis=0, concat_axis=0, tiled=True)]
    unnamed x3, waiting for transfers between devices: 42.3 us -> 69.1 us
    broadcast_in_dim x16 -> x32, local copies, waits for them, and re-layouts: 14.3 us -> 28.5 us  [sent_to_all(): copies = jnp.broadcast_to(array, (lax.axis_size(axis), *array.shape))]
    all_gather x1, waiting for transfers between devices: 53 us -> 40.9 us  [gather_all(): every = lax.all_gather(flat[None], ('section', 'dp'), axis=0, tiled=True)]
    dot_general x12 -> x18, matrix products: 19.6 us -> 28.5 us  [the longest x4 6.63 us: layer_backward(): jnp.einsum('nd,fd->nf', branch_one, output_weight, preferred_element_type...]
  transfers between devices with their start and end apart: 24 -> 52, of which waited for: 22 -> 45; matrix products, arithmetic and copies ran while one was open for 17% -> 24% of each run, Pallas kernels for 0% -> 0%
where the time goes in v4:
time: 1010 us; the launch traced here: 993 us
  waiting for transfers between devices  367 us (36%)
  local copies, waits for them, and re-layouts  224 us (22%)
  starting transfers between devices  208 us (21%)
  matrix products  99.6 us (10%)
  other arithmetic  77.5 us (8%)
  between operations  16.6 us (2%)
    all_to_all x32, waiting for transfers between devices, sent_to_all(): return lax.all_to_all(copies, axis, split_axis=0, concat_axis=0, tiled=True)  167 us
    all_to_all x32, starting transfers between devices, sent_to_all(): return lax.all_to_all(copies, axis, split_axis=0, concat_axis=0, tiled=True)  134 us
    all_to_all x16, waiting for transfers between devices, summed_on_arrival(): lax.all_to_all(parts, axis, split_axis=0, concat_axis=0, tiled=True)  84.9 us
    unnamed x3, waiting for transfers between devices  69.1 us
    all_to_all x16, starting transfers between devices, summed_on_arrival(): lax.all_to_all(parts, axis, split_axis=0, concat_axis=0, tiled=True)  68.9 us
    unnamed x263, local copies, waits for them, and re-layouts  65.3 us
    all_gather x1, waiting for transfers between devices, gather_all(): every = lax.all_gather(flat[None], ('section', 'dp'), axis=0, tiled=True)  40.9 us
    broadcast_in_dim x32, local copies, waits for them, and re-layouts, sent_to_all(): copies = jnp.broadcast_to(array, (lax.axis_size(axis), *array.shape))  28.5 us
  transfers between devices with their start and end apart: 52, of which 45 were waited for; matrix products, arithmetic and copies ran while one was open for 24% of the time, Pallas kernels for 0%

profile of v4, /device:TPU:0, one launch (start us, length us, event | category | flops | bytes accessed | tf_op | source)
XLA Modules:
  0.0 992.6 jit_solution(14977038762248887819)
XLA Ops:
  10.0 18.6 %concatenate.263 = bf16[197632]{0:T(1024)(128)(2,1)} concatenate(bf16[49152]{0:T(1024)(128)(2,1)S(1)} %reshape_squeeze.15, bf16[32]{0:T(256)(128)(2,1)S(1)} %reshape_squeeze.16, bf16[16384]{0:T(1024)(128)(2,1)} %bitcast.671, bf16[16]{0:T(256)(128)(2,1)} %bitcast.674, bf16[65536]{0:T(1024)(128)(2,1)S(1)} %bitcast.638, bf16[64]{0:T(256)(128)(2,1)} %bitcast.675, ...), dimensions={0} | concatenate | bytes 790528 | tf_op jit(solution)/shard_map/concatenate | solution.py:478
  31.7 6.3 all-to-all-start.2
  38.0 6.2 all-to-all-done.2
  48.4 5.9 all-to-all-done
  54.5 40.9 %all-gather.3.cloned.1.call-done = bf16[3162112]{0:T(1024)(128)(2,1)} async-done(((bf16[197632]{0:T(1024)(128)(2,1)}), bf16[3162112]{0:T(1024)(128)(2,1)}) %all-gather.3.cloned.1.call-update) | async-done | bytes 6324240 | tf_op jit(solution)/shard_map/all_gather | solution.py:479
  95.3 6.3 reshape.3028
  107.2 4.4 all-to-all-start.3
  114.4 9.6 all-to-all-done.3
  125.1 4.2 all-to-all-start.1
  135.9 5.4 all-to-all-done.1
  153.6 10.7 %all-to-all-done.8 = bf16[8,384,128]{2,1,0:T(8,128)(2,1)S(1)} async-done(((bf16[8,384,128]{2,1,0:T(8,128)(2,1)}), bf16[8,384,128]{2,1,0:T(8,128)(2,1)S(1)}, u32[]{:S(2)}, u32[]{:S(2)}) %all-to-all-start.8) | async-done | bytes 786464 | tf_op jit(solution)/shard_map/all_to_all | solution.py:52
  169.5 11.1 %all-to-all-done.4 = bf16[8,384,128]{2,1,0:T(8,128)(2,1)S(1)} async-done(((bf16[8,384,128]{2,1,0:T(8,128)(2,1)}), bf16[8,384,128]{2,1,0:T(8,128)(2,1)S(1)}, u32[]{:S(2)}, u32[]{:S(2)}) %all-to-all-start.4) | async-done | bytes 786464 | tf_op jit(solution)/shard_map/all_to_all | solution.py:52
  186.2 6.2 all-to-all-done.9
  196.4 6.1 all-to-all-done.5
  203.9 4.2 all-to-all-start.6
  209.6 4.7 slice_bitcast_fusion
  242.6 6.6 all-to-all-done.7
  253.1 11.3 %all-to-all-done.11 = bf16[8,384,128]{2,1,0:T(8,128)(2,1)S(1)} async-done(((bf16[8,384,128]{2,1,0:T(8,128)(2,1)}), bf16[8,384,128]{2,1,0:T(8,128)(2,1)S(1)}, u32[]{:S(2)}, u32[]{:S(2)}) %all-to-all-start.11) | async-done | bytes 786464 | tf_op jit(solution)/shard_map/all_to_all | solution.py:52
  269.1 6.2 all-to-all-done.14
  279.3 6.1 all-to-all-done.12
  290.4 10.0 %all-to-all-done.13 = bf16[8,384,128]{2,1,0:T(8,128)(2,1)S(1)} async-done(((bf16[8,384,128]{2,1,0:T(8,128)(2,1)}), bf16[8,384,128]{2,1,0:T(8,128)(2,1)S(1)}, u32[]{:S(2)}, u32[]{:S(2)}) %all-to-all-start.13) | async-done | bytes 786464 | tf_op jit(solution)/shard_map/all_to_all | solution.py:19
  301.5 4.4 all-to-all-start.15
  312.0 4.6 all-to-all-done.15
  324.5 4.3 all-to-all-start.20
  330.3 9.4 all-to-all-done.20
  344.6 9.9 all-to-all-done.16
  359.5 6.2 all-to-all-done.21
  371.4 4.5 all-to-all-done.17
  376.9 4.2 all-to-all-start.24
  381.4 9.9 %all-to-all-done.24 = bf16[8,384,128]{2,1,0:T(8,128)(2,1)} async-done(((bf16[8,384,128]{2,1,0:T(8,128)(2,1)}), bf16[8,384,128]{2,1,0:T(8,128)(2,1)}, u32[]{:S(2)}, u32[]{:S(2)}) %all-to-all-start.24) | async-done | bytes 786464 | tf_op jit(solution)/shard_map/all_to_all | solution.py:19
  400.9 7.2 all-to-all-done.28
  410.0 4.2 all-to-all-start.18
  416.8 8.3 all-to-all-done.18
  426.0 4.6 all-to-all-start.22
  441.5 4.2 all-to-all-start.25
  450.1 6.7 all-to-all-done.25
  478.8 8.3 all-to-all-done.29
  495.9 7.0 all-to-all-done.23
  508.5 5.0 all-to-all-done.30
  517.4 6.1 all-to-all-done.26
  527.7 4.4 all-to-all-start.31
  543.2 5.0 all-to-all-start.27
  560.3 4.6 bitcast_reduce_fusion.2
  594.0 5.9 all-to-all-start.32
  612.8 5.7 all-to-all-start.39
  618.5 6.2 all-to-all-done.39
  628.8 6.1 all-to-all-done.33
  664.1 4.2 all-to-all-start.41
  678.6 5.7 all-to-all-start.35
  702.2 5.7 all-to-all-start.42
  707.9 6.2 all-to-all-done.42
  719.5 4.8 all-to-all-done.36
  728.9 4.2 all-to-all-start.43
  748.9 6.1 all-to-all-start.37
  767.8 5.2 bitcast_reduce_fusion
  810.3 5.6 all-to-all-start.44
  818.7 4.9 dynamic-update-slice.2
  825.1 12.4 %dynamic-update-slice.4 = bf16[16,197632]{1,0:T(8,128)(2,1)} dynamic-update-slice(bf16[16,197632]{1,0:T(8,128)(2,1)} %dynamic-update-slice.3, bf16[16,65536]{1,0:T(8,128)(2,1)S(1)} %pad_maximum_fusion.1, s32[]{} %constant.177, s32[]{} %constant.185) | dynamic-update-slice | bytes 4194308
  839.0 12.8 %dynamic-update-slice.6 = bf16[16,197632]{1,0:T(8,128)(2,1)} dynamic-update-slice(bf16[16,197632]{1,0:T(8,128)(2,1)} %dynamic-update-slice.5, bf16[16,65536]{1,0:T(8,128)(2,1)} %pad_maximum_fusion, s32[]{} %constant.177, s32[]{} %constant.189) | dynamic-update-slice | bytes 4194308
  864.5 6.4 reshape.3003
  872.3 5.7 all-to-all-start.47
  878.0 6.4 all-to-all-done.47
  905.4 69.1 %reduce-scatter.5.cloned.1.call-done = bf16[1,1544,128]{2,1,0:T(8,128)(2,1)} async-done(((bf16[1,24704,128]{2,1,0:T(8,128)(2,1)}), bf16[1,1544,128]{2,1,0:T(8,128)(2,1)}) %reduce-scatter.5.cloned.1.call-update) | async-done | bytes 395280
  974.6 4.2 copy.469
  (666 shorter events, 458.3 us)
Async XLA Ops:
  7.2 88.2 %all-gather.3.cloned.1.call-start = ((), (), s32[]{:S(2)}) async-start(), calls=%async_computation.49 | async-start | bytes 6719488 | tf_op jit(solution)/shard_map/all_gather | solution.py:479
  31.7 12.6 %all-to-all-start.2 = ((f32[8,1,768]{2,1,0:T(1,128)}), f32[8,1,768]{2,1,0:T(1,128)S(1)}, u32[]{:S(2)}, u32[]{:S(2)}) async-start(f32[8,1,768]{2,1,0:T(1,128)} %broadcast_in_dim.282), calls=%async_computation.2 | async-start | bytes 49152 | tf_op jit(solution)/shard_map/all_to_all | solution.py:19
  44.9 9.5 all-to-all-start
  54.5 51.4 %copy-start.83 = (f32[384]{0:T(512)}, f32[384]{0:T(512)S(1)}, u32[]{:S(2)}) copy-start(f32[384]{0:T(512)S(1)} %get-tuple-element.323) | copy-start | bytes 4612
  54.5 51.4 %copy-start.85 = (f32[384]{0:T(512)}, f32[384]{0:T(512)S(1)}, u32[]{:S(2)}) copy-start(f32[384]{0:T(512)S(1)} %get-tuple-element.324) | copy-start | bytes 4612
  107.2 16.8 %all-to-all-start.3 = ((bf16[8,384,128]{2,1,0:T(8,128)(2,1)}), bf16[8,384,128]{2,1,0:T(8,128)(2,1)S(1)}, u32[]{:S(2)}, u32[]{:S(2)}) async-start(bf16[8,384,128]{2,1,0:T(8,128)(2,1)} %broadcast_in_dim.283), calls=%async_computation.3 | async-start | bytes 1572864 | tf_op jit(solution)/shard_map/all_to_all | solution.py:19
  125.1 16.2 %all-to-all-start.1 = ((bf16[8,384,128]{2,1,0:T(8,128)(2,1)}), bf16[8,384,128]{2,1,0:T(8,128)(2,1)}, u32[]{:S(2)}, u32[]{:S(2)}) async-start(bf16[8,384,128]{2,1,0:T(8,128)(2,1)} %broadcast_in_dim.281), calls=%async_computation.1 | async-start | bytes 1572864 | tf_op jit(solution)/shard_map/all_to_all | solution.py:19
  148.5 15.8 %all-to-all-start.8 = ((bf16[8,384,128]{2,1,0:T(8,128)(2,1)}), bf16[8,384,128]{2,1,0:T(8,128)(2,1)S(1)}, u32[]{:S(2)}, u32[]{:S(2)}) async-start(bf16[8,384,128]{2,1,0:T(8,128)(2,1)} %bitcast.563), calls=%async_computation.8 | async-start | bytes 1572864 | tf_op jit(solution)/shard_map/all_to_all | solution.py:52
  164.3 16.3 %all-to-all-start.4 = ((bf16[8,384,128]{2,1,0:T(8,128)(2,1)}), bf16[8,384,128]{2,1,0:T(8,128)(2,1)S(1)}, u32[]{:S(2)}, u32[]{:S(2)}) async-start(bf16[8,384,128]{2,1,0:T(8,128)(2,1)} %bitcast.567), calls=%async_computation.4 | async-start | bytes 1572864 | tf_op jit(solution)/shard_map/all_to_all | solution.py:52
  168.5 35.4 %copy-start.97 = (f32[128]{0:T(128)}, f32[128]{0:T(128)S(1)}, u32[]{:S(2)}) copy-start(f32[128]{0:T(128)S(1)} %reshape.3010) | copy-start | bytes 1540
  182.6 9.8 all-to-all-start.9
  193.0 9.5 all-to-all-start.5
  203.9 14.4 %all-to-all-start.6 = ((bf16[8,384,128]{1,2,0:T(8,128)(2,1)}), bf16[8,384,128]{1,2,0:T(8,128)(2,1)}, u32[]{:S(2)}, u32[]{:S(2)}) async-start(bf16[8,384,128]{1,2,0:T(8,128)(2,1)} %broadcast_in_dim.287), calls=%async_computation.6 | async-start | bytes 1572864 | tf_op jit(solution)/shard_map/all_to_all | solution.py:19
  219.3 15.0 %all-to-all-start.10 = ((bf16[8,384,128]{1,2,0:T(8,128)(2,1)}), bf16[8,384,128]{1,2,0:T(8,128)(2,1)}, u32[]{:S(2)}, u32[]{:S(2)}) async-start(bf16[8,384,128]{1,2,0:T(8,128)(2,1)} %broadcast_in_dim.289), calls=%async_computation.10 | async-start | bytes 1572864 | tf_op jit(solution)/shard_map/all_to_all | solution.py:19
  234.3 14.9 %all-to-all-start.7 = ((bf16[8,384,128]{2,1,0:T(8,128)(2,1)}), bf16[8,384,128]{2,1,0:T(8,128)(2,1)S(1)}, u32[]{:S(2)}, u32[]{:S(2)}) async-start(bf16[8,384,128]{2,1,0:T(8,128)(2,1)} %bitcast.565), calls=%async_computation.7 | async-start | bytes 1572864 | tf_op jit(solution)/shard_map/all_to_all | solution.py:52
  249.2 15.2 %all-to-all-start.11 = ((bf16[8,384,128]{2,1,0:T(8,128)(2,1)}), bf16[8,384,128]{2,1,0:T(8,128)(2,1)S(1)}, u32[]{:S(2)}, u32[]{:S(2)}) async-start(bf16[8,384,128]{2,1,0:T(8,128)(2,1)} %bitcast.561), calls=%async_computation.11 | async-start | bytes 1572864 | tf_op jit(solution)/shard_map/all_to_all | solution.py:52
  252.8 33.9 %copy-start.99 = (f32[128]{0:T(128)}, f32[128]{0:T(128)S(1)}, u32[]{:S(2)}) copy-start(f32[128]{0:T(128)S(1)} %reshape.3014) | copy-start | bytes 1540
  253.0 37.3 %copy-start.104 = (bf16[8,32]{1,0:T(8,128)(2,1)S(1)}, bf16[8,32]{1,0:T(8,128)(2,1)}, u32[]{:S(2)}) copy-start(bf16[8,32]{1,0:T(8,128)(2,1)} %get-tuple-element.256) | copy-start | bytes 1540
  264.8 41.8 %copy-start.42 = (bf16[128,8,128]{2,0,1:T(8,128)(2,1)S(1)}, bf16[128,8,128]{2,0,1:T(8,128)(2,1)}, u32[]{:S(2)}) copy-start(bf16[128,8,128]{2,0,1:T(8,128)(2,1)} %get-tuple-element.392) | copy-start | bytes 786436
  265.4 9.9 all-to-all-start.14
  275.9 9.5 all-to-all-start.12
  286.7 13.7 %all-to-all-start.13 = ((bf16[8,384,128]{2,1,0:T(8,128)(2,1)}), bf16[8,384,128]{2,1,0:T(8,128)(2,1)S(1)}, u32[]{:S(2)}, u32[]{:S(2)}) async-start(bf16[8,384,128]{2,1,0:T(8,128)(2,1)} %broadcast_in_dim.291), calls=%async_computation.13 | async-start | bytes 1572864 | tf_op jit(solution)/shard_map/all_to_all | solution.py:19
  301.5 15.1 %all-to-all-start.15 = ((bf16[8,384,128]{2,1,0:T(8,128)(2,1)}), bf16[8,384,128]{2,1,0:T(8,128)(2,1)}, u32[]{:S(2)}, u32[]{:S(2)}) async-start(bf16[8,384,128]{2,1,0:T(8,128)(2,1)} %broadcast_in_dim.293), calls=%async_computation.15 | async-start | bytes 1572864 | tf_op jit(solution)/shard_map/all_to_all | solution.py:19
  324.5 15.2 %all-to-all-start.20 = ((bf16[8,384,128]{2,1,0:T(8,128)(2,1)}), bf16[8,384,128]{2,1,0:T(8,128)(2,1)}, u32[]{:S(2)}, u32[]{:S(2)}) async-start(bf16[8,384,128]{2,1,0:T(8,128)(2,1)} %bitcast.555), calls=%async_computation.20 | async-start | bytes 1572864 | tf_op jit(solution)/shard_map/all_to_all | solution.py:52
  339.7 14.8 %all-to-all-start.16 = ((bf16[8,384,128]{2,1,0:T(8,128)(2,1)}), bf16[8,384,128]{2,1,0:T(8,128)(2,1)S(1)}, u32[]{:S(2)}, u32[]{:S(2)}) async-start(bf16[8,384,128]{2,1,0:T(8,128)(2,1)} %bitcast.559), calls=%async_computation.16 | async-start | bytes 1572864 | tf_op jit(solution)/shard_map/all_to_all | solution.py:52
  343.2 37.9 %copy-start.87 = (f32[8,16]{1,0:T(8,128)S(1)}, f32[8,16]{1,0:T(8,128)}, u32[]{:S(2)}) copy-start(f32[8,16]{1,0:T(8,128)} %get-tuple-element.238) | copy-start | bytes 1540
  356.0 9.8 all-to-all-start.21
  366.4 9.5 all-to-all-start.17
  376.9 14.4 %all-to-all-start.24 = ((bf16[8,384,128]{2,1,0:T(8,128)(2,1)}), bf16[8,384,128]{2,1,0:T(8,128)(2,1)}, u32[]{:S(2)}, u32[]{:S(2)}) async-start(bf16[8,384,128]{2,1,0:T(8,128)(2,1)} %broadcast_in_dim.298), calls=%async_computation.24 | async-start | bytes 1572864 | tf_op jit(solution)/shard_map/all_to_all | solution.py:19
  381.1 33.1 %copy-start.89 = (f32[8,64]{1,0:T(8,128)S(1)}, f32[8,64]{1,0:T(8,128)}, u32[]{:S(2)}) copy-start(f32[8,64]{1,0:T(8,128)} %get-tuple-element.252) | copy-start | bytes 6148
  381.1 33.2 %copy-start.10 = (bf16[8,65536]{1,0:T(8,128)(2,1)S(1)}, bf16[8,65536]{1,0:T(8,128)(2,1)}, u32[]{:S(2)}) copy-start(bf16[8,65536]{1,0:T(8,128)(2,1)} %get-tuple-element.249) | copy-start | bytes 3145732
  393.2 15.0 %all-to-all-start.28 = ((bf16[8,384,128]{2,1,0:T(8,128)(2,1)}), bf16[8,384,128]{2,1,0:T(8,128)(2,1)}, u32[]{:S(2)}, u32[]{:S(2)}) async-start(bf16[8,384,128]{2,1,0:T(8,128)(2,1)} %broadcast_in_dim.301), calls=%async_computation.28 | async-start | bytes 1572864 | tf_op jit(solution)/shard_map/all_to_all | solution.py:19
  410.0 15.1 %all-to-all-start.18 = ((bf16[8,384,128]{1,2,0:T(8,128)(2,1)}), bf16[8,384,128]{1,2,0:T(8,128)(2,1)}, u32[]{:S(2)}, u32[]{:S(2)}) async-start(bf16[8,384,128]{1,2,0:T(8,128)(2,1)} %broadcast_in_dim.295), calls=%async_computation.18 | async-start | bytes 1572864 | tf_op jit(solution)/shard_map/all_to_all | solution.py:19
  426.0 15.5 %all-to-all-start.22 = ((bf16[8,384,128]{1,2,0:T(8,128)(2,1)}), bf16[8,384,128]{1,2,0:T(8,128)(2,1)}, u32[]{:S(2)}, u32[]{:S(2)}) async-start(bf16[8,384,128]{1,2,0:T(8,128)(2,1)} %broadcast_in_dim.297), calls=%async_computation.22 | async-start | bytes 1572864 | tf_op jit(solution)/shard_map/all_to_all | solution.py:19
  441.5 15.2 %all-to-all-start.25 = ((bf16[8,384,128]{2,1,0:T(8,128)(2,1)}), bf16[8,384,128]{2,1,0:T(8,128)(2,1)}, u32[]{:S(2)}, u32[]{:S(2)}) async-start(bf16[8,384,128]{2,1,0:T(8,128)(2,1)} %bitcast.599), calls=%async_computation.25 | async-start | bytes 1572864 | tf_op jit(solution)/shard_map/all_to_all | solution.py:52
  456.8 15.3 %all-to-all-start.19 = ((bf16[8,384,128]{2,1,0:T(8,128)(2,1)}), bf16[8,384,128]{2,1,0:T(8,128)(2,1)}, u32[]{:S(2)}, u32[]{:S(2)}) async-start(bf16[8,384,128]{2,1,0:T(8,128)(2,1)} %bitcast.596), calls=%async_computation.19 | async-start | bytes 1572864 | tf_op jit(solution)/shard_map/all_to_all | solution.py:52
  472.1 15.0 %all-to-all-start.29 = ((bf16[8,384,128]{2,1,0:T(8,128)(2,1)}), bf16[8,384,128]{2,1,0:T(8,128)(2,1)S(1)}, u32[]{:S(2)}, u32[]{:S(2)}) async-start(bf16[8,384,128]{2,1,0:T(8,128)(2,1)} %bitcast.598), calls=%async_computation.29 | async-start | bytes 1572864 | tf_op jit(solution)/shard_map/all_to_all | solution.py:52
  487.0 15.9 %all-to-all-start.23 = ((bf16[8,384,128]{2,1,0:T(8,128)(2,1)}), bf16[8,384,128]{2,1,0:T(8,128)(2,1)}, u32[]{:S(2)}, u32[]{:S(2)}) async-start(bf16[8,384,128]{2,1,0:T(8,128)(2,1)} %bitcast.553), calls=%async_computation.23 | async-start | bytes 1572864 | tf_op jit(solution)/shard_map/all_to_all | solution.py:52
  503.6 9.9 all-to-all-start.30
  514.1 9.5 all-to-all-start.26
  527.7 14.6 %all-to-all-start.31 = ((bf16[8,384,128]{2,1,0:T(8,128)(2,1)}), bf16[8,384,128]{2,1,0:T(8,128)(2,1)}, u32[]{:S(2)}, u32[]{:S(2)}) async-start(bf16[8,384,128]{2,1,0:T(8,128)(2,1)} %broadcast_in_dim.303), calls=%async_computation.31 | async-start | bytes 1572864 | tf_op jit(solution)/shard_map/all_to_all | solution.py:19
  543.2 15.4 %all-to-all-start.27 = ((bf16[8,384,128]{2,1,0:T(8,128)(2,1)}), bf16[8,384,128]{2,1,0:T(8,128)(2,1)}, u32[]{:S(2)}, u32[]{:S(2)}) async-start(bf16[8,384,128]{2,1,0:T(8,128)(2,1)} %broadcast_in_dim.300), calls=%async_computation.27 | async-start | bytes 1572864 | tf_op jit(solution)/shard_map/all_to_all | solution.py:19
  576.4 17.6 %all-to-all-start.38 = ((bf16[8,384,128]{2,1,0:T(8,128)(2,1)}), bf16[8,384,128]{2,1,0:T(8,128)(2,1)}, u32[]{:S(2)}, u32[]{:S(2)}) async-start(bf16[8,384,128]{2,1,0:T(8,128)(2,1)} %bitcast.594), calls=%async_computation.38 | async-start | bytes 1572864 | tf_op jit(solution)/shard_map/all_to_all | solution.py:52
  594.0 17.2 %all-to-all-start.32 = ((bf16[8,384,128]{2,1,0:T(8,128)(2,1)}), bf16[8,384,128]{2,1,0:T(8,128)(2,1)S(1)}, u32[]{:S(2)}, u32[]{:S(2)}) async-start(bf16[8,384,128]{2,1,0:T(8,128)(2,1)} %bitcast.593), calls=%async_computation.32 | async-start | bytes 1572864 | tf_op jit(solution)/shard_map/all_to_all | solution.py:52
  608.8 26.1 %copy-start.27 = (f32[384,128]{1,0:T(8,128)S(1)}, f32[384,128]{1,0:T(8,128)}, u32[]{:S(2)}) copy-start(f32[384,128]{1,0:T(8,128)} %copy-done.26) | copy-start | bytes 589828
  612.8 11.9 %all-to-all-start.39 = ((f32[8,1,768]{2,1,0:T(1,128)}), f32[8,1,768]{2,1,0:T(1,128)S(1)}, u32[]{:S(2)}, u32[]{:S(2)}) async-start(f32[8,1,768]{2,1,0:T(1,128)} %broadcast_in_dim.308), calls=%async_computation.39 | async-start | bytes 49152 | tf_op jit(solution)/shard_map/all_to_all | solution.py:19
  625.4 9.5 all-to-all-start.33
  636.5 13.7 %all-to-all-start.40 = ((bf16[8,384,128]{2,1,0:T(8,128)(2,1)}), bf16[8,384,128]{2,1,0:T(8,128)(2,1)}, u32[]{:S(2)}, u32[]{:S(2)}) async-start(bf16[8,384,128]{2,1,0:T(8,128)(2,1)} %broadcast_in_dim.309), calls=%async_computation.40 | async-start | bytes 1572864 | tf_op jit(solution)/shard_map/all_to_all | solution.py:19
  651.2 13.0 %all-to-all-start.34 = ((bf16[8,384,128]{2,1,0:T(8,128)(2,1)}), bf16[8,384,128]{2,1,0:T(8,128)(2,1)S(1)}, u32[]{:S(2)}, u32[]{:S(2)}) async-start(bf16[8,384,128]{2,1,0:T(8,128)(2,1)} %broadcast_in_dim.305), calls=%async_computation.34 | async-start | bytes 1572864 | tf_op jit(solution)/shard_map/all_to_all | solution.py:19
  664.1 14.4 %all-to-all-start.41 = ((bf16[8,384,128]{2,1,0:T(8,128)(2,1)}), bf16[8,384,128]{2,1,0:T(8,128)(2,1)}, u32[]{:S(2)}, u32[]{:S(2)}) async-start(bf16[8,384,128]{2,1,0:T(8,128)(2,1)} %bitcast.595), calls=%async_computation.41 | async-start | bytes 1572864 | tf_op jit(solution)/shard_map/all_to_all | solution.py:52
  678.6 18.3 %all-to-all-start.35 = ((bf16[8,384,128]{2,1,0:T(8,128)(2,1)}), bf16[8,384,128]{2,1,0:T(8,128)(2,1)}, u32[]{:S(2)}, u32[]{:S(2)}) async-start(bf16[8,384,128]{2,1,0:T(8,128)(2,1)} %bitcast.545), calls=%async_computation.35 | async-start | bytes 1572864 | tf_op jit(solution)/shard_map/all_to_all | solution.py:52
  702.2 11.9 %all-to-all-start.42 = ((f32[8,1,768]{2,1,0:T(1,128)}), f32[8,1,768]{2,1,0:T(1,128)S(1)}, u32[]{:S(2)}, u32[]{:S(2)}) async-start(f32[8,1,768]{2,1,0:T(1,128)} %broadcast_in_dim.310), calls=%async_computation.42 | async-start | bytes 49152 | tf_op jit(solution)/shard_map/all_to_all | solution.py:19
  714.8 9.5 all-to-all-start.36
  728.9 18.1 %all-to-all-start.43 = ((bf16[8,384,128]{2,1,0:T(8,128)(2,1)}), bf16[8,384,128]{2,1,0:T(8,128)(2,1)}, u32[]{:S(2)}, u32[]{:S(2)}) async-start(bf16[8,384,128]{2,1,0:T(8,128)(2,1)} %broadcast_in_dim.311), calls=%async_computation.43 | async-start | bytes 1572864 | tf_op jit(solution)/shard_map/all_to_all | solution.py:19
  733.2 26.9 %copy-start.44 = (bf16[1,8,128,128]{3,1,2,0:T(8,128)(2,1)S(1)}, bf16[1,8,128,128]{3,1,2,0:T(8,128)(2,1)}, u32[]{:S(2)}) copy-start(bf16[1,8,128,128]{3,1,2,0:T(8,128)(2,1)} %copy-done.43) | copy-start | bytes 786436
  748.9 15.6 %all-to-all-start.37 = ((bf16[8,384,128]{2,1,0:T(8,128)(2,1)}), bf16[8,384,128]{2,1,0:T(8,128)(2,1)}, u32[]{:S(2)}, u32[]{:S(2)}) async-start(bf16[8,384,128]{2,1,0:T(8,128)(2,1)} %broadcast_in_dim.307), calls=%async_computation.37 | async-start | bytes 1572864 | tf_op jit(solution)/shard_map/all_to_all | solution.py:19
  793.2 17.1 %all-to-all-start.46 = ((bf16[8,384,128]{2,1,0:T(8,128)(2,1)}), bf16[8,384,128]{2,1,0:T(8,128)(2,1)}, u32[]{:S(2)}, u32[]{:S(2)}) async-start(bf16[8,384,128]{2,1,0:T(8,128)(2,1)} %bitcast.597), calls=%async_computation.46 | async-start | bytes 1572864 | tf_op jit(solution)/shard_map/all_to_all | solution.py:52
  810.3 44.6 %all-to-all-start.44 = ((bf16[8,384,128]{2,1,0:T(8,128)(2,1)}), bf16[8,384,128]{2,1,0:T(8,128)(2,1)}, u32[]{:S(2)}, u32[]{:S(2)}) async-start(bf16[8,384,128]{2,1,0:T(8,128)(2,1)} %bitcast.591), calls=%async_computation.44 | async-start | bytes 1572864 | tf_op jit(solution)/shard_map/all_to_all | solution.py:52
  815.9 158.7 %reduce-scatter.5.cloned.1.call-start = ((), (), s32[]{:S(2)}) async-start(), calls=%async_computation.50 | async-start | bytes 6719488
  870.9 24.2 %copy-start.6 = (f32[384,128]{1,0:T(8,128)S(1)}, f32[384,128]{1,0:T(8,128)}, u32[]{:S(2)}) copy-start(f32[384,128]{1,0:T(8,128)} %copy-done.5) | copy-start | bytes 589828
  872.3 12.0 %all-to-all-start.47 = ((f32[8,1,768]{2,1,0:T(1,128)}), f32[8,1,768]{2,1,0:T(1,128)S(1)}, u32[]{:S(2)}, u32[]{:S(2)}) async-start(f32[8,1,768]{2,1,0:T(1,128)} %broadcast_in_dim.313), calls=%async_computation.47 | async-start | bytes 49152 | tf_op jit(solution)/shard_map/all_to_all | solution.py:19
  885.0 9.5 all-to-all-start.45
  889.2 9.6 collective-permute-start
  895.1 9.4 collective-permute-start.1
  (109 other events, 788.7 us)
Sparse Core Ops, SparseCore 0:
  28.8 66.5 all-gather.2
  871.0 103.4 reduce-scatter.4

commit v5 on v3

--- a/solution.py
+++ b/solution.py
@@ -82,15 +82,14 @@
     )
 
 
-def norm_forward(stream, gain, offset):
-    width_all = stream.shape[1] * lax.axis_size("tensor")
-    totals, squares = in_one((jnp.sum(stream, axis=1), jnp.sum(stream * stream, axis=1)), "tensor")
-    mean_row = (totals / width_all)[:, None]
-    var_row = (squares / width_all)[:, None] - mean_row * mean_row
+def norm_forward(stream, gain_full, offset_full):
+    full = collect(stream, "tensor", 1)
+    mean_row = jnp.mean(full, axis=1, keepdims=True)
+    var_row = jnp.mean(full * full, axis=1, keepdims=True) - mean_row * mean_row
     inv_scale = lax.rsqrt(var_row + epsilon)
+    normed = ((full - mean_row) * inv_scale * gain_full + offset_full).astype(jnp.bfloat16)
     normal_part = (stream - mean_row) * inv_scale
-    normed = (normal_part * gain + offset).astype(jnp.bfloat16)
-    return (collect(normed, "tensor", 1), normal_part, inv_scale)
+    return (normed, normal_part, inv_scale)
 
 
 def norm_backward(partial_term, normal_part, inv_scale, gain):
@@ -221,7 +220,7 @@
     return (packed_grad, packed_weight_grad, bias_pair_grad, output_weight_grad)
 
 
-def layer_forward(stream, weights):
+def layer_forward(stream, weights, full_norms):
     (
         packed_weight,
         bias_pair,
@@ -240,7 +239,7 @@
     rows_count = seq_count * length
     shape_heads = (seq_count, length, width_part // HEAD_DIM, HEAD_DIM)
     stream_rows = stream.reshape(rows_count, width_part)
-    normed_one, normal_one, inv_one = norm_forward(stream_rows, gain_first, shift_first)
+    normed_one, normal_one, inv_one = norm_forward(stream_rows, full_norms[0], full_norms[1])
     queries, keys_in, values_in, logsum, mixed_rows = attention_forward(
         normed_one, packed_weight, bias_pair, shape_heads, rows_count, width_part
     )
@@ -249,7 +248,7 @@
         + branch_sum(jnp.dot(mixed_rows, output_weight, preferred_element_type=jnp.float32))
         + output_bias
     )
-    normed_two, normal_two, inv_two = norm_forward(residual, gain_second, shift_second)
+    normed_two, normal_two, inv_two = norm_forward(residual, full_norms[2], full_norms[3])
     hidden_pre = (
         jnp.dot(normed_two, expand_weight, preferred_element_type=jnp.float32) + expand_bias
     )
@@ -456,12 +455,14 @@
         ),
         dims,
     )
+    norm_params = jnp.stack([w[i] for w in (weights_zero, weights_last) for i in (8, 9, 10, 11)])
+    full_norms = collect(norm_params, "tensor", 1)
     section_index = lax.axis_index("section")
     is_first = section_index == 0
     stream = lax.dynamic_index_in_dim(inputs, section_index, axis=0, keepdims=False)
     out_grad = lax.dynamic_index_in_dim(cotangent, section_index, axis=0, keepdims=False)
-    middle, kept_zero = layer_forward(stream, weights_zero)
-    final, kept_last = layer_forward(middle, weights_last)
+    middle, kept_zero = layer_forward(stream, weights_zero, full_norms[:4])
+    final, kept_last = layer_forward(middle, weights_last, full_norms[4:])
     swap = [(0, 1), (1, 0)]
     other_out = lax.ppermute(jnp.where(is_first, final, middle), "section", swap)
     middle_grad, grads_last = layer_backward(out_grad, kept_last, weights_last)

time: 822 us -> 911 us (1.11)
  other arithmetic: 52.9 us -> 109 us
  blocking collectives: 76.9 us -> 32.9 us
  local copies, waits for them, and re-layouts: 177 us -> 218 us
  waiting for transfers between devices: 322 us -> 352 us
    all_to_all x2 -> x0, blocking collectives: 46.4 us -> none  [summed_on_arrival(): lax.all_to_all(parts, axis, split_axis=0, concat_axis=0, tiled=True)]
    all_to_all x14 -> x11, waiting for transfers between devices: 115 us -> 160 us  [sent_to_all(): return lax.all_to_all(copies, axis, split_axis=0, concat_axis=0, tiled=True)]
    all_gather x1, waiting for transfers between devices: 53 us -> 20.3 us  [gather_all(): every = lax.all_gather(flat[None], ('section', 'dp'), axis=0, tiled=True)]
    convert_element_type x5 -> x10, other arithmetic: 2.59 us -> 23.2 us  [the longest x8 21.1 us: norm_forward(): ((full - mean_row) * inv_scale * gain_full + offset_full).astype(jnp.bflo...]
    all_to_all x6 -> x8, waiting for transfers between devices: 90.3 us -> 110 us  [summed_on_arrival(): lax.all_to_all(parts, axis, split_axis=0, concat_axis=0, tiled=True)]
    reduce_sum x5 -> x8, other arithmetic: 1.2 us -> 15.2 us  [the longest x4 7.81 us: norm_forward(): mean_row = jnp.mean(full, axis=1, keepdims=True)]
    all_to_all x6 -> x8, starting transfers between devices: 25.9 us -> 38.7 us  [summed_on_arrival(): lax.all_to_all(parts, axis, split_axis=0, concat_axis=0, tiled=True)]
    all_to_all x14 -> x11, starting transfers between devices: 59.1 us -> 51.8 us  [sent_to_all(): return lax.all_to_all(copies, axis, split_axis=0, concat_axis=0, tiled=True)]
  transfers between devices with their start and end apart: 24 -> 23, of which waited for: 22 -> 19; matrix products, arithmetic and copies ran while one was open for 17% -> 21% of each run, Pallas kernels for 0% -> 0%
where the time goes in v5:
time: 911 us; the launch traced here: 897 us
  waiting for transfers between devices  352 us (39%)
  local copies, waits for them, and re-layouts  218 us (24%)
  other arithmetic  109 us (12%)
  starting transfers between devices  95.2 us (10%)
  matrix products  73.4 us (8%)
  blocking collectives  32.9 us (4%)
  between operations  16.6 us (2%)
    all_to_all x11, waiting for transfers between devices, sent_to_all(): return lax.all_to_all(copies, axis, split_axis=0, concat_axis=0, tiled=True)  160 us
    all_to_all x8, waiting for transfers between devices, summed_on_arrival(): lax.all_to_all(parts, axis, split_axis=0, concat_axis=0, tiled=True)  110 us
    unnamed x334, local copies, waits for them, and re-layouts  63.8 us
    all_to_all x11, starting transfers between devices, sent_to_all(): return lax.all_to_all(copies, axis, split_axis=0, concat_axis=0, tiled=True)  51.8 us
    unnamed x3, waiting for transfers between devices  42 us
    all_to_all x8, starting transfers between devices, summed_on_arrival(): lax.all_to_all(parts, axis, split_axis=0, concat_axis=0, tiled=True)  38.7 us
    all_to_all x2, blocking collectives, sent_to_all(): return lax.all_to_all(copies, axis, split_axis=0, concat_axis=0, tiled=True)  32.9 us
    convert_element_type x8, other arithmetic, norm_forward(): ((full - mean_row) * inv_scale * gain_full + offset_full).astype(jnp.bflo...  21.1 us
  transfers between devices with their start and end apart: 23, of which 19 were waited for; matrix products, arithmetic and copies ran while one was open for 21% of the time, Pallas kernels for 0%

profile of v5, /device:TPU:0, one launch (start us, length us, event | category | flops | bytes accessed | tf_op | source)
XLA Modules:
  0.0 897.0 jit_solution(4468710643210920202)
XLA Ops:
  10.1 18.6 %concatenate.94 = bf16[197632]{0:T(1024)(128)(2,1)} concatenate(bf16[49152]{0:T(1024)(128)(2,1)S(1)} %reshape_squeeze.15, bf16[32]{0:T(256)(128)(2,1)S(1)} %reshape_squeeze.16, bf16[16384]{0:T(1024)(128)(2,1)} %bitcast.721, bf16[16]{0:T(256)(128)(2,1)} %bitcast.724, bf16[65536]{0:T(1024)(128)(2,1)S(1)} %bitcast.691, bf16[64]{0:T(256)(128)(2,1)} %bitcast.725, ...), dimensions={0} | concatenate | bytes 790528 | tf_op jit(solution)/shard_map/concatenate | solution.py:408
  30.8 6.3 all-to-all-start
  38.2 47.0 %all-to-all-done = f32[8,768,128]{1,2,0:T(8,128)S(1)} async-done(((f32[8,768,128]{1,2,0:T(8,128)}), f32[8,768,128]{1,2,0:T(8,128)S(1)}, u32[]{:S(2)}, u32[]{:S(2)}) %all-to-all-start) | async-done | bytes 3145760 | tf_op jit(solution)/shard_map/all_to_all | solution.py:18
  85.7 20.3 %all-gather.3.cloned.1.call-done = bf16[3162112]{0:T(1024)(128)(2,1)} async-done(((bf16[197632]{0:T(1024)(128)(2,1)}), bf16[3162112]{0:T(1024)(128)(2,1)}) %all-gather.3.cloned.1.call-update) | async-done | bytes 6324240 | tf_op jit(solution)/shard_map/all_gather | solution.py:409
  106.0 6.3 reshape.2272
  121.1 4.9 all-to-all-start.1
  130.0 3.3 reshape_reshape.24
  145.2 6.2 all-to-all-start.2
  151.4 20.3 %all-to-all-done.2 = bf16[8,768,128]{2,1,0:T(8,128)(2,1)} async-done(((bf16[8,768,128]{2,1,0:T(8,128)(2,1)}), bf16[8,768,128]{2,1,0:T(8,128)(2,1)}, u32[]{:S(2)}, u32[]{:S(2)}) %all-to-all-start.2) | async-done | bytes 1572896 | tf_op jit(solution)/shard_map/all_to_all | solution.py:51
  175.2 2.9 broadcast_in_dim.189
  178.1 4.5 all-to-all-start.3
  182.6 5.3 fusion.157
  192.5 3.3 bitcast_bitcast_fusion.8
  198.1 21.9 %all-to-all-done.3 = f32[8,768,128]{1,2,0:T(8,128)} async-done(((f32[8,768,128]{1,2,0:T(8,128)}), f32[8,768,128]{1,2,0:T(8,128)}, u32[]{:S(2)}, u32[]{:S(2)}) %all-to-all-start.3) | async-done | bytes 3145760 | tf_op jit(solution)/shard_map/all_to_all | solution.py:18
  232.5 4.4 all-to-all-start.4
  237.0 20.4 %all-to-all-done.4 = bf16[8,768,128]{2,1,0:T(8,128)(2,1)} async-done(((bf16[8,768,128]{2,1,0:T(8,128)(2,1)}), bf16[8,768,128]{2,1,0:T(8,128)(2,1)}, u32[]{:S(2)}, u32[]{:S(2)}) %all-to-all-start.4) | async-done | bytes 1572896 | tf_op jit(solution)/shard_map/all_to_all | solution.py:51
  263.7 5.1 all-to-all-start.5
  271.2 3.3 reshape_reshape.26
  276.7 29.6 %all-to-all-done.5 = f32[8,768,128]{1,2,0:T(8,128)} async-done(((f32[8,768,128]{1,2,0:T(8,128)}), f32[8,768,128]{1,2,0:T(8,128)}, u32[]{:S(2)}, u32[]{:S(2)}) %all-to-all-start.5) | async-done | bytes 3145760 | tf_op jit(solution)/shard_map/all_to_all | solution.py:18
  321.0 4.4 all-to-all-start.6
  326.1 20.0 %all-to-all-done.6 = bf16[8,768,128]{2,1,0:T(8,128)(2,1)} async-done(((bf16[8,768,128]{2,1,0:T(8,128)(2,1)}), bf16[8,768,128]{2,1,0:T(8,128)(2,1)}, u32[]{:S(2)}, u32[]{:S(2)}) %all-to-all-start.6) | async-done | bytes 1572896 | tf_op jit(solution)/shard_map/all_to_all | solution.py:51
  354.3 4.4 all-to-all-start.7
  360.4 35.7 %all-to-all-done.7 = f32[8,768,128]{1,2,0:T(8,128)} async-done(((f32[8,768,128]{1,2,0:T(8,128)}), f32[8,768,128]{1,2,0:T(8,128)}, u32[]{:S(2)}, u32[]{:S(2)}) %all-to-all-start.7) | async-done | bytes 3145760 | tf_op jit(solution)/shard_map/all_to_all | solution.py:18
  398.5 4.5 all-to-all-start.9
  416.7 6.8 all-to-all-done.9
  423.5 5.0 fusion.162
  431.0 4.3 all-to-all-start.10
  436.6 19.3 %all-to-all-done.10 = bf16[8,768,128]{2,1,0:T(8,128)(2,1)} async-done(((bf16[8,768,128]{2,1,0:T(8,128)(2,1)}), bf16[8,768,128]{2,1,0:T(8,128)(2,1)}, u32[]{:S(2)}, u32[]{:S(2)}) %all-to-all-start.10) | async-done | bytes 1572896 | tf_op jit(solution)/shard_map/all_to_all | solution.py:51
  460.1 9.8 %all_to_all.109 = f32[8,1,1536]{2,1,0:T(1,128)} all-to-all(f32[8,1,1536]{2,1,0:T(1,128)S(1)} %broadcast_in_dim.193), channel_id=1, replica_groups=mesh['section'=2,'dp'=8,'tensor'=8] {'tensor'}, dimensions={0} | all-to-all | bytes 98304 | tf_op jit(solution)/shard_map/all_to_all | solution.py:18
  475.5 23.1 %all_to_all.110 = bf16[8,768,128]{2,1,0:T(8,128)(2,1)S(1)} all-to-all(bf16[8,768,128]{2,1,0:T(8,128)(2,1)S(1)} %broadcast_in_dim.194), channel_id=1, replica_groups=mesh['section'=2,'dp'=8,'tensor'=8] {'tensor'}, dimensions={0} | all-to-all | bytes 3145728 | tf_op jit(solution)/shard_map/all_to_all | solution.py:18
  499.8 5.0 bitcast_reduce_fusion.2
  520.5 4.3 all-to-all-start.13
  536.5 3.5 fusion.9
  540.1 3.6 fusion.13
  546.6 5.6 all-to-all-start.14
  552.3 3.6 fusion.5
  560.5 4.7 all-to-all-start.15
  565.3 3.4 convolution_convert_fusion.8
  593.4 4.1 fusion.163
  605.1 5.7 all-to-all-start.16
  610.7 3.0 pad_maximum_fusion.1
  616.4 9.8 %all-to-all-done.16 = bf16[8,768,128]{2,1,0:T(8,128)(2,1)S(1)} async-done(((bf16[8,768,128]{2,1,0:T(8,128)(2,1)}), bf16[8,768,128]{2,1,0:T(8,128)(2,1)S(1)}, u32[]{:S(2)}, u32[]{:S(2)}) %all-to-all-start.16) | async-done | bytes 1572896 | tf_op jit(solution)/shard_map/all_to_all | solution.py:51
  627.6 3.8 all-to-all-start.17
  631.4 3.1 fusion.76
  640.7 4.3 all-to-all-start.18
  645.1 3.0 pad_maximum_fusion
  651.7 12.2 %all-to-all-done.18 = bf16[8,768,128]{2,1,0:T(8,128)(2,1)} async-done(((bf16[8,768,128]{2,1,0:T(8,128)(2,1)}), bf16[8,768,128]{2,1,0:T(8,128)(2,1)}, u32[]{:S(2)}, u32[]{:S(2)}) %all-to-all-start.18) | async-done | bytes 1572896 | tf_op jit(solution)/shard_map/all_to_all | solution.py:18
  666.0 5.1 bitcast_reduce_fusion
  671.1 4.2 multiply_reduce_fusion
  687.9 3.3 fusion.70
  692.9 3.6 all-to-all-start.19
  707.4 4.9 dynamic-update-slice.2
  713.8 13.0 %dynamic-update-slice.4 = bf16[16,197632]{1,0:T(8,128)(2,1)} dynamic-update-slice(bf16[16,197632]{1,0:T(8,128)(2,1)} %dynamic-update-slice.3, bf16[16,65536]{1,0:T(8,128)(2,1)} %pad_maximum_fusion.1, s32[]{} %constant.164, s32[]{} %constant.172) | dynamic-update-slice | bytes 4194308
  728.3 12.8 %dynamic-update-slice.6 = bf16[16,197632]{1,0:T(8,128)(2,1)} dynamic-update-slice(bf16[16,197632]{1,0:T(8,128)(2,1)} %dynamic-update-slice.5, bf16[16,65536]{1,0:T(8,128)(2,1)} %pad_maximum_fusion, s32[]{} %constant.164, s32[]{} %constant.176) | dynamic-update-slice | bytes 4194308
  752.6 6.5 reshape.2235
  764.9 5.8 all-to-all-start.8
  770.9 20.0 %all-to-all-done.8 = bf16[8,768,128]{2,1,0:T(8,128)(2,1)} async-done(((bf16[8,768,128]{2,1,0:T(8,128)(2,1)}), bf16[8,768,128]{2,1,0:T(8,128)(2,1)}, u32[]{:S(2)}, u32[]{:S(2)}) %all-to-all-start.8) | async-done | bytes 1572896 | tf_op jit(solution)/shard_map/all_to_all | solution.py:51
  793.9 3.6 all-to-all-start.20
  804.0 3.5 fusion.90
  807.6 3.4 fusion.107
  813.5 8.2 collective-permute-done
  823.7 12.1 %collective-permute-done.1 = f32[1,768,128]{2,1,0:T(8,128)S(1)} collective-permute-done((f32[1,768,128]{2,1,0:T(8,128)S(1)}, f32[1,768,128]{2,1,0:T(8,128)S(1)}, u32[]{:S(2)}, u32[]{:S(2)}) %collective-permute-start.1) | collective-permute-done | bytes 393248 | tf_op jit(solution)/shard_map/ppermute | solution.py:470
  836.7 42.0 %reduce-scatter.5.cloned.1.call-done = bf16[1,1544,128]{2,1,0:T(8,128)(2,1)} async-done(((bf16[1,24704,128]{2,1,0:T(8,128)(2,1)}), bf16[1,1544,128]{2,1,0:T(8,128)(2,1)}) %reduce-scatter.5.cloned.1.call-update) | async-done | bytes 395280
  878.7 4.2 copy.311
  (576 shorter events, 270.4 us)
Async XLA Ops:
  7.2 21.5 %copy-start.15 = (f32[2,1,768,128]{3,2,1,0:T(8,128)S(1)}, f32[2,1,768,128]{3,2,1,0:T(8,128)}, u32[]{:S(2)}) copy-start(f32[2,1,768,128]{3,2,1,0:T(8,128)} %param.14) | copy-start | bytes 2359300
  7.2 98.8 %all-gather.3.cloned.1.call-start = ((), (), s32[]{:S(2)}) async-start(), calls=%async_computation.22 | async-start | bytes 6719488 | tf_op jit(solution)/shard_map/all_gather | solution.py:409
  30.8 54.3 %all-to-all-start = ((f32[8,768,128]{1,2,0:T(8,128)}), f32[8,768,128]{1,2,0:T(8,128)S(1)}, u32[]{:S(2)}, u32[]{:S(2)}) async-start(f32[8,768,128]{1,2,0:T(8,128)} %broadcast_in_dim.183), calls=%async_computation | async-start | bytes 6291456 | tf_op jit(solution)/shard_map/all_to_all | solution.py:18
  85.7 50.5 %copy-start.68 = (f32[768]{0:T(1024)}, f32[768]{0:T(1024)S(1)}, u32[]{:S(2)}) copy-start(f32[768]{0:T(1024)S(1)} %get-tuple-element.245) | copy-start | bytes 9220
  85.7 50.5 %copy-start.70 = (f32[768]{0:T(1024)}, f32[768]{0:T(1024)S(1)}, u32[]{:S(2)}) copy-start(f32[768]{0:T(1024)S(1)} %get-tuple-element.246) | copy-start | bytes 9220
  121.1 14.4 %all-to-all-start.1 = ((bf16[8,8,128]{2,1,0:T(8,128)(2,1)}), bf16[8,8,128]{2,1,0:T(8,128)(2,1)S(1)}, u32[]{:S(2)}, u32[]{:S(2)}) async-start(bf16[8,8,128]{2,1,0:T(8,128)(2,1)} %broadcast_in_dim.186), calls=%async_computation.1 | async-start | bytes 32768 | tf_op jit(solution)/shard_map/all_to_all | solution.py:18
  136.1 90.0 %copy-start.96 = (f32[1,8,128]{2,0,1:T(1,128)}, f32[1,8,128]{2,0,1:T(1,128)S(1)}, u32[]{:S(2)}) copy-start(f32[1,8,128]{2,0,1:T(1,128)S(1)} %get-tuple-element.223) | copy-start | bytes 12292
  136.1 90.0 %copy-start.98 = (f32[1,8,128]{2,0,1:T(1,128)}, f32[1,8,128]{2,0,1:T(1,128)S(1)}, u32[]{:S(2)}) copy-start(f32[1,8,128]{2,0,1:T(1,128)S(1)} %get-tuple-element.224) | copy-start | bytes 12292
  145.2 26.5 %all-to-all-start.2 = ((bf16[8,768,128]{2,1,0:T(8,128)(2,1)}), bf16[8,768,128]{2,1,0:T(8,128)(2,1)}, u32[]{:S(2)}, u32[]{:S(2)}) async-start(bf16[8,768,128]{2,1,0:T(8,128)(2,1)} %bitcast.636), calls=%async_computation.2 | async-start | bytes 3145728 | tf_op jit(solution)/shard_map/all_to_all | solution.py:51
  151.4 26.7 %copy-start.114 = (f32[128]{0:T(128)}, f32[128]{0:T(128)S(1)}, u32[]{:S(2)}) copy-start(f32[128]{0:T(128)S(1)} %reshape.2241) | copy-start | bytes 1540
  174.2 84.9 %copy-start.6 = (f32[768,128]{1,0:T(8,128)}, f32[768,128]{1,0:T(8,128)S(1)}, u32[]{:S(2)}) copy-start(f32[768,128]{1,0:T(8,128)S(1)} %add_add_fusion.2) | copy-start | bytes 1179652
  178.1 41.8 %all-to-all-start.3 = ((f32[8,768,128]{1,2,0:T(8,128)}), f32[8,768,128]{1,2,0:T(8,128)}, u32[]{:S(2)}, u32[]{:S(2)}) async-start(f32[8,768,128]{1,2,0:T(8,128)} %broadcast_in_dim.189), calls=%async_computation.3 | async-start | bytes 6291456 | tf_op jit(solution)/shard_map/all_to_all | solution.py:18
  232.5 25.0 %all-to-all-start.4 = ((bf16[8,768,128]{2,1,0:T(8,128)(2,1)}), bf16[8,768,128]{2,1,0:T(8,128)(2,1)}, u32[]{:S(2)}, u32[]{:S(2)}) async-start(bf16[8,768,128]{2,1,0:T(8,128)(2,1)} %bitcast.637), calls=%async_computation.4 | async-start | bytes 3145728 | tf_op jit(solution)/shard_map/all_to_all | solution.py:51
  237.0 26.7 %copy-start.116 = (f32[128]{0:T(128)}, f32[128]{0:T(128)S(1)}, u32[]{:S(2)}) copy-start(f32[128]{0:T(128)S(1)} %reshape.2245) | copy-start | bytes 1540
  263.7 42.5 %all-to-all-start.5 = ((f32[8,768,128]{1,2,0:T(8,128)}), f32[8,768,128]{1,2,0:T(8,128)}, u32[]{:S(2)}, u32[]{:S(2)}) async-start(f32[8,768,128]{1,2,0:T(8,128)} %broadcast_in_dim.190), calls=%async_computation.5 | async-start | bytes 6291456 | tf_op jit(solution)/shard_map/all_to_all | solution.py:18
  321.0 25.0 %all-to-all-start.6 = ((bf16[8,768,128]{2,1,0:T(8,128)(2,1)}), bf16[8,768,128]{2,1,0:T(8,128)(2,1)}, u32[]{:S(2)}, u32[]{:S(2)}) async-start(bf16[8,768,128]{2,1,0:T(8,128)(2,1)} %bitcast.638), calls=%async_computation.6 | async-start | bytes 3145728 | tf_op jit(solution)/shard_map/all_to_all | solution.py:51
  354.3 41.8 %all-to-all-start.7 = ((f32[8,768,128]{1,2,0:T(8,128)}), f32[8,768,128]{1,2,0:T(8,128)}, u32[]{:S(2)}, u32[]{:S(2)}) async-start(f32[8,768,128]{1,2,0:T(8,128)} %broadcast_in_dim.191), calls=%async_computation.7 | async-start | bytes 6291456 | tf_op jit(solution)/shard_map/all_to_all | solution.py:18
  398.5 25.0 %all-to-all-start.9 = ((bf16[8,768,128]{2,1,0:T(8,128)(2,1)}), bf16[8,768,128]{2,1,0:T(8,128)(2,1)}, u32[]{:S(2)}, u32[]{:S(2)}) async-start(bf16[8,768,128]{2,1,0:T(8,128)(2,1)} %broadcast_in_dim.192), calls=%async_computation.9 | async-start | bytes 3145728 | tf_op jit(solution)/shard_map/all_to_all | solution.py:18
  431.0 24.9 %all-to-all-start.10 = ((bf16[8,768,128]{2,1,0:T(8,128)(2,1)}), bf16[8,768,128]{2,1,0:T(8,128)(2,1)}, u32[]{:S(2)}, u32[]{:S(2)}) async-start(bf16[8,768,128]{2,1,0:T(8,128)(2,1)} %bitcast.639), calls=%async_computation.10 | async-start | bytes 3145728 | tf_op jit(solution)/shard_map/all_to_all | solution.py:51
  472.1 32.7 %slice-start.2 = ((s8[4718592]{0:T(1024)(128)(4,1)}), s8[4194304]{0:T(1024)(128)(4,1)S(1)}, s32[]{:S(2)}) async-start(s8[4718592]{0:T(1024)(128)(4,1)} %bitcast.629), calls=%async_computation.26 | async-start | bytes 8388608
  475.3 23.3 %copy-start.50 = (bf16[1,8,128,128]{3,1,2,0:T(8,128)(2,1)S(1)}, bf16[1,8,128,128]{3,1,2,0:T(8,128)(2,1)}, u32[]{:S(2)}) copy-start(bf16[1,8,128,128]{3,1,2,0:T(8,128)(2,1)} %get-tuple-element.203) | copy-start | bytes 786436
  475.5 24.3 %copy-start.4 = (pred[768,768]{0,1:T(8,128)(4,1)S(1)}, pred[768,768]{0,1:T(8,128)(4,1)}, u32[]{:S(2)}) copy-start(pred[768,768]{0,1:T(8,128)(4,1)} %iota_compare_fusion) | copy-start | bytes 1769476
  475.5 24.3 %copy-start.87 = (f32[2,768]{1,0:T(2,128)S(1)}, f32[2,768]{1,0:T(2,128)}, u32[]{:S(2)}) copy-start(f32[2,768]{1,0:T(2,128)} %copy-done.86) | copy-start | bytes 18436
  520.5 23.3 %all-to-all-start.13 = ((bf16[8,768,128]{2,1,0:T(8,128)(2,1)}), bf16[8,768,128]{2,1,0:T(8,128)(2,1)}, u32[]{:S(2)}, u32[]{:S(2)}) async-start(bf16[8,768,128]{2,1,0:T(8,128)(2,1)} %bitcast.633), calls=%async_computation.13 | async-start | bytes 3145728 | tf_op jit(solution)/shard_map/all_to_all | solution.py:51
  543.7 8.5 copy-start.62
  543.7 8.5 copy-start.89
  543.7 8.5 copy-start.91
  546.6 11.9 %all-to-all-start.14 = ((f32[8,1,1536]{2,1,0:T(1,128)}), f32[8,1,1536]{2,1,0:T(1,128)S(1)}, u32[]{:S(2)}, u32[]{:S(2)}) async-start(f32[8,1,1536]{2,1,0:T(1,128)} %broadcast_in_dim.195), calls=%async_computation.14 | async-start | bytes 98304 | tf_op jit(solution)/shard_map/all_to_all | solution.py:18
  560.5 32.8 %all-to-all-start.15 = ((bf16[8,768,128]{2,1,0:T(8,128)(2,1)}), bf16[8,768,128]{2,1,0:T(8,128)(2,1)}, u32[]{:S(2)}, u32[]{:S(2)}) async-start(bf16[8,768,128]{2,1,0:T(8,128)(2,1)} %broadcast_in_dim.196), calls=%async_computation.15 | async-start | bytes 3145728 | tf_op jit(solution)/shard_map/all_to_all | solution.py:18
  605.1 21.1 %all-to-all-start.16 = ((bf16[8,768,128]{2,1,0:T(8,128)(2,1)}), bf16[8,768,128]{2,1,0:T(8,128)(2,1)S(1)}, u32[]{:S(2)}, u32[]{:S(2)}) async-start(bf16[8,768,128]{2,1,0:T(8,128)(2,1)} %bitcast.635), calls=%async_computation.16 | async-start | bytes 3145728 | tf_op jit(solution)/shard_map/all_to_all | solution.py:51
  613.7 12.7 %copy-start.7 = (f32[768,128]{1,0:T(8,128)S(1)}, f32[768,128]{1,0:T(8,128)}, u32[]{:S(2)}) copy-start(f32[768,128]{1,0:T(8,128)} %copy-done.6) | copy-start | bytes 1179652
  613.7 12.7 %copy-start.118 = (f32[128]{0:T(128)S(1)}, f32[128]{0:T(128)}, u32[]{:S(2)}) copy-start(f32[128]{0:T(128)} %reshape.2257) | copy-start | bytes 1540
  627.6 10.1 %all-to-all-start.17 = ((f32[8,1,1536]{2,1,0:T(1,128)}), f32[8,1,1536]{2,1,0:T(1,128)S(1)}, u32[]{:S(2)}, u32[]{:S(2)}) async-start(f32[8,1,1536]{2,1,0:T(1,128)} %broadcast_in_dim.197), calls=%async_computation.17 | async-start | bytes 98304 | tf_op jit(solution)/shard_map/all_to_all | solution.py:18
  640.7 23.1 %all-to-all-start.18 = ((bf16[8,768,128]{2,1,0:T(8,128)(2,1)}), bf16[8,768,128]{2,1,0:T(8,128)(2,1)}, u32[]{:S(2)}, u32[]{:S(2)}) async-start(bf16[8,768,128]{2,1,0:T(8,128)(2,1)} %broadcast_in_dim.198), calls=%async_computation.18 | async-start | bytes 3145728 | tf_op jit(solution)/shard_map/all_to_all | solution.py:18
  648.1 17.8 %copy-start.5 = (pred[768,768]{0,1:T(8,128)(4,1)S(1)}, pred[768,768]{0,1:T(8,128)(4,1)}, u32[]{:S(2)}) copy-start(pred[768,768]{0,1:T(8,128)(4,1)} %iota_compare_fusion) | copy-start | bytes 1769476
  666.0 9.4 %slice-start = ((s8[4718592]{0:T(1024)(128)(4,1)}), s8[4194304]{0:T(1024)(128)(4,1)S(1)}, s32[]{:S(2)}) async-start(s8[4718592]{0:T(1024)(128)(4,1)} %bitcast.627), calls=%async_computation.24 | async-start | bytes 8388608
  692.9 49.6 %all-to-all-start.19 = ((bf16[8,768,128]{2,1,0:T(8,128)(2,1)}), bf16[8,768,128]{2,1,0:T(8,128)(2,1)S(1)}, u32[]{:S(2)}, u32[]{:S(2)}) async-start(bf16[8,768,128]{2,1,0:T(8,128)(2,1)} %bitcast.632), calls=%async_computation.19 | async-start | bytes 3145728 | tf_op jit(solution)/shard_map/all_to_all | solution.py:51
  696.5 182.2 %reduce-scatter.5.cloned.1.call-start = ((), (), s32[]{:S(2)}) async-start(), calls=%async_computation.23 | async-start | bytes 6719488
  702.4 9.9 %copy-start.112 = (bf16[16,16]{1,0:T(8,128)(2,1)S(1)}, bf16[16,16]{1,0:T(8,128)(2,1)}, u32[]{:S(2)}) copy-start(bf16[16,16]{1,0:T(8,128)(2,1)} %pad_maximum_fusion.19) | copy-start | bytes 1540
  713.8 13.0 %copy-start.111 = (bf16[16,64]{1,0:T(8,128)(2,1)S(1)}, bf16[16,64]{1,0:T(8,128)(2,1)}, u32[]{:S(2)}) copy-start(bf16[16,64]{1,0:T(8,128)(2,1)} %pad_maximum_fusion.18) | copy-start | bytes 6148
  728.3 12.8 %copy-start.108 = (bf16[16,16]{1,0:T(8,128)(2,1)S(1)}, bf16[16,16]{1,0:T(8,128)(2,1)}, u32[]{:S(2)}) copy-start(bf16[16,16]{1,0:T(8,128)(2,1)} %pad_maximum_fusion.17) | copy-start | bytes 1540
  743.7 15.4 %copy-start.21 = (f32[768,128]{1,0:T(8,128)}, f32[768,128]{1,0:T(8,128)S(1)}, u32[]{:S(2)}) copy-start(f32[768,128]{1,0:T(8,128)S(1)} %convert_reduce_fusion) | copy-start | bytes 1179652
  764.8 32.7 %copy-start.10 = (f32[768,128]{1,0:T(8,128)S(1)}, f32[768,128]{1,0:T(8,128)}, u32[]{:S(2)}) copy-start(f32[768,128]{1,0:T(8,128)} %copy-done.9) | copy-start | bytes 1179652
  764.8 32.7 %copy-start.12 = (f32[768,128]{1,0:T(8,128)S(1)}, f32[768,128]{1,0:T(8,128)}, u32[]{:S(2)}) copy-start(f32[768,128]{1,0:T(8,128)} %copy-done.11) | copy-start | bytes 1179652
  764.8 32.7 %copy-start.17 = (f32[2,1,768,128]{3,2,1,0:T(8,128)S(1)}, f32[2,1,768,128]{3,2,1,0:T(8,128)}, u32[]{:S(2)}) copy-start(f32[2,1,768,128]{3,2,1,0:T(8,128)} %param.14) | copy-start | bytes 2359300
  764.8 32.7 %copy-start.102 = (f32[128]{0:T(128)S(1)}, f32[128]{0:T(128)}, u32[]{:S(2)}) copy-start(f32[128]{0:T(128)} %reshape.2250) | copy-start | bytes 1540
  764.9 32.7 %copy-start.115 = (f32[128]{0:T(128)S(1)}, f32[128]{0:T(128)}, u32[]{:S(2)}) copy-start(f32[128]{0:T(128)} %copy-done.114) | copy-start | bytes 1540
  764.9 32.7 %copy-start.117 = (f32[128]{0:T(128)S(1)}, f32[128]{0:T(128)}, u32[]{:S(2)}) copy-start(f32[128]{0:T(128)} %copy-done.116) | copy-start | bytes 1540
  764.9 25.9 %all-to-all-start.8 = ((bf16[8,768,128]{2,1,0:T(8,128)(2,1)}), bf16[8,768,128]{2,1,0:T(8,128)(2,1)}, u32[]{:S(2)}, u32[]{:S(2)}) async-start(bf16[8,768,128]{2,1,0:T(8,128)(2,1)} %bitcast.634), calls=%async_computation.8 | async-start | bytes 3145728 | tf_op jit(solution)/shard_map/all_to_all | solution.py:51
  770.8 33.1 %copy-start.14 = (f32[768,128]{1,0:T(8,128)S(1)}, f32[768,128]{1,0:T(8,128)}, u32[]{:S(2)}) copy-start(f32[768,128]{1,0:T(8,128)} %copy-done.13) | copy-start | bytes 1179652
  770.8 33.1 %copy-start.60 = (f32[768]{0:T(1024)S(1)}, f32[768]{0:T(1024)}, u32[]{:S(2)}) copy-start(f32[768]{0:T(1024)} %copy-done.58) | copy-start | bytes 9220
  770.8 33.1 %copy-start.63 = (f32[768]{0:T(1024)S(1)}, f32[768]{0:T(1024)}, u32[]{:S(2)}) copy-start(f32[768]{0:T(1024)} %copy-done.61) | copy-start | bytes 9220
  770.8 33.1 %copy-start.73 = (f32[768]{0:T(1024)S(1)}, f32[768]{0:T(1024)}, u32[]{:S(2)}) copy-start(f32[768]{0:T(1024)} %copy-done.72) | copy-start | bytes 9220
  770.8 33.1 %copy-start.75 = (f32[768]{0:T(1024)S(1)}, f32[768]{0:T(1024)}, u32[]{:S(2)}) copy-start(f32[768]{0:T(1024)} %copy-done.74) | copy-start | bytes 9220
  770.8 33.1 %copy-start.77 = (f32[768]{0:T(1024)S(1)}, f32[768]{0:T(1024)}, u32[]{:S(2)}) copy-start(f32[768]{0:T(1024)} %copy-done.76) | copy-start | bytes 9220
  770.8 33.1 %copy-start.79 = (f32[768]{0:T(1024)S(1)}, f32[768]{0:T(1024)}, u32[]{:S(2)}) copy-start(f32[768]{0:T(1024)} %copy-done.78) | copy-start | bytes 9220
  770.8 33.1 %copy-start.81 = (f32[768]{0:T(1024)S(1)}, f32[768]{0:T(1024)}, u32[]{:S(2)}) copy-start(f32[768]{0:T(1024)} %copy-done.80) | copy-start | bytes 9220
  770.8 33.1 %copy-start.83 = (f32[768]{0:T(1024)S(1)}, f32[768]{0:T(1024)}, u32[]{:S(2)}) copy-start(f32[768]{0:T(1024)} %copy-done.82) | copy-start | bytes 9220
  770.8 33.1 %copy-start.113 = (f32[128]{0:T(128)S(1)}, f32[128]{0:T(128)}, u32[]{:S(2)}) copy-start(f32[128]{0:T(128)} %reshape.2255) | copy-start | bytes 1540
  770.9 33.1 %copy-start.119 = (f32[128]{0:T(128)S(1)}, f32[128]{0:T(128)}, u32[]{:S(2)}) copy-start(f32[128]{0:T(128)} %reshape.2257) | copy-start | bytes 1540
  770.9 33.1 %copy-start.121 = (f32[128]{0:T(128)S(1)}, f32[128]{0:T(128)}, u32[]{:S(2)}) copy-start(f32[128]{0:T(128)} %reshape.2256) | copy-start | bytes 1540
  793.9 9.9 %all-to-all-start.20 = ((f32[8,1,1536]{2,1,0:T(1,128)}), f32[8,1,1536]{2,1,0:T(1,128)S(1)}, u32[]{:S(2)}, u32[]{:S(2)}) async-start(f32[8,1,1536]{2,1,0:T(1,128)} %broadcast_in_dim.199), calls=%async_computation.20 | async-start | bytes 98304 | tf_op jit(solution)/shard_map/all_to_all | solution.py:18
  799.5 22.2 %collective-permute-start = (f32[1,768,128]{2,1,0:T(8,128)}, f32[1,768,128]{2,1,0:T(8,128)}, u32[]{:S(2)}, u32[]{:S(2)}) collective-permute-start(f32[1,768,128]{2,1,0:T(8,128)} %fusion.124), channel_id=1, source_target_pairs={{0,64},{64,0},{1,65},{65,1},{2,66},{66,2},{3,67},{67,3},{4,68},{68... | collective-permute-start | bytes 1179656 | tf_op jit(solution)/shard_map/ppermute | solution.py:467
  811.0 24.8 %collective-permute-start.1 = (f32[1,768,128]{2,1,0:T(8,128)S(1)}, f32[1,768,128]{2,1,0:T(8,128)S(1)}, u32[]{:S(2)}, u32[]{:S(2)}) collective-permute-start(f32[1,768,128]{2,1,0:T(8,128)S(1)} %fusion.90), channel_id=1, source_target_pairs={{0,64},{64,0},{1,65},{65,1},{2,66},{66,2},{3,67},{67,3},{4,68},{68... | collective-permute-start | bytes 1179656 | tf_op jit(solution)/shard_map/ppermute | solution.py:470
  (116 other events, 364.4 us)
Sparse Core Ops, SparseCore 0:
  28.8 77.1 all-gather.2
  759.3 119.4 reduce-scatter.4

commit v6 on v3

--- a/solution.py
+++ b/solution.py
@@ -403,23 +403,25 @@
     return tuple(reduced)
 
 
-def gather_all(weights, dims):
-    peers = lax.axis_size("dp")
+def unpack_layer(rows, weights, dims):
+    peers = rows.shape[0]
+    gathered, at = ([], 0)
+    for w, d in zip(weights, dims):
+        part = rows[:, at : at + w.size].reshape(peers, *w.shape)
+        part = jnp.moveaxis(part, 0, d)
+        shape = part.shape
+        gathered.append(part.reshape(*shape[:d], shape[d] * shape[d + 1], *shape[d + 2 :]))
+        at += w.size
+    return tuple(gathered)
+
+
+def gather_all(weights, dims, is_first):
     size = sum(w.size for w in weights)
-    flat = jnp.concatenate([w.reshape(-1) for w in weights] + [jnp.zeros((-size % 1024,), jnp.bfloat16)])
-    every = lax.all_gather(flat[None], ("section", "dp"), axis=0, tiled=True)
-    layers = []
-    for layer_index in range(every.shape[0] // peers):
-        rows = every[layer_index * peers : (layer_index + 1) * peers]
-        gathered, at = ([], 0)
-        for w, d in zip(weights, dims):
-            part = rows[:, at : at + w.size].reshape(peers, *w.shape)
-            part = jnp.moveaxis(part, 0, d)
-            shape = part.shape
-            gathered.append(part.reshape(*shape[:d], shape[d] * shape[d + 1], *shape[d + 2 :]))
-            at += w.size
-        layers.append(tuple(gathered))
-    return layers
+    own = jnp.concatenate([w.reshape(-1) for w in weights] + [jnp.zeros((-size % 1024,), jnp.bfloat16)])
+    other = lax.ppermute(own, "section", [(0, 1), (1, 0)])
+    first_rows = lax.all_gather(jnp.where(is_first, own, other)[None], "dp", axis=0, tiled=True)
+    last_rows = lax.all_gather(jnp.where(is_first, other, own)[None], "dp", axis=0, tiled=True)
+    return (unpack_layer(first_rows, weights, dims), unpack_layer(last_rows, weights, dims))
 
 
 def shards(
@@ -439,6 +441,8 @@
     shift_second,
 ):
     dims = (0, 1, 1, 0, 0, 0, 1, 0, 0, 0, 0, 0)
+    section_index = lax.axis_index("section")
+    is_first = section_index == 0
     weights_zero, weights_last = gather_all(
         (
             packed_weight[0],
@@ -455,24 +459,26 @@
             shift_second[0],
         ),
         dims,
-    )
-    section_index = lax.axis_index("section")
-    is_first = section_index == 0
+        is_first,
+    )
     stream = lax.dynamic_index_in_dim(inputs, section_index, axis=0, keepdims=False)
     out_grad = lax.dynamic_index_in_dim(cotangent, section_index, axis=0, keepdims=False)
     middle, kept_zero = layer_forward(stream, weights_zero)
     final, kept_last = layer_forward(middle, weights_last)
-    swap = [(0, 1), (1, 0)]
-    other_out = lax.ppermute(jnp.where(is_first, final, middle), "section", swap)
+    other_middle = lax.ppermute(middle, "section", [(1, 0)])
+    other_final = lax.ppermute(final, "section", [(0, 1)])
     middle_grad, grads_last = layer_backward(out_grad, kept_last, weights_last)
+    other_middle_grad = lax.ppermute(middle_grad, "section", [(0, 1)])
     input_grad, grads_zero = layer_backward(middle_grad, kept_zero, weights_zero)
-    other_grad = lax.ppermute(jnp.where(is_first, middle_grad, input_grad), "section", swap)
+    other_input_grad = lax.ppermute(input_grad, "section", [(1, 0)])
     reduced = sum_at_end(grads_zero, grads_last, dims)
     section_outputs = jnp.where(
-        is_first, jnp.stack([middle, other_out]), jnp.stack([other_out, final])
+        is_first, jnp.stack([middle, other_middle]), jnp.stack([other_final, final])
     )[None]
     section_grads = jnp.where(
-        is_first, jnp.stack([input_grad, other_grad]), jnp.stack([other_grad, middle_grad])
+        is_first,
+        jnp.stack([input_grad, other_input_grad]),
+        jnp.stack([other_middle_grad, middle_grad]),
     )[None]
     return (section_outputs, section_grads) + tuple(reduced)
 

time: 822 us -> 783 us (0.953)
  waiting for transfers between devices: 322 us -> 268 us
  blocking collectives: 76.9 us -> 89.5 us
  starting transfers between devices: 89.5 us -> 98.3 us
    all_gather x1 -> x2, waiting for transfers between devices: 53 us -> 17.5 us  [the longest x1 17.5 us: gather_all(): lax.all_gather(jnp.where(is_first, own, other)[None], 'dp', axis=0, tiled...]
    ppermute x2 -> x5, starting transfers between devices: 4.25 us -> 18.3 us  [the longest x1 6.35 us: shards(): other_final = lax.ppermute(final, 'section', [(0, 1)])]
    all_to_all x2 -> x3, blocking collectives: 30.5 us -> 43.1 us  [sent_to_all(): return lax.all_to_all(copies, axis, split_axis=0, concat_axis=0, tiled=True)]
    unnamed x228 -> x276, local copies, waits for them, and re-layouts: 62.8 us -> 72.3 us
    concatenate x1, local copies, waits for them, and re-layouts: 18.6 us -> 10.2 us  [gather_all(): jnp.concatenate([w.reshape(-1) for w in weights] + [jnp.zeros((-size % 10...]
    all_to_all x14 -> x13, waiting for transfers between devices: 115 us -> 108 us  [sent_to_all(): return lax.all_to_all(copies, axis, split_axis=0, concat_axis=0, tiled=True)]
    unnamed x3 -> x4, waiting for transfers between devices: 42.3 us -> 36.4 us
    all_to_all x14 -> x13, starting transfers between devices: 59.1 us -> 53.3 us  [sent_to_all(): return lax.all_to_all(copies, axis, split_axis=0, concat_axis=0, tiled=True)]
  transfers between devices with their start and end apart: 24 -> 27, of which waited for: 22 -> 23; matrix products, arithmetic and copies ran while one was open for 17% -> 19% of each run, Pallas kernels for 0% -> 0%
where the time goes in v6:
time: 783 us; the launch traced here: 771 us
  waiting for transfers between devices  268 us (34%)
  local copies, waits for them, and re-layouts  172 us (22%)
  starting transfers between devices  98.3 us (13%)
  blocking collectives  89.5 us (11%)
  matrix products  74.2 us (9%)
  other arithmetic  51.9 us (7%)
  between operations  16.4 us (2%)
    all_to_all x13, waiting for transfers between devices, sent_to_all(): return lax.all_to_all(copies, axis, split_axis=0, concat_axis=0, tiled=True)  108 us
    all_to_all x6, waiting for transfers between devices, summed_on_arrival(): lax.all_to_all(parts, axis, split_axis=0, concat_axis=0, tiled=True)  85.1 us
    unnamed x276, local copies, waits for them, and re-layouts  72.3 us
    all_to_all x13, starting transfers between devices, sent_to_all(): return lax.all_to_all(copies, axis, split_axis=0, concat_axis=0, tiled=True)  53.3 us
    all_to_all x2, blocking collectives, summed_on_arrival(): lax.all_to_all(parts, axis, split_axis=0, concat_axis=0, tiled=True)  46.4 us
    all_to_all x3, blocking collectives, sent_to_all(): return lax.all_to_all(copies, axis, split_axis=0, concat_axis=0, tiled=True)  43.1 us
    unnamed x4, waiting for transfers between devices  36.4 us
    all_to_all x6, starting transfers between devices, summed_on_arrival(): lax.all_to_all(parts, axis, split_axis=0, concat_axis=0, tiled=True)  26.1 us
  transfers between devices with their start and end apart: 27, of which 23 were waited for; matrix products, arithmetic and copies ran while one was open for 19% of the time, Pallas kernels for 0%

profile of v6, /device:TPU:0, one launch (start us, length us, event | category | flops | bytes accessed | tf_op | source)
XLA Modules:
  0.0 770.9 jit_solution(9388489846848891309)
XLA Ops:
  10.1 10.2 %concatenate.107 = bf16[197632]{0:T(1024)(128)(2,1)S(1)} concatenate(bf16[49152]{0:T(1024)(128)(2,1)S(1)} %reshape_squeeze.15, bf16[32]{0:T(256)(128)(2,1)S(1)} %reshape_squeeze.16, bf16[16384]{0:T(1024)(128)(2,1)} %bitcast.639, bf16[16]{0:T(256)(128)(2,1)} %bitcast.642, bf16[65536]{0:T(1024)(128)(2,1)S(1)} %bitcast.623, bf16[64]{0:T(256)(128)(2,1)} %bitcast.643, ...), dimensions={0} | concatenate | bytes 790528 | tf_op jit(solution)/shard_map/concatenate | solution.py:420
  23.3 9.2 %collective-permute-done = bf16[197632]{0:T(1024)(128)(2,1)S(1)} collective-permute-done((bf16[197632]{0:T(1024)(128)(2,1)S(1)}, bf16[197632]{0:T(1024)(128)(2,1)S(1)}, u32[]{:S(2)}, u32[]{:S(2)}) %collective-permute-start) | collective-permute-done | bytes 395296 | tf_op jit(solution)/shard_map/ppermute | solution.py:421
  33.9 12.6 %all_to_all.128 = f32[8,1,1536]{2,1,0:T(1,128)S(1)} all-to-all(f32[8,1,1536]{2,1,0:T(1,128)S(1)} %broadcast_in_dim.195), channel_id=1, replica_groups=mesh['section'=2,'dp'=8,'tensor'=8] {'tensor'}, dimensions={0} | all-to-all | bytes 98304 | tf_op jit(solution)/shard_map/all_to_all | solution.py:18
  46.5 17.5 %all-gather.5.cloned.1.call-done = bf16[1581056]{0:T(1024)(128)(2,1)} async-done(((bf16[197632]{0:T(1024)(128)(2,1)}), bf16[1581056]{0:T(1024)(128)(2,1)}) %all-gather.5.cloned.1.call-update) | async-done | bytes 3162128 | tf_op jit(solution)/shard_map/all_gather | solution.py:422
  64.1 3.2 reshape.2326
  70.5 5.3 all-to-all-start.1
  80.5 16.2 %all-to-all-done.1 = bf16[8,768,128]{2,1,0:T(8,128)(2,1)} async-done(((bf16[8,768,128]{2,1,0:T(8,128)(2,1)}), bf16[8,768,128]{2,1,0:T(8,128)(2,1)}, u32[]{:S(2)}, u32[]{:S(2)}) %all-to-all-start.1) | async-done | bytes 1572896 | tf_op jit(solution)/shard_map/all_to_all | solution.py:18
  106.0 3.6 all-to-all-start.2
  109.7 20.5 %all-to-all-done.2 = bf16[8,768,128]{2,1,0:T(8,128)(2,1)S(1)} async-done(((bf16[8,768,128]{2,1,0:T(8,128)(2,1)}), bf16[8,768,128]{2,1,0:T(8,128)(2,1)S(1)}, u32[]{:S(2)}, u32[]{:S(2)}) %all-to-all-start.2) | async-done | bytes 1572896 | tf_op jit(solution)/shard_map/all_to_all | solution.py:51
  131.9 3.6 all-to-all-start.3
  136.4 5.4 all-to-all-done.3
  143.5 4.3 all-to-all-start.4
  147.9 3.5 fusion.142
  155.7 11.7 %all-to-all-done.4 = bf16[8,768,128]{1,2,0:T(8,128)(2,1)} async-done(((bf16[8,768,128]{1,2,0:T(8,128)(2,1)}), bf16[8,768,128]{1,2,0:T(8,128)(2,1)}, u32[]{:S(2)}, u32[]{:S(2)}) %all-to-all-start.4) | async-done | bytes 1572896 | tf_op jit(solution)/shard_map/all_to_all | solution.py:18
  172.7 3.7 all-to-all-start.5
  176.5 5.0 reshape.2327
  181.5 15.5 %all-to-all-done.5 = bf16[8,768,128]{2,1,0:T(8,128)(2,1)S(1)} async-done(((bf16[8,768,128]{2,1,0:T(8,128)(2,1)}), bf16[8,768,128]{2,1,0:T(8,128)(2,1)S(1)}, u32[]{:S(2)}, u32[]{:S(2)}) %all-to-all-start.5) | async-done | bytes 1572896 | tf_op jit(solution)/shard_map/all_to_all | solution.py:51
  198.3 3.6 all-to-all-start.6
  203.6 4.7 all-to-all-done.6
  209.9 4.8 all-to-all-start.7
  220.1 14.2 %all-to-all-done.7 = bf16[8,768,128]{2,1,0:T(8,128)(2,1)} async-done(((bf16[8,768,128]{2,1,0:T(8,128)(2,1)}), bf16[8,768,128]{2,1,0:T(8,128)(2,1)}, u32[]{:S(2)}, u32[]{:S(2)}) %all-to-all-start.7) | async-done | bytes 1572896 | tf_op jit(solution)/shard_map/all_to_all | solution.py:18
  243.4 3.6 all-to-all-start.8
  247.1 20.5 %all-to-all-done.8 = bf16[8,768,128]{2,1,0:T(8,128)(2,1)S(1)} async-done(((bf16[8,768,128]{2,1,0:T(8,128)(2,1)}), bf16[8,768,128]{2,1,0:T(8,128)(2,1)S(1)}, u32[]{:S(2)}, u32[]{:S(2)}) %all-to-all-start.8) | async-done | bytes 1572896 | tf_op jit(solution)/shard_map/all_to_all | solution.py:51
  268.9 3.6 all-to-all-start.9
  272.7 6.1 all-to-all-done.9
  280.6 4.3 all-to-all-start.10
  286.0 18.5 %all-to-all-done.10 = bf16[8,768,128]{1,2,0:T(8,128)(2,1)} async-done(((bf16[8,768,128]{1,2,0:T(8,128)(2,1)}), bf16[8,768,128]{1,2,0:T(8,128)(2,1)}, u32[]{:S(2)}, u32[]{:S(2)}) %all-to-all-start.10) | async-done | bytes 1572896 | tf_op jit(solution)/shard_map/all_to_all | solution.py:18
  305.8 3.8 all-to-all-start.12
  310.4 3.6 slice_bitcast_fusion
  316.7 3.8 convolution_add_fusion
  320.5 9.7 %all-to-all-done.12 = bf16[8,768,128]{2,1,0:T(8,128)(2,1)S(1)} async-done(((bf16[8,768,128]{2,1,0:T(8,128)(2,1)}), bf16[8,768,128]{2,1,0:T(8,128)(2,1)S(1)}, u32[]{:S(2)}, u32[]{:S(2)}) %all-to-all-start.12) | async-done | bytes 1572896 | tf_op jit(solution)/shard_map/all_to_all | solution.py:18
  330.2 5.0 fusion.145
  337.5 25.2 %all_to_all.129 = bf16[8,768,128]{2,1,0:T(8,128)(2,1)S(1)} all-to-all(bf16[8,768,128]{2,1,0:T(8,128)(2,1)S(1)} %bitcast.570), channel_id=1, replica_groups=mesh['section'=2,'dp'=8,'tensor'=8] {'tensor'}, dimensions={0} | all-to-all | bytes 3145728 | tf_op jit(solution)/shard_map/all_to_all | solution.py:51
  364.5 8.7 %all_to_all.130 = f32[8,1,1536]{2,1,0:T(1,128)S(1)} all-to-all(f32[8,1,1536]{2,1,0:T(1,128)S(1)} %broadcast_in_dim.209), channel_id=1, replica_groups=mesh['section'=2,'dp'=8,'tensor'=8] {'tensor'}, dimensions={0} | all-to-all | bytes 98304 | tf_op jit(solution)/shard_map/all_to_all | solution.py:18
  377.5 21.8 %all_to_all.131 = bf16[8,768,128]{2,1,0:T(8,128)(2,1)S(1)} all-to-all(bf16[8,768,128]{2,1,0:T(8,128)(2,1)S(1)} %broadcast_in_dim.210), channel_id=1, replica_groups=mesh['section'=2,'dp'=8,'tensor'=8] {'tensor'}, dimensions={0} | all-to-all | bytes 3145728 | tf_op jit(solution)/shard_map/all_to_all | solution.py:18
  413.5 21.3 %all_to_all.132 = bf16[8,768,128]{2,1,0:T(8,128)(2,1)S(1)} all-to-all(bf16[8,768,128]{2,1,0:T(8,128)(2,1)S(1)} %bitcast.571), channel_id=1, replica_groups=mesh['section'=2,'dp'=8,'tensor'=8] {'tensor'}, dimensions={0} | all-to-all | bytes 3145728 | tf_op jit(solution)/shard_map/all_to_all | solution.py:51
  438.2 3.3 all-to-all-start.17
  451.7 4.7 all-to-all-start.18
  456.4 3.6 convolution_convert_fusion.8
  482.1 4.3 fusion.146
  486.5 3.4 convolution_convert_fusion.9
  495.0 5.7 all-to-all-start.19
  506.4 8.9 %all-to-all-done.19 = bf16[8,768,128]{2,1,0:T(8,128)(2,1)S(1)} async-done(((bf16[8,768,128]{2,1,0:T(8,128)(2,1)}), bf16[8,768,128]{2,1,0:T(8,128)(2,1)S(1)}, u32[]{:S(2)}, u32[]{:S(2)}) %all-to-all-start.19) | async-done | bytes 1572896 | tf_op jit(solution)/shard_map/all_to_all | solution.py:51
  516.6 3.8 all-to-all-start.20
  529.7 4.3 all-to-all-start.21
  538.8 13.2 %all-to-all-done.21 = bf16[8,768,128]{2,1,0:T(8,128)(2,1)} async-done(((bf16[8,768,128]{2,1,0:T(8,128)(2,1)}), bf16[8,768,128]{2,1,0:T(8,128)(2,1)}, u32[]{:S(2)}, u32[]{:S(2)}) %all-to-all-start.21) | async-done | bytes 1572896 | tf_op jit(solution)/shard_map/all_to_all | solution.py:18
  554.1 4.6 bitcast_reduce_fusion
  558.7 4.2 multiply_reduce_fusion
  574.3 3.8 all-to-all-start.22
  587.1 4.9 dynamic-update-slice.2
  593.5 13.0 %dynamic-update-slice.4 = bf16[16,197632]{1,0:T(8,128)(2,1)} dynamic-update-slice(bf16[16,197632]{1,0:T(8,128)(2,1)} %dynamic-update-slice.3, bf16[16,65536]{1,0:T(8,128)(2,1)} %pad_maximum_fusion.1, s32[]{} %constant.165, s32[]{} %constant.173) | dynamic-update-slice | bytes 4194308
  607.9 12.7 %dynamic-update-slice.6 = bf16[16,197632]{1,0:T(8,128)(2,1)} dynamic-update-slice(bf16[16,197632]{1,0:T(8,128)(2,1)} %dynamic-update-slice.5, bf16[16,65536]{1,0:T(8,128)(2,1)} %pad_maximum_fusion, s32[]{} %constant.165, s32[]{} %constant.177) | dynamic-update-slice | bytes 4194308
  631.8 6.4 reshape.2301
  645.3 5.8 all-to-all-start.11
  651.4 19.7 %all-to-all-done.11 = bf16[8,768,128]{2,1,0:T(8,128)(2,1)} async-done(((bf16[8,768,128]{2,1,0:T(8,128)(2,1)}), bf16[8,768,128]{2,1,0:T(8,128)(2,1)}, u32[]{:S(2)}, u32[]{:S(2)}) %all-to-all-start.11) | async-done | bytes 1572896 | tf_op jit(solution)/shard_map/all_to_all | solution.py:51
  671.8 3.6 all-to-all-start.23
  677.8 3.9 all-to-all-done.23
  682.0 3.6 fusion.55
  686.9 6.1 collective-permute-start.4
  696.7 6.3 collective-permute-start.2
  703.1 5.2 collective-permute-done.3
  712.3 3.7 collective-permute-done.1
  717.0 36.0 %reduce-scatter.5.cloned.1.call-done = bf16[1,1544,128]{2,1,0:T(8,128)(2,1)} async-done(((bf16[1,24704,128]{2,1,0:T(8,128)(2,1)}), bf16[1,1544,128]{2,1,0:T(8,128)(2,1)}) %reduce-scatter.5.cloned.1.call-update) | async-done | bytes 395280
  753.0 4.2 copy.345
  (530 shorter events, 213.4 us)
Async XLA Ops:
  7.2 56.9 %all-gather.5.cloned.1.call-start = ((), (), s32[]{:S(2)}) async-start(), calls=%async_computation.25 | async-start | bytes 3557376 | tf_op jit(solution)/shard_map/all_gather | solution.py:422
  9.0 24.4 %copy-start.14 = (f32[2,1,768,128]{3,2,1,0:T(8,128)S(1)}, f32[2,1,768,128]{3,2,1,0:T(8,128)}, u32[]{:S(2)}) copy-start(f32[2,1,768,128]{3,2,1,0:T(8,128)} %param.14) | copy-start | bytes 2359300
  20.2 12.3 %collective-permute-start = (bf16[197632]{0:T(1024)(128)(2,1)S(1)}, bf16[197632]{0:T(1024)(128)(2,1)S(1)}, u32[]{:S(2)}, u32[]{:S(2)}) collective-permute-start(bf16[197632]{0:T(1024)(128)(2,1)S(1)} %concatenate.107), channel_id=1, source_target_pairs={{0,64},{64,0},{1,65},{65,1},{2,66},{66,2},{3,67},{67,3},{4,68},{68... | collective-permute-start | bytes 1185800 | tf_op jit(solution)/shard_map/ppermute | solution.py:421
  46.5 21.0 %copy-start.67 = (f32[768]{0:T(1024)}, f32[768]{0:T(1024)S(1)}, u32[]{:S(2)}) copy-start(f32[768]{0:T(1024)S(1)} %get-tuple-element.235) | copy-start | bytes 9220
  46.5 21.0 %copy-start.69 = (f32[768]{0:T(1024)}, f32[768]{0:T(1024)S(1)}, u32[]{:S(2)}) copy-start(f32[768]{0:T(1024)S(1)} %get-tuple-element.236) | copy-start | bytes 9220
  70.5 26.3 %all-to-all-start.1 = ((bf16[8,768,128]{2,1,0:T(8,128)(2,1)}), bf16[8,768,128]{2,1,0:T(8,128)(2,1)}, u32[]{:S(2)}, u32[]{:S(2)}) async-start(bf16[8,768,128]{2,1,0:T(8,128)(2,1)} %broadcast_in_dim.198), calls=%async_computation.1 | async-start | bytes 3145728 | tf_op jit(solution)/shard_map/all_to_all | solution.py:18
  76.7 22.5 %copy-start.102 = (f32[2,64]{1,0:T(2,128)}, f32[2,64]{1,0:T(2,128)S(1)}, u32[]{:S(2)}) copy-start(f32[2,64]{1,0:T(2,128)S(1)} %reshape.2306) | copy-start | bytes 1540
  76.8 24.6 %copy-start.113 = (f32[2,64]{1,0:T(2,128)}, f32[2,64]{1,0:T(2,128)S(1)}, u32[]{:S(2)}) copy-start(f32[2,64]{1,0:T(2,128)S(1)} %reshape.2305) | copy-start | bytes 1540
  106.0 24.2 %all-to-all-start.2 = ((bf16[8,768,128]{2,1,0:T(8,128)(2,1)}), bf16[8,768,128]{2,1,0:T(8,128)(2,1)S(1)}, u32[]{:S(2)}, u32[]{:S(2)}) async-start(bf16[8,768,128]{2,1,0:T(8,128)(2,1)} %bitcast.550), calls=%async_computation.2 | async-start | bytes 3145728 | tf_op jit(solution)/shard_map/all_to_all | solution.py:51
  109.6 20.8 %copy-start.15 = (f32[2,1,768,128]{3,2,1,0:T(8,128)S(1)}, f32[2,1,768,128]{3,2,1,0:T(8,128)}, u32[]{:S(2)}) copy-start(f32[2,1,768,128]{3,2,1,0:T(8,128)} %param.14) | copy-start | bytes 2359300
  109.7 21.1 %copy-start.109 = (f32[128]{0:T(128)}, f32[128]{0:T(128)S(1)}, u32[]{:S(2)}) copy-start(f32[128]{0:T(128)S(1)} %reshape.2307) | copy-start | bytes 1540
  131.9 9.9 %all-to-all-start.3 = ((f32[8,1,1536]{2,1,0:T(1,128)}), f32[8,1,1536]{2,1,0:T(1,128)S(1)}, u32[]{:S(2)}, u32[]{:S(2)}) async-start(f32[8,1,1536]{2,1,0:T(1,128)} %broadcast_in_dim.201), calls=%async_computation.3 | async-start | bytes 98304 | tf_op jit(solution)/shard_map/all_to_all | solution.py:18
  135.5 41.0 %all-gather.7.cloned.1.call-start = ((), (), s32[]{:S(2)}) async-start(), calls=%async_computation.26 | async-start | bytes 3557376 | tf_op jit(solution)/shard_map/all_gather | solution.py:423
  143.5 23.8 %all-to-all-start.4 = ((bf16[8,768,128]{1,2,0:T(8,128)(2,1)}), bf16[8,768,128]{1,2,0:T(8,128)(2,1)}, u32[]{:S(2)}, u32[]{:S(2)}) async-start(bf16[8,768,128]{1,2,0:T(8,128)(2,1)} %broadcast_in_dim.202), calls=%async_computation.4 | async-start | bytes 3145728 | tf_op jit(solution)/shard_map/all_to_all | solution.py:18
  172.7 24.3 %all-to-all-start.5 = ((bf16[8,768,128]{2,1,0:T(8,128)(2,1)}), bf16[8,768,128]{2,1,0:T(8,128)(2,1)S(1)}, u32[]{:S(2)}, u32[]{:S(2)}) async-start(bf16[8,768,128]{2,1,0:T(8,128)(2,1)} %bitcast.548), calls=%async_computation.5 | async-start | bytes 3145728 | tf_op jit(solution)/shard_map/all_to_all | solution.py:51
  176.5 20.8 %copy-start.111 = (f32[128]{0:T(128)}, f32[128]{0:T(128)S(1)}, u32[]{:S(2)}) copy-start(f32[128]{0:T(128)S(1)} %reshape.2311) | copy-start | bytes 1540
  197.5 70.3 %copy-start.6 = (f32[768,128]{1,0:T(8,128)}, f32[768,128]{1,0:T(8,128)S(1)}, u32[]{:S(2)}) copy-start(f32[768,128]{1,0:T(8,128)S(1)} %get-tuple-element.191) | copy-start | bytes 1179652
  198.3 9.9 %all-to-all-start.6 = ((f32[8,1,1536]{2,1,0:T(1,128)}), f32[8,1,1536]{2,1,0:T(1,128)S(1)}, u32[]{:S(2)}, u32[]{:S(2)}) async-start(f32[8,1,1536]{2,1,0:T(1,128)} %broadcast_in_dim.203), calls=%async_computation.6 | async-start | bytes 98304 | tf_op jit(solution)/shard_map/all_to_all | solution.py:18
  209.9 24.3 %all-to-all-start.7 = ((bf16[8,768,128]{2,1,0:T(8,128)(2,1)}), bf16[8,768,128]{2,1,0:T(8,128)(2,1)}, u32[]{:S(2)}, u32[]{:S(2)}) async-start(bf16[8,768,128]{2,1,0:T(8,128)(2,1)} %broadcast_in_dim.205), calls=%async_computation.7 | async-start | bytes 3145728 | tf_op jit(solution)/shard_map/all_to_all | solution.py:18
  215.6 21.0 %copy-start.104 = (f32[2,64]{1,0:T(2,128)}, f32[2,64]{1,0:T(2,128)S(1)}, u32[]{:S(2)}) copy-start(f32[2,64]{1,0:T(2,128)S(1)} %reshape.2315) | copy-start | bytes 1540
  215.7 23.2 %copy-start.115 = (f32[2,64]{1,0:T(2,128)}, f32[2,64]{1,0:T(2,128)S(1)}, u32[]{:S(2)}) copy-start(f32[2,64]{1,0:T(2,128)S(1)} %reshape.2314) | copy-start | bytes 1540
  243.4 24.2 %all-to-all-start.8 = ((bf16[8,768,128]{2,1,0:T(8,128)(2,1)}), bf16[8,768,128]{2,1,0:T(8,128)(2,1)S(1)}, u32[]{:S(2)}, u32[]{:S(2)}) async-start(bf16[8,768,128]{2,1,0:T(8,128)(2,1)} %bitcast.546), calls=%async_computation.8 | async-start | bytes 3145728 | tf_op jit(solution)/shard_map/all_to_all | solution.py:51
  247.1 21.1 %copy-start.95 = (f32[128]{0:T(128)}, f32[128]{0:T(128)S(1)}, u32[]{:S(2)}) copy-start(f32[128]{0:T(128)S(1)} %reshape.2316) | copy-start | bytes 1540
  268.9 9.9 %all-to-all-start.9 = ((f32[8,1,1536]{2,1,0:T(1,128)}), f32[8,1,1536]{2,1,0:T(1,128)S(1)}, u32[]{:S(2)}, u32[]{:S(2)}) async-start(f32[8,1,1536]{2,1,0:T(1,128)} %broadcast_in_dim.206), calls=%async_computation.9 | async-start | bytes 98304 | tf_op jit(solution)/shard_map/all_to_all | solution.py:18
  272.6 90.3 %copy-start.87 = (f32[128]{0:T(128)}, f32[128]{0:T(128)S(1)}, u32[]{:S(2)}) copy-start(f32[128]{0:T(128)S(1)} %reshape.2317) | copy-start | bytes 1540
  278.9 95.7 %copy-start.63 = (f32[768]{0:T(1024)}, f32[768]{0:T(1024)S(1)}, u32[]{:S(2)}) copy-start(f32[768]{0:T(1024)S(1)} %get-tuple-element.229) | copy-start | bytes 9220
  278.9 95.7 %copy-start.65 = (f32[768]{0:T(1024)}, f32[768]{0:T(1024)S(1)}, u32[]{:S(2)}) copy-start(f32[768]{0:T(1024)S(1)} %get-tuple-element.230) | copy-start | bytes 9220
  280.6 23.8 %all-to-all-start.10 = ((bf16[8,768,128]{1,2,0:T(8,128)(2,1)}), bf16[8,768,128]{1,2,0:T(8,128)(2,1)}, u32[]{:S(2)}, u32[]{:S(2)}) async-start(bf16[8,768,128]{1,2,0:T(8,128)(2,1)} %broadcast_in_dim.207), calls=%async_computation.10 | async-start | bytes 3145728 | tf_op jit(solution)/shard_map/all_to_all | solution.py:18
  305.8 24.4 %all-to-all-start.12 = ((bf16[8,768,128]{2,1,0:T(8,128)(2,1)}), bf16[8,768,128]{2,1,0:T(8,128)(2,1)S(1)}, u32[]{:S(2)}, u32[]{:S(2)}) async-start(bf16[8,768,128]{2,1,0:T(8,128)(2,1)} %broadcast_in_dim.208), calls=%async_computation.12 | async-start | bytes 3145728 | tf_op jit(solution)/shard_map/all_to_all | solution.py:18
  337.5 63.7 %slice-start.2 = ((s8[4718592]{0:T(1024)(128)(4,1)}), s8[524288]{0:T(1024)(128)(4,1)S(1)}, s32[]{:S(2)}) async-start(s8[4718592]{0:T(1024)(128)(4,1)} %bitcast.564), calls=%async_computation.30 | async-start | bytes 1048576
  374.6 26.6 %slice-start.3 = ((s8[4718592]{0:T(1024)(128)(4,1)}), s8[4194304]{0:T(1024)(128)(4,1)S(1)}, s32[]{:S(2)}) async-start(s8[4718592]{0:T(1024)(128)(4,1)} %bitcast.564), calls=%async_computation.31 | async-start | bytes 8388608
  377.5 23.0 %copy-start.49 = (bf16[1,8,128,128]{3,1,2,0:T(8,128)(2,1)S(1)}, bf16[1,8,128,128]{3,1,2,0:T(8,128)(2,1)}, u32[]{:S(2)}) copy-start(bf16[1,8,128,128]{3,1,2,0:T(8,128)(2,1)} %copy-done.48) | copy-start | bytes 786436
  438.2 9.6 %all-to-all-start.17 = ((f32[8,1,1536]{2,1,0:T(1,128)}), f32[8,1,1536]{2,1,0:T(1,128)S(1)}, u32[]{:S(2)}, u32[]{:S(2)}) async-start(f32[8,1,1536]{2,1,0:T(1,128)} %broadcast_in_dim.211), calls=%async_computation.17 | async-start | bytes 98304 | tf_op jit(solution)/shard_map/all_to_all | solution.py:18
  451.7 30.5 %all-to-all-start.18 = ((bf16[8,768,128]{2,1,0:T(8,128)(2,1)}), bf16[8,768,128]{2,1,0:T(8,128)(2,1)}, u32[]{:S(2)}, u32[]{:S(2)}) async-start(bf16[8,768,128]{2,1,0:T(8,128)(2,1)} %broadcast_in_dim.212), calls=%async_computation.18 | async-start | bytes 3145728 | tf_op jit(solution)/shard_map/all_to_all | solution.py:18
  495.0 20.2 %all-to-all-start.19 = ((bf16[8,768,128]{2,1,0:T(8,128)(2,1)}), bf16[8,768,128]{2,1,0:T(8,128)(2,1)S(1)}, u32[]{:S(2)}, u32[]{:S(2)}) async-start(bf16[8,768,128]{2,1,0:T(8,128)(2,1)} %bitcast.569), calls=%async_computation.19 | async-start | bytes 3145728 | tf_op jit(solution)/shard_map/all_to_all | solution.py:51
  516.6 10.1 %all-to-all-start.20 = ((f32[8,1,1536]{2,1,0:T(1,128)}), f32[8,1,1536]{2,1,0:T(1,128)S(1)}, u32[]{:S(2)}, u32[]{:S(2)}) async-start(f32[8,1,1536]{2,1,0:T(1,128)} %broadcast_in_dim.213), calls=%async_computation.20 | async-start | bytes 98304 | tf_op jit(solution)/shard_map/all_to_all | solution.py:18
  529.7 22.3 %all-to-all-start.21 = ((bf16[8,768,128]{2,1,0:T(8,128)(2,1)}), bf16[8,768,128]{2,1,0:T(8,128)(2,1)}, u32[]{:S(2)}, u32[]{:S(2)}) async-start(bf16[8,768,128]{2,1,0:T(8,128)(2,1)} %broadcast_in_dim.214), calls=%async_computation.21 | async-start | bytes 3145728 | tf_op jit(solution)/shard_map/all_to_all | solution.py:18
  574.3 47.8 %all-to-all-start.22 = ((bf16[8,768,128]{2,1,0:T(8,128)(2,1)}), bf16[8,768,128]{2,1,0:T(8,128)(2,1)S(1)}, u32[]{:S(2)}, u32[]{:S(2)}) async-start(bf16[8,768,128]{2,1,0:T(8,128)(2,1)} %bitcast.568), calls=%async_computation.22 | async-start | bytes 3145728 | tf_op jit(solution)/shard_map/all_to_all | solution.py:51
  578.1 174.9 %reduce-scatter.5.cloned.1.call-start = ((), (), s32[]{:S(2)}) async-start(), calls=%async_computation.27 | async-start | bytes 6719488
  645.3 25.8 %all-to-all-start.11 = ((bf16[8,768,128]{2,1,0:T(8,128)(2,1)}), bf16[8,768,128]{2,1,0:T(8,128)(2,1)}, u32[]{:S(2)}, u32[]{:S(2)}) async-start(bf16[8,768,128]{2,1,0:T(8,128)(2,1)} %bitcast.544), calls=%async_computation.11 | async-start | bytes 3145728 | tf_op jit(solution)/shard_map/all_to_all | solution.py:51
  651.1 30.6 %copy-start.9 = (f32[768,128]{1,0:T(8,128)S(1)}, f32[768,128]{1,0:T(8,128)}, u32[]{:S(2)}) copy-start(f32[768,128]{1,0:T(8,128)} %copy-done.8) | copy-start | bytes 1179652
  651.1 30.6 %copy-start.11 = (f32[768,128]{1,0:T(8,128)S(1)}, f32[768,128]{1,0:T(8,128)}, u32[]{:S(2)}) copy-start(f32[768,128]{1,0:T(8,128)} %copy-done.10) | copy-start | bytes 1179652
  651.1 30.6 %copy-start.13 = (f32[768,128]{1,0:T(8,128)S(1)}, f32[768,128]{1,0:T(8,128)}, u32[]{:S(2)}) copy-start(f32[768,128]{1,0:T(8,128)} %copy-done.12) | copy-start | bytes 1179652
  651.2 30.6 %copy-start.22 = (f32[768,128]{1,0:T(8,128)S(1)}, f32[768,128]{1,0:T(8,128)}, u32[]{:S(2)}) copy-start(f32[768,128]{1,0:T(8,128)} %copy-done.21) | copy-start | bytes 1179652
  651.2 30.6 %copy-start.24 = (f32[768,128]{1,0:T(8,128)S(1)}, f32[768,128]{1,0:T(8,128)}, u32[]{:S(2)}) copy-start(f32[768,128]{1,0:T(8,128)} %copy-done.23) | copy-start | bytes 1179652
  651.2 30.6 %copy-start.64 = (f32[768]{0:T(1024)S(1)}, f32[768]{0:T(1024)}, u32[]{:S(2)}) copy-start(f32[768]{0:T(1024)} %copy-done.63) | copy-start | bytes 9220
  651.2 30.6 %copy-start.66 = (f32[768]{0:T(1024)S(1)}, f32[768]{0:T(1024)}, u32[]{:S(2)}) copy-start(f32[768]{0:T(1024)} %copy-done.65) | copy-start | bytes 9220
  651.2 30.6 %copy-start.72 = (f32[768]{0:T(1024)S(1)}, f32[768]{0:T(1024)}, u32[]{:S(2)}) copy-start(f32[768]{0:T(1024)} %copy-done.71) | copy-start | bytes 9220
  651.2 30.6 %copy-start.74 = (f32[768]{0:T(1024)S(1)}, f32[768]{0:T(1024)}, u32[]{:S(2)}) copy-start(f32[768]{0:T(1024)} %copy-done.73) | copy-start | bytes 9220
  651.2 30.6 %copy-start.76 = (f32[768]{0:T(1024)S(1)}, f32[768]{0:T(1024)}, u32[]{:S(2)}) copy-start(f32[768]{0:T(1024)} %copy-done.75) | copy-start | bytes 9220
  651.2 30.6 %copy-start.78 = (f32[768]{0:T(1024)S(1)}, f32[768]{0:T(1024)}, u32[]{:S(2)}) copy-start(f32[768]{0:T(1024)} %copy-done.77) | copy-start | bytes 9220
  651.2 30.6 %copy-start.80 = (f32[768]{0:T(1024)S(1)}, f32[768]{0:T(1024)}, u32[]{:S(2)}) copy-start(f32[768]{0:T(1024)} %copy-done.79) | copy-start | bytes 9220
  651.2 30.6 %copy-start.82 = (f32[768]{0:T(1024)S(1)}, f32[768]{0:T(1024)}, u32[]{:S(2)}) copy-start(f32[768]{0:T(1024)} %copy-done.81) | copy-start | bytes 9220
  651.3 30.6 %copy-start.88 = (f32[128]{0:T(128)S(1)}, f32[128]{0:T(128)}, u32[]{:S(2)}) copy-start(f32[128]{0:T(128)} %copy-done.87) | copy-start | bytes 1540
  651.3 30.6 %copy-start.91 = (f32[128]{0:T(128)S(1)}, f32[128]{0:T(128)}, u32[]{:S(2)}) copy-start(f32[128]{0:T(128)} %copy-done.89) | copy-start | bytes 1540
  651.3 30.6 %copy-start.94 = (f32[128]{0:T(128)S(1)}, f32[128]{0:T(128)}, u32[]{:S(2)}) copy-start(f32[128]{0:T(128)} %copy-done.92) | copy-start | bytes 1540
  651.3 30.6 %copy-start.96 = (f32[128]{0:T(128)S(1)}, f32[128]{0:T(128)}, u32[]{:S(2)}) copy-start(f32[128]{0:T(128)} %copy-done.95) | copy-start | bytes 1540
  651.3 30.6 %copy-start.110 = (f32[128]{0:T(128)S(1)}, f32[128]{0:T(128)}, u32[]{:S(2)}) copy-start(f32[128]{0:T(128)} %copy-done.109) | copy-start | bytes 1540
  651.3 30.6 %copy-start.112 = (f32[128]{0:T(128)S(1)}, f32[128]{0:T(128)}, u32[]{:S(2)}) copy-start(f32[128]{0:T(128)} %copy-done.111) | copy-start | bytes 1540
  671.8 9.9 %all-to-all-start.23 = ((f32[8,1,1536]{2,1,0:T(1,128)}), f32[8,1,1536]{2,1,0:T(1,128)S(1)}, u32[]{:S(2)}, u32[]{:S(2)}) async-start(f32[8,1,1536]{2,1,0:T(1,128)} %broadcast_in_dim.215), calls=%async_computation.23 | async-start | bytes 98304 | tf_op jit(solution)/shard_map/all_to_all | solution.py:18
  685.6 22.7 %collective-permute-start.3 = (f32[1,768,128]{2,1,0:T(8,128)S(1)}, f32[1,768,128]{2,1,0:T(8,128)S(1)}, u32[]{:S(2)}, u32[]{:S(2)}) collective-permute-start(f32[1,768,128]{2,1,0:T(8,128)S(1)} %get-tuple-element.187), channel_id=1, source_target_pairs={{64,0},{65,1},{66,2},{67,3},{68,4},{69,5},{70,6},{71,7},{72,8},{73... | collective-permute-start | bytes 1179656 | tf_op jit(solution)/shard_map/ppermute | solution.py:473
  686.9 21.4 %collective-permute-start.4 = (f32[1,768,128]{2,1,0:T(8,128)S(1)}, f32[1,768,128]{2,1,0:T(8,128)S(1)}, u32[]{:S(2)}, u32[]{:S(2)}) collective-permute-start(f32[1,768,128]{2,1,0:T(8,128)S(1)} %get-tuple-element.188), channel_id=1, source_target_pairs={{0,64},{1,65},{2,66},{3,67},{4,68},{5,69},{6,70},{7,71},{8,72},{9,... | collective-permute-start | bytes 1179656 | tf_op jit(solution)/shard_map/ppermute | solution.py:471
  693.0 23.0 %collective-permute-start.1 = (f32[1,768,128]{2,1,0:T(8,128)S(1)}, f32[1,768,128]{2,1,0:T(8,128)S(1)}, u32[]{:S(2)}, u32[]{:S(2)}) collective-permute-start(f32[1,768,128]{2,1,0:T(8,128)S(1)} %get-tuple-element.189), channel_id=1, source_target_pairs={{64,0},{65,1},{66,2},{67,3},{68,4},{69,5},{70,6},{71,7},{72,8},{73... | collective-permute-start | bytes 1179656 | tf_op jit(solution)/shard_map/ppermute | solution.py:468
  696.7 15.6 %collective-permute-start.2 = (f32[1,768,128]{2,1,0:T(8,128)S(1)}, f32[1,768,128]{2,1,0:T(8,128)S(1)}, u32[]{:S(2)}, u32[]{:S(2)}) collective-permute-start(f32[1,768,128]{2,1,0:T(8,128)S(1)} %fusion.88), channel_id=1, source_target_pairs={{0,64},{1,65},{2,66},{3,67},{4,68},{5,69},{6,70},{7,71},{8,72},{9,... | collective-permute-start | bytes 1179656 | tf_op jit(solution)/shard_map/ppermute | solution.py:469
  (92 other events, 356.7 us)
Sparse Core Ops, SparseCore 0:
  33.6 30.4 all-gather.4
  138.6 27.8 all-gather.6
  638.4 114.4 reduce-scatter.4

commit v7 on v6

--- a/solution.py
+++ b/solution.py
@@ -378,50 +378,78 @@
     return flat.reshape(block_shape)
 
 
+def split_by_size(arrays):
+    big = [i for i, a in enumerate(arrays) if a[0].size % 128 == 0]
+    small = [i for i, a in enumerate(arrays) if a[0].size % 128 != 0]
+    return (big, small)
+
+
+def in_rows(blocks, big, small):
+    count = blocks[0].shape[0]
+    rest = jnp.concatenate([blocks[i].reshape(count, -1) for i in small], axis=1)
+    spare = -rest.shape[1] % 2048
+    rest = jnp.concatenate([rest, jnp.zeros((count, spare), rest.dtype)], axis=1)
+    rows = [blocks[i].reshape(count, -1, 128) for i in big] + [rest.reshape(count, -1, 128)]
+    return jnp.concatenate(rows, axis=1)
+
+
+def out_of_rows(rows, shapes, big, small):
+    count = rows.shape[0]
+    parts, at = ({}, 0)
+    for i in big:
+        height = math.prod(shapes[i]) // 128
+        parts[i] = rows[:, at : at + height].reshape(count, *shapes[i])
+        at += height
+    rest = rows[:, at:].reshape(count, -1)
+    at = 0
+    for i in small:
+        width = math.prod(shapes[i])
+        parts[i] = rest[:, at : at + width].reshape(count, *shapes[i])
+        at += width
+    return [parts[i] for i in range(len(shapes))]
+
+
 def sum_at_end(grads_zero, grads_last, dims):
     peers = lax.axis_size("dp")
-    pieces = [
+    blocks = [
         jnp.concatenate(
             [as_blocks(g0.astype(jnp.bfloat16), d, peers), as_blocks(g1.astype(jnp.bfloat16), d, peers)]
         )
         for g0, g1, d in zip(grads_zero, grads_last, dims)
     ]
-    widths = [p.shape[1] for p in pieces]
-    spare = -sum(widths) % 1024
-    pieces.append(jnp.zeros((2 * peers, spare), jnp.bfloat16))
+    big, small = split_by_size(blocks)
+    rows = in_rows(blocks, big, small)
     total = lax.psum_scatter(
-        jnp.concatenate(pieces, axis=1).reshape(1, -1, 128),
-        ("section", "dp"),
-        scatter_dimension=1,
-        tiled=True,
-    ).reshape(1, -1)
-    reduced, at = ([], 0)
-    for g, d, w in zip(grads_zero, dims, widths):
-        piece = total[0, at : at + w].astype(jnp.float32)
-        reduced.append(from_blocks(piece, g.shape, d, peers)[None])
-        at += w
-    return tuple(reduced)
-
-
-def unpack_layer(rows, weights, dims):
-    peers = rows.shape[0]
-    gathered, at = ([], 0)
-    for w, d in zip(weights, dims):
-        part = rows[:, at : at + w.size].reshape(peers, *w.shape)
+        rows.reshape(-1, 128), ("section", "dp"), scatter_dimension=0, tiled=True
+    )
+    shapes = [block.shape[1:] for block in blocks]
+    parts = out_of_rows(total[None], shapes, big, small)
+    return tuple(
+        from_blocks(part[0].astype(jnp.float32), g.shape, d, peers)[None]
+        for part, g, d in zip(parts, grads_zero, dims)
+    )
+
+
+def unpack_layer(gathered_rows, weights, dims, big, small):
+    parts = out_of_rows(gathered_rows, [w.shape for w in weights], big, small)
+    gathered = []
+    for part, d in zip(parts, dims):
         part = jnp.moveaxis(part, 0, d)
         shape = part.shape
         gathered.append(part.reshape(*shape[:d], shape[d] * shape[d + 1], *shape[d + 2 :]))
-        at += w.size
     return tuple(gathered)
 
 
 def gather_all(weights, dims, is_first):
-    size = sum(w.size for w in weights)
-    own = jnp.concatenate([w.reshape(-1) for w in weights] + [jnp.zeros((-size % 1024,), jnp.bfloat16)])
+    big, small = split_by_size([w[None] for w in weights])
+    own = in_rows([w[None] for w in weights], big, small)[0]
     other = lax.ppermute(own, "section", [(0, 1), (1, 0)])
-    first_rows = lax.all_gather(jnp.where(is_first, own, other)[None], "dp", axis=0, tiled=True)
-    last_rows = lax.all_gather(jnp.where(is_first, other, own)[None], "dp", axis=0, tiled=True)
-    return (unpack_layer(first_rows, weights, dims), unpack_layer(last_rows, weights, dims))
+    first_rows = lax.all_gather(jnp.where(is_first, own, other), "dp", axis=0, tiled=False)
+    last_rows = lax.all_gather(jnp.where(is_first, other, own), "dp", axis=0, tiled=False)
+    return (
+        unpack_layer(first_rows, weights, dims, big, small),
+        unpack_layer(last_rows, weights, dims, big, small),
+    )
 
 
 def shards(

time: 783 us -> 727 us (0.928)
  local copies, waits for them, and re-layouts: 172 us -> 113 us
  waiting for transfers between devices: 268 us -> 233 us
  blocking collectives: 89.5 us -> 117 us
  other arithmetic: 51.9 us -> 66 us
    unnamed x276 -> x296, local copies, waits for them, and re-layouts: 72.3 us -> 19.1 us
    unnamed x4 -> x3, waiting for transfers between devices: 36.4 us -> 0.73 us
    reduce_scatter x0 -> x1, waiting for transfers between devices: none -> 33.6 us  [sum_at_end(): lax.psum_scatter(rows.reshape(-1, 128), ('section', 'dp'), scatter_dimens...]
    all_to_all x3 -> x5, blocking collectives: 43.1 us -> 70.6 us  [sent_to_all(): return lax.all_to_all(copies, axis, split_axis=0, concat_axis=0, tiled=True)]
    all_to_all x13 -> x11, waiting for transfers between devices: 108 us -> 89.7 us  [sent_to_all(): return lax.all_to_all(copies, axis, split_axis=0, concat_axis=0, tiled=True)]
    all_to_all x6, waiting for transfers between devices: 85.1 us -> 72.4 us  [summed_on_arrival(): lax.all_to_all(parts, axis, split_axis=0, concat_axis=0, tiled=True)]
    another operation x6 -> x3, local copies, waits for them, and re-layouts: 10.6 us -> 1.88 us  [the longest x2 1.15 us: in_rows(): blocks[i].reshape(count, -1, 128)]
    all_gather x2 -> x0, local copies, waits for them, and re-layouts: 8.19 us -> none  [the longest x1 4.97 us: gather_all(): lax.all_gather(jnp.where(is_first, other, own)[None], 'dp', axis=0, tiled...]
  transfers between devices with their start and end apart: 27 -> 25, of which waited for: 23 -> 20; matrix products, arithmetic and copies ran while one was open for 19% -> 19% of each run, Pallas kernels for 0% -> 0%
where the time goes in v7:
time: 727 us; the launch traced here: 716 us
  waiting for transfers between devices  233 us (32%)
  blocking collectives  117 us (16%)
  local copies, waits for them, and re-layouts  113 us (16%)
  starting transfers between devices  93 us (13%)
  matrix products  77.8 us (11%)
  other arithmetic  66 us (9%)
  between operations  16.1 us (2%)
    all_to_all x11, waiting for transfers between devices, sent_to_all(): return lax.all_to_all(copies, axis, split_axis=0, concat_axis=0, tiled=True)  89.7 us
    all_to_all x6, waiting for transfers between devices, summed_on_arrival(): lax.all_to_all(parts, axis, split_axis=0, concat_axis=0, tiled=True)  72.4 us
    all_to_all x5, blocking collectives, sent_to_all(): return lax.all_to_all(copies, axis, split_axis=0, concat_axis=0, tiled=True)  70.6 us
    all_to_all x11, starting transfers between devices, sent_to_all(): return lax.all_to_all(copies, axis, split_axis=0, concat_axis=0, tiled=True)  47.7 us
    all_to_all x2, blocking collectives, summed_on_arrival(): lax.all_to_all(parts, axis, split_axis=0, concat_axis=0, tiled=True)  46.5 us
    reduce_scatter x1, waiting for transfers between devices, sum_at_end(): lax.psum_scatter(rows.reshape(-1, 128), ('section', 'dp'), scatter_dimens...  33.6 us
    all_to_all x6, starting transfers between devices, summed_on_arrival(): lax.all_to_all(parts, axis, split_axis=0, concat_axis=0, tiled=True)  27.2 us
    unnamed x296, local copies, waits for them, and re-layouts  19.1 us
  transfers between devices with their start and end apart: 25, of which 20 were waited for; matrix products, arithmetic and copies ran while one was open for 19% of the time, Pallas kernels for 0%

profile of v7, /device:TPU:0, one launch (start us, length us, event | category | flops | bytes accessed | tf_op | source)
XLA Modules:
  0.0 716.0 jit_solution(9050220283220438425)
XLA Ops:
  12.8 3.2 collective-permute-start
  16.0 9.2 %collective-permute-done = bf16[1552,128]{1,0:T(8,128)(2,1)S(1)} collective-permute-done((bf16[1552,128]{1,0:T(8,128)(2,1)S(1)}, bf16[1552,128]{1,0:T(8,128)(2,1)S(1)}, u32[]{:S(2)}, u32[]{:S(2)}) %collective-permute-start) | collective-permute-done | bytes 397344 | tf_op jit(solution)/shard_map/ppermute | solution.py:446
  26.6 12.6 %all_to_all.128 = f32[8,1,1536]{2,1,0:T(1,128)S(1)} all-to-all(f32[8,1,1536]{2,1,0:T(1,128)S(1)} %broadcast_in_dim.192), channel_id=1, replica_groups=mesh['section'=2,'dp'=8,'tensor'=8] {'tensor'}, dimensions={0} | all-to-all | bytes 98304 | tf_op jit(solution)/shard_map/all_to_all | solution.py:18
  39.2 17.6 %all-gather.5.cloned.1.call-done = bf16[12416,128]{1,0:T(8,128)(2,1)} async-done(((bf16[1552,128]{1,0:T(8,128)(2,1)}), bf16[12416,128]{1,0:T(8,128)(2,1)}) %all-gather.5.cloned.1.call-update) | async-done | bytes 3178512 | tf_op jit(solution)/shard_map/all_gather | solution.py:447
  59.4 5.3 all-to-all-start.1
  70.0 15.7 %all-to-all-done.1 = bf16[8,768,128]{2,1,0:T(8,128)(2,1)} async-done(((bf16[8,768,128]{2,1,0:T(8,128)(2,1)}), bf16[8,768,128]{2,1,0:T(8,128)(2,1)}, u32[]{:S(2)}, u32[]{:S(2)}) %all-to-all-start.1) | async-done | bytes 1572896 | tf_op jit(solution)/shard_map/all_to_all | solution.py:18
  95.1 3.6 all-to-all-start.2
  99.6 19.8 %all-to-all-done.2 = bf16[8,768,128]{2,1,0:T(8,128)(2,1)S(1)} async-done(((bf16[8,768,128]{2,1,0:T(8,128)(2,1)}), bf16[8,768,128]{2,1,0:T(8,128)(2,1)S(1)}, u32[]{:S(2)}, u32[]{:S(2)}) %all-to-all-start.2) | async-done | bytes 1572896 | tf_op jit(solution)/shard_map/all_to_all | solution.py:51
  121.0 3.6 all-to-all-start.3
  124.8 6.1 all-to-all-done.3
  132.7 4.8 all-to-all-start.4
  138.2 2.7 fusion.140
  144.7 12.2 %all-to-all-done.4 = bf16[8,768,128]{1,2,0:T(8,128)(2,1)} async-done(((bf16[8,768,128]{1,2,0:T(8,128)(2,1)}), bf16[8,768,128]{1,2,0:T(8,128)(2,1)}, u32[]{:S(2)}, u32[]{:S(2)}) %all-to-all-start.4) | async-done | bytes 1572896 | tf_op jit(solution)/shard_map/all_to_all | solution.py:18
  156.9 2.8 convolution_add_fusion.1
  162.3 3.6 all-to-all-start.5
  167.4 19.1 %all-to-all-done.5 = bf16[8,768,128]{2,1,0:T(8,128)(2,1)S(1)} async-done(((bf16[8,768,128]{2,1,0:T(8,128)(2,1)}), bf16[8,768,128]{2,1,0:T(8,128)(2,1)S(1)}, u32[]{:S(2)}, u32[]{:S(2)}) %all-to-all-start.5) | async-done | bytes 1572896 | tf_op jit(solution)/shard_map/all_to_all | solution.py:51
  187.7 3.6 all-to-all-start.6
  193.0 4.6 all-to-all-done.6
  199.3 4.3 all-to-all-start.7
  208.6 14.5 %all-to-all-done.7 = bf16[8,768,128]{2,1,0:T(8,128)(2,1)} async-done(((bf16[8,768,128]{2,1,0:T(8,128)(2,1)}), bf16[8,768,128]{2,1,0:T(8,128)(2,1)}, u32[]{:S(2)}, u32[]{:S(2)}) %all-to-all-start.7) | async-done | bytes 1572896 | tf_op jit(solution)/shard_map/all_to_all | solution.py:18
  232.3 3.8 all-to-all-start.8
  236.6 20.0 %all-to-all-done.8 = bf16[8,768,128]{2,1,0:T(8,128)(2,1)S(1)} async-done(((bf16[8,768,128]{2,1,0:T(8,128)(2,1)}), bf16[8,768,128]{2,1,0:T(8,128)(2,1)S(1)}, u32[]{:S(2)}, u32[]{:S(2)}) %all-to-all-start.8) | async-done | bytes 1572896 | tf_op jit(solution)/shard_map/all_to_all | solution.py:51
  258.4 3.6 all-to-all-start.9
  263.5 4.8 all-to-all-done.9
  270.6 4.3 all-to-all-start.10
  276.0 18.5 %all-to-all-done.10 = bf16[8,768,128]{1,2,0:T(8,128)(2,1)} async-done(((bf16[8,768,128]{1,2,0:T(8,128)(2,1)}), bf16[8,768,128]{1,2,0:T(8,128)(2,1)}, u32[]{:S(2)}, u32[]{:S(2)}) %all-to-all-start.10) | async-done | bytes 1572896 | tf_op jit(solution)/shard_map/all_to_all | solution.py:18
  295.8 3.8 all-to-all-start.12
  302.3 3.1 slice_bitcast_fusion
  307.8 3.9 convolution_add_fusion
  311.7 8.5 %all-to-all-done.12 = bf16[8,768,128]{2,1,0:T(8,128)(2,1)S(1)} async-done(((bf16[8,768,128]{2,1,0:T(8,128)(2,1)}), bf16[8,768,128]{2,1,0:T(8,128)(2,1)S(1)}, u32[]{:S(2)}, u32[]{:S(2)}) %all-to-all-start.12) | async-done | bytes 1572896 | tf_op jit(solution)/shard_map/all_to_all | solution.py:18
  320.2 5.0 fusion.143
  326.5 25.2 %all_to_all.129 = bf16[8,768,128]{2,1,0:T(8,128)(2,1)S(1)} all-to-all(bf16[8,768,128]{2,1,0:T(8,128)(2,1)S(1)} %bitcast.544), channel_id=1, replica_groups=mesh['section'=2,'dp'=8,'tensor'=8] {'tensor'}, dimensions={0} | all-to-all | bytes 3145728 | tf_op jit(solution)/shard_map/all_to_all | solution.py:51
  354.8 8.7 %all_to_all.130 = f32[8,1,1536]{2,1,0:T(1,128)S(1)} all-to-all(f32[8,1,1536]{2,1,0:T(1,128)S(1)} %broadcast_in_dim.204), channel_id=1, replica_groups=mesh['section'=2,'dp'=8,'tensor'=8] {'tensor'}, dimensions={0} | all-to-all | bytes 98304 | tf_op jit(solution)/shard_map/all_to_all | solution.py:18
  366.7 21.5 %all_to_all.131 = bf16[8,768,128]{2,1,0:T(8,128)(2,1)S(1)} all-to-all(bf16[8,768,128]{2,1,0:T(8,128)(2,1)S(1)} %broadcast_in_dim.205), channel_id=1, replica_groups=mesh['section'=2,'dp'=8,'tensor'=8] {'tensor'}, dimensions={0} | all-to-all | bytes 3145728 | tf_op jit(solution)/shard_map/all_to_all | solution.py:18
  403.3 21.2 %all_to_all.132 = bf16[8,768,128]{2,1,0:T(8,128)(2,1)S(1)} all-to-all(bf16[8,768,128]{2,1,0:T(8,128)(2,1)S(1)} %bitcast.545), channel_id=1, replica_groups=mesh['section'=2,'dp'=8,'tensor'=8] {'tensor'}, dimensions={0} | all-to-all | bytes 3145728 | tf_op jit(solution)/shard_map/all_to_all | solution.py:51
  427.6 9.4 %all_to_all.133 = f32[8,1,1536]{2,1,0:T(1,128)} all-to-all(f32[8,1,1536]{2,1,0:T(1,128)S(1)} %broadcast_in_dim.206), channel_id=1, replica_groups=mesh['section'=2,'dp'=8,'tensor'=8] {'tensor'}, dimensions={0} | all-to-all | bytes 98304 | tf_op jit(solution)/shard_map/all_to_all | solution.py:18
  442.3 18.5 %all_to_all.134 = bf16[8,768,128]{2,1,0:T(8,128)(2,1)S(1)} all-to-all(bf16[8,768,128]{2,1,0:T(8,128)(2,1)S(1)} %broadcast_in_dim.207), channel_id=1, replica_groups=mesh['section'=2,'dp'=8,'tensor'=8] {'tensor'}, dimensions={0} | all-to-all | bytes 3145728 | tf_op jit(solution)/shard_map/all_to_all | solution.py:18
  460.9 4.5 fusion.144
  467.9 4.7 all-to-all-start.19
  477.1 3.6 convolution_convert_fusion.8
  483.2 3.0 fusion.43
  498.2 5.7 all-to-all-start.20
  516.0 5.0 all-to-all-start.21
  527.8 3.2 concatenate.135
  533.2 3.7 convolution_convert_fusion.9
  541.1 3.1 fusion.42
  552.0 5.1 bitcast_reduce_fusion
  557.1 4.2 multiply_reduce_fusion
  570.9 5.7 all-to-all-start.22
  580.8 3.2 concatenate.134
  585.2 2.8 maximum_dynamic-update-slice_fusion.2
  599.2 2.8 fusion.33
  603.5 5.8 all-to-all-start.11
  609.6 13.5 %all-to-all-done.11 = bf16[8,768,128]{2,1,0:T(8,128)(2,1)} async-done(((bf16[8,768,128]{2,1,0:T(8,128)(2,1)}), bf16[8,768,128]{2,1,0:T(8,128)(2,1)}, u32[]{:S(2)}, u32[]{:S(2)}) %all-to-all-start.11) | async-done | bytes 1572896 | tf_op jit(solution)/shard_map/all_to_all | solution.py:51
  623.7 3.6 all-to-all-start.23
  629.7 3.9 all-to-all-done.23
  633.9 3.6 fusion.55
  638.8 6.1 collective-permute-start.4
  646.4 3.4 fusion.72
  649.9 6.1 collective-permute-start.2
  656.1 3.6 collective-permute-done.3
  659.6 2.9 collective-permute-done.4
  663.4 3.3 collective-permute-done.2
  667.7 33.6 %reduce-scatter.2.cloned.1.call-done = bf16[1552,128]{1,0:T(8,128)(2,1)} async-done(((bf16[24832,128]{1,0:T(8,128)(2,1)}), bf16[1552,128]{1,0:T(8,128)(2,1)}) %reduce-scatter.2.cloned.1.call-update) | async-done | bytes 397328 | tf_op jit(solution)/shard_map/reduce_scatter | solution.py:422
  (545 shorter events, 197.6 us)
Async XLA Ops:
  7.2 49.6 %all-gather.5.cloned.1.call-start = ((), (), s32[]{:S(2)}) async-start(), calls=%async_computation.26 | async-start | bytes 3575808 | tf_op jit(solution)/shard_map/all_gather | solution.py:447
  9.0 17.1 %copy-start.5 = (f32[2,1,768,128]{3,2,1,0:T(8,128)S(1)}, f32[2,1,768,128]{3,2,1,0:T(8,128)}, u32[]{:S(2)}) copy-start(f32[2,1,768,128]{3,2,1,0:T(8,128)} %param.14) | copy-start | bytes 2359300
  12.8 12.4 %collective-permute-start = (bf16[1552,128]{1,0:T(8,128)(2,1)S(1)}, bf16[1552,128]{1,0:T(8,128)(2,1)S(1)}, u32[]{:S(2)}, u32[]{:S(2)}) collective-permute-start(bf16[1552,128]{1,0:T(8,128)(2,1)S(1)} %bitcast.599), channel_id=1, source_target_pairs={{0,64},{64,0},{1,65},{65,1},{2,66},{66,2},{3,67},{67,3},{4,68},{68... | collective-permute-start | bytes 1191944 | tf_op jit(solution)/shard_map/ppermute | solution.py:446
  39.2 20.3 %copy-start.62 = (f32[768]{0:T(1024)}, f32[768]{0:T(1024)S(1)}, u32[]{:S(2)}) copy-start(f32[768]{0:T(1024)S(1)} %get-tuple-element.237) | copy-start | bytes 9220
  39.2 20.3 %copy-start.64 = (f32[768]{0:T(1024)}, f32[768]{0:T(1024)S(1)}, u32[]{:S(2)}) copy-start(f32[768]{0:T(1024)S(1)} %get-tuple-element.238) | copy-start | bytes 9220
  59.4 26.3 %all-to-all-start.1 = ((bf16[8,768,128]{2,1,0:T(8,128)(2,1)}), bf16[8,768,128]{2,1,0:T(8,128)(2,1)}, u32[]{:S(2)}, u32[]{:S(2)}) async-start(bf16[8,768,128]{2,1,0:T(8,128)(2,1)} %broadcast_in_dim.194), calls=%async_computation.1 | async-start | bytes 3145728 | tf_op jit(solution)/shard_map/all_to_all | solution.py:18
  66.4 21.9 %copy-start.103 = (f32[2,64]{1,0:T(2,128)}, f32[2,64]{1,0:T(2,128)S(1)}, u32[]{:S(2)}) copy-start(f32[2,64]{1,0:T(2,128)S(1)} %reshape.2290) | copy-start | bytes 1540
  66.4 24.1 %copy-start.119 = (f32[2,64]{1,0:T(2,128)}, f32[2,64]{1,0:T(2,128)S(1)}, u32[]{:S(2)}) copy-start(f32[2,64]{1,0:T(2,128)S(1)} %reshape.2289) | copy-start | bytes 1540
  95.1 24.2 %all-to-all-start.2 = ((bf16[8,768,128]{2,1,0:T(8,128)(2,1)}), bf16[8,768,128]{2,1,0:T(8,128)(2,1)S(1)}, u32[]{:S(2)}, u32[]{:S(2)}) async-start(bf16[8,768,128]{2,1,0:T(8,128)(2,1)} %bitcast.525), calls=%async_computation.2 | async-start | bytes 3145728 | tf_op jit(solution)/shard_map/all_to_all | solution.py:51
  98.7 67.3 %all-gather.7.cloned.1.call-start = ((), (), s32[]{:S(2)}) async-start(), calls=%async_computation.27 | async-start | bytes 3575808 | tf_op jit(solution)/shard_map/all_gather | solution.py:448
  99.6 20.3 %copy-start.115 = (f32[128]{0:T(128)}, f32[128]{0:T(128)S(1)}, u32[]{:S(2)}) copy-start(f32[128]{0:T(128)S(1)} %reshape.2291) | copy-start | bytes 1540
  121.0 9.9 %all-to-all-start.3 = ((f32[8,1,1536]{2,1,0:T(1,128)}), f32[8,1,1536]{2,1,0:T(1,128)S(1)}, u32[]{:S(2)}, u32[]{:S(2)}) async-start(f32[8,1,1536]{2,1,0:T(1,128)} %broadcast_in_dim.197), calls=%async_computation.3 | async-start | bytes 98304 | tf_op jit(solution)/shard_map/all_to_all | solution.py:18
  132.7 24.3 %all-to-all-start.4 = ((bf16[8,768,128]{1,2,0:T(8,128)(2,1)}), bf16[8,768,128]{1,2,0:T(8,128)(2,1)}, u32[]{:S(2)}, u32[]{:S(2)}) async-start(bf16[8,768,128]{1,2,0:T(8,128)(2,1)} %broadcast_in_dim.198), calls=%async_computation.4 | async-start | bytes 3145728 | tf_op jit(solution)/shard_map/all_to_all | solution.py:18
  162.3 24.2 %all-to-all-start.5 = ((bf16[8,768,128]{2,1,0:T(8,128)(2,1)}), bf16[8,768,128]{2,1,0:T(8,128)(2,1)S(1)}, u32[]{:S(2)}, u32[]{:S(2)}) async-start(bf16[8,768,128]{2,1,0:T(8,128)(2,1)} %bitcast.523), calls=%async_computation.5 | async-start | bytes 3145728 | tf_op jit(solution)/shard_map/all_to_all | solution.py:51
  166.0 21.0 %copy-start.117 = (f32[128]{0:T(128)}, f32[128]{0:T(128)S(1)}, u32[]{:S(2)}) copy-start(f32[128]{0:T(128)S(1)} %reshape.2295) | copy-start | bytes 1540
  186.7 12.6 %copy-start.15 = (f32[768,128]{1,0:T(8,128)}, f32[768,128]{1,0:T(8,128)S(1)}, u32[]{:S(2)}) copy-start(f32[768,128]{1,0:T(8,128)S(1)} %convert_reduce_fusion.6) | copy-start | bytes 1179652
  187.7 9.9 %all-to-all-start.6 = ((f32[8,1,1536]{2,1,0:T(1,128)}), f32[8,1,1536]{2,1,0:T(1,128)S(1)}, u32[]{:S(2)}, u32[]{:S(2)}) async-start(f32[8,1,1536]{2,1,0:T(1,128)} %broadcast_in_dim.199), calls=%async_computation.6 | async-start | bytes 98304 | tf_op jit(solution)/shard_map/all_to_all | solution.py:18
  199.3 23.8 %all-to-all-start.7 = ((bf16[8,768,128]{2,1,0:T(8,128)(2,1)}), bf16[8,768,128]{2,1,0:T(8,128)(2,1)}, u32[]{:S(2)}, u32[]{:S(2)}) async-start(bf16[8,768,128]{2,1,0:T(8,128)(2,1)} %broadcast_in_dim.200), calls=%async_computation.7 | async-start | bytes 3145728 | tf_op jit(solution)/shard_map/all_to_all | solution.py:18
  205.7 19.8 %copy-start.105 = (f32[2,64]{1,0:T(2,128)}, f32[2,64]{1,0:T(2,128)S(1)}, u32[]{:S(2)}) copy-start(f32[2,64]{1,0:T(2,128)S(1)} %reshape.2299) | copy-start | bytes 1540
  205.8 22.0 %copy-start.121 = (f32[2,64]{1,0:T(2,128)}, f32[2,64]{1,0:T(2,128)S(1)}, u32[]{:S(2)}) copy-start(f32[2,64]{1,0:T(2,128)S(1)} %reshape.2298) | copy-start | bytes 1540
  208.6 16.7 %copy-start.46 = (bf16[1024,3,128]{0,2,1:T(8,128)(2,1)}, bf16[1024,3,128]{0,2,1:T(8,128)(2,1)S(1)}, u32[]{:S(2)}) copy-start(bf16[1024,3,128]{0,2,1:T(8,128)(2,1)S(1)} %copy.209) | copy-start | bytes 2359300
  232.3 24.4 %all-to-all-start.8 = ((bf16[8,768,128]{2,1,0:T(8,128)(2,1)}), bf16[8,768,128]{2,1,0:T(8,128)(2,1)S(1)}, u32[]{:S(2)}, u32[]{:S(2)}) async-start(bf16[8,768,128]{2,1,0:T(8,128)(2,1)} %bitcast.521), calls=%async_computation.8 | async-start | bytes 3145728 | tf_op jit(solution)/shard_map/all_to_all | solution.py:51
  257.6 13.1 %copy-start.11 = (f32[768,128]{1,0:T(8,128)}, f32[768,128]{1,0:T(8,128)S(1)}, u32[]{:S(2)}) copy-start(f32[768,128]{1,0:T(8,128)S(1)} %get-tuple-element.190) | copy-start | bytes 1179652
  258.4 9.9 %all-to-all-start.9 = ((f32[8,1,1536]{2,1,0:T(1,128)}), f32[8,1,1536]{2,1,0:T(1,128)S(1)}, u32[]{:S(2)}, u32[]{:S(2)}) async-start(f32[8,1,1536]{2,1,0:T(1,128)} %broadcast_in_dim.201), calls=%async_computation.9 | async-start | bytes 98304 | tf_op jit(solution)/shard_map/all_to_all | solution.py:18
  270.6 23.8 %all-to-all-start.10 = ((bf16[8,768,128]{1,2,0:T(8,128)(2,1)}), bf16[8,768,128]{1,2,0:T(8,128)(2,1)}, u32[]{:S(2)}, u32[]{:S(2)}) async-start(bf16[8,768,128]{1,2,0:T(8,128)(2,1)} %broadcast_in_dim.202), calls=%async_computation.10 | async-start | bytes 3145728 | tf_op jit(solution)/shard_map/all_to_all | solution.py:18
  295.8 24.4 %all-to-all-start.12 = ((bf16[8,768,128]{2,1,0:T(8,128)(2,1)}), bf16[8,768,128]{2,1,0:T(8,128)(2,1)S(1)}, u32[]{:S(2)}, u32[]{:S(2)}) async-start(bf16[8,768,128]{2,1,0:T(8,128)(2,1)} %broadcast_in_dim.203), calls=%async_computation.12 | async-start | bytes 3145728 | tf_op jit(solution)/shard_map/all_to_all | solution.py:18
  326.5 64.4 %slice-start.2 = ((s8[4718592]{0:T(1024)(128)(4,1)}), s8[524288]{0:T(1024)(128)(4,1)S(1)}, s32[]{:S(2)}) async-start(s8[4718592]{0:T(1024)(128)(4,1)} %bitcast.537), calls=%async_computation.30 | async-start | bytes 1048576
  353.9 12.6 %copy-start.3 = (f32[768,128]{1,0:T(8,128)}, f32[768,128]{1,0:T(8,128)S(1)}, u32[]{:S(2)}) copy-start(f32[768,128]{1,0:T(8,128)S(1)} %convert_reduce_fusion.3) | copy-start | bytes 1179652
  363.6 27.4 %slice-start.3 = ((s8[4718592]{0:T(1024)(128)(4,1)}), s8[4194304]{0:T(1024)(128)(4,1)S(1)}, s32[]{:S(2)}) async-start(s8[4718592]{0:T(1024)(128)(4,1)} %bitcast.537), calls=%async_computation.31 | async-start | bytes 8388608
  442.3 18.5 %copy-start.135 = (f32[768,512]{1,0:T(8,128)S(1)}, f32[768,512]{1,0:T(8,128)}, u32[]{:S(2)}) copy-start(f32[768,512]{1,0:T(8,128)} %copy-done.134) | copy-start | bytes 4718596
  467.9 27.2 %all-to-all-start.19 = ((bf16[8,768,128]{2,1,0:T(8,128)(2,1)}), bf16[8,768,128]{2,1,0:T(8,128)(2,1)}, u32[]{:S(2)}, u32[]{:S(2)}) async-start(bf16[8,768,128]{2,1,0:T(8,128)(2,1)} %bitcast.543), calls=%async_computation.19 | async-start | bytes 3145728 | tf_op jit(solution)/shard_map/all_to_all | solution.py:51
  498.2 12.1 %all-to-all-start.20 = ((f32[8,1,1536]{2,1,0:T(1,128)}), f32[8,1,1536]{2,1,0:T(1,128)}, u32[]{:S(2)}, u32[]{:S(2)}) async-start(f32[8,1,1536]{2,1,0:T(1,128)} %broadcast_in_dim.208), calls=%async_computation.20 | async-start | bytes 98304 | tf_op jit(solution)/shard_map/all_to_all | solution.py:18
  516.0 7.6 %copy-start.52 = (bf16[768,1,128]{2,0,1:T(8,128)(2,1)S(1)}, bf16[768,1,128]{2,0,1:T(8,128)(2,1)}, u32[]{:S(2)}) copy-start(bf16[768,1,128]{2,0,1:T(8,128)(2,1)} %copy-done.51) | copy-start | bytes 589828
  516.0 7.6 %copy-start.53 = (bf16[768,1,128]{2,0,1:T(8,128)(2,1)S(1)}, bf16[768,1,128]{2,0,1:T(8,128)(2,1)}, u32[]{:S(2)}) copy-start(bf16[768,1,128]{2,0,1:T(8,128)(2,1)} %copy.223) | copy-start | bytes 589828
  516.0 33.9 %all-to-all-start.21 = ((bf16[8,768,128]{2,1,0:T(8,128)(2,1)}), bf16[8,768,128]{2,1,0:T(8,128)(2,1)}, u32[]{:S(2)}, u32[]{:S(2)}) async-start(bf16[8,768,128]{2,1,0:T(8,128)(2,1)} %broadcast_in_dim.209), calls=%async_computation.21 | async-start | bytes 3145728 | tf_op jit(solution)/shard_map/all_to_all | solution.py:18
  552.0 9.4 %slice-start = ((s8[4718592]{0:T(1024)(128)(4,1)}), s8[4194304]{0:T(1024)(128)(4,1)S(1)}, s32[]{:S(2)}) async-start(s8[4718592]{0:T(1024)(128)(4,1)} %bitcast.535), calls=%async_computation.28 | async-start | bytes 8388608
  570.9 21.9 %all-to-all-start.22 = ((bf16[8,768,128]{2,1,0:T(8,128)(2,1)}), bf16[8,768,128]{2,1,0:T(8,128)(2,1)S(1)}, u32[]{:S(2)}, u32[]{:S(2)}) async-start(bf16[8,768,128]{2,1,0:T(8,128)(2,1)} %bitcast.542), calls=%async_computation.22 | async-start | bytes 3145728 | tf_op jit(solution)/shard_map/all_to_all | solution.py:51
  576.6 124.7 %reduce-scatter.2.cloned.1.call-start = ((), (), s32[]{:S(2)}) async-start(), calls=%async_computation.25 | async-start | bytes 6754304 | tf_op jit(solution)/shard_map/reduce_scatter | solution.py:422
  603.5 30.2 %copy-start.18 = (f32[768,128]{1,0:T(8,128)S(1)}, f32[768,128]{1,0:T(8,128)}, u32[]{:S(2)}) copy-start(f32[768,128]{1,0:T(8,128)} %copy-done.17) | copy-start | bytes 1179652
  603.5 19.6 %all-to-all-start.11 = ((bf16[8,768,128]{2,1,0:T(8,128)(2,1)}), bf16[8,768,128]{2,1,0:T(8,128)(2,1)}, u32[]{:S(2)}, u32[]{:S(2)}) async-start(bf16[8,768,128]{2,1,0:T(8,128)(2,1)} %bitcast.519), calls=%async_computation.11 | async-start | bytes 3145728 | tf_op jit(solution)/shard_map/all_to_all | solution.py:51
  609.3 24.4 %copy-start.4 = (f32[768,128]{1,0:T(8,128)S(1)}, f32[768,128]{1,0:T(8,128)}, u32[]{:S(2)}) copy-start(f32[768,128]{1,0:T(8,128)} %copy-done.3) | copy-start | bytes 1179652
  609.3 24.4 %copy-start.6 = (f32[2,1,768,128]{3,2,1,0:T(8,128)S(1)}, f32[2,1,768,128]{3,2,1,0:T(8,128)}, u32[]{:S(2)}) copy-start(f32[2,1,768,128]{3,2,1,0:T(8,128)} %param.14) | copy-start | bytes 2359300
  609.3 24.4 %copy-start.14 = (f32[768,128]{1,0:T(8,128)S(1)}, f32[768,128]{1,0:T(8,128)}, u32[]{:S(2)}) copy-start(f32[768,128]{1,0:T(8,128)} %copy-done.13) | copy-start | bytes 1179652
  609.3 24.4 %copy-start.16 = (f32[768,128]{1,0:T(8,128)S(1)}, f32[768,128]{1,0:T(8,128)}, u32[]{:S(2)}) copy-start(f32[768,128]{1,0:T(8,128)} %copy-done.15) | copy-start | bytes 1179652
  609.3 24.4 %copy-start.58 = (f32[768]{0:T(1024)S(1)}, f32[768]{0:T(1024)}, u32[]{:S(2)}) copy-start(f32[768]{0:T(1024)} %copy-done.56) | copy-start | bytes 9220
  609.3 24.4 %copy-start.61 = (f32[768]{0:T(1024)S(1)}, f32[768]{0:T(1024)}, u32[]{:S(2)}) copy-start(f32[768]{0:T(1024)} %copy-done.59) | copy-start | bytes 9220
  609.3 24.4 %copy-start.68 = (f32[768]{0:T(1024)S(1)}, f32[768]{0:T(1024)}, u32[]{:S(2)}) copy-start(f32[768]{0:T(1024)} %copy-done.67) | copy-start | bytes 9220
  609.4 24.4 %copy-start.70 = (f32[768]{0:T(1024)S(1)}, f32[768]{0:T(1024)}, u32[]{:S(2)}) copy-start(f32[768]{0:T(1024)} %copy-done.69) | copy-start | bytes 9220
  609.4 24.4 %copy-start.72 = (f32[768]{0:T(1024)S(1)}, f32[768]{0:T(1024)}, u32[]{:S(2)}) copy-start(f32[768]{0:T(1024)} %copy-done.71) | copy-start | bytes 9220
  609.4 24.4 %copy-start.74 = (f32[768]{0:T(1024)S(1)}, f32[768]{0:T(1024)}, u32[]{:S(2)}) copy-start(f32[768]{0:T(1024)} %copy-done.73) | copy-start | bytes 9220
  609.4 24.4 %copy-start.76 = (f32[768]{0:T(1024)S(1)}, f32[768]{0:T(1024)}, u32[]{:S(2)}) copy-start(f32[768]{0:T(1024)} %copy-done.75) | copy-start | bytes 9220
  609.4 24.4 %copy-start.78 = (f32[768]{0:T(1024)S(1)}, f32[768]{0:T(1024)}, u32[]{:S(2)}) copy-start(f32[768]{0:T(1024)} %copy-done.77) | copy-start | bytes 9220
  609.4 24.4 %copy-start.85 = (f32[128]{0:T(128)S(1)}, f32[128]{0:T(128)}, u32[]{:S(2)}) copy-start(f32[128]{0:T(128)} %copy-done.83) | copy-start | bytes 1540
  609.4 24.4 %copy-start.88 = (f32[128]{0:T(128)S(1)}, f32[128]{0:T(128)}, u32[]{:S(2)}) copy-start(f32[128]{0:T(128)} %copy-done.86) | copy-start | bytes 1540
  609.4 24.4 %copy-start.91 = (f32[128]{0:T(128)S(1)}, f32[128]{0:T(128)}, u32[]{:S(2)}) copy-start(f32[128]{0:T(128)} %copy-done.89) | copy-start | bytes 1540
  609.4 24.4 %copy-start.93 = (f32[128]{0:T(128)S(1)}, f32[128]{0:T(128)}, u32[]{:S(2)}) copy-start(f32[128]{0:T(128)} %reshape.2300) | copy-start | bytes 1540
  609.4 24.4 %copy-start.116 = (f32[128]{0:T(128)S(1)}, f32[128]{0:T(128)}, u32[]{:S(2)}) copy-start(f32[128]{0:T(128)} %copy-done.115) | copy-start | bytes 1540
  609.5 24.4 %copy-start.118 = (f32[128]{0:T(128)S(1)}, f32[128]{0:T(128)}, u32[]{:S(2)}) copy-start(f32[128]{0:T(128)} %copy-done.117) | copy-start | bytes 1540
  623.7 9.9 %all-to-all-start.23 = ((f32[8,1,1536]{2,1,0:T(1,128)}), f32[8,1,1536]{2,1,0:T(1,128)S(1)}, u32[]{:S(2)}, u32[]{:S(2)}) async-start(f32[8,1,1536]{2,1,0:T(1,128)} %broadcast_in_dim.210), calls=%async_computation.23 | async-start | bytes 98304 | tf_op jit(solution)/shard_map/all_to_all | solution.py:18
  633.9 12.5 %copy-start.24 = (f32[2,1,768,128]{3,2,1,0:T(8,128)S(1)}, f32[2,1,768,128]{3,2,1,0:T(8,128)}, u32[]{:S(2)}) copy-start(f32[2,1,768,128]{3,2,1,0:T(8,128)} %param.15) | copy-start | bytes 2359300
  637.5 22.1 %collective-permute-start.3 = (f32[1,768,128]{2,1,0:T(8,128)S(1)}, f32[1,768,128]{2,1,0:T(8,128)S(1)}, u32[]{:S(2)}, u32[]{:S(2)}) collective-permute-start(f32[1,768,128]{2,1,0:T(8,128)S(1)} %get-tuple-element.187), channel_id=1, source_target_pairs={{64,0},{65,1},{66,2},{67,3},{68,4},{69,5},{70,6},{71,7},{72,8},{73... | collective-permute-start | bytes 1179656 | tf_op jit(solution)/shard_map/ppermute | solution.py:501
  638.8 23.7 %collective-permute-start.4 = (f32[1,768,128]{2,1,0:T(8,128)S(1)}, f32[1,768,128]{2,1,0:T(8,128)S(1)}, u32[]{:S(2)}, u32[]{:S(2)}) collective-permute-start(f32[1,768,128]{2,1,0:T(8,128)S(1)} %get-tuple-element.188), channel_id=1, source_target_pairs={{0,64},{1,65},{2,66},{3,67},{4,68},{5,69},{6,70},{7,71},{8,72},{9,... | collective-permute-start | bytes 1179656 | tf_op jit(solution)/shard_map/ppermute | solution.py:499
  645.0 21.8 %collective-permute-start.1 = (f32[1,768,128]{2,1,0:T(8,128)S(1)}, f32[1,768,128]{2,1,0:T(8,128)S(1)}, u32[]{:S(2)}, u32[]{:S(2)}) collective-permute-start(f32[1,768,128]{2,1,0:T(8,128)S(1)} %get-tuple-element.189), channel_id=1, source_target_pairs={{64,0},{65,1},{66,2},{67,3},{68,4},{69,5},{70,6},{71,7},{72,8},{73... | collective-permute-start | bytes 1179656 | tf_op jit(solution)/shard_map/ppermute | solution.py:496
  649.9 16.9 %collective-permute-start.2 = (f32[1,768,128]{2,1,0:T(8,128)S(1)}, f32[1,768,128]{2,1,0:T(8,128)S(1)}, u32[]{:S(2)}, u32[]{:S(2)}) collective-permute-start(f32[1,768,128]{2,1,0:T(8,128)S(1)} %fusion.88), channel_id=1, source_target_pairs={{0,64},{1,65},{2,66},{3,67},{4,68},{5,69},{6,70},{7,71},{8,72},{9,... | collective-permute-start | bytes 1179656 | tf_op jit(solution)/shard_map/ppermute | solution.py:497
  (101 other events, 268.6 us)
Sparse Core Ops, SparseCore 0:
  26.2 30.4 all-gather.4
  101.8 27.8 all-gather.6
  596.8 104.4 reduce-scatter.1

commit v8 on v7

--- a/solution.py
+++ b/solution.py
@@ -409,7 +409,16 @@
     return [parts[i] for i in range(len(shapes))]
 
 
-def sum_at_end(grads_zero, grads_last, dims):
+def reduce_blocks(blocks):
+    big, small = split_by_size(blocks)
+    rows = in_rows(blocks, big, small)
+    total = lax.psum_scatter(
+        rows.reshape(-1, 128), ("section", "dp"), scatter_dimension=0, tiled=True
+    )
+    return [part[0] for part in out_of_rows(total[None], [b.shape[1:] for b in blocks], big, small)]
+
+
+def sum_at_end(grads_zero, grads_last, dims, late):
     peers = lax.axis_size("dp")
     blocks = [
         jnp.concatenate(
@@ -417,16 +426,12 @@
         )
         for g0, g1, d in zip(grads_zero, grads_last, dims)
     ]
-    big, small = split_by_size(blocks)
-    rows = in_rows(blocks, big, small)
-    total = lax.psum_scatter(
-        rows.reshape(-1, 128), ("section", "dp"), scatter_dimension=0, tiled=True
-    )
-    shapes = [block.shape[1:] for block in blocks]
-    parts = out_of_rows(total[None], shapes, big, small)
+    early = [i for i in range(len(blocks)) if i not in late]
+    parts = dict(zip(early, reduce_blocks([blocks[i] for i in early])))
+    parts.update(zip(late, reduce_blocks([blocks[i] for i in late])))
     return tuple(
-        from_blocks(part[0].astype(jnp.float32), g.shape, d, peers)[None]
-        for part, g, d in zip(parts, grads_zero, dims)
+        from_blocks(parts[i].astype(jnp.float32), g.shape, d, peers)[None]
+        for i, (g, d) in enumerate(zip(grads_zero, dims))
     )
 
 
@@ -499,7 +504,7 @@
     other_middle_grad = lax.ppermute(middle_grad, "section", [(0, 1)])
     input_grad, grads_zero = layer_backward(middle_grad, kept_zero, weights_zero)
     other_input_grad = lax.ppermute(input_grad, "section", [(1, 0)])
-    reduced = sum_at_end(grads_zero, grads_last, dims)
+    reduced = sum_at_end(grads_zero, grads_last, dims, (0, 1, 8, 9))
     section_outputs = jnp.where(
         is_first, jnp.stack([middle, other_middle]), jnp.stack([other_final, final])
     )[None]

time: 727 us -> 767 us (1.055)
  blocking collectives: 117 us -> 144 us
  waiting for transfers between devices: 233 us -> 249 us
  local copies, waits for them, and re-layouts: 113 us -> 100 us
  other arithmetic: 66 us -> 77.1 us
    concatenate x0 -> x2, other arithmetic: none -> 21.1 us  [in_rows(): return jnp.concatenate(rows, axis=1)]
    reduce_scatter x1 -> x2, waiting for transfers between devices: 33.6 us -> 50.9 us  [reduce_blocks(): lax.psum_scatter(rows.reshape(-1, 128), ('section', 'dp'), scatter_dimens...]
    all_to_all x2 -> x3, blocking collectives: 46.5 us -> 63.5 us  [summed_on_arrival(): lax.all_to_all(parts, axis, split_axis=0, concat_axis=0, tiled=True)]
    all_to_all x5 -> x6, blocking collectives: 70.6 us -> 80 us  [sent_to_all(): return lax.all_to_all(copies, axis, split_axis=0, concat_axis=0, tiled=True)]
    all_to_all x11 -> x10, starting transfers between devices: 47.7 us -> 55 us  [sent_to_all(): return lax.all_to_all(copies, axis, split_axis=0, concat_axis=0, tiled=True)]
    all_to_all x6 -> x5, starting transfers between devices: 27.2 us -> 21.8 us  [summed_on_arrival(): lax.all_to_all(parts, axis, split_axis=0, concat_axis=0, tiled=True)]
    all_to_all x11 -> x10, waiting for transfers between devices: 89.7 us -> 93.3 us  [sent_to_all(): return lax.all_to_all(copies, axis, split_axis=0, concat_axis=0, tiled=True)]
    unnamed x296 -> x276, local copies, waits for them, and re-layouts: 19.1 us -> 18 us
  transfers between devices with their start and end apart: 25 -> 24, of which waited for: 20 -> 18; matrix products, arithmetic and copies ran while one was open for 19% -> 18% of each run, Pallas kernels for 0% -> 0%
where the time goes in v8:
time: 767 us; the launch traced here: 762 us
  waiting for transfers between devices  249 us (32%)
  blocking collectives  144 us (19%)
  local copies, waits for them, and re-layouts  100 us (13%)
  starting transfers between devices  95.4 us (12%)
  matrix products  80 us (10%)
  other arithmetic  77.1 us (10%)
  between operations  16.3 us (2%)
    all_to_all x10, waiting for transfers between devices, sent_to_all(): return lax.all_to_all(copies, axis, split_axis=0, concat_axis=0, tiled=True)  93.3 us
    all_to_all x6, blocking collectives, sent_to_all(): return lax.all_to_all(copies, axis, split_axis=0, concat_axis=0, tiled=True)  80 us
    all_to_all x5, waiting for transfers between devices, summed_on_arrival(): lax.all_to_all(parts, axis, split_axis=0, concat_axis=0, tiled=True)  73.4 us
    all_to_all x3, blocking collectives, summed_on_arrival(): lax.all_to_all(parts, axis, split_axis=0, concat_axis=0, tiled=True)  63.5 us
    all_to_all x10, starting transfers between devices, sent_to_all(): return lax.all_to_all(copies, axis, split_axis=0, concat_axis=0, tiled=True)  55 us
    reduce_scatter x2, waiting for transfers between devices, reduce_blocks(): lax.psum_scatter(rows.reshape(-1, 128), ('section', 'dp'), scatter_dimens...  50.9 us
    all_to_all x5, starting transfers between devices, summed_on_arrival(): lax.all_to_all(parts, axis, split_axis=0, concat_axis=0, tiled=True)  21.8 us
    concatenate x2, other arithmetic, in_rows(): return jnp.concatenate(rows, axis=1)  21.1 us
  transfers between devices with their start and end apart: 24, of which 18 were waited for; matrix products, arithmetic and copies ran while one was open for 18% of the time, Pallas kernels for 0%

profile of v8, /device:TPU:0, one launch (start us, length us, event | category | flops | bytes accessed | tf_op | source)
XLA Modules:
  0.0 761.9 jit_solution(2843238061951891495)
XLA Ops:
  12.8 3.2 collective-permute-start
  16.0 9.2 %collective-permute-done = bf16[1552,128]{1,0:T(8,128)(2,1)S(1)} collective-permute-done((bf16[1552,128]{1,0:T(8,128)(2,1)S(1)}, bf16[1552,128]{1,0:T(8,128)(2,1)S(1)}, u32[]{:S(2)}, u32[]{:S(2)}) %collective-permute-start) | collective-permute-done | bytes 397344 | tf_op jit(solution)/shard_map/ppermute | solution.py:451
  26.6 12.6 %all_to_all.128 = f32[8,1,1536]{2,1,0:T(1,128)S(1)} all-to-all(f32[8,1,1536]{2,1,0:T(1,128)S(1)} %broadcast_in_dim.198), channel_id=1, replica_groups=mesh['section'=2,'dp'=8,'tensor'=8] {'tensor'}, dimensions={0} | all-to-all | bytes 98304 | tf_op jit(solution)/shard_map/all_to_all | solution.py:18
  39.2 17.6 %all-gather.5.cloned.1.call-done = bf16[12416,128]{1,0:T(8,128)(2,1)} async-done(((bf16[1552,128]{1,0:T(8,128)(2,1)}), bf16[12416,128]{1,0:T(8,128)(2,1)}) %all-gather.5.cloned.1.call-update) | async-done | bytes 3178512 | tf_op jit(solution)/shard_map/all_gather | solution.py:452
  59.5 5.3 all-to-all-start.1
  70.0 15.7 %all-to-all-done.1 = bf16[8,768,128]{2,1,0:T(8,128)(2,1)} async-done(((bf16[8,768,128]{2,1,0:T(8,128)(2,1)}), bf16[8,768,128]{2,1,0:T(8,128)(2,1)}, u32[]{:S(2)}, u32[]{:S(2)}) %all-to-all-start.1) | async-done | bytes 1572896 | tf_op jit(solution)/shard_map/all_to_all | solution.py:18
  95.1 3.6 all-to-all-start.2
  99.5 19.8 %all-to-all-done.2 = bf16[8,768,128]{2,1,0:T(8,128)(2,1)S(1)} async-done(((bf16[8,768,128]{2,1,0:T(8,128)(2,1)}), bf16[8,768,128]{2,1,0:T(8,128)(2,1)S(1)}, u32[]{:S(2)}, u32[]{:S(2)}) %all-to-all-start.2) | async-done | bytes 1572896 | tf_op jit(solution)/shard_map/all_to_all | solution.py:51
  121.0 3.6 all-to-all-start.3
  124.8 6.1 all-to-all-done.3
  132.7 4.6 all-to-all-start.4
  138.1 2.7 fusion.140
  144.6 12.2 %all-to-all-done.4 = bf16[8,768,128]{1,2,0:T(8,128)(2,1)} async-done(((bf16[8,768,128]{1,2,0:T(8,128)(2,1)}), bf16[8,768,128]{1,2,0:T(8,128)(2,1)}, u32[]{:S(2)}, u32[]{:S(2)}) %all-to-all-start.4) | async-done | bytes 1572896 | tf_op jit(solution)/shard_map/all_to_all | solution.py:18
  156.8 2.8 convolution_add_fusion.1
  162.2 3.6 all-to-all-start.5
  166.7 19.7 %all-to-all-done.5 = bf16[8,768,128]{2,1,0:T(8,128)(2,1)S(1)} async-done(((bf16[8,768,128]{2,1,0:T(8,128)(2,1)}), bf16[8,768,128]{2,1,0:T(8,128)(2,1)S(1)}, u32[]{:S(2)}, u32[]{:S(2)}) %all-to-all-start.5) | async-done | bytes 1572896 | tf_op jit(solution)/shard_map/all_to_all | solution.py:51
  187.6 3.6 all-to-all-start.6
  192.1 5.5 all-to-all-done.6
  199.3 4.3 all-to-all-start.7
  210.9 12.2 %all-to-all-done.7 = bf16[8,768,128]{2,1,0:T(8,128)(2,1)} async-done(((bf16[8,768,128]{2,1,0:T(8,128)(2,1)}), bf16[8,768,128]{2,1,0:T(8,128)(2,1)}, u32[]{:S(2)}, u32[]{:S(2)}) %all-to-all-start.7) | async-done | bytes 1572896 | tf_op jit(solution)/shard_map/all_to_all | solution.py:18
  232.5 4.3 all-to-all-start.8
  236.8 20.4 %all-to-all-done.8 = bf16[8,768,128]{2,1,0:T(8,128)(2,1)} async-done(((bf16[8,768,128]{2,1,0:T(8,128)(2,1)}), bf16[8,768,128]{2,1,0:T(8,128)(2,1)}, u32[]{:S(2)}, u32[]{:S(2)}) %all-to-all-start.8) | async-done | bytes 1572896 | tf_op jit(solution)/shard_map/all_to_all | solution.py:51
  259.9 3.6 all-to-all-start.9
  263.7 6.1 all-to-all-done.9
  271.6 17.1 %all-to-all-start.10 = ((bf16[8,768,128]{1,2,0:T(8,128)(2,1)}), bf16[8,768,128]{1,2,0:T(8,128)(2,1)}, u32[]{:S(2)}, u32[]{:S(2)}) async-start(bf16[8,768,128]{1,2,0:T(8,128)(2,1)} %broadcast_in_dim.208), calls=%async_computation.10 | async-start | bytes 3145728 | tf_op jit(solution)/shard_map/all_to_all | solution.py:18
  289.8 18.5 %all-to-all-done.10 = bf16[8,768,128]{1,2,0:T(8,128)(2,1)} async-done(((bf16[8,768,128]{1,2,0:T(8,128)(2,1)}), bf16[8,768,128]{1,2,0:T(8,128)(2,1)}, u32[]{:S(2)}, u32[]{:S(2)}) %all-to-all-start.10) | async-done | bytes 1572896 | tf_op jit(solution)/shard_map/all_to_all | solution.py:18
  309.7 4.3 all-to-all-start.12
  314.8 3.1 slice_bitcast_fusion
  320.4 3.9 convolution_add_fusion
  324.3 10.2 %all-to-all-done.12 = bf16[8,768,128]{2,1,0:T(8,128)(2,1)} async-done(((bf16[8,768,128]{2,1,0:T(8,128)(2,1)}), bf16[8,768,128]{2,1,0:T(8,128)(2,1)}, u32[]{:S(2)}, u32[]{:S(2)}) %all-to-all-start.12) | async-done | bytes 1572896 | tf_op jit(solution)/shard_map/all_to_all | solution.py:18
  334.5 5.0 fusion.143
  340.8 25.2 %all_to_all.129 = bf16[8,768,128]{2,1,0:T(8,128)(2,1)S(1)} all-to-all(bf16[8,768,128]{2,1,0:T(8,128)(2,1)S(1)} %bitcast.554), channel_id=1, replica_groups=mesh['section'=2,'dp'=8,'tensor'=8] {'tensor'}, dimensions={0} | all-to-all | bytes 3145728 | tf_op jit(solution)/shard_map/all_to_all | solution.py:51
  368.7 9.4 %all_to_all.130 = f32[8,1,1536]{2,1,0:T(1,128)} all-to-all(f32[8,1,1536]{2,1,0:T(1,128)S(1)} %broadcast_in_dim.210), channel_id=1, replica_groups=mesh['section'=2,'dp'=8,'tensor'=8] {'tensor'}, dimensions={0} | all-to-all | bytes 98304 | tf_op jit(solution)/shard_map/all_to_all | solution.py:18
  382.2 21.2 %all_to_all.131 = bf16[8,768,128]{2,1,0:T(8,128)(2,1)S(1)} all-to-all(bf16[8,768,128]{2,1,0:T(8,128)(2,1)S(1)} %broadcast_in_dim.211), channel_id=1, replica_groups=mesh['section'=2,'dp'=8,'tensor'=8] {'tensor'}, dimensions={0} | all-to-all | bytes 3145728 | tf_op jit(solution)/shard_map/all_to_all | solution.py:18
  417.1 20.0 %all_to_all.132 = bf16[8,768,128]{2,1,0:T(8,128)(2,1)S(1)} all-to-all(bf16[8,768,128]{2,1,0:T(8,128)(2,1)S(1)} %bitcast.555), channel_id=1, replica_groups=mesh['section'=2,'dp'=8,'tensor'=8] {'tensor'}, dimensions={0} | all-to-all | bytes 3145728 | tf_op jit(solution)/shard_map/all_to_all | solution.py:51
  439.8 8.9 %all_to_all.133 = f32[8,1,1536]{2,1,0:T(1,128)S(1)} all-to-all(f32[8,1,1536]{2,1,0:T(1,128)S(1)} %broadcast_in_dim.212), channel_id=1, replica_groups=mesh['section'=2,'dp'=8,'tensor'=8] {'tensor'}, dimensions={0} | all-to-all | bytes 98304 | tf_op jit(solution)/shard_map/all_to_all | solution.py:18
  450.8 18.5 %all_to_all.134 = bf16[8,768,128]{2,1,0:T(8,128)(2,1)S(1)} all-to-all(bf16[8,768,128]{2,1,0:T(8,128)(2,1)S(1)} %broadcast_in_dim.213), channel_id=1, replica_groups=mesh['section'=2,'dp'=8,'tensor'=8] {'tensor'}, dimensions={0} | all-to-all | bytes 3145728 | tf_op jit(solution)/shard_map/all_to_all | solution.py:18
  469.4 4.5 fusion.144
  475.2 18.3 %all_to_all.135 = bf16[8,768,128]{2,1,0:T(8,128)(2,1)S(1)} all-to-all(bf16[8,768,128]{2,1,0:T(8,128)(2,1)S(1)} %bitcast.556), channel_id=1, replica_groups=mesh['section'=2,'dp'=8,'tensor'=8] {'tensor'}, dimensions={0} | all-to-all | bytes 3145728 | tf_op jit(solution)/shard_map/all_to_all | solution.py:51
  496.5 9.4 %all_to_all.136 = f32[8,1,1536]{2,1,0:T(1,128)} all-to-all(f32[8,1,1536]{2,1,0:T(1,128)S(1)} %broadcast_in_dim.214), channel_id=1, replica_groups=mesh['section'=2,'dp'=8,'tensor'=8] {'tensor'}, dimensions={0} | all-to-all | bytes 98304 | tf_op jit(solution)/shard_map/all_to_all | solution.py:18
  511.6 4.3 all-to-all-start.21
  520.3 3.6 convolution_convert_fusion.8
  526.5 2.9 all-to-all-done.21
  531.4 5.2 bitcast_reduce_fusion
  536.6 4.2 multiply_reduce_fusion
  548.6 4.3 all-to-all-start.22
  553.1 3.1 fusion.43
  560.0 2.7 copy.288
  569.3 3.2 concatenate.141
  579.4 3.2 concatenate.140
  591.5 3.6 convolution_convert_fusion.9
  600.3 3.1 fusion.42
  610.1 18.4 %pad_maximum_fusion = bf16[16,1168,128]{2,1,0:T(8,128)(2,1)} fusion(bf16[16,16,128]{2,1,0:T(8,128)(2,1)S(1)} %bitcast.618, bf16[8,512,128]{2,1,0:T(8,128)(2,1)S(1)} %bitcast.559, bf16[8,512,128]{2,1,0:T(8,128)(2,1)S(1)} %bitcast.560, bf16[8,512,128]{2,1,0:T(8,128)(2,1)S(1)} %copy-done.16, bf16[8,512,128]{2,1,0:T(8,128)(2,1)S(1)} %copy-done.18, ...), kind=kLoop, calls=%fused_computation | loop fusion | flops 28704768 | bytes 9568256 | tf_op jit(solution)/shard_map/concatenate | solution.py:393
  631.0 2.8 fusion.33
  635.4 6.0 all-to-all-start.11
  641.7 13.5 %all-to-all-done.11 = bf16[8,768,128]{2,1,0:T(8,128)(2,1)} async-done(((bf16[8,768,128]{2,1,0:T(8,128)(2,1)}), bf16[8,768,128]{2,1,0:T(8,128)(2,1)}, u32[]{:S(2)}, u32[]{:S(2)}) %all-to-all-start.11) | async-done | bytes 1572896 | tf_op jit(solution)/shard_map/all_to_all | solution.py:51
  655.8 4.2 all-to-all-start.23
  662.4 4.0 all-to-all-done.23
  666.7 3.6 fusion.55
  671.5 6.1 collective-permute-start.4
  679.1 3.4 fusion.72
  682.6 6.1 collective-permute-start.2
  689.8 4.2 collective-permute-done.2
  698.5 50.9 %reduce-scatter.5.cloned.1.call-done = bf16[1168,128]{1,0:T(8,128)(2,1)} async-done(((bf16[18688,128]{1,0:T(8,128)(2,1)}), bf16[1168,128]{1,0:T(8,128)(2,1)}) %reduce-scatter.5.cloned.1.call-update) | async-done | bytes 299024 | tf_op jit(solution)/shard_map/reduce_scatter | solution.py:415
  (528 shorter events, 179.2 us)
Async XLA Ops:
  7.2 49.6 %all-gather.5.cloned.1.call-start = ((), (), s32[]{:S(2)}) async-start(), calls=%async_computation.28 | async-start | bytes 3575808 | tf_op jit(solution)/shard_map/all_gather | solution.py:452
  9.0 17.1 %copy-start.6 = (f32[2,1,768,128]{3,2,1,0:T(8,128)S(1)}, f32[2,1,768,128]{3,2,1,0:T(8,128)}, u32[]{:S(2)}) copy-start(f32[2,1,768,128]{3,2,1,0:T(8,128)} %param.14) | copy-start | bytes 2359300
  12.8 12.4 %collective-permute-start = (bf16[1552,128]{1,0:T(8,128)(2,1)S(1)}, bf16[1552,128]{1,0:T(8,128)(2,1)S(1)}, u32[]{:S(2)}, u32[]{:S(2)}) collective-permute-start(bf16[1552,128]{1,0:T(8,128)(2,1)S(1)} %bitcast.610), channel_id=1, source_target_pairs={{0,64},{64,0},{1,65},{65,1},{2,66},{66,2},{3,67},{67,3},{4,68},{68... | collective-permute-start | bytes 1191944 | tf_op jit(solution)/shard_map/ppermute | solution.py:451
  39.2 20.3 %copy-start.60 = (f32[768]{0:T(1024)}, f32[768]{0:T(1024)S(1)}, u32[]{:S(2)}) copy-start(f32[768]{0:T(1024)S(1)} %get-tuple-element.251) | copy-start | bytes 9220
  39.2 20.3 %copy-start.62 = (f32[768]{0:T(1024)}, f32[768]{0:T(1024)S(1)}, u32[]{:S(2)}) copy-start(f32[768]{0:T(1024)S(1)} %get-tuple-element.252) | copy-start | bytes 9220
  59.5 26.3 %all-to-all-start.1 = ((bf16[8,768,128]{2,1,0:T(8,128)(2,1)}), bf16[8,768,128]{2,1,0:T(8,128)(2,1)}, u32[]{:S(2)}, u32[]{:S(2)}) async-start(bf16[8,768,128]{2,1,0:T(8,128)(2,1)} %broadcast_in_dim.200), calls=%async_computation.1 | async-start | bytes 3145728 | tf_op jit(solution)/shard_map/all_to_all | solution.py:18
  66.4 21.9 %copy-start.96 = (f32[2,64]{1,0:T(2,128)}, f32[2,64]{1,0:T(2,128)S(1)}, u32[]{:S(2)}) copy-start(f32[2,64]{1,0:T(2,128)S(1)} %reshape.2302) | copy-start | bytes 1540
  66.5 24.1 %copy-start.105 = (f32[2,64]{1,0:T(2,128)}, f32[2,64]{1,0:T(2,128)S(1)}, u32[]{:S(2)}) copy-start(f32[2,64]{1,0:T(2,128)S(1)} %reshape.2301) | copy-start | bytes 1540
  95.1 24.2 %all-to-all-start.2 = ((bf16[8,768,128]{2,1,0:T(8,128)(2,1)}), bf16[8,768,128]{2,1,0:T(8,128)(2,1)S(1)}, u32[]{:S(2)}, u32[]{:S(2)}) async-start(bf16[8,768,128]{2,1,0:T(8,128)(2,1)} %bitcast.533), calls=%async_computation.2 | async-start | bytes 3145728 | tf_op jit(solution)/shard_map/all_to_all | solution.py:51
  98.7 67.2 %all-gather.7.cloned.1.call-start = ((), (), s32[]{:S(2)}) async-start(), calls=%async_computation.29 | async-start | bytes 3575808 | tf_op jit(solution)/shard_map/all_gather | solution.py:453
  99.5 20.3 %copy-start.101 = (f32[128]{0:T(128)}, f32[128]{0:T(128)S(1)}, u32[]{:S(2)}) copy-start(f32[128]{0:T(128)S(1)} %reshape.2303) | copy-start | bytes 1540
  121.0 9.9 %all-to-all-start.3 = ((f32[8,1,1536]{2,1,0:T(1,128)}), f32[8,1,1536]{2,1,0:T(1,128)S(1)}, u32[]{:S(2)}, u32[]{:S(2)}) async-start(f32[8,1,1536]{2,1,0:T(1,128)} %broadcast_in_dim.203), calls=%async_computation.3 | async-start | bytes 98304 | tf_op jit(solution)/shard_map/all_to_all | solution.py:18
  132.7 24.1 %all-to-all-start.4 = ((bf16[8,768,128]{1,2,0:T(8,128)(2,1)}), bf16[8,768,128]{1,2,0:T(8,128)(2,1)}, u32[]{:S(2)}, u32[]{:S(2)}) async-start(bf16[8,768,128]{1,2,0:T(8,128)(2,1)} %broadcast_in_dim.204), calls=%async_computation.4 | async-start | bytes 3145728 | tf_op jit(solution)/shard_map/all_to_all | solution.py:18
  162.2 24.2 %all-to-all-start.5 = ((bf16[8,768,128]{2,1,0:T(8,128)(2,1)}), bf16[8,768,128]{2,1,0:T(8,128)(2,1)S(1)}, u32[]{:S(2)}, u32[]{:S(2)}) async-start(bf16[8,768,128]{2,1,0:T(8,128)(2,1)} %bitcast.531), calls=%async_computation.5 | async-start | bytes 3145728 | tf_op jit(solution)/shard_map/all_to_all | solution.py:51
  165.9 21.0 %copy-start.103 = (f32[128]{0:T(128)}, f32[128]{0:T(128)S(1)}, u32[]{:S(2)}) copy-start(f32[128]{0:T(128)S(1)} %reshape.2307) | copy-start | bytes 1540
  166.7 36.9 %copy-start.64 = (bf16[1,8,16,128]{3,1,2,0:T(8,128)(2,1)}, bf16[1,8,16,128]{3,1,2,0:T(8,128)(2,1)S(1)}, u32[]{:S(2)}) copy-start(bf16[1,8,16,128]{3,1,2,0:T(8,128)(2,1)S(1)} %copy.393) | copy-start | bytes 98308
  186.6 12.7 %copy-start.12 = (f32[768,128]{1,0:T(8,128)}, f32[768,128]{1,0:T(8,128)S(1)}, u32[]{:S(2)}) copy-start(f32[768,128]{1,0:T(8,128)S(1)} %convert_reduce_fusion.6) | copy-start | bytes 1179652
  187.6 9.9 %all-to-all-start.6 = ((f32[8,1,1536]{2,1,0:T(1,128)}), f32[8,1,1536]{2,1,0:T(1,128)S(1)}, u32[]{:S(2)}, u32[]{:S(2)}) async-start(f32[8,1,1536]{2,1,0:T(1,128)} %broadcast_in_dim.205), calls=%async_computation.6 | async-start | bytes 98304 | tf_op jit(solution)/shard_map/all_to_all | solution.py:18
  199.3 23.8 %all-to-all-start.7 = ((bf16[8,768,128]{2,1,0:T(8,128)(2,1)}), bf16[8,768,128]{2,1,0:T(8,128)(2,1)}, u32[]{:S(2)}, u32[]{:S(2)}) async-start(bf16[8,768,128]{2,1,0:T(8,128)(2,1)} %broadcast_in_dim.206), calls=%async_computation.7 | async-start | bytes 3145728 | tf_op jit(solution)/shard_map/all_to_all | solution.py:18
  205.9 19.7 %copy-start.98 = (f32[2,64]{1,0:T(2,128)}, f32[2,64]{1,0:T(2,128)S(1)}, u32[]{:S(2)}) copy-start(f32[2,64]{1,0:T(2,128)S(1)} %reshape.2311) | copy-start | bytes 1540
  205.9 21.9 %copy-start.107 = (f32[2,64]{1,0:T(2,128)}, f32[2,64]{1,0:T(2,128)S(1)}, u32[]{:S(2)}) copy-start(f32[2,64]{1,0:T(2,128)S(1)} %reshape.2310) | copy-start | bytes 1540
  232.5 24.8 %all-to-all-start.8 = ((bf16[8,768,128]{2,1,0:T(8,128)(2,1)}), bf16[8,768,128]{2,1,0:T(8,128)(2,1)}, u32[]{:S(2)}, u32[]{:S(2)}) async-start(bf16[8,768,128]{2,1,0:T(8,128)(2,1)} %bitcast.553), calls=%async_computation.8 | async-start | bytes 3145728 | tf_op jit(solution)/shard_map/all_to_all | solution.py:51
  236.8 22.4 %copy-start.91 = (f32[128]{0:T(128)}, f32[128]{0:T(128)S(1)}, u32[]{:S(2)}) copy-start(f32[128]{0:T(128)S(1)} %reshape.2312) | copy-start | bytes 1540
  259.9 9.9 %all-to-all-start.9 = ((f32[8,1,1536]{2,1,0:T(1,128)}), f32[8,1,1536]{2,1,0:T(1,128)S(1)}, u32[]{:S(2)}, u32[]{:S(2)}) async-start(f32[8,1,1536]{2,1,0:T(1,128)} %broadcast_in_dim.207), calls=%async_computation.9 | async-start | bytes 98304 | tf_op jit(solution)/shard_map/all_to_all | solution.py:18
  269.9 109.1 %copy-start.56 = (f32[768]{0:T(1024)}, f32[768]{0:T(1024)S(1)}, u32[]{:S(2)}) copy-start(f32[768]{0:T(1024)S(1)} %get-tuple-element.245) | copy-start | bytes 9220
  269.9 109.1 %copy-start.58 = (f32[768]{0:T(1024)}, f32[768]{0:T(1024)S(1)}, u32[]{:S(2)}) copy-start(f32[768]{0:T(1024)S(1)} %get-tuple-element.246) | copy-start | bytes 9220
  271.6 36.6 %all-to-all-start.10 = ((bf16[8,768,128]{1,2,0:T(8,128)(2,1)}), bf16[8,768,128]{1,2,0:T(8,128)(2,1)}, u32[]{:S(2)}, u32[]{:S(2)}) async-start(bf16[8,768,128]{1,2,0:T(8,128)(2,1)} %broadcast_in_dim.208), calls=%async_computation.10 | async-start | bytes 3145728 | tf_op jit(solution)/shard_map/all_to_all | solution.py:18
  309.7 24.8 %all-to-all-start.12 = ((bf16[8,768,128]{2,1,0:T(8,128)(2,1)}), bf16[8,768,128]{2,1,0:T(8,128)(2,1)}, u32[]{:S(2)}, u32[]{:S(2)}) async-start(bf16[8,768,128]{2,1,0:T(8,128)(2,1)} %broadcast_in_dim.209), calls=%async_computation.12 | async-start | bytes 3145728 | tf_op jit(solution)/shard_map/all_to_all | solution.py:18
  340.8 65.4 %slice-start.2 = ((s8[4718592]{0:T(1024)(128)(4,1)}), s8[524288]{0:T(1024)(128)(4,1)S(1)}, s32[]{:S(2)}) async-start(s8[4718592]{0:T(1024)(128)(4,1)} %bitcast.546), calls=%async_computation.32 | async-start | bytes 1048576
  379.0 27.2 %slice-start.3 = ((s8[4718592]{0:T(1024)(128)(4,1)}), s8[4194304]{0:T(1024)(128)(4,1)S(1)}, s32[]{:S(2)}) async-start(s8[4718592]{0:T(1024)(128)(4,1)} %bitcast.546), calls=%async_computation.33 | async-start | bytes 8388608
  438.3 10.5 %copy-start.23 = (f32[768,128]{1,0:T(8,128)S(1)}, f32[768,128]{1,0:T(8,128)}, u32[]{:S(2)}) copy-start(f32[768,128]{1,0:T(8,128)} %copy-done.22) | copy-start | bytes 1179652
  439.0 11.7 %copy-start.4 = (f32[768,128]{1,0:T(8,128)}, f32[768,128]{1,0:T(8,128)S(1)}, u32[]{:S(2)}) copy-start(f32[768,128]{1,0:T(8,128)S(1)} %convert_reduce_fusion.2) | copy-start | bytes 1179652
  450.8 18.6 %copy-start.124 = (f32[768,512]{1,0:T(8,128)S(1)}, f32[768,512]{1,0:T(8,128)}, u32[]{:S(2)}) copy-start(f32[768,512]{1,0:T(8,128)} %copy-done.123) | copy-start | bytes 4718596
  511.6 17.7 %all-to-all-start.21 = ((bf16[8,768,128]{2,1,0:T(8,128)(2,1)}), bf16[8,768,128]{2,1,0:T(8,128)(2,1)}, u32[]{:S(2)}, u32[]{:S(2)}) async-start(bf16[8,768,128]{2,1,0:T(8,128)(2,1)} %broadcast_in_dim.215), calls=%async_computation.21 | async-start | bytes 3145728 | tf_op jit(solution)/shard_map/all_to_all | solution.py:18
  531.4 9.4 %slice-start = ((s8[4718592]{0:T(1024)(128)(4,1)}), s8[4194304]{0:T(1024)(128)(4,1)S(1)}, s32[]{:S(2)}) async-start(s8[4718592]{0:T(1024)(128)(4,1)} %bitcast.544), calls=%async_computation.30 | async-start | bytes 8388608
  548.6 34.1 %all-to-all-start.22 = ((bf16[8,768,128]{2,1,0:T(8,128)(2,1)}), bf16[8,768,128]{2,1,0:T(8,128)(2,1)}, u32[]{:S(2)}, u32[]{:S(2)}) async-start(bf16[8,768,128]{2,1,0:T(8,128)(2,1)} %bitcast.552), calls=%async_computation.22 | async-start | bytes 3145728 | tf_op jit(solution)/shard_map/all_to_all | solution.py:51
  552.9 142.1 %reduce-scatter.3.cloned.1.call-start = ((), (), s32[]{:S(2)}) async-start(), calls=%async_computation.26 | async-start | bytes 1740800 | tf_op jit(solution)/shard_map/reduce_scatter | solution.py:415
  591.3 158.1 %reduce-scatter.5.cloned.1.call-start = ((), (), s32[]{:S(2)}) async-start(), calls=%async_computation.27 | async-start | bytes 5083136 | tf_op jit(solution)/shard_map/reduce_scatter | solution.py:415
  635.4 31.1 %copy-start.15 = (f32[768,128]{1,0:T(8,128)S(1)}, f32[768,128]{1,0:T(8,128)}, u32[]{:S(2)}) copy-start(f32[768,128]{1,0:T(8,128)} %copy-done.14) | copy-start | bytes 1179652
  635.4 19.8 %all-to-all-start.11 = ((bf16[8,768,128]{2,1,0:T(8,128)(2,1)}), bf16[8,768,128]{2,1,0:T(8,128)(2,1)}, u32[]{:S(2)}, u32[]{:S(2)}) async-start(bf16[8,768,128]{2,1,0:T(8,128)(2,1)} %bitcast.527), calls=%async_computation.11 | async-start | bytes 3145728 | tf_op jit(solution)/shard_map/all_to_all | solution.py:51
  641.4 25.0 %copy-start.5 = (f32[768,128]{1,0:T(8,128)S(1)}, f32[768,128]{1,0:T(8,128)}, u32[]{:S(2)}) copy-start(f32[768,128]{1,0:T(8,128)} %copy-done.4) | copy-start | bytes 1179652
  641.4 25.0 %copy-start.7 = (f32[2,1,768,128]{3,2,1,0:T(8,128)S(1)}, f32[2,1,768,128]{3,2,1,0:T(8,128)}, u32[]{:S(2)}) copy-start(f32[2,1,768,128]{3,2,1,0:T(8,128)} %param.14) | copy-start | bytes 2359300
  641.4 25.0 %copy-start.11 = (f32[768,128]{1,0:T(8,128)S(1)}, f32[768,128]{1,0:T(8,128)}, u32[]{:S(2)}) copy-start(f32[768,128]{1,0:T(8,128)} %copy-done.10) | copy-start | bytes 1179652
  641.4 25.0 %copy-start.13 = (f32[768,128]{1,0:T(8,128)S(1)}, f32[768,128]{1,0:T(8,128)}, u32[]{:S(2)}) copy-start(f32[768,128]{1,0:T(8,128)} %copy-done.12) | copy-start | bytes 1179652
  641.5 25.0 %copy-start.57 = (f32[768]{0:T(1024)S(1)}, f32[768]{0:T(1024)}, u32[]{:S(2)}) copy-start(f32[768]{0:T(1024)} %copy-done.56) | copy-start | bytes 9220
  641.5 25.0 %copy-start.59 = (f32[768]{0:T(1024)S(1)}, f32[768]{0:T(1024)}, u32[]{:S(2)}) copy-start(f32[768]{0:T(1024)} %copy-done.58) | copy-start | bytes 9220
  641.5 25.0 %copy-start.67 = (f32[768]{0:T(1024)S(1)}, f32[768]{0:T(1024)}, u32[]{:S(2)}) copy-start(f32[768]{0:T(1024)} %copy-done.66) | copy-start | bytes 9220
  641.5 25.0 %copy-start.69 = (f32[768]{0:T(1024)S(1)}, f32[768]{0:T(1024)}, u32[]{:S(2)}) copy-start(f32[768]{0:T(1024)} %copy-done.68) | copy-start | bytes 9220
  641.5 25.0 %copy-start.71 = (f32[768]{0:T(1024)S(1)}, f32[768]{0:T(1024)}, u32[]{:S(2)}) copy-start(f32[768]{0:T(1024)} %copy-done.70) | copy-start | bytes 9220
  641.5 25.0 %copy-start.73 = (f32[768]{0:T(1024)S(1)}, f32[768]{0:T(1024)}, u32[]{:S(2)}) copy-start(f32[768]{0:T(1024)} %copy-done.72) | copy-start | bytes 9220
  641.5 25.0 %copy-start.75 = (f32[768]{0:T(1024)S(1)}, f32[768]{0:T(1024)}, u32[]{:S(2)}) copy-start(f32[768]{0:T(1024)} %copy-done.74) | copy-start | bytes 9220
  641.5 25.0 %copy-start.77 = (f32[768]{0:T(1024)S(1)}, f32[768]{0:T(1024)}, u32[]{:S(2)}) copy-start(f32[768]{0:T(1024)} %copy-done.76) | copy-start | bytes 9220
  641.5 25.0 %copy-start.84 = (f32[128]{0:T(128)S(1)}, f32[128]{0:T(128)}, u32[]{:S(2)}) copy-start(f32[128]{0:T(128)} %copy-done.82) | copy-start | bytes 1540
  641.6 25.0 %copy-start.87 = (f32[128]{0:T(128)S(1)}, f32[128]{0:T(128)}, u32[]{:S(2)}) copy-start(f32[128]{0:T(128)} %copy-done.85) | copy-start | bytes 1540
  641.6 25.0 %copy-start.90 = (f32[128]{0:T(128)S(1)}, f32[128]{0:T(128)}, u32[]{:S(2)}) copy-start(f32[128]{0:T(128)} %copy-done.88) | copy-start | bytes 1540
  641.6 25.0 %copy-start.92 = (f32[128]{0:T(128)S(1)}, f32[128]{0:T(128)}, u32[]{:S(2)}) copy-start(f32[128]{0:T(128)} %copy-done.91) | copy-start | bytes 1540
  641.6 25.0 %copy-start.102 = (f32[128]{0:T(128)S(1)}, f32[128]{0:T(128)}, u32[]{:S(2)}) copy-start(f32[128]{0:T(128)} %copy-done.101) | copy-start | bytes 1540
  641.6 25.0 %copy-start.104 = (f32[128]{0:T(128)S(1)}, f32[128]{0:T(128)}, u32[]{:S(2)}) copy-start(f32[128]{0:T(128)} %copy-done.103) | copy-start | bytes 1540
  655.8 10.6 %all-to-all-start.23 = ((f32[8,1,1536]{2,1,0:T(1,128)}), f32[8,1,1536]{2,1,0:T(1,128)S(1)}, u32[]{:S(2)}, u32[]{:S(2)}) async-start(f32[8,1,1536]{2,1,0:T(1,128)} %broadcast_in_dim.216), calls=%async_computation.23 | async-start | bytes 98304 | tf_op jit(solution)/shard_map/all_to_all | solution.py:18
  666.6 12.4 %copy-start.21 = (f32[2,1,768,128]{3,2,1,0:T(8,128)S(1)}, f32[2,1,768,128]{3,2,1,0:T(8,128)}, u32[]{:S(2)}) copy-start(f32[2,1,768,128]{3,2,1,0:T(8,128)} %param.15) | copy-start | bytes 2359300
  670.2 18.5 %collective-permute-start.3 = (f32[1,768,128]{2,1,0:T(8,128)S(1)}, f32[1,768,128]{2,1,0:T(8,128)S(1)}, u32[]{:S(2)}, u32[]{:S(2)}) collective-permute-start(f32[1,768,128]{2,1,0:T(8,128)S(1)} %get-tuple-element.201), channel_id=1, source_target_pairs={{64,0},{65,1},{66,2},{67,3},{68,4},{69,5},{70,6},{71,7},{72,8},{73... | collective-permute-start | bytes 1179656 | tf_op jit(solution)/shard_map/ppermute | solution.py:506
  671.5 17.3 %collective-permute-start.4 = (f32[1,768,128]{2,1,0:T(8,128)S(1)}, f32[1,768,128]{2,1,0:T(8,128)S(1)}, u32[]{:S(2)}, u32[]{:S(2)}) collective-permute-start(f32[1,768,128]{2,1,0:T(8,128)S(1)} %get-tuple-element.202), channel_id=1, source_target_pairs={{0,64},{1,65},{2,66},{3,67},{4,68},{5,69},{6,70},{7,71},{8,72},{9,... | collective-permute-start | bytes 1179656 | tf_op jit(solution)/shard_map/ppermute | solution.py:504
  677.6 16.3 %collective-permute-start.1 = (f32[1,768,128]{2,1,0:T(8,128)S(1)}, f32[1,768,128]{2,1,0:T(8,128)S(1)}, u32[]{:S(2)}, u32[]{:S(2)}) collective-permute-start(f32[1,768,128]{2,1,0:T(8,128)S(1)} %get-tuple-element.203), channel_id=1, source_target_pairs={{64,0},{65,1},{66,2},{67,3},{68,4},{69,5},{70,6},{71,7},{72,8},{73... | collective-permute-start | bytes 1179656 | tf_op jit(solution)/shard_map/ppermute | solution.py:501
  682.6 11.4 %collective-permute-start.2 = (f32[1,768,128]{2,1,0:T(8,128)S(1)}, f32[1,768,128]{2,1,0:T(8,128)S(1)}, u32[]{:S(2)}, u32[]{:S(2)}) collective-permute-start(f32[1,768,128]{2,1,0:T(8,128)S(1)} %fusion.88), channel_id=1, source_target_pairs={{0,64},{1,65},{2,66},{3,67},{4,68},{5,69},{6,70},{7,71},{8,72},{9,... | collective-permute-start | bytes 1179656 | tf_op jit(solution)/shard_map/ppermute | solution.py:502
  (89 other events, 251.2 us)
Sparse Core Ops, SparseCore 0:
  26.2 30.4 all-gather.4
  101.8 27.8 all-gather.6
  591.4 68.8 reduce-scatter.2
  664.8 84.5 reduce-scatter.4

commit v9 on v7

--- a/solution.py
+++ b/solution.py
@@ -82,7 +82,7 @@
     )
 
 
-def norm_forward(stream, gain, offset):
+def norm_forward(stream, gain, offset, extra=None):
     width_all = stream.shape[1] * lax.axis_size("tensor")
     totals, squares = in_one((jnp.sum(stream, axis=1), jnp.sum(stream * stream, axis=1)), "tensor")
     mean_row = (totals / width_all)[:, None]
@@ -90,7 +90,10 @@
     inv_scale = lax.rsqrt(var_row + epsilon)
     normal_part = (stream - mean_row) * inv_scale
     normed = (normal_part * gain + offset).astype(jnp.bfloat16)
-    return (collect(normed, "tensor", 1), normal_part, inv_scale)
+    if extra is None:
+        return (collect(normed, "tensor", 1), normal_part, inv_scale, None)
+    both = collect(jnp.stack([normed, extra]), "tensor", 2)
+    return (both[0], normal_part, inv_scale, both[1])
 
 
 def norm_backward(partial_term, normal_part, inv_scale, gain):
@@ -221,7 +224,7 @@
     return (packed_grad, packed_weight_grad, bias_pair_grad, output_weight_grad)
 
 
-def layer_forward(stream, weights):
+def layer_forward(stream, weights, extra=None):
     (
         packed_weight,
         bias_pair,
@@ -240,7 +243,9 @@
     rows_count = seq_count * length
     shape_heads = (seq_count, length, width_part // HEAD_DIM, HEAD_DIM)
     stream_rows = stream.reshape(rows_count, width_part)
-    normed_one, normal_one, inv_one = norm_forward(stream_rows, gain_first, shift_first)
+    normed_one, normal_one, inv_one, extra_full = norm_forward(
+        stream_rows, gain_first, shift_first, extra
+    )
     queries, keys_in, values_in, logsum, mixed_rows = attention_forward(
         normed_one, packed_weight, bias_pair, shape_heads, rows_count, width_part
     )
@@ -249,7 +254,7 @@
         + branch_sum(jnp.dot(mixed_rows, output_weight, preferred_element_type=jnp.float32))
         + output_bias
     )
-    normed_two, normal_two, inv_two = norm_forward(residual, gain_second, shift_second)
+    normed_two, normal_two, inv_two, _ = norm_forward(residual, gain_second, shift_second)
     hidden_pre = (
         jnp.dot(normed_two, expand_weight, preferred_element_type=jnp.float32) + expand_bias
     )
@@ -274,10 +279,10 @@
         hidden_pre,
         hidden,
     )
-    return (result.reshape(stream.shape), kept_values)
-
-
-def layer_backward(out_grad, kept_values, weights):
+    return (result.reshape(stream.shape), kept_values, extra_full)
+
+
+def layer_backward(out_grad, kept_values, weights, branch_two=None):
     (
         packed_weight,
         bias_pair,
@@ -312,7 +317,8 @@
     shape_heads = (seq_count, length, width_part // HEAD_DIM, HEAD_DIM)
     grad_rows = out_grad.reshape(rows_count, width_part)
     contract_bias_grad = jnp.sum(grad_rows, axis=0)
-    branch_two = branch_grad(grad_rows)
+    if branch_two is None:
+        branch_two = branch_grad(grad_rows)
     contract_weight_grad = jnp.einsum(
         "nf,nd->fd", hidden, branch_two, preferred_element_type=jnp.float32
     )
@@ -491,11 +497,12 @@
     )
     stream = lax.dynamic_index_in_dim(inputs, section_index, axis=0, keepdims=False)
     out_grad = lax.dynamic_index_in_dim(cotangent, section_index, axis=0, keepdims=False)
-    middle, kept_zero = layer_forward(stream, weights_zero)
-    final, kept_last = layer_forward(middle, weights_last)
+    grad_rows = out_grad.reshape(-1, out_grad.shape[-1]).astype(jnp.bfloat16)
+    middle, kept_zero, grad_full = layer_forward(stream, weights_zero, grad_rows)
+    final, kept_last, _ = layer_forward(middle, weights_last)
     other_middle = lax.ppermute(middle, "section", [(1, 0)])
     other_final = lax.ppermute(final, "section", [(0, 1)])
-    middle_grad, grads_last = layer_backward(out_grad, kept_last, weights_last)
+    middle_grad, grads_last = layer_backward(out_grad, kept_last, weights_last, grad_full)
     other_middle_grad = lax.ppermute(middle_grad, "section", [(0, 1)])
     input_grad, grads_zero = layer_backward(middle_grad, kept_zero, weights_zero)
     other_input_grad = lax.ppermute(input_grad, "section", [(1, 0)])

time: 727 us -> 713 us (0.981)
  waiting for transfers between devices: 233 us -> 246 us
  other arithmetic: 66 us -> 55.5 us
  local copies, waits for them, and re-layouts: 113 us -> 103 us
    all_to_all x11, waiting for transfers between devices: 89.7 us -> 101 us  [sent_to_all(): return lax.all_to_all(copies, axis, split_axis=0, concat_axis=0, tiled=True)]
    all_to_all x5 -> x4, blocking collectives: 70.6 us -> 66 us  [sent_to_all(): return lax.all_to_all(copies, axis, split_axis=0, concat_axis=0, tiled=True)]
    unnamed x296 -> x220, local copies, waits for them, and re-layouts: 19.1 us -> 15 us
  transfers between devices with their start and end apart: 25 -> 25, of which waited for: 20 -> 21; matrix products, arithmetic and copies ran while one was open for 19% -> 16% of each run, Pallas kernels for 0% -> 0%
where the time goes in v9:
time: 713 us; the launch traced here: 700 us
  waiting for transfers between devices  246 us (35%)
  blocking collectives  113 us (16%)
  local copies, waits for them, and re-layouts  103 us (14%)
  starting transfers between devices  94.9 us (13%)
  matrix products  71.6 us (10%)
  other arithmetic  55.5 us (8%)
  between operations  15.8 us (2%)
    all_to_all x11, waiting for transfers between devices, sent_to_all(): return lax.all_to_all(copies, axis, split_axis=0, concat_axis=0, tiled=True)  101 us
    all_to_all x6, waiting for transfers between devices, summed_on_arrival(): lax.all_to_all(parts, axis, split_axis=0, concat_axis=0, tiled=True)  73.6 us
    all_to_all x4, blocking collectives, sent_to_all(): return lax.all_to_all(copies, axis, split_axis=0, concat_axis=0, tiled=True)  66 us
    all_to_all x11, starting transfers between devices, sent_to_all(): return lax.all_to_all(copies, axis, split_axis=0, concat_axis=0, tiled=True)  49.6 us
    all_to_all x2, blocking collectives, summed_on_arrival(): lax.all_to_all(parts, axis, split_axis=0, concat_axis=0, tiled=True)  46.6 us
    reduce_scatter x1, waiting for transfers between devices, sum_at_end(): lax.psum_scatter(rows.reshape(-1, 128), ('section', 'dp'), scatter_dimens...  33.8 us
    all_to_all x6, starting transfers between devices, summed_on_arrival(): lax.all_to_all(parts, axis, split_axis=0, concat_axis=0, tiled=True)  27.1 us
    all_gather x1, waiting for transfers between devices, gather_all(): lax.all_gather(jnp.where(is_first, own, other), 'dp', axis=0, tiled=False)  16.8 us
  transfers between devices with their start and end apart: 25, of which 21 were waited for; matrix products, arithmetic and copies ran while one was open for 16% of the time, Pallas kernels for 0%

profile of v9, /device:TPU:0, one launch (start us, length us, event | category | flops | bytes accessed | tf_op | source)
XLA Modules:
  0.0 699.7 jit_solution(2810011349746095076)
XLA Ops:
  12.8 3.2 collective-permute-start
  16.0 9.2 %collective-permute-done = bf16[1552,128]{1,0:T(8,128)(2,1)S(1)} collective-permute-done((bf16[1552,128]{1,0:T(8,128)(2,1)S(1)}, bf16[1552,128]{1,0:T(8,128)(2,1)S(1)}, u32[]{:S(2)}, u32[]{:S(2)}) %collective-permute-start) | collective-permute-done | bytes 397344 | tf_op jit(solution)/shard_map/ppermute | solution.py:452
  27.2 6.5 all-to-all-start
  34.7 5.3 all-to-all-done
  40.0 16.8 %all-gather.5.cloned.1.call-done = bf16[12416,128]{1,0:T(8,128)(2,1)} async-done(((bf16[1552,128]{1,0:T(8,128)(2,1)}), bf16[12416,128]{1,0:T(8,128)(2,1)}) %all-gather.5.cloned.1.call-update) | async-done | bytes 3178512 | tf_op jit(solution)/shard_map/all_gather | solution.py:453
  60.5 5.3 all-to-all-start.1
  73.3 30.3 %all-to-all-done.1 = bf16[8,2,768,128]{3,2,1,0:T(8,128)(2,1)} async-done(((bf16[8,2,768,128]{3,2,1,0:T(8,128)(2,1)}), bf16[8,2,768,128]{3,2,1,0:T(8,128)(2,1)}, u32[]{:S(2)}, u32[]{:S(2)}) %all-to-all-start.1) | async-done | bytes 3145760 | tf_op jit(solution)/shard_map/all_to_all | solution.py:18
  103.6 4.7 copy.246
  108.2 3.4 fusion.132
  119.7 3.6 all-to-all-start.2
  124.1 19.8 %all-to-all-done.2 = bf16[8,768,128]{2,1,0:T(8,128)(2,1)S(1)} async-done(((bf16[8,768,128]{2,1,0:T(8,128)(2,1)}), bf16[8,768,128]{2,1,0:T(8,128)(2,1)S(1)}, u32[]{:S(2)}, u32[]{:S(2)}) %all-to-all-start.2) | async-done | bytes 1572896 | tf_op jit(solution)/shard_map/all_to_all | solution.py:51
  145.5 3.6 all-to-all-start.3
  149.3 6.1 all-to-all-done.3
  157.2 4.6 all-to-all-start.4
  162.0 2.7 fusion.131
  168.5 12.9 %all-to-all-done.4 = bf16[8,768,128]{1,2,0:T(8,128)(2,1)} async-done(((bf16[8,768,128]{1,2,0:T(8,128)(2,1)}), bf16[8,768,128]{1,2,0:T(8,128)(2,1)}, u32[]{:S(2)}, u32[]{:S(2)}) %all-to-all-start.4) | async-done | bytes 1572896 | tf_op jit(solution)/shard_map/all_to_all | solution.py:18
  181.3 2.8 convolution_add_fusion.1
  186.8 3.6 all-to-all-start.5
  191.2 19.7 %all-to-all-done.5 = bf16[8,768,128]{2,1,0:T(8,128)(2,1)S(1)} async-done(((bf16[8,768,128]{2,1,0:T(8,128)(2,1)}), bf16[8,768,128]{2,1,0:T(8,128)(2,1)S(1)}, u32[]{:S(2)}, u32[]{:S(2)}) %all-to-all-start.5) | async-done | bytes 1572896 | tf_op jit(solution)/shard_map/all_to_all | solution.py:51
  212.3 3.6 all-to-all-start.6
  216.7 5.5 all-to-all-done.6
  223.9 4.3 all-to-all-start.7
  232.5 15.2 %all-to-all-done.7 = bf16[8,768,128]{2,1,0:T(8,128)(2,1)} async-done(((bf16[8,768,128]{2,1,0:T(8,128)(2,1)}), bf16[8,768,128]{2,1,0:T(8,128)(2,1)}, u32[]{:S(2)}, u32[]{:S(2)}) %all-to-all-start.7) | async-done | bytes 1572896 | tf_op jit(solution)/shard_map/all_to_all | solution.py:18
  256.9 3.6 all-to-all-start.8
  260.6 20.5 %all-to-all-done.8 = bf16[8,768,128]{2,1,0:T(8,128)(2,1)S(1)} async-done(((bf16[8,768,128]{2,1,0:T(8,128)(2,1)}), bf16[8,768,128]{2,1,0:T(8,128)(2,1)S(1)}, u32[]{:S(2)}, u32[]{:S(2)}) %all-to-all-start.8) | async-done | bytes 1572896 | tf_op jit(solution)/shard_map/all_to_all | solution.py:51
  282.4 3.6 all-to-all-start.9
  286.2 6.1 all-to-all-done.9
  294.2 4.3 all-to-all-start.10
  305.1 12.8 %all-to-all-done.10 = bf16[8,768,128]{1,2,0:T(8,128)(2,1)} async-done(((bf16[8,768,128]{1,2,0:T(8,128)(2,1)}), bf16[8,768,128]{1,2,0:T(8,128)(2,1)}, u32[]{:S(2)}, u32[]{:S(2)}) %all-to-all-start.10) | async-done | bytes 1572896 | tf_op jit(solution)/shard_map/all_to_all | solution.py:18
  318.0 2.8 convolution_add_fusion
  320.9 2.7 fusion.121
  324.9 25.3 %all_to_all.123 = bf16[8,768,128]{2,1,0:T(8,128)(2,1)} all-to-all(bf16[8,768,128]{2,1,0:T(8,128)(2,1)S(1)} %bitcast.507), channel_id=1, replica_groups=mesh['section'=2,'dp'=8,'tensor'=8] {'tensor'}, dimensions={0} | all-to-all | bytes 3145728 | tf_op jit(solution)/shard_map/all_to_all | solution.py:51
  352.8 8.7 %all_to_all.124 = f32[8,1,1536]{2,1,0:T(1,128)S(1)} all-to-all(f32[8,1,1536]{2,1,0:T(1,128)S(1)} %broadcast_in_dim.200), channel_id=1, replica_groups=mesh['section'=2,'dp'=8,'tensor'=8] {'tensor'}, dimensions={0} | all-to-all | bytes 98304 | tf_op jit(solution)/shard_map/all_to_all | solution.py:18
  365.2 29.8 %all_to_all.125 = bf16[8,768,128]{2,1,0:T(8,128)(2,1)S(1)} all-to-all(bf16[8,768,128]{2,1,0:T(8,128)(2,1)S(1)} %broadcast_in_dim.201), channel_id=1, replica_groups=mesh['section'=2,'dp'=8,'tensor'=8] {'tensor'}, dimensions={0} | all-to-all | bytes 3145728 | tf_op jit(solution)/shard_map/all_to_all | solution.py:18
  408.5 21.3 %all_to_all.126 = bf16[8,768,128]{2,1,0:T(8,128)(2,1)S(1)} all-to-all(bf16[8,768,128]{2,1,0:T(8,128)(2,1)S(1)} %bitcast.508), channel_id=1, replica_groups=mesh['section'=2,'dp'=8,'tensor'=8] {'tensor'}, dimensions={0} | all-to-all | bytes 3145728 | tf_op jit(solution)/shard_map/all_to_all | solution.py:51
  432.3 8.8 %all_to_all.127 = f32[8,1,1536]{2,1,0:T(1,128)S(1)} all-to-all(f32[8,1,1536]{2,1,0:T(1,128)S(1)} %broadcast_in_dim.202), channel_id=1, replica_groups=mesh['section'=2,'dp'=8,'tensor'=8] {'tensor'}, dimensions={0} | all-to-all | bytes 98304 | tf_op jit(solution)/shard_map/all_to_all | solution.py:18
  443.7 18.7 %all_to_all.128 = bf16[8,768,128]{2,1,0:T(8,128)(2,1)S(1)} all-to-all(bf16[8,768,128]{2,1,0:T(8,128)(2,1)S(1)} %broadcast_in_dim.203), channel_id=1, replica_groups=mesh['section'=2,'dp'=8,'tensor'=8] {'tensor'}, dimensions={0} | all-to-all | bytes 3145728 | tf_op jit(solution)/shard_map/all_to_all | solution.py:18
  462.4 4.0 fusion.135
  469.0 4.7 all-to-all-start.18
  474.9 3.6 convolution_convert_fusion.8
  480.9 3.1 fusion.34
  493.3 5.7 all-to-all-start.19
  502.0 3.2 all-to-all-done.19
  508.2 4.4 all-to-all-start.20
  516.9 3.2 concatenate.135
  522.3 3.6 convolution_convert_fusion.9
  530.1 3.0 fusion.33
  539.0 4.0 bitcast_reduce_fusion
  543.0 4.2 multiply_reduce_fusion
  550.3 2.8 copy.294
  556.0 5.7 all-to-all-start.21
  570.6 2.7 maximum_dynamic-update-slice_fusion.2
  586.0 5.8 all-to-all-start.11
  592.0 13.6 %all-to-all-done.11 = bf16[8,768,128]{2,1,0:T(8,128)(2,1)} async-done(((bf16[8,768,128]{2,1,0:T(8,128)(2,1)}), bf16[8,768,128]{2,1,0:T(8,128)(2,1)}, u32[]{:S(2)}, u32[]{:S(2)}) %all-to-all-start.11) | async-done | bytes 1572896 | tf_op jit(solution)/shard_map/all_to_all | solution.py:51
  606.3 3.6 all-to-all-start.22
  612.3 3.9 all-to-all-done.22
  616.4 3.7 fusion.46
  621.4 6.1 collective-permute-start.4
  628.9 3.4 fusion.63
  632.4 6.1 collective-permute-start.2
  638.6 3.5 collective-permute-done.3
  642.1 2.7 collective-permute-done.4
  645.8 4.2 collective-permute-done.2
  651.3 33.8 %reduce-scatter.2.cloned.1.call-done = bf16[1552,128]{1,0:T(8,128)(2,1)} async-done(((bf16[24832,128]{1,0:T(8,128)(2,1)}), bf16[1552,128]{1,0:T(8,128)(2,1)}) %reduce-scatter.2.cloned.1.call-update) | async-done | bytes 397328 | tf_op jit(solution)/shard_map/reduce_scatter | solution.py:428
  (469 shorter events, 173.8 us)
Async XLA Ops:
  7.2 49.7 %all-gather.5.cloned.1.call-start = ((), (), s32[]{:S(2)}) async-start(), calls=%async_computation.25 | async-start | bytes 3575808 | tf_op jit(solution)/shard_map/all_gather | solution.py:453
  9.0 17.1 %copy-start.8 = (f32[2,1,768,128]{3,2,1,0:T(8,128)S(1)}, f32[2,1,768,128]{3,2,1,0:T(8,128)}, u32[]{:S(2)}) copy-start(f32[2,1,768,128]{3,2,1,0:T(8,128)} %param.14) | copy-start | bytes 2359300
  12.8 12.4 %collective-permute-start = (bf16[1552,128]{1,0:T(8,128)(2,1)S(1)}, bf16[1552,128]{1,0:T(8,128)(2,1)S(1)}, u32[]{:S(2)}, u32[]{:S(2)}) collective-permute-start(bf16[1552,128]{1,0:T(8,128)(2,1)S(1)} %bitcast.565), channel_id=1, source_target_pairs={{0,64},{64,0},{1,65},{65,1},{2,66},{66,2},{3,67},{67,3},{4,68},{68... | collective-permute-start | bytes 1191944 | tf_op jit(solution)/shard_map/ppermute | solution.py:452
  27.2 12.8 %all-to-all-start = ((f32[8,1,1536]{2,1,0:T(1,128)}), f32[8,1,1536]{2,1,0:T(1,128)S(1)}, u32[]{:S(2)}, u32[]{:S(2)}) async-start(f32[8,1,1536]{2,1,0:T(1,128)} %broadcast_in_dim.189), calls=%async_computation | async-start | bytes 98304 | tf_op jit(solution)/shard_map/all_to_all | solution.py:18
  60.5 43.1 %all-to-all-start.1 = ((bf16[8,2,768,128]{3,2,1,0:T(8,128)(2,1)}), bf16[8,2,768,128]{3,2,1,0:T(8,128)(2,1)}, u32[]{:S(2)}, u32[]{:S(2)}) async-start(bf16[8,2,768,128]{3,2,1,0:T(8,128)(2,1)} %broadcast_in_dim.191), calls=%async_computation.1 | async-start | bytes 6291456 | tf_op jit(solution)/shard_map/all_to_all | solution.py:18
  68.2 44.6 %copy-start.77 = (f32[2,64]{1,0:T(2,128)}, f32[2,64]{1,0:T(2,128)S(1)}, u32[]{:S(2)}) copy-start(f32[2,64]{1,0:T(2,128)S(1)} %reshape.2387) | copy-start | bytes 1540
  68.3 46.8 %copy-start.87 = (f32[2,64]{1,0:T(2,128)}, f32[2,64]{1,0:T(2,128)S(1)}, u32[]{:S(2)}) copy-start(f32[2,64]{1,0:T(2,128)S(1)} %reshape.2386) | copy-start | bytes 1540
  119.7 24.2 %all-to-all-start.2 = ((bf16[8,768,128]{2,1,0:T(8,128)(2,1)}), bf16[8,768,128]{2,1,0:T(8,128)(2,1)S(1)}, u32[]{:S(2)}, u32[]{:S(2)}) async-start(bf16[8,768,128]{2,1,0:T(8,128)(2,1)} %bitcast.488), calls=%async_computation.2 | async-start | bytes 3145728 | tf_op jit(solution)/shard_map/all_to_all | solution.py:51
  123.3 67.1 %all-gather.7.cloned.1.call-start = ((), (), s32[]{:S(2)}) async-start(), calls=%async_computation.26 | async-start | bytes 3575808 | tf_op jit(solution)/shard_map/all_gather | solution.py:454
  124.1 20.3 %copy-start.83 = (f32[128]{0:T(128)}, f32[128]{0:T(128)S(1)}, u32[]{:S(2)}) copy-start(f32[128]{0:T(128)S(1)} %reshape.2388) | copy-start | bytes 1540
  145.5 9.9 %all-to-all-start.3 = ((f32[8,1,1536]{2,1,0:T(1,128)}), f32[8,1,1536]{2,1,0:T(1,128)S(1)}, u32[]{:S(2)}, u32[]{:S(2)}) async-start(f32[8,1,1536]{2,1,0:T(1,128)} %broadcast_in_dim.194), calls=%async_computation.3 | async-start | bytes 98304 | tf_op jit(solution)/shard_map/all_to_all | solution.py:18
  149.2 8.0 %copy-start.67 = (f32[128]{0:T(128)}, f32[128]{0:T(128)S(1)}, u32[]{:S(2)}) copy-start(f32[128]{0:T(128)S(1)} %reshape.2389) | copy-start | bytes 1540
  157.2 24.1 %all-to-all-start.4 = ((bf16[8,768,128]{1,2,0:T(8,128)(2,1)}), bf16[8,768,128]{1,2,0:T(8,128)(2,1)}, u32[]{:S(2)}, u32[]{:S(2)}) async-start(bf16[8,768,128]{1,2,0:T(8,128)(2,1)} %broadcast_in_dim.195), calls=%async_computation.4 | async-start | bytes 3145728 | tf_op jit(solution)/shard_map/all_to_all | solution.py:18
  186.8 24.2 %all-to-all-start.5 = ((bf16[8,768,128]{2,1,0:T(8,128)(2,1)}), bf16[8,768,128]{2,1,0:T(8,128)(2,1)S(1)}, u32[]{:S(2)}, u32[]{:S(2)}) async-start(bf16[8,768,128]{2,1,0:T(8,128)(2,1)} %bitcast.486), calls=%async_computation.5 | async-start | bytes 3145728 | tf_op jit(solution)/shard_map/all_to_all | solution.py:51
  190.4 21.0 %copy-start.85 = (f32[128]{0:T(128)}, f32[128]{0:T(128)S(1)}, u32[]{:S(2)}) copy-start(f32[128]{0:T(128)S(1)} %reshape.2392) | copy-start | bytes 1540
  211.2 12.8 %copy-start.17 = (f32[768,128]{1,0:T(8,128)}, f32[768,128]{1,0:T(8,128)S(1)}, u32[]{:S(2)}) copy-start(f32[768,128]{1,0:T(8,128)S(1)} %convert_reduce_fusion.6) | copy-start | bytes 1179652
  211.5 69.9 %copy-start.2 = (f32[768,128]{1,0:T(8,128)}, f32[768,128]{1,0:T(8,128)S(1)}, u32[]{:S(2)}) copy-start(f32[768,128]{1,0:T(8,128)S(1)} %get-tuple-element.207) | copy-start | bytes 1179652
  212.3 9.9 %all-to-all-start.6 = ((f32[8,1,1536]{2,1,0:T(1,128)}), f32[8,1,1536]{2,1,0:T(1,128)S(1)}, u32[]{:S(2)}, u32[]{:S(2)}) async-start(f32[8,1,1536]{2,1,0:T(1,128)} %broadcast_in_dim.196), calls=%async_computation.6 | async-start | bytes 98304 | tf_op jit(solution)/shard_map/all_to_all | solution.py:18
  216.6 7.3 %copy-start.69 = (f32[128]{0:T(128)}, f32[128]{0:T(128)S(1)}, u32[]{:S(2)}) copy-start(f32[128]{0:T(128)S(1)} %reshape.2393) | copy-start | bytes 1540
  223.9 23.8 %all-to-all-start.7 = ((bf16[8,768,128]{2,1,0:T(8,128)(2,1)}), bf16[8,768,128]{2,1,0:T(8,128)(2,1)}, u32[]{:S(2)}, u32[]{:S(2)}) async-start(bf16[8,768,128]{2,1,0:T(8,128)(2,1)} %broadcast_in_dim.197), calls=%async_computation.7 | async-start | bytes 3145728 | tf_op jit(solution)/shard_map/all_to_all | solution.py:18
  229.6 20.5 %copy-start.79 = (f32[2,64]{1,0:T(2,128)}, f32[2,64]{1,0:T(2,128)S(1)}, u32[]{:S(2)}) copy-start(f32[2,64]{1,0:T(2,128)S(1)} %reshape.2396) | copy-start | bytes 1540
  229.7 22.7 %copy-start.89 = (f32[2,64]{1,0:T(2,128)}, f32[2,64]{1,0:T(2,128)S(1)}, u32[]{:S(2)}) copy-start(f32[2,64]{1,0:T(2,128)S(1)} %reshape.2395) | copy-start | bytes 1540
  232.5 17.4 %copy-start.52 = (bf16[1024,3,128]{0,2,1:T(8,128)(2,1)}, bf16[1024,3,128]{0,2,1:T(8,128)(2,1)S(1)}, u32[]{:S(2)}) copy-start(bf16[1024,3,128]{0,2,1:T(8,128)(2,1)S(1)} %copy.259) | copy-start | bytes 2359300
  256.9 24.2 %all-to-all-start.8 = ((bf16[8,768,128]{2,1,0:T(8,128)(2,1)}), bf16[8,768,128]{2,1,0:T(8,128)(2,1)S(1)}, u32[]{:S(2)}, u32[]{:S(2)}) async-start(bf16[8,768,128]{2,1,0:T(8,128)(2,1)} %bitcast.484), calls=%async_computation.8 | async-start | bytes 3145728 | tf_op jit(solution)/shard_map/all_to_all | solution.py:51
  260.6 21.0 %copy-start.72 = (f32[128]{0:T(128)}, f32[128]{0:T(128)S(1)}, u32[]{:S(2)}) copy-start(f32[128]{0:T(128)S(1)} %reshape.2397) | copy-start | bytes 1540
  281.7 12.5 %copy-start.13 = (f32[768,128]{1,0:T(8,128)}, f32[768,128]{1,0:T(8,128)S(1)}, u32[]{:S(2)}) copy-start(f32[768,128]{1,0:T(8,128)S(1)} %get-tuple-element.206) | copy-start | bytes 1179652
  282.4 9.9 %all-to-all-start.9 = ((f32[8,1,1536]{2,1,0:T(1,128)}), f32[8,1,1536]{2,1,0:T(1,128)S(1)}, u32[]{:S(2)}, u32[]{:S(2)}) async-start(f32[8,1,1536]{2,1,0:T(1,128)} %broadcast_in_dim.198), calls=%async_computation.9 | async-start | bytes 98304 | tf_op jit(solution)/shard_map/all_to_all | solution.py:18
  286.2 65.8 %copy-start.65 = (f32[128]{0:T(128)}, f32[128]{0:T(128)S(1)}, u32[]{:S(2)}) copy-start(f32[128]{0:T(128)S(1)} %reshape.2398) | copy-start | bytes 1540
  294.2 23.8 %all-to-all-start.10 = ((bf16[8,768,128]{1,2,0:T(8,128)(2,1)}), bf16[8,768,128]{1,2,0:T(8,128)(2,1)}, u32[]{:S(2)}, u32[]{:S(2)}) async-start(bf16[8,768,128]{1,2,0:T(8,128)(2,1)} %broadcast_in_dim.199), calls=%async_computation.10 | async-start | bytes 3145728 | tf_op jit(solution)/shard_map/all_to_all | solution.py:18
  324.9 72.0 %slice-start.2 = ((s8[4718592]{0:T(1024)(128)(4,1)}), s8[524288]{0:T(1024)(128)(4,1)S(1)}, s32[]{:S(2)}) async-start(s8[4718592]{0:T(1024)(128)(4,1)} %bitcast.500), calls=%async_computation.29 | async-start | bytes 1048576
  350.2 12.7 %copy-start.23 = (f32[2,1,768,128]{3,2,1,0:T(8,128)S(1)}, f32[2,1,768,128]{3,2,1,0:T(8,128)}, u32[]{:S(2)}) copy-start(f32[2,1,768,128]{3,2,1,0:T(8,128)} %param.15) | copy-start | bytes 2359300
  352.0 13.0 %copy-start.4 = (f32[768,128]{1,0:T(8,128)}, f32[768,128]{1,0:T(8,128)S(1)}, u32[]{:S(2)}) copy-start(f32[768,128]{1,0:T(8,128)S(1)} %convert_reduce_fusion.3) | copy-start | bytes 1179652
  362.9 33.9 %slice-start.3 = ((s8[4718592]{0:T(1024)(128)(4,1)}), s8[4194304]{0:T(1024)(128)(4,1)S(1)}, s32[]{:S(2)}) async-start(s8[4718592]{0:T(1024)(128)(4,1)} %bitcast.500), calls=%async_computation.30 | async-start | bytes 8388608
  443.7 18.7 %copy-start.96 = (f32[768,512]{1,0:T(8,128)S(1)}, f32[768,512]{1,0:T(8,128)}, u32[]{:S(2)}) copy-start(f32[768,512]{1,0:T(8,128)} %copy-done.95) | copy-start | bytes 4718596
  469.0 21.5 %all-to-all-start.18 = ((bf16[8,768,128]{2,1,0:T(8,128)(2,1)}), bf16[8,768,128]{2,1,0:T(8,128)(2,1)}, u32[]{:S(2)}, u32[]{:S(2)}) async-start(bf16[8,768,128]{2,1,0:T(8,128)(2,1)} %bitcast.506), calls=%async_computation.18 | async-start | bytes 3145728 | tf_op jit(solution)/shard_map/all_to_all | solution.py:51
  492.1 13.2 %copy-start.6 = (f32[768,128]{1,0:T(8,128)}, f32[768,128]{1,0:T(8,128)S(1)}, u32[]{:S(2)}) copy-start(f32[768,128]{1,0:T(8,128)S(1)} %convert_reduce_fusion.1) | copy-start | bytes 1179652
  493.3 12.0 %all-to-all-start.19 = ((f32[8,1,1536]{2,1,0:T(1,128)}), f32[8,1,1536]{2,1,0:T(1,128)S(1)}, u32[]{:S(2)}, u32[]{:S(2)}) async-start(f32[8,1,1536]{2,1,0:T(1,128)} %broadcast_in_dim.204), calls=%async_computation.19 | async-start | bytes 98304 | tf_op jit(solution)/shard_map/all_to_all | solution.py:18
  508.2 4.6 copy-start.57
  508.2 4.6 copy-start.58
  508.2 4.6 copy-start.59
  508.2 28.6 %all-to-all-start.20 = ((bf16[8,768,128]{2,1,0:T(8,128)(2,1)}), bf16[8,768,128]{2,1,0:T(8,128)(2,1)}, u32[]{:S(2)}, u32[]{:S(2)}) async-start(bf16[8,768,128]{2,1,0:T(8,128)(2,1)} %broadcast_in_dim.205), calls=%async_computation.20 | async-start | bytes 3145728 | tf_op jit(solution)/shard_map/all_to_all | solution.py:18
  534.3 4.6 copy-start.62
  539.0 8.3 %slice-start = ((s8[4718592]{0:T(1024)(128)(4,1)}), s8[4194304]{0:T(1024)(128)(4,1)S(1)}, s32[]{:S(2)}) async-start(s8[4718592]{0:T(1024)(128)(4,1)} %bitcast.498), calls=%async_computation.27 | async-start | bytes 8388608
  556.0 5.8 copy-start.54
  556.0 22.1 %all-to-all-start.21 = ((bf16[8,768,128]{2,1,0:T(8,128)(2,1)}), bf16[8,768,128]{2,1,0:T(8,128)(2,1)S(1)}, u32[]{:S(2)}, u32[]{:S(2)}) async-start(bf16[8,768,128]{2,1,0:T(8,128)(2,1)} %bitcast.505), calls=%async_computation.21 | async-start | bytes 3145728 | tf_op jit(solution)/shard_map/all_to_all | solution.py:51
  561.8 123.2 %reduce-scatter.2.cloned.1.call-start = ((), (), s32[]{:S(2)}) async-start(), calls=%async_computation.24 | async-start | bytes 6754304 | tf_op jit(solution)/shard_map/reduce_scatter | solution.py:428
  586.0 5.9 copy-start.74
  586.0 19.6 %all-to-all-start.11 = ((bf16[8,768,128]{2,1,0:T(8,128)(2,1)}), bf16[8,768,128]{2,1,0:T(8,128)(2,1)}, u32[]{:S(2)}, u32[]{:S(2)}) async-start(bf16[8,768,128]{2,1,0:T(8,128)(2,1)} %bitcast.482), calls=%async_computation.11 | async-start | bytes 3145728 | tf_op jit(solution)/shard_map/all_to_all | solution.py:51
  591.8 24.4 %copy-start.5 = (f32[768,128]{1,0:T(8,128)S(1)}, f32[768,128]{1,0:T(8,128)}, u32[]{:S(2)}) copy-start(f32[768,128]{1,0:T(8,128)} %copy-done.4) | copy-start | bytes 1179652
  591.8 24.4 %copy-start.7 = (f32[768,128]{1,0:T(8,128)S(1)}, f32[768,128]{1,0:T(8,128)}, u32[]{:S(2)}) copy-start(f32[768,128]{1,0:T(8,128)} %copy-done.6) | copy-start | bytes 1179652
  591.9 24.4 %copy-start.16 = (f32[768,128]{1,0:T(8,128)S(1)}, f32[768,128]{1,0:T(8,128)}, u32[]{:S(2)}) copy-start(f32[768,128]{1,0:T(8,128)} %copy-done.15) | copy-start | bytes 1179652
  591.9 24.4 %copy-start.18 = (f32[768,128]{1,0:T(8,128)S(1)}, f32[768,128]{1,0:T(8,128)}, u32[]{:S(2)}) copy-start(f32[768,128]{1,0:T(8,128)} %copy-done.17) | copy-start | bytes 1179652
  591.9 24.4 %copy-start.66 = (f32[128]{0:T(128)S(1)}, f32[128]{0:T(128)}, u32[]{:S(2)}) copy-start(f32[128]{0:T(128)} %copy-done.65) | copy-start | bytes 1540
  591.9 24.4 %copy-start.71 = (f32[128]{0:T(128)S(1)}, f32[128]{0:T(128)}, u32[]{:S(2)}) copy-start(f32[128]{0:T(128)} %copy-done.69) | copy-start | bytes 1540
  591.9 24.4 %copy-start.73 = (f32[128]{0:T(128)S(1)}, f32[128]{0:T(128)}, u32[]{:S(2)}) copy-start(f32[128]{0:T(128)} %copy-done.72) | copy-start | bytes 1540
  591.9 24.4 %copy-start.84 = (f32[128]{0:T(128)S(1)}, f32[128]{0:T(128)}, u32[]{:S(2)}) copy-start(f32[128]{0:T(128)} %copy-done.83) | copy-start | bytes 1540
  591.9 24.4 %copy-start.86 = (f32[128]{0:T(128)S(1)}, f32[128]{0:T(128)}, u32[]{:S(2)}) copy-start(f32[128]{0:T(128)} %copy-done.85) | copy-start | bytes 1540
  606.3 9.9 %all-to-all-start.22 = ((f32[8,1,1536]{2,1,0:T(1,128)}), f32[8,1,1536]{2,1,0:T(1,128)S(1)}, u32[]{:S(2)}, u32[]{:S(2)}) async-start(f32[8,1,1536]{2,1,0:T(1,128)} %broadcast_in_dim.206), calls=%async_computation.22 | async-start | bytes 98304 | tf_op jit(solution)/shard_map/all_to_all | solution.py:18
  616.3 12.6 %copy-start.24 = (f32[2,1,768,128]{3,2,1,0:T(8,128)S(1)}, f32[2,1,768,128]{3,2,1,0:T(8,128)}, u32[]{:S(2)}) copy-start(f32[2,1,768,128]{3,2,1,0:T(8,128)} %param.15) | copy-start | bytes 2359300
  620.1 22.0 %collective-permute-start.3 = (f32[1,768,128]{2,1,0:T(8,128)S(1)}, f32[1,768,128]{2,1,0:T(8,128)S(1)}, u32[]{:S(2)}, u32[]{:S(2)}) collective-permute-start(f32[1,768,128]{2,1,0:T(8,128)S(1)} %get-tuple-element.203), channel_id=1, source_target_pairs={{64,0},{65,1},{66,2},{67,3},{68,4},{69,5},{70,6},{71,7},{72,8},{73... | collective-permute-start | bytes 1179656 | tf_op jit(solution)/shard_map/ppermute | solution.py:508
  621.4 23.4 %collective-permute-start.4 = (f32[1,768,128]{2,1,0:T(8,128)S(1)}, f32[1,768,128]{2,1,0:T(8,128)S(1)}, u32[]{:S(2)}, u32[]{:S(2)}) collective-permute-start(f32[1,768,128]{2,1,0:T(8,128)S(1)} %get-tuple-element.204), channel_id=1, source_target_pairs={{0,64},{1,65},{2,66},{3,67},{4,68},{5,69},{6,70},{7,71},{8,72},{9,... | collective-permute-start | bytes 1179656 | tf_op jit(solution)/shard_map/ppermute | solution.py:506
  627.5 4.9 copy-start.27
  627.5 22.8 %collective-permute-start.1 = (f32[1,768,128]{2,1,0:T(8,128)S(1)}, f32[1,768,128]{2,1,0:T(8,128)S(1)}, u32[]{:S(2)}, u32[]{:S(2)}) collective-permute-start(f32[1,768,128]{2,1,0:T(8,128)S(1)} %get-tuple-element.205), channel_id=1, source_target_pairs={{64,0},{65,1},{66,2},{67,3},{68,4},{69,5},{70,6},{71,7},{72,8},{73... | collective-permute-start | bytes 1179656 | tf_op jit(solution)/shard_map/ppermute | solution.py:503
  632.4 17.6 %collective-permute-start.2 = (f32[1,768,128]{2,1,0:T(8,128)S(1)}, f32[1,768,128]{2,1,0:T(8,128)S(1)}, u32[]{:S(2)}, u32[]{:S(2)}) collective-permute-start(f32[1,768,128]{2,1,0:T(8,128)S(1)} %fusion.79), channel_id=1, source_target_pairs={{0,64},{1,65},{2,66},{3,67},{4,68},{5,69},{6,70},{7,71},{8,72},{9,... | collective-permute-start | bytes 1179656 | tf_op jit(solution)/shard_map/ppermute | solution.py:504
  (63 other events, 130.0 us)
Sparse Core Ops, SparseCore 0:
  26.3 30.4 all-gather.4
  126.4 27.8 all-gather.6
  580.9 104.0 reduce-scatter.1

commit v10 on v9

--- a/solution.py
+++ b/solution.py
@@ -503,17 +503,18 @@
     other_middle = lax.ppermute(middle, "section", [(1, 0)])
     other_final = lax.ppermute(final, "section", [(0, 1)])
     middle_grad, grads_last = layer_backward(out_grad, kept_last, weights_last, grad_full)
-    other_middle_grad = lax.ppermute(middle_grad, "section", [(0, 1)])
     input_grad, grads_zero = layer_backward(middle_grad, kept_zero, weights_zero)
-    other_input_grad = lax.ppermute(input_grad, "section", [(1, 0)])
+    other_grad = lax.ppermute(
+        jnp.where(is_first, middle_grad, input_grad), "section", [(0, 1), (1, 0)]
+    )
     reduced = sum_at_end(grads_zero, grads_last, dims)
     section_outputs = jnp.where(
         is_first, jnp.stack([middle, other_middle]), jnp.stack([other_final, final])
     )[None]
     section_grads = jnp.where(
         is_first,
-        jnp.stack([input_grad, other_input_grad]),
-        jnp.stack([other_middle_grad, middle_grad]),
+        jnp.stack([input_grad, other_grad]),
+        jnp.stack([other_grad, middle_grad]),
     )[None]
     return (section_outputs, section_grads) + tuple(reduced)
 

time: 713 us -> 716 us (level)
  transfers between devices with their start and end apart: 25 -> 24, of which waited for: 21 -> 20; matrix products, arithmetic and copies ran while one was open for 16% -> 16% of each run, Pallas kernels for 0% -> 0%
where the time goes in v10:
time: 716 us; the launch traced here: 702 us
  waiting for transfers between devices  253 us (35%)
  blocking collectives  113 us (16%)
  local copies, waits for them, and re-layouts  103 us (14%)
  starting transfers between devices  90.1 us (13%)
  matrix products  71.6 us (10%)
  other arithmetic  55.6 us (8%)
  between operations  15.8 us (2%)
    all_to_all x11, waiting for transfers between devices, sent_to_all(): return lax.all_to_all(copies, axis, split_axis=0, concat_axis=0, tiled=True)  102 us
    all_to_all x6, waiting for transfers between devices, summed_on_arrival(): lax.all_to_all(parts, axis, split_axis=0, concat_axis=0, tiled=True)  73.6 us
    all_to_all x4, blocking collectives, sent_to_all(): return lax.all_to_all(copies, axis, split_axis=0, concat_axis=0, tiled=True)  66 us
    all_to_all x11, starting transfers between devices, sent_to_all(): return lax.all_to_all(copies, axis, split_axis=0, concat_axis=0, tiled=True)  49.6 us
    all_to_all x2, blocking collectives, summed_on_arrival(): lax.all_to_all(parts, axis, split_axis=0, concat_axis=0, tiled=True)  46.6 us
    reduce_scatter x1, waiting for transfers between devices, sum_at_end(): lax.psum_scatter(rows.reshape(-1, 128), ('section', 'dp'), scatter_dimens...  39.2 us
    all_to_all x6, starting transfers between devices, summed_on_arrival(): lax.all_to_all(parts, axis, split_axis=0, concat_axis=0, tiled=True)  27.1 us
    all_gather x1, waiting for transfers between devices, gather_all(): lax.all_gather(jnp.where(is_first, own, other), 'dp', axis=0, tiled=False)  16.8 us
  transfers between devices with their start and end apart: 24, of which 20 were waited for; matrix products, arithmetic and copies ran while one was open for 16% of the time, Pallas kernels for 0%

profile of v10, /device:TPU:0, one launch (start us, length us, event | category | flops | bytes accessed | tf_op | source)
XLA Modules:
  0.0 702.0 jit_solution(11952771297615228910)
XLA Ops:
  12.8 3.2 collective-permute-start
  16.0 9.2 %collective-permute-done = bf16[1552,128]{1,0:T(8,128)(2,1)S(1)} collective-permute-done((bf16[1552,128]{1,0:T(8,128)(2,1)S(1)}, bf16[1552,128]{1,0:T(8,128)(2,1)S(1)}, u32[]{:S(2)}, u32[]{:S(2)}) %collective-permute-start) | collective-permute-done | bytes 397344 | tf_op jit(solution)/shard_map/ppermute | solution.py:452
  27.2 6.5 all-to-all-start
  34.7 5.3 all-to-all-done
  40.0 16.8 %all-gather.5.cloned.1.call-done = bf16[12416,128]{1,0:T(8,128)(2,1)} async-done(((bf16[1552,128]{1,0:T(8,128)(2,1)}), bf16[12416,128]{1,0:T(8,128)(2,1)}) %all-gather.5.cloned.1.call-update) | async-done | bytes 3178512 | tf_op jit(solution)/shard_map/all_gather | solution.py:453
  60.5 5.3 all-to-all-start.1
  73.3 30.3 %all-to-all-done.1 = bf16[8,2,768,128]{3,2,1,0:T(8,128)(2,1)} async-done(((bf16[8,2,768,128]{3,2,1,0:T(8,128)(2,1)}), bf16[8,2,768,128]{3,2,1,0:T(8,128)(2,1)}, u32[]{:S(2)}, u32[]{:S(2)}) %all-to-all-start.1) | async-done | bytes 3145760 | tf_op jit(solution)/shard_map/all_to_all | solution.py:18
  103.6 4.6 copy.246
  108.2 3.4 fusion.132
  119.7 3.6 all-to-all-start.2
  124.1 19.8 %all-to-all-done.2 = bf16[8,768,128]{2,1,0:T(8,128)(2,1)S(1)} async-done(((bf16[8,768,128]{2,1,0:T(8,128)(2,1)}), bf16[8,768,128]{2,1,0:T(8,128)(2,1)S(1)}, u32[]{:S(2)}, u32[]{:S(2)}) %all-to-all-start.2) | async-done | bytes 1572896 | tf_op jit(solution)/shard_map/all_to_all | solution.py:51
  145.5 3.6 all-to-all-start.3
  149.3 6.1 all-to-all-done.3
  157.2 4.6 all-to-all-start.4
  161.9 2.7 fusion.131
  168.4 12.9 %all-to-all-done.4 = bf16[8,768,128]{1,2,0:T(8,128)(2,1)} async-done(((bf16[8,768,128]{1,2,0:T(8,128)(2,1)}), bf16[8,768,128]{1,2,0:T(8,128)(2,1)}, u32[]{:S(2)}, u32[]{:S(2)}) %all-to-all-start.4) | async-done | bytes 1572896 | tf_op jit(solution)/shard_map/all_to_all | solution.py:18
  181.3 2.8 convolution_add_fusion.1
  186.8 3.6 all-to-all-start.5
  191.2 19.7 %all-to-all-done.5 = bf16[8,768,128]{2,1,0:T(8,128)(2,1)S(1)} async-done(((bf16[8,768,128]{2,1,0:T(8,128)(2,1)}), bf16[8,768,128]{2,1,0:T(8,128)(2,1)S(1)}, u32[]{:S(2)}, u32[]{:S(2)}) %all-to-all-start.5) | async-done | bytes 1572896 | tf_op jit(solution)/shard_map/all_to_all | solution.py:51
  212.3 3.6 all-to-all-start.6
  216.7 5.5 all-to-all-done.6
  223.9 4.3 all-to-all-start.7
  232.5 15.2 %all-to-all-done.7 = bf16[8,768,128]{2,1,0:T(8,128)(2,1)} async-done(((bf16[8,768,128]{2,1,0:T(8,128)(2,1)}), bf16[8,768,128]{2,1,0:T(8,128)(2,1)}, u32[]{:S(2)}, u32[]{:S(2)}) %all-to-all-start.7) | async-done | bytes 1572896 | tf_op jit(solution)/shard_map/all_to_all | solution.py:18
  256.9 3.6 all-to-all-start.8
  260.6 20.5 %all-to-all-done.8 = bf16[8,768,128]{2,1,0:T(8,128)(2,1)S(1)} async-done(((bf16[8,768,128]{2,1,0:T(8,128)(2,1)}), bf16[8,768,128]{2,1,0:T(8,128)(2,1)S(1)}, u32[]{:S(2)}, u32[]{:S(2)}) %all-to-all-start.8) | async-done | bytes 1572896 | tf_op jit(solution)/shard_map/all_to_all | solution.py:51
  282.4 3.6 all-to-all-start.9
  286.2 6.1 all-to-all-done.9
  294.2 4.3 all-to-all-start.10
  298.6 2.7 fusion.130
  305.1 12.8 %all-to-all-done.10 = bf16[8,768,128]{1,2,0:T(8,128)(2,1)} async-done(((bf16[8,768,128]{1,2,0:T(8,128)(2,1)}), bf16[8,768,128]{1,2,0:T(8,128)(2,1)}, u32[]{:S(2)}, u32[]{:S(2)}) %all-to-all-start.10) | async-done | bytes 1572896 | tf_op jit(solution)/shard_map/all_to_all | solution.py:18
  318.0 2.8 convolution_add_fusion
  320.9 2.7 fusion.122
  324.9 25.3 %all_to_all.123 = bf16[8,768,128]{2,1,0:T(8,128)(2,1)} all-to-all(bf16[8,768,128]{2,1,0:T(8,128)(2,1)S(1)} %bitcast.506), channel_id=1, replica_groups=mesh['section'=2,'dp'=8,'tensor'=8] {'tensor'}, dimensions={0} | all-to-all | bytes 3145728 | tf_op jit(solution)/shard_map/all_to_all | solution.py:51
  352.8 8.7 %all_to_all.124 = f32[8,1,1536]{2,1,0:T(1,128)S(1)} all-to-all(f32[8,1,1536]{2,1,0:T(1,128)S(1)} %broadcast_in_dim.200), channel_id=1, replica_groups=mesh['section'=2,'dp'=8,'tensor'=8] {'tensor'}, dimensions={0} | all-to-all | bytes 98304 | tf_op jit(solution)/shard_map/all_to_all | solution.py:18
  365.2 29.8 %all_to_all.125 = bf16[8,768,128]{2,1,0:T(8,128)(2,1)S(1)} all-to-all(bf16[8,768,128]{2,1,0:T(8,128)(2,1)S(1)} %broadcast_in_dim.201), channel_id=1, replica_groups=mesh['section'=2,'dp'=8,'tensor'=8] {'tensor'}, dimensions={0} | all-to-all | bytes 3145728 | tf_op jit(solution)/shard_map/all_to_all | solution.py:18
  408.5 21.3 %all_to_all.126 = bf16[8,768,128]{2,1,0:T(8,128)(2,1)S(1)} all-to-all(bf16[8,768,128]{2,1,0:T(8,128)(2,1)S(1)} %bitcast.507), channel_id=1, replica_groups=mesh['section'=2,'dp'=8,'tensor'=8] {'tensor'}, dimensions={0} | all-to-all | bytes 3145728 | tf_op jit(solution)/shard_map/all_to_all | solution.py:51
  432.3 8.8 %all_to_all.127 = f32[8,1,1536]{2,1,0:T(1,128)S(1)} all-to-all(f32[8,1,1536]{2,1,0:T(1,128)S(1)} %broadcast_in_dim.202), channel_id=1, replica_groups=mesh['section'=2,'dp'=8,'tensor'=8] {'tensor'}, dimensions={0} | all-to-all | bytes 98304 | tf_op jit(solution)/shard_map/all_to_all | solution.py:18
  443.7 18.7 %all_to_all.128 = bf16[8,768,128]{2,1,0:T(8,128)(2,1)S(1)} all-to-all(bf16[8,768,128]{2,1,0:T(8,128)(2,1)S(1)} %broadcast_in_dim.203), channel_id=1, replica_groups=mesh['section'=2,'dp'=8,'tensor'=8] {'tensor'}, dimensions={0} | all-to-all | bytes 3145728 | tf_op jit(solution)/shard_map/all_to_all | solution.py:18
  462.5 4.0 fusion.135
  469.0 4.7 all-to-all-start.18
  474.9 3.6 convolution_convert_fusion.8
  480.9 3.1 fusion.34
  493.3 5.7 all-to-all-start.19
  502.1 3.2 all-to-all-done.19
  508.2 4.4 all-to-all-start.20
  516.9 3.2 concatenate.135
  522.3 3.6 convolution_convert_fusion.9
  530.1 3.0 fusion.33
  538.9 4.0 bitcast_reduce_fusion
  542.9 4.2 multiply_reduce_fusion
  550.2 2.8 copy.294
  556.0 5.7 all-to-all-start.21
  570.5 2.7 maximum_dynamic-update-slice_fusion.2
  586.0 5.8 all-to-all-start.11
  592.0 13.6 %all-to-all-done.11 = bf16[8,768,128]{2,1,0:T(8,128)(2,1)} async-done(((bf16[8,768,128]{2,1,0:T(8,128)(2,1)}), bf16[8,768,128]{2,1,0:T(8,128)(2,1)}, u32[]{:S(2)}, u32[]{:S(2)}) %all-to-all-start.11) | async-done | bytes 1572896 | tf_op jit(solution)/shard_map/all_to_all | solution.py:51
  606.2 3.6 all-to-all-start.22
  612.3 4.1 all-to-all-done.22
  616.5 3.8 fusion.47
  620.3 2.6 collective-permute-start.3
  624.4 3.4 fusion.64
  627.8 6.1 collective-permute-start.2
  634.0 6.2 collective-permute-done.3
  641.1 5.5 collective-permute-done.2
  648.1 39.2 %reduce-scatter.2.cloned.1.call-done = bf16[1552,128]{1,0:T(8,128)(2,1)} async-done(((bf16[24832,128]{1,0:T(8,128)(2,1)}), bf16[1552,128]{1,0:T(8,128)(2,1)}) %reduce-scatter.2.cloned.1.call-update) | async-done | bytes 397328 | tf_op jit(solution)/shard_map/reduce_scatter | solution.py:428
  (467 shorter events, 170.1 us)
Async XLA Ops:
  7.2 49.7 %all-gather.5.cloned.1.call-start = ((), (), s32[]{:S(2)}) async-start(), calls=%async_computation.25 | async-start | bytes 3575808 | tf_op jit(solution)/shard_map/all_gather | solution.py:453
  9.0 17.1 %copy-start.8 = (f32[2,1,768,128]{3,2,1,0:T(8,128)S(1)}, f32[2,1,768,128]{3,2,1,0:T(8,128)}, u32[]{:S(2)}) copy-start(f32[2,1,768,128]{3,2,1,0:T(8,128)} %param.14) | copy-start | bytes 2359300
  12.8 12.4 %collective-permute-start = (bf16[1552,128]{1,0:T(8,128)(2,1)S(1)}, bf16[1552,128]{1,0:T(8,128)(2,1)S(1)}, u32[]{:S(2)}, u32[]{:S(2)}) collective-permute-start(bf16[1552,128]{1,0:T(8,128)(2,1)S(1)} %bitcast.564), channel_id=1, source_target_pairs={{0,64},{64,0},{1,65},{65,1},{2,66},{66,2},{3,67},{67,3},{4,68},{68... | collective-permute-start | bytes 1191944 | tf_op jit(solution)/shard_map/ppermute | solution.py:452
  27.2 12.8 %all-to-all-start = ((f32[8,1,1536]{2,1,0:T(1,128)}), f32[8,1,1536]{2,1,0:T(1,128)S(1)}, u32[]{:S(2)}, u32[]{:S(2)}) async-start(f32[8,1,1536]{2,1,0:T(1,128)} %broadcast_in_dim.189), calls=%async_computation | async-start | bytes 98304 | tf_op jit(solution)/shard_map/all_to_all | solution.py:18
  60.5 43.1 %all-to-all-start.1 = ((bf16[8,2,768,128]{3,2,1,0:T(8,128)(2,1)}), bf16[8,2,768,128]{3,2,1,0:T(8,128)(2,1)}, u32[]{:S(2)}, u32[]{:S(2)}) async-start(bf16[8,2,768,128]{3,2,1,0:T(8,128)(2,1)} %broadcast_in_dim.191), calls=%async_computation.1 | async-start | bytes 6291456 | tf_op jit(solution)/shard_map/all_to_all | solution.py:18
  68.2 44.6 %copy-start.77 = (f32[2,64]{1,0:T(2,128)}, f32[2,64]{1,0:T(2,128)S(1)}, u32[]{:S(2)}) copy-start(f32[2,64]{1,0:T(2,128)S(1)} %reshape.2098) | copy-start | bytes 1540
  68.3 46.8 %copy-start.87 = (f32[2,64]{1,0:T(2,128)}, f32[2,64]{1,0:T(2,128)S(1)}, u32[]{:S(2)}) copy-start(f32[2,64]{1,0:T(2,128)S(1)} %reshape.2097) | copy-start | bytes 1540
  119.7 24.2 %all-to-all-start.2 = ((bf16[8,768,128]{2,1,0:T(8,128)(2,1)}), bf16[8,768,128]{2,1,0:T(8,128)(2,1)S(1)}, u32[]{:S(2)}, u32[]{:S(2)}) async-start(bf16[8,768,128]{2,1,0:T(8,128)(2,1)} %bitcast.487), calls=%async_computation.2 | async-start | bytes 3145728 | tf_op jit(solution)/shard_map/all_to_all | solution.py:51
  123.3 67.1 %all-gather.7.cloned.1.call-start = ((), (), s32[]{:S(2)}) async-start(), calls=%async_computation.26 | async-start | bytes 3575808 | tf_op jit(solution)/shard_map/all_gather | solution.py:454
  124.1 20.3 %copy-start.83 = (f32[128]{0:T(128)}, f32[128]{0:T(128)S(1)}, u32[]{:S(2)}) copy-start(f32[128]{0:T(128)S(1)} %reshape.2099) | copy-start | bytes 1540
  145.5 9.9 %all-to-all-start.3 = ((f32[8,1,1536]{2,1,0:T(1,128)}), f32[8,1,1536]{2,1,0:T(1,128)S(1)}, u32[]{:S(2)}, u32[]{:S(2)}) async-start(f32[8,1,1536]{2,1,0:T(1,128)} %broadcast_in_dim.194), calls=%async_computation.3 | async-start | bytes 98304 | tf_op jit(solution)/shard_map/all_to_all | solution.py:18
  149.2 8.0 %copy-start.67 = (f32[128]{0:T(128)}, f32[128]{0:T(128)S(1)}, u32[]{:S(2)}) copy-start(f32[128]{0:T(128)S(1)} %reshape.2100) | copy-start | bytes 1540
  157.2 24.1 %all-to-all-start.4 = ((bf16[8,768,128]{1,2,0:T(8,128)(2,1)}), bf16[8,768,128]{1,2,0:T(8,128)(2,1)}, u32[]{:S(2)}, u32[]{:S(2)}) async-start(bf16[8,768,128]{1,2,0:T(8,128)(2,1)} %broadcast_in_dim.195), calls=%async_computation.4 | async-start | bytes 3145728 | tf_op jit(solution)/shard_map/all_to_all | solution.py:18
  186.8 24.2 %all-to-all-start.5 = ((bf16[8,768,128]{2,1,0:T(8,128)(2,1)}), bf16[8,768,128]{2,1,0:T(8,128)(2,1)S(1)}, u32[]{:S(2)}, u32[]{:S(2)}) async-start(bf16[8,768,128]{2,1,0:T(8,128)(2,1)} %bitcast.485), calls=%async_computation.5 | async-start | bytes 3145728 | tf_op jit(solution)/shard_map/all_to_all | solution.py:51
  190.4 21.0 %copy-start.85 = (f32[128]{0:T(128)}, f32[128]{0:T(128)S(1)}, u32[]{:S(2)}) copy-start(f32[128]{0:T(128)S(1)} %reshape.2103) | copy-start | bytes 1540
  211.2 12.8 %copy-start.17 = (f32[768,128]{1,0:T(8,128)}, f32[768,128]{1,0:T(8,128)S(1)}, u32[]{:S(2)}) copy-start(f32[768,128]{1,0:T(8,128)S(1)} %convert_reduce_fusion.6) | copy-start | bytes 1179652
  211.5 69.9 %copy-start.2 = (f32[768,128]{1,0:T(8,128)}, f32[768,128]{1,0:T(8,128)S(1)}, u32[]{:S(2)}) copy-start(f32[768,128]{1,0:T(8,128)S(1)} %get-tuple-element.206) | copy-start | bytes 1179652
  212.3 9.9 %all-to-all-start.6 = ((f32[8,1,1536]{2,1,0:T(1,128)}), f32[8,1,1536]{2,1,0:T(1,128)S(1)}, u32[]{:S(2)}, u32[]{:S(2)}) async-start(f32[8,1,1536]{2,1,0:T(1,128)} %broadcast_in_dim.196), calls=%async_computation.6 | async-start | bytes 98304 | tf_op jit(solution)/shard_map/all_to_all | solution.py:18
  216.6 7.3 %copy-start.69 = (f32[128]{0:T(128)}, f32[128]{0:T(128)S(1)}, u32[]{:S(2)}) copy-start(f32[128]{0:T(128)S(1)} %reshape.2104) | copy-start | bytes 1540
  223.9 23.8 %all-to-all-start.7 = ((bf16[8,768,128]{2,1,0:T(8,128)(2,1)}), bf16[8,768,128]{2,1,0:T(8,128)(2,1)}, u32[]{:S(2)}, u32[]{:S(2)}) async-start(bf16[8,768,128]{2,1,0:T(8,128)(2,1)} %broadcast_in_dim.197), calls=%async_computation.7 | async-start | bytes 3145728 | tf_op jit(solution)/shard_map/all_to_all | solution.py:18
  229.6 20.5 %copy-start.79 = (f32[2,64]{1,0:T(2,128)}, f32[2,64]{1,0:T(2,128)S(1)}, u32[]{:S(2)}) copy-start(f32[2,64]{1,0:T(2,128)S(1)} %reshape.2107) | copy-start | bytes 1540
  229.7 22.7 %copy-start.89 = (f32[2,64]{1,0:T(2,128)}, f32[2,64]{1,0:T(2,128)S(1)}, u32[]{:S(2)}) copy-start(f32[2,64]{1,0:T(2,128)S(1)} %reshape.2106) | copy-start | bytes 1540
  232.5 17.4 %copy-start.52 = (bf16[1024,3,128]{0,2,1:T(8,128)(2,1)}, bf16[1024,3,128]{0,2,1:T(8,128)(2,1)S(1)}, u32[]{:S(2)}) copy-start(bf16[1024,3,128]{0,2,1:T(8,128)(2,1)S(1)} %copy.259) | copy-start | bytes 2359300
  256.9 24.2 %all-to-all-start.8 = ((bf16[8,768,128]{2,1,0:T(8,128)(2,1)}), bf16[8,768,128]{2,1,0:T(8,128)(2,1)S(1)}, u32[]{:S(2)}, u32[]{:S(2)}) async-start(bf16[8,768,128]{2,1,0:T(8,128)(2,1)} %bitcast.483), calls=%async_computation.8 | async-start | bytes 3145728 | tf_op jit(solution)/shard_map/all_to_all | solution.py:51
  260.6 21.0 %copy-start.72 = (f32[128]{0:T(128)}, f32[128]{0:T(128)S(1)}, u32[]{:S(2)}) copy-start(f32[128]{0:T(128)S(1)} %reshape.2108) | copy-start | bytes 1540
  281.7 12.5 %copy-start.13 = (f32[768,128]{1,0:T(8,128)}, f32[768,128]{1,0:T(8,128)S(1)}, u32[]{:S(2)}) copy-start(f32[768,128]{1,0:T(8,128)S(1)} %get-tuple-element.205) | copy-start | bytes 1179652
  282.4 9.9 %all-to-all-start.9 = ((f32[8,1,1536]{2,1,0:T(1,128)}), f32[8,1,1536]{2,1,0:T(1,128)S(1)}, u32[]{:S(2)}, u32[]{:S(2)}) async-start(f32[8,1,1536]{2,1,0:T(1,128)} %broadcast_in_dim.198), calls=%async_computation.9 | async-start | bytes 98304 | tf_op jit(solution)/shard_map/all_to_all | solution.py:18
  286.2 65.8 %copy-start.65 = (f32[128]{0:T(128)}, f32[128]{0:T(128)S(1)}, u32[]{:S(2)}) copy-start(f32[128]{0:T(128)S(1)} %reshape.2109) | copy-start | bytes 1540
  294.2 23.8 %all-to-all-start.10 = ((bf16[8,768,128]{1,2,0:T(8,128)(2,1)}), bf16[8,768,128]{1,2,0:T(8,128)(2,1)}, u32[]{:S(2)}, u32[]{:S(2)}) async-start(bf16[8,768,128]{1,2,0:T(8,128)(2,1)} %broadcast_in_dim.199), calls=%async_computation.10 | async-start | bytes 3145728 | tf_op jit(solution)/shard_map/all_to_all | solution.py:18
  324.9 72.0 %slice-start.2 = ((s8[4718592]{0:T(1024)(128)(4,1)}), s8[524288]{0:T(1024)(128)(4,1)S(1)}, s32[]{:S(2)}) async-start(s8[4718592]{0:T(1024)(128)(4,1)} %bitcast.499), calls=%async_computation.29 | async-start | bytes 1048576
  350.2 12.7 %copy-start.23 = (f32[2,1,768,128]{3,2,1,0:T(8,128)S(1)}, f32[2,1,768,128]{3,2,1,0:T(8,128)}, u32[]{:S(2)}) copy-start(f32[2,1,768,128]{3,2,1,0:T(8,128)} %param.15) | copy-start | bytes 2359300
  352.0 13.0 %copy-start.4 = (f32[768,128]{1,0:T(8,128)}, f32[768,128]{1,0:T(8,128)S(1)}, u32[]{:S(2)}) copy-start(f32[768,128]{1,0:T(8,128)S(1)} %convert_reduce_fusion.3) | copy-start | bytes 1179652
  362.9 33.9 %slice-start.3 = ((s8[4718592]{0:T(1024)(128)(4,1)}), s8[4194304]{0:T(1024)(128)(4,1)S(1)}, s32[]{:S(2)}) async-start(s8[4718592]{0:T(1024)(128)(4,1)} %bitcast.499), calls=%async_computation.30 | async-start | bytes 8388608
  443.7 18.7 %copy-start.96 = (f32[768,512]{1,0:T(8,128)S(1)}, f32[768,512]{1,0:T(8,128)}, u32[]{:S(2)}) copy-start(f32[768,512]{1,0:T(8,128)} %copy-done.95) | copy-start | bytes 4718596
  469.0 21.5 %all-to-all-start.18 = ((bf16[8,768,128]{2,1,0:T(8,128)(2,1)}), bf16[8,768,128]{2,1,0:T(8,128)(2,1)}, u32[]{:S(2)}, u32[]{:S(2)}) async-start(bf16[8,768,128]{2,1,0:T(8,128)(2,1)} %bitcast.505), calls=%async_computation.18 | async-start | bytes 3145728 | tf_op jit(solution)/shard_map/all_to_all | solution.py:51
  492.1 13.2 %copy-start.6 = (f32[768,128]{1,0:T(8,128)}, f32[768,128]{1,0:T(8,128)S(1)}, u32[]{:S(2)}) copy-start(f32[768,128]{1,0:T(8,128)S(1)} %convert_reduce_fusion.1) | copy-start | bytes 1179652
  493.3 12.0 %all-to-all-start.19 = ((f32[8,1,1536]{2,1,0:T(1,128)}), f32[8,1,1536]{2,1,0:T(1,128)S(1)}, u32[]{:S(2)}, u32[]{:S(2)}) async-start(f32[8,1,1536]{2,1,0:T(1,128)} %broadcast_in_dim.204), calls=%async_computation.19 | async-start | bytes 98304 | tf_op jit(solution)/shard_map/all_to_all | solution.py:18
  508.2 4.5 copy-start.57
  508.2 4.5 copy-start.58
  508.2 4.5 copy-start.59
  508.2 28.6 %all-to-all-start.20 = ((bf16[8,768,128]{2,1,0:T(8,128)(2,1)}), bf16[8,768,128]{2,1,0:T(8,128)(2,1)}, u32[]{:S(2)}, u32[]{:S(2)}) async-start(bf16[8,768,128]{2,1,0:T(8,128)(2,1)} %broadcast_in_dim.205), calls=%async_computation.20 | async-start | bytes 3145728 | tf_op jit(solution)/shard_map/all_to_all | solution.py:18
  534.3 4.6 copy-start.62
  538.9 8.3 %slice-start = ((s8[4718592]{0:T(1024)(128)(4,1)}), s8[4194304]{0:T(1024)(128)(4,1)S(1)}, s32[]{:S(2)}) async-start(s8[4718592]{0:T(1024)(128)(4,1)} %bitcast.497), calls=%async_computation.27 | async-start | bytes 8388608
  542.9 4.3 slice-start.1
  556.0 5.8 copy-start.54
  556.0 22.1 %all-to-all-start.21 = ((bf16[8,768,128]{2,1,0:T(8,128)(2,1)}), bf16[8,768,128]{2,1,0:T(8,128)(2,1)S(1)}, u32[]{:S(2)}, u32[]{:S(2)}) async-start(bf16[8,768,128]{2,1,0:T(8,128)(2,1)} %bitcast.504), calls=%async_computation.21 | async-start | bytes 3145728 | tf_op jit(solution)/shard_map/all_to_all | solution.py:51
  561.7 125.6 %reduce-scatter.2.cloned.1.call-start = ((), (), s32[]{:S(2)}) async-start(), calls=%async_computation.24 | async-start | bytes 6754304 | tf_op jit(solution)/shard_map/reduce_scatter | solution.py:428
  586.0 5.9 copy-start.74
  586.0 19.6 %all-to-all-start.11 = ((bf16[8,768,128]{2,1,0:T(8,128)(2,1)}), bf16[8,768,128]{2,1,0:T(8,128)(2,1)}, u32[]{:S(2)}, u32[]{:S(2)}) async-start(bf16[8,768,128]{2,1,0:T(8,128)(2,1)} %bitcast.481), calls=%async_computation.11 | async-start | bytes 3145728 | tf_op jit(solution)/shard_map/all_to_all | solution.py:51
  591.8 24.6 %copy-start.5 = (f32[768,128]{1,0:T(8,128)S(1)}, f32[768,128]{1,0:T(8,128)}, u32[]{:S(2)}) copy-start(f32[768,128]{1,0:T(8,128)} %copy-done.4) | copy-start | bytes 1179652
  591.8 24.6 %copy-start.7 = (f32[768,128]{1,0:T(8,128)S(1)}, f32[768,128]{1,0:T(8,128)}, u32[]{:S(2)}) copy-start(f32[768,128]{1,0:T(8,128)} %copy-done.6) | copy-start | bytes 1179652
  591.8 24.6 %copy-start.16 = (f32[768,128]{1,0:T(8,128)S(1)}, f32[768,128]{1,0:T(8,128)}, u32[]{:S(2)}) copy-start(f32[768,128]{1,0:T(8,128)} %copy-done.15) | copy-start | bytes 1179652
  591.8 24.6 %copy-start.18 = (f32[768,128]{1,0:T(8,128)S(1)}, f32[768,128]{1,0:T(8,128)}, u32[]{:S(2)}) copy-start(f32[768,128]{1,0:T(8,128)} %copy-done.17) | copy-start | bytes 1179652
  591.9 24.6 %copy-start.66 = (f32[128]{0:T(128)S(1)}, f32[128]{0:T(128)}, u32[]{:S(2)}) copy-start(f32[128]{0:T(128)} %copy-done.65) | copy-start | bytes 1540
  591.9 24.6 %copy-start.71 = (f32[128]{0:T(128)S(1)}, f32[128]{0:T(128)}, u32[]{:S(2)}) copy-start(f32[128]{0:T(128)} %copy-done.69) | copy-start | bytes 1540
  591.9 24.6 %copy-start.73 = (f32[128]{0:T(128)S(1)}, f32[128]{0:T(128)}, u32[]{:S(2)}) copy-start(f32[128]{0:T(128)} %copy-done.72) | copy-start | bytes 1540
  591.9 24.6 %copy-start.84 = (f32[128]{0:T(128)S(1)}, f32[128]{0:T(128)}, u32[]{:S(2)}) copy-start(f32[128]{0:T(128)} %copy-done.83) | copy-start | bytes 1540
  591.9 24.6 %copy-start.86 = (f32[128]{0:T(128)S(1)}, f32[128]{0:T(128)}, u32[]{:S(2)}) copy-start(f32[128]{0:T(128)} %copy-done.85) | copy-start | bytes 1540
  606.2 10.1 %all-to-all-start.22 = ((f32[8,1,1536]{2,1,0:T(1,128)}), f32[8,1,1536]{2,1,0:T(1,128)S(1)}, u32[]{:S(2)}, u32[]{:S(2)}) async-start(f32[8,1,1536]{2,1,0:T(1,128)} %broadcast_in_dim.206), calls=%async_computation.22 | async-start | bytes 98304 | tf_op jit(solution)/shard_map/all_to_all | solution.py:18
  616.5 7.8 %copy-start.24 = (f32[2,1,768,128]{3,2,1,0:T(8,128)S(1)}, f32[2,1,768,128]{3,2,1,0:T(8,128)}, u32[]{:S(2)}) copy-start(f32[2,1,768,128]{3,2,1,0:T(8,128)} %param.15) | copy-start | bytes 2359300
  620.3 19.9 %collective-permute-start.3 = (f32[1,768,128]{2,1,0:T(8,128)S(1)}, f32[1,768,128]{2,1,0:T(8,128)S(1)}, u32[]{:S(2)}, u32[]{:S(2)}) collective-permute-start(f32[1,768,128]{2,1,0:T(8,128)S(1)} %get-tuple-element.203), channel_id=1, source_target_pairs={{0,64},{64,0},{1,65},{65,1},{2,66},{66,2},{3,67},{67,3},{4,68},{68... | collective-permute-start | bytes 1179656 | tf_op jit(solution)/shard_map/ppermute | solution.py:507
  622.9 4.8 copy-start.27
  622.9 24.3 %collective-permute-start.1 = (f32[1,768,128]{2,1,0:T(8,128)S(1)}, f32[1,768,128]{2,1,0:T(8,128)S(1)}, u32[]{:S(2)}, u32[]{:S(2)}) collective-permute-start(f32[1,768,128]{2,1,0:T(8,128)S(1)} %get-tuple-element.204), channel_id=1, source_target_pairs={{64,0},{65,1},{66,2},{67,3},{68,4},{69,5},{70,6},{71,7},{72,8},{73... | collective-permute-start | bytes 1179656 | tf_op jit(solution)/shard_map/ppermute | solution.py:503
  627.8 18.8 %collective-permute-start.2 = (f32[1,768,128]{2,1,0:T(8,128)S(1)}, f32[1,768,128]{2,1,0:T(8,128)S(1)}, u32[]{:S(2)}, u32[]{:S(2)}) collective-permute-start(f32[1,768,128]{2,1,0:T(8,128)S(1)} %fusion.80), channel_id=1, source_target_pairs={{0,64},{1,65},{2,66},{3,67},{4,68},{5,69},{6,70},{7,71},{8,72},{9,... | collective-permute-start | bytes 1179656 | tf_op jit(solution)/shard_map/ppermute | solution.py:504
  (62 other events, 125.9 us)
Sparse Core Ops, SparseCore 0:
  26.3 30.4 all-gather.4
  126.4 27.8 all-gather.6
  580.9 106.4 reduce-scatter.1

commit v11 on v9

--- a/solution.py
+++ b/solution.py
@@ -46,8 +46,7 @@
     return jnp.moveaxis(array.reshape(*before, peers, -1, *after), dim, 0)
 
 
-def summed_on_arrival(array, axis, dim):
-    parts = in_blocks(array, dim, lax.axis_size(axis))
+def summed_on_arrival(parts, axis):
     arrived = lax.all_to_all(parts, axis, split_axis=0, concat_axis=0, tiled=True)
     return arrived.astype(jnp.float32).sum(axis=0)
 
@@ -97,8 +96,8 @@
 
 
 def norm_backward(partial_term, normal_part, inv_scale, gain):
-    width_all = partial_term.shape[1]
-    d_normed = summed_on_arrival(partial_term.astype(jnp.bfloat16), "tensor", 1)
+    width_all = partial_term.shape[0] * partial_term.shape[2]
+    d_normed = summed_on_arrival(partial_term.astype(jnp.bfloat16), "tensor")
     gain_grad = jnp.sum(d_normed * normal_part, axis=0)
     offset_grad = jnp.sum(d_normed, axis=0)
     scaled = d_normed * gain
@@ -111,8 +110,15 @@
     return (stream_grad, gain_grad, offset_grad)
 
 
+def blocked_product(spec, rows, weight, dim):
+    peers = lax.axis_size("tensor")
+    shape = weight.shape
+    blocked = weight.reshape(*shape[:dim], peers, shape[dim] // peers, *shape[dim + 1 :])
+    return jnp.einsum(spec, rows, blocked, preferred_element_type=jnp.float32)
+
+
 def branch_sum(partial_term):
-    return summed_on_arrival(partial_term.astype(jnp.bfloat16), "tensor", 1)
+    return summed_on_arrival(partial_term.astype(jnp.bfloat16), "tensor")
 
 
 def branch_grad(stream_grad):
@@ -251,7 +257,7 @@
     )
     residual = (
         stream_rows
-        + branch_sum(jnp.dot(mixed_rows, output_weight, preferred_element_type=jnp.float32))
+        + branch_sum(blocked_product("nf,ftd->tnd", mixed_rows, output_weight, 1))
         + output_bias
     )
     normed_two, normal_two, inv_two, _ = norm_forward(residual, gain_second, shift_second)
@@ -261,7 +267,7 @@
     hidden = gelu_tanh(hidden_pre).astype(jnp.bfloat16)
     result = (
         residual
-        + branch_sum(jnp.dot(hidden, contract_weight, preferred_element_type=jnp.float32))
+        + branch_sum(blocked_product("nf,ftd->tnd", hidden, contract_weight, 1))
         + contract_bias
     )
     kept_values = (
@@ -331,7 +337,7 @@
         "nd,nf->df", normed_two, pre_grad, preferred_element_type=jnp.float32
     )
     second_grad, gain_second_grad, shift_second_grad = norm_backward(
-        jnp.einsum("nf,df->nd", pre_grad, expand_weight, preferred_element_type=jnp.float32),
+        blocked_product("nf,tdf->tnd", pre_grad, expand_weight, 0),
         normal_two,
         inv_two,
         gain_second,
@@ -348,7 +354,7 @@
         width_part,
     )
     first_grad, gain_first_grad, shift_first_grad = norm_backward(
-        jnp.einsum("ncf,dcf->nd", packed_grad, packed_weight, preferred_element_type=jnp.float32),
+        blocked_product("ncf,tdcf->tnd", packed_grad, packed_weight, 0),
         normal_one,
         inv_one,
         gain_first,

time: 713 us -> 762 us (1.069)
  blocking collectives: 113 us -> 68.1 us
  local copies, waits for them, and re-layouts: 103 us -> 133 us
  waiting for transfers between devices: 246 us -> 274 us
  starting transfers between devices: 94.9 us -> 114 us
  matrix products: 71.6 us -> 85.1 us
    all_to_all x4 -> x2, blocking collectives: 66 us -> 18 us  [sent_to_all(): return lax.all_to_all(copies, axis, split_axis=0, concat_axis=0, tiled=True)]
    all_to_all x11 -> x13, waiting for transfers between devices: 101 us -> 127 us  [sent_to_all(): return lax.all_to_all(copies, axis, split_axis=0, concat_axis=0, tiled=True)]
    all_to_all x11 -> x13, starting transfers between devices: 49.6 us -> 67 us  [sent_to_all(): return lax.all_to_all(copies, axis, split_axis=0, concat_axis=0, tiled=True)]
    unnamed x220 -> x316, local copies, waits for them, and re-layouts: 15 us -> 30.2 us
    reshape x8 -> x0, local copies, waits for them, and re-layouts: 9.43 us -> none  [in_blocks(): return jnp.moveaxis(array.reshape(*before, peers, -1, *after), dim, 0)]
  transfers between devices with their start and end apart: 25 -> 27, of which waited for: 21 -> 22; matrix products, arithmetic and copies ran while one was open for 16% -> 19% of each run, Pallas kernels for 0% -> 0%
where the time goes in v11:
time: 762 us; the launch traced here: 748 us
  waiting for transfers between devices  274 us (36%)
  local copies, waits for them, and re-layouts  133 us (17%)
  starting transfers between devices  114 us (15%)
  matrix products  85.1 us (11%)
  blocking collectives  68.1 us (9%)
  other arithmetic  58.7 us (8%)
  between operations  16.1 us (2%)
    all_to_all x13, waiting for transfers between devices, sent_to_all(): return lax.all_to_all(copies, axis, split_axis=0, concat_axis=0, tiled=True)  127 us
    all_to_all x6, waiting for transfers between devices, summed_on_arrival(): lax.all_to_all(parts, axis, split_axis=0, concat_axis=0, tiled=True)  76.7 us
    all_to_all x13, starting transfers between devices, sent_to_all(): return lax.all_to_all(copies, axis, split_axis=0, concat_axis=0, tiled=True)  67 us
    all_to_all x2, blocking collectives, summed_on_arrival(): lax.all_to_all(parts, axis, split_axis=0, concat_axis=0, tiled=True)  50.1 us
    reduce_scatter x1, waiting for transfers between devices, sum_at_end(): lax.psum_scatter(rows.reshape(-1, 128), ('section', 'dp'), scatter_dimens...  31 us
    unnamed x316, local copies, waits for them, and re-layouts  30.2 us
    all_to_all x6, starting transfers between devices, summed_on_arrival(): lax.all_to_all(parts, axis, split_axis=0, concat_axis=0, tiled=True)  27.9 us
    all_to_all x2, blocking collectives, sent_to_all(): return lax.all_to_all(copies, axis, split_axis=0, concat_axis=0, tiled=True)  18 us
  transfers between devices with their start and end apart: 27, of which 22 were waited for; matrix products, arithmetic and copies ran while one was open for 19% of the time, Pallas kernels for 0%

profile of v11, /device:TPU:0, one launch (start us, length us, event | category | flops | bytes accessed | tf_op | source)
XLA Modules:
  0.0 748.4 jit_solution(8208169959730828056)
XLA Ops:
  12.8 3.2 collective-permute-start
  16.0 9.2 %collective-permute-done = bf16[1552,128]{1,0:T(8,128)(2,1)S(1)} collective-permute-done((bf16[1552,128]{1,0:T(8,128)(2,1)S(1)}, bf16[1552,128]{1,0:T(8,128)(2,1)S(1)}, u32[]{:S(2)}, u32[]{:S(2)}) %collective-permute-start) | collective-permute-done | bytes 397344 | tf_op jit(solution)/shard_map/ppermute | solution.py:458
  27.8 6.5 all-to-all-start
  34.5 6.1 all-to-all-done
  40.6 16.3 %all-gather.5.cloned.1.call-done = bf16[12416,128]{1,0:T(8,128)(2,1)} async-done(((bf16[1552,128]{1,0:T(8,128)(2,1)}), bf16[12416,128]{1,0:T(8,128)(2,1)}) %all-gather.5.cloned.1.call-update) | async-done | bytes 3178512 | tf_op jit(solution)/shard_map/all_gather | solution.py:459
  61.1 5.3 all-to-all-start.1
  71.6 32.6 %all-to-all-done.1 = bf16[8,2,768,128]{3,2,1,0:T(8,128)(2,1)} async-done(((bf16[8,2,768,128]{3,2,1,0:T(8,128)(2,1)}), bf16[8,2,768,128]{3,2,1,0:T(8,128)(2,1)}, u32[]{:S(2)}, u32[]{:S(2)}) %all-to-all-start.1) | async-done | bytes 3145760 | tf_op jit(solution)/shard_map/all_to_all | solution.py:18
  104.2 4.7 copy.280
  108.9 3.4 fusion.149
  120.6 3.6 all-to-all-start.2
  125.1 19.8 %all-to-all-done.2 = bf16[8,768,128]{1,2,0:T(8,128)(2,1)S(1)} async-done(((bf16[8,768,128]{1,2,0:T(8,128)(2,1)}), bf16[8,768,128]{1,2,0:T(8,128)(2,1)S(1)}, u32[]{:S(2)}, u32[]{:S(2)}) %all-to-all-start.2) | async-done | bytes 1572896 | tf_op jit(solution)/shard_map/all_to_all | solution.py:50
  146.0 3.6 all-to-all-start.3
  149.8 6.1 all-to-all-done.3
  157.4 4.5 all-to-all-start.4
  169.6 11.9 %all-to-all-done.4 = bf16[8,768,128]{1,2,0:T(8,128)(2,1)} async-done(((bf16[8,768,128]{1,2,0:T(8,128)(2,1)}), bf16[8,768,128]{1,2,0:T(8,128)(2,1)}, u32[]{:S(2)}, u32[]{:S(2)}) %all-to-all-start.4) | async-done | bytes 1572896 | tf_op jit(solution)/shard_map/all_to_all | solution.py:18
  181.5 2.8 convolution_add_fusion.1
  187.8 3.6 all-to-all-start.5
  192.9 19.1 %all-to-all-done.5 = bf16[8,768,128]{1,2,0:T(8,128)(2,1)S(1)} async-done(((bf16[8,768,128]{1,2,0:T(8,128)(2,1)}), bf16[8,768,128]{1,2,0:T(8,128)(2,1)S(1)}, u32[]{:S(2)}, u32[]{:S(2)}) %all-to-all-start.5) | async-done | bytes 1572896 | tf_op jit(solution)/shard_map/all_to_all | solution.py:50
  213.7 3.6 all-to-all-start.6
  219.0 4.6 all-to-all-done.6
  225.4 4.3 all-to-all-start.7
  236.6 12.7 %all-to-all-done.7 = bf16[8,768,128]{2,1,0:T(8,128)(2,1)} async-done(((bf16[8,768,128]{2,1,0:T(8,128)(2,1)}), bf16[8,768,128]{2,1,0:T(8,128)(2,1)}, u32[]{:S(2)}, u32[]{:S(2)}) %all-to-all-start.7) | async-done | bytes 1572896 | tf_op jit(solution)/shard_map/all_to_all | solution.py:18
  258.2 4.3 all-to-all-start.8
  262.6 20.4 %all-to-all-done.8 = bf16[8,768,128]{1,2,0:T(8,128)(2,1)} async-done(((bf16[8,768,128]{1,2,0:T(8,128)(2,1)}), bf16[8,768,128]{1,2,0:T(8,128)(2,1)}, u32[]{:S(2)}, u32[]{:S(2)}) %all-to-all-start.8) | async-done | bytes 1572896 | tf_op jit(solution)/shard_map/all_to_all | solution.py:50
  285.5 3.6 all-to-all-start.9
  289.3 6.1 all-to-all-done.9
  296.9 4.3 all-to-all-start.10
  301.2 2.7 fusion.148
  309.2 11.5 %all-to-all-done.10 = bf16[8,768,128]{1,2,0:T(8,128)(2,1)} async-done(((bf16[8,768,128]{1,2,0:T(8,128)(2,1)}), bf16[8,768,128]{1,2,0:T(8,128)(2,1)}, u32[]{:S(2)}, u32[]{:S(2)}) %all-to-all-start.10) | async-done | bytes 1572896 | tf_op jit(solution)/shard_map/all_to_all | solution.py:18
  320.7 2.8 convolution_add_fusion
  327.3 25.1 %all_to_all.123 = bf16[8,768,128]{1,2,0:T(8,128)(2,1)S(1)} all-to-all(bf16[8,768,128]{1,2,0:T(8,128)(2,1)S(1)} %fusion.28), channel_id=1, replica_groups=mesh['section'=2,'dp'=8,'tensor'=8] {'tensor'}, dimensions={0} | all-to-all | bytes 3145728 | tf_op jit(solution)/shard_map/all_to_all | solution.py:50
  354.5 8.7 %all_to_all.124 = f32[8,1,1536]{2,1,0:T(1,128)S(1)} all-to-all(f32[8,1,1536]{2,1,0:T(1,128)S(1)} %broadcast_in_dim.200), channel_id=1, replica_groups=mesh['section'=2,'dp'=8,'tensor'=8] {'tensor'}, dimensions={0} | all-to-all | bytes 98304 | tf_op jit(solution)/shard_map/all_to_all | solution.py:18
  365.7 12.3 %all-to-all-start.14 = ((bf16[8,768,128]{2,1,0:T(8,128)(2,1)}), bf16[8,768,128]{2,1,0:T(8,128)(2,1)S(1)}, u32[]{:S(2)}, u32[]{:S(2)}) async-start(bf16[8,768,128]{2,1,0:T(8,128)(2,1)} %broadcast_in_dim.201), calls=%async_computation.14 | async-start | bytes 3145728 | tf_op jit(solution)/shard_map/all_to_all | solution.py:18
  380.5 15.4 %all-to-all-done.14 = bf16[8,768,128]{2,1,0:T(8,128)(2,1)S(1)} async-done(((bf16[8,768,128]{2,1,0:T(8,128)(2,1)}), bf16[8,768,128]{2,1,0:T(8,128)(2,1)S(1)}, u32[]{:S(2)}, u32[]{:S(2)}) %all-to-all-start.14) | async-done | bytes 1572896 | tf_op jit(solution)/shard_map/all_to_all | solution.py:18
  397.7 5.1 bitcast_reduce_fusion.2
  402.8 4.2 multiply_reduce_fusion.1
  412.8 25.0 %all_to_all.125 = bf16[8,768,128]{1,2,0:T(8,128)(2,1)S(1)} all-to-all(bf16[8,768,128]{1,2,0:T(8,128)(2,1)S(1)} %fusion.24), channel_id=1, replica_groups=mesh['section'=2,'dp'=8,'tensor'=8] {'tensor'}, dimensions={0} | all-to-all | bytes 3145728 | tf_op jit(solution)/shard_map/all_to_all | solution.py:50
  439.6 9.4 %all_to_all.126 = f32[8,1,1536]{2,1,0:T(1,128)} all-to-all(f32[8,1,1536]{2,1,0:T(1,128)S(1)} %broadcast_in_dim.202), channel_id=1, replica_groups=mesh['section'=2,'dp'=8,'tensor'=8] {'tensor'}, dimensions={0} | all-to-all | bytes 98304 | tf_op jit(solution)/shard_map/all_to_all | solution.py:18
  459.2 4.3 all-to-all-start.17
  466.0 15.3 %all-to-all-done.17 = bf16[8,768,128]{2,1,0:T(8,128)(2,1)} async-done(((bf16[8,768,128]{2,1,0:T(8,128)(2,1)}), bf16[8,768,128]{2,1,0:T(8,128)(2,1)}, u32[]{:S(2)}, u32[]{:S(2)}) %all-to-all-start.17) | async-done | bytes 1572896 | tf_op jit(solution)/shard_map/all_to_all | solution.py:18
  481.3 4.9 fusion.152
  489.4 4.7 all-to-all-start.18
  498.0 3.4 convolution_convert_fusion.8
  503.9 3.1 fusion.34
  518.9 5.7 all-to-all-start.19
  524.5 3.4 fusion.30
  540.4 5.3 all-to-all-start.20
  554.0 2.8 copy.327
  556.7 3.2 concatenate.135
  581.4 4.5 bitcast_reduce_fusion
  585.9 4.2 multiply_reduce_fusion
  599.5 5.8 all-to-all-start.21
  612.7 3.2 concatenate.134
  627.9 3.8 fusion.27
  631.6 5.8 all-to-all-start.11
  637.7 17.4 %all-to-all-done.11 = bf16[8,768,128]{1,2,0:T(8,128)(2,1)} async-done(((bf16[8,768,128]{1,2,0:T(8,128)(2,1)}), bf16[8,768,128]{1,2,0:T(8,128)(2,1)}, u32[]{:S(2)}, u32[]{:S(2)}) %all-to-all-start.11) | async-done | bytes 1572896 | tf_op jit(solution)/shard_map/all_to_all | solution.py:50
  655.8 3.6 all-to-all-start.22
  661.8 3.9 all-to-all-done.22
  669.7 6.1 collective-permute-start.4
  679.3 6.8 collective-permute-start.2
  686.2 5.9 collective-permute-done.3
  693.4 3.4 collective-permute-done.2
  696.8 3.8 collective-permute-done.1
  702.8 31.0 %reduce-scatter.2.cloned.1.call-done = bf16[1552,128]{1,0:T(8,128)(2,1)} async-done(((bf16[24832,128]{1,0:T(8,128)(2,1)}), bf16[1552,128]{1,0:T(8,128)(2,1)}) %reduce-scatter.2.cloned.1.call-update) | async-done | bytes 397328 | tf_op jit(solution)/shard_map/reduce_scatter | solution.py:434
  (564 shorter events, 218.8 us)
Async XLA Ops:
  7.2 49.7 %all-gather.5.cloned.1.call-start = ((), (), s32[]{:S(2)}) async-start(), calls=%async_computation.25 | async-start | bytes 3575808 | tf_op jit(solution)/shard_map/all_gather | solution.py:459
  9.0 17.2 %copy-start.65 = (f32[2,1,768,128]{3,2,1,0:T(8,128)S(1)}, f32[2,1,768,128]{3,2,1,0:T(8,128)}, u32[]{:S(2)}) copy-start(f32[2,1,768,128]{3,2,1,0:T(8,128)} %param.15) | copy-start | bytes 2359300
  12.8 12.4 %collective-permute-start = (bf16[1552,128]{1,0:T(8,128)(2,1)S(1)}, bf16[1552,128]{1,0:T(8,128)(2,1)S(1)}, u32[]{:S(2)}, u32[]{:S(2)}) collective-permute-start(bf16[1552,128]{1,0:T(8,128)(2,1)S(1)} %bitcast.534), channel_id=1, source_target_pairs={{0,64},{64,0},{1,65},{65,1},{2,66},{66,2},{3,67},{67,3},{4,68},{68... | collective-permute-start | bytes 1191944 | tf_op jit(solution)/shard_map/ppermute | solution.py:458
  27.8 12.8 %all-to-all-start = ((f32[8,1,1536]{2,1,0:T(1,128)}), f32[8,1,1536]{2,1,0:T(1,128)S(1)}, u32[]{:S(2)}, u32[]{:S(2)}) async-start(f32[8,1,1536]{2,1,0:T(1,128)} %broadcast_in_dim.190), calls=%async_computation | async-start | bytes 98304 | tf_op jit(solution)/shard_map/all_to_all | solution.py:18
  40.6 17.3 %copy-start.71 = (f32[768]{0:T(1024)}, f32[768]{0:T(1024)S(1)}, u32[]{:S(2)}) copy-start(f32[768]{0:T(1024)S(1)} %get-tuple-element.259) | copy-start | bytes 9220
  40.6 17.3 %copy-start.73 = (f32[768]{0:T(1024)}, f32[768]{0:T(1024)S(1)}, u32[]{:S(2)}) copy-start(f32[768]{0:T(1024)S(1)} %get-tuple-element.260) | copy-start | bytes 9220
  61.1 43.1 %all-to-all-start.1 = ((bf16[8,2,768,128]{3,2,1,0:T(8,128)(2,1)}), bf16[8,2,768,128]{3,2,1,0:T(8,128)(2,1)}, u32[]{:S(2)}, u32[]{:S(2)}) async-start(bf16[8,2,768,128]{3,2,1,0:T(8,128)(2,1)} %broadcast_in_dim.191), calls=%async_computation.1 | async-start | bytes 6291456 | tf_op jit(solution)/shard_map/all_to_all | solution.py:18
  69.0 44.5 %copy-start.113 = (f32[2,64]{1,0:T(2,128)}, f32[2,64]{1,0:T(2,128)S(1)}, u32[]{:S(2)}) copy-start(f32[2,64]{1,0:T(2,128)S(1)} %reshape.2346) | copy-start | bytes 1540
  69.1 46.7 %copy-start.128 = (f32[2,64]{1,0:T(2,128)}, f32[2,64]{1,0:T(2,128)S(1)}, u32[]{:S(2)}) copy-start(f32[2,64]{1,0:T(2,128)S(1)} %reshape.2345) | copy-start | bytes 1540
  120.6 24.2 %all-to-all-start.2 = ((bf16[8,768,128]{1,2,0:T(8,128)(2,1)}), bf16[8,768,128]{1,2,0:T(8,128)(2,1)S(1)}, u32[]{:S(2)}, u32[]{:S(2)}) async-start(bf16[8,768,128]{1,2,0:T(8,128)(2,1)} %fusion.22), calls=%async_computation.2 | async-start | bytes 3145728 | tf_op jit(solution)/shard_map/all_to_all | solution.py:50
  124.3 67.2 %all-gather.7.cloned.1.call-start = ((), (), s32[]{:S(2)}) async-start(), calls=%async_computation.26 | async-start | bytes 3575808 | tf_op jit(solution)/shard_map/all_gather | solution.py:460
  125.1 20.1 %copy-start.117 = (f32[128]{0:T(128)}, f32[128]{0:T(128)S(1)}, u32[]{:S(2)}) copy-start(f32[128]{0:T(128)S(1)} %reshape.2347) | copy-start | bytes 1540
  145.3 67.0 %copy-start.6 = (f32[768,128]{0,1:T(8,128)}, f32[768,128]{0,1:T(8,128)S(1)}, u32[]{:S(2)}) copy-start(f32[768,128]{0,1:T(8,128)S(1)} %get-tuple-element.210) | copy-start | bytes 1179652
  146.0 9.9 %all-to-all-start.3 = ((f32[8,1,1536]{2,1,0:T(1,128)}), f32[8,1,1536]{2,1,0:T(1,128)S(1)}, u32[]{:S(2)}, u32[]{:S(2)}) async-start(f32[8,1,1536]{2,1,0:T(1,128)} %broadcast_in_dim.194), calls=%async_computation.3 | async-start | bytes 98304 | tf_op jit(solution)/shard_map/all_to_all | solution.py:18
  157.4 24.1 %all-to-all-start.4 = ((bf16[8,768,128]{1,2,0:T(8,128)(2,1)}), bf16[8,768,128]{1,2,0:T(8,128)(2,1)}, u32[]{:S(2)}, u32[]{:S(2)}) async-start(bf16[8,768,128]{1,2,0:T(8,128)(2,1)} %broadcast_in_dim.195), calls=%async_computation.4 | async-start | bytes 3145728 | tf_op jit(solution)/shard_map/all_to_all | solution.py:18
  187.8 24.2 %all-to-all-start.5 = ((bf16[8,768,128]{1,2,0:T(8,128)(2,1)}), bf16[8,768,128]{1,2,0:T(8,128)(2,1)S(1)}, u32[]{:S(2)}, u32[]{:S(2)}) async-start(bf16[8,768,128]{1,2,0:T(8,128)(2,1)} %fusion.26), calls=%async_computation.5 | async-start | bytes 3145728 | tf_op jit(solution)/shard_map/all_to_all | solution.py:50
  191.5 20.9 %copy-start.119 = (f32[128]{0:T(128)}, f32[128]{0:T(128)S(1)}, u32[]{:S(2)}) copy-start(f32[128]{0:T(128)S(1)} %reshape.2351) | copy-start | bytes 1540
  213.0 71.7 %copy-start.12 = (f32[768,128]{0,1:T(8,128)}, f32[768,128]{0,1:T(8,128)S(1)}, u32[]{:S(2)}) copy-start(f32[768,128]{0,1:T(8,128)S(1)} %get-tuple-element.209) | copy-start | bytes 1179652
  213.7 9.9 %all-to-all-start.6 = ((f32[8,1,1536]{2,1,0:T(1,128)}), f32[8,1,1536]{2,1,0:T(1,128)S(1)}, u32[]{:S(2)}, u32[]{:S(2)}) async-start(f32[8,1,1536]{2,1,0:T(1,128)} %broadcast_in_dim.196), calls=%async_computation.6 | async-start | bytes 98304 | tf_op jit(solution)/shard_map/all_to_all | solution.py:18
  225.4 23.8 %all-to-all-start.7 = ((bf16[8,768,128]{2,1,0:T(8,128)(2,1)}), bf16[8,768,128]{2,1,0:T(8,128)(2,1)}, u32[]{:S(2)}, u32[]{:S(2)}) async-start(bf16[8,768,128]{2,1,0:T(8,128)(2,1)} %broadcast_in_dim.197), calls=%async_computation.7 | async-start | bytes 3145728 | tf_op jit(solution)/shard_map/all_to_all | solution.py:18
  232.8 19.0 %copy-start.115 = (f32[2,64]{1,0:T(2,128)}, f32[2,64]{1,0:T(2,128)S(1)}, u32[]{:S(2)}) copy-start(f32[2,64]{1,0:T(2,128)S(1)} %reshape.2355) | copy-start | bytes 1540
  232.9 21.2 %copy-start.130 = (f32[2,64]{1,0:T(2,128)}, f32[2,64]{1,0:T(2,128)S(1)}, u32[]{:S(2)}) copy-start(f32[2,64]{1,0:T(2,128)S(1)} %reshape.2354) | copy-start | bytes 1540
  233.0 23.5 %copy-start.39 = (bf16[8,128,128]{1,2,0:T(8,128)(2,1)}, bf16[8,128,128]{1,2,0:T(8,128)(2,1)S(1)}, u32[]{:S(2)}) copy-start(bf16[8,128,128]{1,2,0:T(8,128)(2,1)S(1)} %copy.376) | copy-start | bytes 786436
  258.2 24.8 %all-to-all-start.8 = ((bf16[8,768,128]{1,2,0:T(8,128)(2,1)}), bf16[8,768,128]{1,2,0:T(8,128)(2,1)}, u32[]{:S(2)}, u32[]{:S(2)}) async-start(bf16[8,768,128]{1,2,0:T(8,128)(2,1)} %fusion.23), calls=%async_computation.8 | async-start | bytes 3145728 | tf_op jit(solution)/shard_map/all_to_all | solution.py:50
  262.6 22.2 %copy-start.98 = (f32[128]{0:T(128)}, f32[128]{0:T(128)S(1)}, u32[]{:S(2)}) copy-start(f32[128]{0:T(128)S(1)} %reshape.2356) | copy-start | bytes 1540
  262.6 26.5 %copy-start.109 = (f32[8,16]{1,0:T(8,128)S(1)}, f32[8,16]{1,0:T(8,128)}, u32[]{:S(2)}) copy-start(f32[8,16]{1,0:T(8,128)} %get-tuple-element.229) | copy-start | bytes 1540
  262.6 26.6 %copy-start.108 = (f32[8,16]{1,0:T(8,128)S(1)}, f32[8,16]{1,0:T(8,128)}, u32[]{:S(2)}) copy-start(f32[8,16]{1,0:T(8,128)} %get-tuple-element.228) | copy-start | bytes 1540
  285.5 9.9 %all-to-all-start.9 = ((f32[8,1,1536]{2,1,0:T(1,128)}), f32[8,1,1536]{2,1,0:T(1,128)S(1)}, u32[]{:S(2)}, u32[]{:S(2)}) async-start(f32[8,1,1536]{2,1,0:T(1,128)} %broadcast_in_dim.198), calls=%async_computation.9 | async-start | bytes 98304 | tf_op jit(solution)/shard_map/all_to_all | solution.py:18
  289.2 74.1 %copy-start.100 = (f32[128]{0:T(128)}, f32[128]{0:T(128)S(1)}, u32[]{:S(2)}) copy-start(f32[128]{0:T(128)S(1)} %reshape.2357) | copy-start | bytes 1540
  295.5 67.8 %copy-start.67 = (f32[768]{0:T(1024)}, f32[768]{0:T(1024)S(1)}, u32[]{:S(2)}) copy-start(f32[768]{0:T(1024)S(1)} %get-tuple-element.253) | copy-start | bytes 9220
  295.5 67.8 %copy-start.69 = (f32[768]{0:T(1024)}, f32[768]{0:T(1024)S(1)}, u32[]{:S(2)}) copy-start(f32[768]{0:T(1024)S(1)} %get-tuple-element.254) | copy-start | bytes 9220
  296.9 23.8 %all-to-all-start.10 = ((bf16[8,768,128]{1,2,0:T(8,128)(2,1)}), bf16[8,768,128]{1,2,0:T(8,128)(2,1)}, u32[]{:S(2)}, u32[]{:S(2)}) async-start(bf16[8,768,128]{1,2,0:T(8,128)(2,1)} %broadcast_in_dim.199), calls=%async_computation.10 | async-start | bytes 3145728 | tf_op jit(solution)/shard_map/all_to_all | solution.py:18
  365.7 30.2 %all-to-all-start.14 = ((bf16[8,768,128]{2,1,0:T(8,128)(2,1)}), bf16[8,768,128]{2,1,0:T(8,128)(2,1)S(1)}, u32[]{:S(2)}, u32[]{:S(2)}) async-start(bf16[8,768,128]{2,1,0:T(8,128)(2,1)} %broadcast_in_dim.201), calls=%async_computation.14 | async-start | bytes 3145728 | tf_op jit(solution)/shard_map/all_to_all | solution.py:18
  459.2 22.1 %all-to-all-start.17 = ((bf16[8,768,128]{2,1,0:T(8,128)(2,1)}), bf16[8,768,128]{2,1,0:T(8,128)(2,1)}, u32[]{:S(2)}, u32[]{:S(2)}) async-start(bf16[8,768,128]{2,1,0:T(8,128)(2,1)} %broadcast_in_dim.203), calls=%async_computation.17 | async-start | bytes 3145728 | tf_op jit(solution)/shard_map/all_to_all | solution.py:18
  489.4 26.3 %all-to-all-start.18 = ((bf16[8,768,128]{1,2,0:T(8,128)(2,1)}), bf16[8,768,128]{1,2,0:T(8,128)(2,1)}, u32[]{:S(2)}, u32[]{:S(2)}) async-start(bf16[8,768,128]{1,2,0:T(8,128)(2,1)} %fusion.29), calls=%async_computation.18 | async-start | bytes 3145728 | tf_op jit(solution)/shard_map/all_to_all | solution.py:50
  518.9 12.1 %all-to-all-start.19 = ((f32[8,1,1536]{2,1,0:T(1,128)}), f32[8,1,1536]{2,1,0:T(1,128)}, u32[]{:S(2)}, u32[]{:S(2)}) async-start(f32[8,1,1536]{2,1,0:T(1,128)} %broadcast_in_dim.204), calls=%async_computation.19 | async-start | bytes 98304 | tf_op jit(solution)/shard_map/all_to_all | solution.py:18
  540.4 38.9 %all-to-all-start.20 = ((bf16[8,768,128]{2,1,0:T(8,128)(2,1)}), bf16[8,768,128]{2,1,0:T(8,128)(2,1)}, u32[]{:S(2)}, u32[]{:S(2)}) async-start(bf16[8,768,128]{2,1,0:T(8,128)(2,1)} %broadcast_in_dim.205), calls=%async_computation.20 | async-start | bytes 3145728 | tf_op jit(solution)/shard_map/all_to_all | solution.py:18
  599.5 25.2 %all-to-all-start.21 = ((bf16[8,768,128]{1,2,0:T(8,128)(2,1)}), bf16[8,768,128]{1,2,0:T(8,128)(2,1)S(1)}, u32[]{:S(2)}, u32[]{:S(2)}) async-start(bf16[8,768,128]{1,2,0:T(8,128)(2,1)} %fusion.25), calls=%async_computation.21 | async-start | bytes 3145728 | tf_op jit(solution)/shard_map/all_to_all | solution.py:50
  605.4 128.4 %reduce-scatter.2.cloned.1.call-start = ((), (), s32[]{:S(2)}) async-start(), calls=%async_computation.24 | async-start | bytes 6754304 | tf_op jit(solution)/shard_map/reduce_scatter | solution.py:434
  631.6 23.5 %all-to-all-start.11 = ((bf16[8,768,128]{1,2,0:T(8,128)(2,1)}), bf16[8,768,128]{1,2,0:T(8,128)(2,1)}, u32[]{:S(2)}, u32[]{:S(2)}) async-start(bf16[8,768,128]{1,2,0:T(8,128)(2,1)} %fusion.27), calls=%async_computation.11 | async-start | bytes 3145728 | tf_op jit(solution)/shard_map/all_to_all | solution.py:50
  637.4 28.3 %copy-start.5 = (f32[768,128]{0,1:T(8,128)S(1)}, f32[768,128]{0,1:T(8,128)}, u32[]{:S(2)}) copy-start(f32[768,128]{0,1:T(8,128)} %copy-done.4) | copy-start | bytes 1179652
  637.4 28.3 %copy-start.9 = (f32[768,128]{0,1:T(8,128)S(1)}, f32[768,128]{0,1:T(8,128)}, u32[]{:S(2)}) copy-start(f32[768,128]{0,1:T(8,128)} %copy-done.8) | copy-start | bytes 1179652
  637.4 28.3 %copy-start.11 = (f32[768,128]{0,1:T(8,128)S(1)}, f32[768,128]{0,1:T(8,128)}, u32[]{:S(2)}) copy-start(f32[768,128]{0,1:T(8,128)} %copy-done.10) | copy-start | bytes 1179652
  637.5 28.3 %copy-start.18 = (f32[768,128]{0,1:T(8,128)S(1)}, f32[768,128]{0,1:T(8,128)}, u32[]{:S(2)}) copy-start(f32[768,128]{0,1:T(8,128)} %copy-done.17) | copy-start | bytes 1179652
  637.5 28.3 %copy-start.20 = (f32[768,128]{0,1:T(8,128)S(1)}, f32[768,128]{0,1:T(8,128)}, u32[]{:S(2)}) copy-start(f32[768,128]{0,1:T(8,128)} %copy-done.19) | copy-start | bytes 1179652
  637.5 28.3 %copy-start.68 = (f32[768]{0:T(1024)S(1)}, f32[768]{0:T(1024)}, u32[]{:S(2)}) copy-start(f32[768]{0:T(1024)} %copy-done.67) | copy-start | bytes 9220
  637.5 28.3 %copy-start.70 = (f32[768]{0:T(1024)S(1)}, f32[768]{0:T(1024)}, u32[]{:S(2)}) copy-start(f32[768]{0:T(1024)} %copy-done.69) | copy-start | bytes 9220
  637.5 28.3 %copy-start.77 = (f32[768]{0:T(1024)S(1)}, f32[768]{0:T(1024)}, u32[]{:S(2)}) copy-start(f32[768]{0:T(1024)} %copy-done.76) | copy-start | bytes 9220
  637.5 28.3 %copy-start.79 = (f32[768]{0:T(1024)S(1)}, f32[768]{0:T(1024)}, u32[]{:S(2)}) copy-start(f32[768]{0:T(1024)} %copy-done.78) | copy-start | bytes 9220
  637.5 28.3 %copy-start.81 = (f32[768]{0:T(1024)S(1)}, f32[768]{0:T(1024)}, u32[]{:S(2)}) copy-start(f32[768]{0:T(1024)} %copy-done.80) | copy-start | bytes 9220
  637.5 28.3 %copy-start.83 = (f32[768]{0:T(1024)S(1)}, f32[768]{0:T(1024)}, u32[]{:S(2)}) copy-start(f32[768]{0:T(1024)} %copy-done.82) | copy-start | bytes 9220
  637.5 28.3 %copy-start.85 = (f32[768]{0:T(1024)S(1)}, f32[768]{0:T(1024)}, u32[]{:S(2)}) copy-start(f32[768]{0:T(1024)} %copy-done.84) | copy-start | bytes 9220
  637.5 28.3 %copy-start.87 = (f32[768]{0:T(1024)S(1)}, f32[768]{0:T(1024)}, u32[]{:S(2)}) copy-start(f32[768]{0:T(1024)} %copy-done.86) | copy-start | bytes 9220
  637.6 28.3 %copy-start.94 = (f32[128]{0:T(128)S(1)}, f32[128]{0:T(128)}, u32[]{:S(2)}) copy-start(f32[128]{0:T(128)} %copy-done.92) | copy-start | bytes 1540
  637.6 28.3 %copy-start.97 = (f32[128]{0:T(128)S(1)}, f32[128]{0:T(128)}, u32[]{:S(2)}) copy-start(f32[128]{0:T(128)} %copy-done.95) | copy-start | bytes 1540
  637.6 28.3 %copy-start.99 = (f32[128]{0:T(128)S(1)}, f32[128]{0:T(128)}, u32[]{:S(2)}) copy-start(f32[128]{0:T(128)} %copy-done.98) | copy-start | bytes 1540
  637.6 28.3 %copy-start.101 = (f32[128]{0:T(128)S(1)}, f32[128]{0:T(128)}, u32[]{:S(2)}) copy-start(f32[128]{0:T(128)} %copy-done.100) | copy-start | bytes 1540
  637.6 28.3 %copy-start.118 = (f32[128]{0:T(128)S(1)}, f32[128]{0:T(128)}, u32[]{:S(2)}) copy-start(f32[128]{0:T(128)} %copy-done.117) | copy-start | bytes 1540
  637.6 28.3 %copy-start.120 = (f32[128]{0:T(128)S(1)}, f32[128]{0:T(128)}, u32[]{:S(2)}) copy-start(f32[128]{0:T(128)} %copy-done.119) | copy-start | bytes 1540
  655.8 9.9 %all-to-all-start.22 = ((f32[8,1,1536]{2,1,0:T(1,128)}), f32[8,1,1536]{2,1,0:T(1,128)S(1)}, u32[]{:S(2)}, u32[]{:S(2)}) async-start(f32[8,1,1536]{2,1,0:T(1,128)} %broadcast_in_dim.206), calls=%async_computation.22 | async-start | bytes 98304 | tf_op jit(solution)/shard_map/all_to_all | solution.py:18
  668.4 23.8 %collective-permute-start.3 = (f32[1,768,128]{1,2,0:T(8,128)S(1)}, f32[1,768,128]{1,2,0:T(8,128)S(1)}, u32[]{:S(2)}, u32[]{:S(2)}) collective-permute-start(f32[1,768,128]{1,2,0:T(8,128)S(1)} %get-tuple-element.205), channel_id=1, source_target_pairs={{64,0},{65,1},{66,2},{67,3},{68,4},{69,5},{70,6},{71,7},{72,8},{73... | collective-permute-start | bytes 1179656 | tf_op jit(solution)/shard_map/ppermute | solution.py:514
  669.7 22.5 %collective-permute-start.4 = (f32[1,768,128]{1,2,0:T(8,128)S(1)}, f32[1,768,128]{1,2,0:T(8,128)S(1)}, u32[]{:S(2)}, u32[]{:S(2)}) collective-permute-start(f32[1,768,128]{1,2,0:T(8,128)S(1)} %get-tuple-element.206), channel_id=1, source_target_pairs={{0,64},{1,65},{2,66},{3,67},{4,68},{5,69},{6,70},{7,71},{8,72},{9,... | collective-permute-start | bytes 1179656 | tf_op jit(solution)/shard_map/ppermute | solution.py:512
  675.8 24.7 %collective-permute-start.1 = (f32[1,768,128]{1,2,0:T(8,128)}, f32[1,768,128]{1,2,0:T(8,128)}, u32[]{:S(2)}, u32[]{:S(2)}) collective-permute-start(f32[1,768,128]{1,2,0:T(8,128)} %get-tuple-element.207), channel_id=1, source_target_pairs={{64,0},{65,1},{66,2},{67,3},{68,4},{69,5},{70,6},{71,7},{72,8},{73... | collective-permute-start | bytes 1179656 | tf_op jit(solution)/shard_map/ppermute | solution.py:509
  679.3 17.5 %collective-permute-start.2 = (f32[1,768,128]{1,2,0:T(8,128)S(1)}, f32[1,768,128]{1,2,0:T(8,128)S(1)}, u32[]{:S(2)}, u32[]{:S(2)}) collective-permute-start(f32[1,768,128]{1,2,0:T(8,128)S(1)} %fusion.90), channel_id=1, source_target_pairs={{0,64},{1,65},{2,66},{3,67},{4,68},{5,69},{6,70},{7,71},{8,72},{9,... | collective-permute-start | bytes 1179656 | tf_op jit(solution)/shard_map/ppermute | solution.py:510
  (109 other events, 349.3 us)
Sparse Core Ops, SparseCore 0:
  26.3 30.4 all-gather.4
  126.8 27.8 all-gather.6
  626.8 106.9 reduce-scatter.1

commit v12 on v9

--- a/solution.py
+++ b/solution.py
@@ -504,6 +504,9 @@
     other_final = lax.ppermute(final, "section", [(0, 1)])
     middle_grad, grads_last = layer_backward(out_grad, kept_last, weights_last, grad_full)
     other_middle_grad = lax.ppermute(middle_grad, "section", [(0, 1)])
+    middle_grad, other_middle, other_final = lax.optimization_barrier(
+        (middle_grad, other_middle, other_final)
+    )
     input_grad, grads_zero = layer_backward(middle_grad, kept_zero, weights_zero)
     other_input_grad = lax.ppermute(input_grad, "section", [(1, 0)])
     reduced = sum_at_end(grads_zero, grads_last, dims)

time: 713 us -> 779 us (1.093)
  waiting for transfers between devices: 246 us -> 313 us
  blocking collectives: 113 us -> 58.1 us
  local copies, waits for them, and re-layouts: 103 us -> 134 us
  matrix products: 71.6 us -> 83.4 us
  starting transfers between devices: 94.9 us -> 104 us
    reduce_scatter x1, waiting for transfers between devices: 33.8 us -> 74.4 us  [sum_at_end(): lax.psum_scatter(rows.reshape(-1, 128), ('section', 'dp'), scatter_dimens...]
    all_to_all x4 -> x2, blocking collectives: 66 us -> 33.1 us  [sent_to_all(): return lax.all_to_all(copies, axis, split_axis=0, concat_axis=0, tiled=True)]
    all_to_all x2 -> x1, blocking collectives: 46.6 us -> 25.1 us  [summed_on_arrival(): lax.all_to_all(parts, axis, split_axis=0, concat_axis=0, tiled=True)]
    all_to_all x6 -> x7, waiting for transfers between devices: 73.6 us -> 85.8 us  [summed_on_arrival(): lax.all_to_all(parts, axis, split_axis=0, concat_axis=0, tiled=True)]
    all_to_all x11 -> x13, starting transfers between devices: 49.6 us -> 59.2 us  [sent_to_all(): return lax.all_to_all(copies, axis, split_axis=0, concat_axis=0, tiled=True)]
    all_to_all x11 -> x13, waiting for transfers between devices: 101 us -> 109 us  [sent_to_all(): return lax.all_to_all(copies, axis, split_axis=0, concat_axis=0, tiled=True)]
    all_to_all x6 -> x7, starting transfers between devices: 27.1 us -> 31.9 us  [summed_on_arrival(): lax.all_to_all(parts, axis, split_axis=0, concat_axis=0, tiled=True)]
    unnamed x220 -> x282, local copies, waits for them, and re-layouts: 15 us -> 18.9 us
  transfers between devices with their start and end apart: 25 -> 28, of which waited for: 21 -> 22; matrix products, arithmetic and copies ran while one was open for 16% -> 22% of each run, Pallas kernels for 0% -> 0%
where the time goes in v12:
time: 779 us; the launch traced here: 767 us
  waiting for transfers between devices  313 us (40%)
  local copies, waits for them, and re-layouts  134 us (17%)
  starting transfers between devices  104 us (13%)
  matrix products  83.4 us (11%)
  other arithmetic  59.1 us (8%)
  blocking collectives  58.1 us (7%)
  between operations  16.2 us (2%)
    all_to_all x13, waiting for transfers between devices, sent_to_all(): return lax.all_to_all(copies, axis, split_axis=0, concat_axis=0, tiled=True)  109 us
    all_to_all x7, waiting for transfers between devices, summed_on_arrival(): lax.all_to_all(parts, axis, split_axis=0, concat_axis=0, tiled=True)  85.8 us
    reduce_scatter x1, waiting for transfers between devices, sum_at_end(): lax.psum_scatter(rows.reshape(-1, 128), ('section', 'dp'), scatter_dimens...  74.4 us
    all_to_all x13, starting transfers between devices, sent_to_all(): return lax.all_to_all(copies, axis, split_axis=0, concat_axis=0, tiled=True)  59.2 us
    all_to_all x2, blocking collectives, sent_to_all(): return lax.all_to_all(copies, axis, split_axis=0, concat_axis=0, tiled=True)  33.1 us
    all_to_all x7, starting transfers between devices, summed_on_arrival(): lax.all_to_all(parts, axis, split_axis=0, concat_axis=0, tiled=True)  31.9 us
    all_to_all x1, blocking collectives, summed_on_arrival(): lax.all_to_all(parts, axis, split_axis=0, concat_axis=0, tiled=True)  25.1 us
    unnamed x282, local copies, waits for them, and re-layouts  18.9 us
  transfers between devices with their start and end apart: 28, of which 22 were waited for; matrix products, arithmetic and copies ran while one was open for 22% of the time, Pallas kernels for 0%

profile of v12, /device:TPU:0, one launch (start us, length us, event | category | flops | bytes accessed | tf_op | source)
XLA Modules:
  0.0 767.0 jit_solution(12824719553807184499)
XLA Ops:
  12.8 3.2 collective-permute-start
  16.0 9.2 %collective-permute-done = bf16[1552,128]{1,0:T(8,128)(2,1)S(1)} collective-permute-done((bf16[1552,128]{1,0:T(8,128)(2,1)S(1)}, bf16[1552,128]{1,0:T(8,128)(2,1)S(1)}, u32[]{:S(2)}, u32[]{:S(2)}) %collective-permute-start) | collective-permute-done | bytes 397344 | tf_op jit(solution)/shard_map/ppermute | solution.py:452
  27.2 6.5 all-to-all-start
  34.7 5.3 all-to-all-done
  40.0 16.8 %all-gather.5.cloned.1.call-done = bf16[12416,128]{1,0:T(8,128)(2,1)} async-done(((bf16[1552,128]{1,0:T(8,128)(2,1)}), bf16[12416,128]{1,0:T(8,128)(2,1)}) %all-gather.5.cloned.1.call-update) | async-done | bytes 3178512 | tf_op jit(solution)/shard_map/all_gather | solution.py:453
  61.0 5.3 all-to-all-start.1
  71.6 32.6 %all-to-all-done.1 = bf16[8,2,768,128]{3,2,1,0:T(8,128)(2,1)} async-done(((bf16[8,2,768,128]{3,2,1,0:T(8,128)(2,1)}), bf16[8,2,768,128]{3,2,1,0:T(8,128)(2,1)}, u32[]{:S(2)}, u32[]{:S(2)}) %all-to-all-start.1) | async-done | bytes 3145760 | tf_op jit(solution)/shard_map/all_to_all | solution.py:18
  104.1 4.7 copy.246
  108.8 3.3 fusion.121
  120.2 3.6 all-to-all-start.2
  124.7 19.8 %all-to-all-done.2 = bf16[8,768,128]{2,1,0:T(8,128)(2,1)S(1)} async-done(((bf16[8,768,128]{2,1,0:T(8,128)(2,1)}), bf16[8,768,128]{2,1,0:T(8,128)(2,1)S(1)}, u32[]{:S(2)}, u32[]{:S(2)}) %all-to-all-start.2) | async-done | bytes 1572896 | tf_op jit(solution)/shard_map/all_to_all | solution.py:51
  145.7 3.6 all-to-all-start.3
  150.9 4.8 all-to-all-done.3
  157.4 4.5 all-to-all-start.4
  169.2 12.2 %all-to-all-done.4 = bf16[8,768,128]{1,2,0:T(8,128)(2,1)} async-done(((bf16[8,768,128]{1,2,0:T(8,128)(2,1)}), bf16[8,768,128]{1,2,0:T(8,128)(2,1)}, u32[]{:S(2)}, u32[]{:S(2)}) %all-to-all-start.4) | async-done | bytes 1572896 | tf_op jit(solution)/shard_map/all_to_all | solution.py:18
  181.4 2.8 convolution_add_fusion.1
  186.9 4.4 all-to-all-start.5
  192.3 19.6 %all-to-all-done.5 = bf16[8,768,128]{2,1,0:T(8,128)(2,1)} async-done(((bf16[8,768,128]{2,1,0:T(8,128)(2,1)}), bf16[8,768,128]{2,1,0:T(8,128)(2,1)}, u32[]{:S(2)}, u32[]{:S(2)}) %all-to-all-start.5) | async-done | bytes 1572896 | tf_op jit(solution)/shard_map/all_to_all | solution.py:51
  214.6 3.6 all-to-all-start.6
  219.1 5.5 all-to-all-done.6
  226.3 4.3 all-to-all-start.7
  237.9 12.2 %all-to-all-done.7 = bf16[8,768,128]{2,1,0:T(8,128)(2,1)} async-done(((bf16[8,768,128]{2,1,0:T(8,128)(2,1)}), bf16[8,768,128]{2,1,0:T(8,128)(2,1)}, u32[]{:S(2)}, u32[]{:S(2)}) %all-to-all-start.7) | async-done | bytes 1572896 | tf_op jit(solution)/shard_map/all_to_all | solution.py:18
  259.5 3.8 all-to-all-start.8
  263.8 20.0 %all-to-all-done.8 = bf16[8,768,128]{2,1,0:T(8,128)(2,1)S(1)} async-done(((bf16[8,768,128]{2,1,0:T(8,128)(2,1)}), bf16[8,768,128]{2,1,0:T(8,128)(2,1)S(1)}, u32[]{:S(2)}, u32[]{:S(2)}) %all-to-all-start.8) | async-done | bytes 1572896 | tf_op jit(solution)/shard_map/all_to_all | solution.py:51
  285.8 3.9 all-to-all-start.9
  291.1 4.8 all-to-all-done.9
  297.7 4.3 all-to-all-start.10
  309.3 12.1 %all-to-all-done.10 = bf16[8,768,128]{1,2,0:T(8,128)(2,1)} async-done(((bf16[8,768,128]{1,2,0:T(8,128)(2,1)}), bf16[8,768,128]{1,2,0:T(8,128)(2,1)}, u32[]{:S(2)}, u32[]{:S(2)}) %all-to-all-start.10) | async-done | bytes 1572896 | tf_op jit(solution)/shard_map/all_to_all | solution.py:18
  321.5 2.8 convolution_add_fusion
  328.4 25.1 %all_to_all.123 = bf16[8,768,128]{2,1,0:T(8,128)(2,1)S(1)} all-to-all(bf16[8,768,128]{2,1,0:T(8,128)(2,1)S(1)} %bitcast.486), channel_id=1, replica_groups=mesh['section'=2,'dp'=8,'tensor'=8] {'tensor'}, dimensions={0} | all-to-all | bytes 3145728 | tf_op jit(solution)/shard_map/all_to_all | solution.py:51
  355.7 8.7 %all_to_all.124 = f32[8,1,1536]{2,1,0:T(1,128)S(1)} all-to-all(f32[8,1,1536]{2,1,0:T(1,128)S(1)} %broadcast_in_dim.200), channel_id=1, replica_groups=mesh['section'=2,'dp'=8,'tensor'=8] {'tensor'}, dimensions={0} | all-to-all | bytes 98304 | tf_op jit(solution)/shard_map/all_to_all | solution.py:18
  366.9 3.6 all-to-all-start.13
  370.5 2.8 fusion.28
  374.8 13.8 %all-to-all-done.13 = bf16[8,768,128]{2,1,0:T(8,128)(2,1)S(1)} async-done(((bf16[8,768,128]{2,1,0:T(8,128)(2,1)}), bf16[8,768,128]{2,1,0:T(8,128)(2,1)S(1)}, u32[]{:S(2)}, u32[]{:S(2)}) %all-to-all-start.13) | async-done | bytes 1572896 | tf_op jit(solution)/shard_map/all_to_all | solution.py:18
  388.6 4.8 all-to-all-start.16
  395.3 4.4 bitcast_reduce_fusion.2
  399.7 4.4 multiply_reduce_fusion.1
  404.9 5.1 multiply_convert_fusion.1
  421.0 5.8 all-to-all-start.14
  429.8 16.3 %all-to-all-done.14 = bf16[8,768,128]{2,1,0:T(8,128)(2,1)S(1)} async-done(((bf16[8,768,128]{2,1,0:T(8,128)(2,1)}), bf16[8,768,128]{2,1,0:T(8,128)(2,1)S(1)}, u32[]{:S(2)}, u32[]{:S(2)}) %all-to-all-start.14) | async-done | bytes 1572896 | tf_op jit(solution)/shard_map/all_to_all | solution.py:51
  448.9 4.0 all-to-all-start.15
  455.1 4.6 collective-permute-start.2
  464.4 3.8 collective-permute-done.2
  468.9 4.8 collective-permute-done.1
  474.7 24.4 %all_to_all.125 = bf16[8,768,128]{2,1,0:T(8,128)(2,1)S(1)} all-to-all(bf16[8,768,128]{2,1,0:T(8,128)(2,1)S(1)} %broadcast_in_dim.203), channel_id=1, replica_groups=mesh['section'=2,'dp'=8,'tensor'=8] {'tensor'}, dimensions={0} | all-to-all | bytes 3145728 | tf_op jit(solution)/shard_map/all_to_all | solution.py:18
  499.1 4.6 fusion.125
  506.1 3.6 all-to-all-start.18
  512.7 4.0 fusion.34
  516.7 10.1 %all-to-all-done.18 = bf16[8,768,128]{2,1,0:T(8,128)(2,1)S(1)} async-done(((bf16[8,768,128]{2,1,0:T(8,128)(2,1)}), bf16[8,768,128]{2,1,0:T(8,128)(2,1)S(1)}, u32[]{:S(2)}, u32[]{:S(2)}) %all-to-all-start.18) | async-done | bytes 1572896 | tf_op jit(solution)/shard_map/all_to_all | solution.py:51
  529.6 4.0 all-to-all-start.19
  533.6 3.6 convolution_convert_fusion.8
  554.8 6.0 all-to-all-start.20
  569.5 3.2 concatenate.135
  576.6 3.6 convolution_convert_fusion.9
  585.7 3.1 fusion.33
  598.2 4.5 bitcast_reduce_fusion
  602.7 4.2 multiply_reduce_fusion
  610.4 2.8 copy.294
  617.5 5.8 all-to-all-start.21
  630.7 3.2 concatenate.134
  646.0 5.7 all-to-all-start.22
  651.8 6.2 all-to-all-done.22
  670.8 5.9 collective-permute-done.3
  677.7 74.4 %reduce-scatter.2.cloned.1.call-done = bf16[1552,128]{1,0:T(8,128)(2,1)} async-done(((bf16[24832,128]{1,0:T(8,128)(2,1)}), bf16[1552,128]{1,0:T(8,128)(2,1)}) %reduce-scatter.2.cloned.1.call-update) | async-done | bytes 397328 | tf_op jit(solution)/shard_map/reduce_scatter | solution.py:428
  (533 shorter events, 216.6 us)
Async XLA Ops:
  7.2 49.6 %all-gather.5.cloned.1.call-start = ((), (), s32[]{:S(2)}) async-start(), calls=%async_computation.25 | async-start | bytes 3575808 | tf_op jit(solution)/shard_map/all_gather | solution.py:453
  9.0 17.1 %copy-start.2 = (f32[2,1,768,128]{3,2,1,0:T(8,128)S(1)}, f32[2,1,768,128]{3,2,1,0:T(8,128)}, u32[]{:S(2)}) copy-start(f32[2,1,768,128]{3,2,1,0:T(8,128)} %param.14) | copy-start | bytes 2359300
  12.8 12.4 %collective-permute-start = (bf16[1552,128]{1,0:T(8,128)(2,1)S(1)}, bf16[1552,128]{1,0:T(8,128)(2,1)S(1)}, u32[]{:S(2)}, u32[]{:S(2)}) collective-permute-start(bf16[1552,128]{1,0:T(8,128)(2,1)S(1)} %bitcast.542), channel_id=1, source_target_pairs={{0,64},{64,0},{1,65},{65,1},{2,66},{66,2},{3,67},{67,3},{4,68},{68... | collective-permute-start | bytes 1191944 | tf_op jit(solution)/shard_map/ppermute | solution.py:452
  27.2 12.8 %all-to-all-start = ((f32[8,1,1536]{2,1,0:T(1,128)}), f32[8,1,1536]{2,1,0:T(1,128)S(1)}, u32[]{:S(2)}, u32[]{:S(2)}) async-start(f32[8,1,1536]{2,1,0:T(1,128)} %broadcast_in_dim.189), calls=%async_computation | async-start | bytes 98304 | tf_op jit(solution)/shard_map/all_to_all | solution.py:18
  57.6 9.0 %copy-start.70 = (bf16[1,8,16,128]{3,1,2,0:T(8,128)(2,1)}, bf16[1,8,16,128]{3,1,2,0:T(8,128)(2,1)S(1)}, u32[]{:S(2)}) copy-start(bf16[1,8,16,128]{3,1,2,0:T(8,128)(2,1)S(1)} %copy.391) | copy-start | bytes 98308
  61.0 43.1 %all-to-all-start.1 = ((bf16[8,2,768,128]{3,2,1,0:T(8,128)(2,1)}), bf16[8,2,768,128]{3,2,1,0:T(8,128)(2,1)}, u32[]{:S(2)}, u32[]{:S(2)}) async-start(bf16[8,2,768,128]{3,2,1,0:T(8,128)(2,1)} %broadcast_in_dim.191), calls=%async_computation.1 | async-start | bytes 6291456 | tf_op jit(solution)/shard_map/all_to_all | solution.py:18
  67.9 45.5 %copy-start.102 = (f32[2,64]{1,0:T(2,128)}, f32[2,64]{1,0:T(2,128)S(1)}, u32[]{:S(2)}) copy-start(f32[2,64]{1,0:T(2,128)S(1)} %reshape.1912) | copy-start | bytes 1540
  68.0 47.7 %copy-start.118 = (f32[2,64]{1,0:T(2,128)}, f32[2,64]{1,0:T(2,128)S(1)}, u32[]{:S(2)}) copy-start(f32[2,64]{1,0:T(2,128)S(1)} %reshape.1911) | copy-start | bytes 1540
  120.2 24.2 %all-to-all-start.2 = ((bf16[8,768,128]{2,1,0:T(8,128)(2,1)}), bf16[8,768,128]{2,1,0:T(8,128)(2,1)S(1)}, u32[]{:S(2)}, u32[]{:S(2)}) async-start(bf16[8,768,128]{2,1,0:T(8,128)(2,1)} %bitcast.463), calls=%async_computation.2 | async-start | bytes 3145728 | tf_op jit(solution)/shard_map/all_to_all | solution.py:51
  123.8 67.5 %all-gather.7.cloned.1.call-start = ((), (), s32[]{:S(2)}) async-start(), calls=%async_computation.26 | async-start | bytes 3575808 | tf_op jit(solution)/shard_map/all_gather | solution.py:454
  124.7 20.3 %copy-start.89 = (f32[128]{0:T(128)}, f32[128]{0:T(128)S(1)}, u32[]{:S(2)}) copy-start(f32[128]{0:T(128)S(1)} %reshape.1913) | copy-start | bytes 1540
  144.7 308.2 %copy-start.10 = (f32[768,128]{1,0:T(8,128)}, f32[768,128]{1,0:T(8,128)S(1)}, u32[]{:S(2)}) copy-start(f32[768,128]{1,0:T(8,128)S(1)} %convert_reduce_fusion.7) | copy-start | bytes 1179652
  145.0 68.6 %copy-start.12 = (f32[768,128]{1,0:T(8,128)}, f32[768,128]{1,0:T(8,128)S(1)}, u32[]{:S(2)}) copy-start(f32[768,128]{1,0:T(8,128)S(1)} %get-tuple-element.210) | copy-start | bytes 1179652
  145.7 9.9 %all-to-all-start.3 = ((f32[8,1,1536]{2,1,0:T(1,128)}), f32[8,1,1536]{2,1,0:T(1,128)S(1)}, u32[]{:S(2)}, u32[]{:S(2)}) async-start(f32[8,1,1536]{2,1,0:T(1,128)} %broadcast_in_dim.194), calls=%async_computation.3 | async-start | bytes 98304 | tf_op jit(solution)/shard_map/all_to_all | solution.py:18
  157.4 24.0 %all-to-all-start.4 = ((bf16[8,768,128]{1,2,0:T(8,128)(2,1)}), bf16[8,768,128]{1,2,0:T(8,128)(2,1)}, u32[]{:S(2)}, u32[]{:S(2)}) async-start(bf16[8,768,128]{1,2,0:T(8,128)(2,1)} %broadcast_in_dim.195), calls=%async_computation.4 | async-start | bytes 3145728 | tf_op jit(solution)/shard_map/all_to_all | solution.py:18
  186.9 25.0 %all-to-all-start.5 = ((bf16[8,768,128]{2,1,0:T(8,128)(2,1)}), bf16[8,768,128]{2,1,0:T(8,128)(2,1)}, u32[]{:S(2)}, u32[]{:S(2)}) async-start(bf16[8,768,128]{2,1,0:T(8,128)(2,1)} %bitcast.483), calls=%async_computation.5 | async-start | bytes 3145728 | tf_op jit(solution)/shard_map/all_to_all | solution.py:51
  192.2 38.5 %copy-start.69 = (bf16[1,8,16,128]{3,1,2,0:T(8,128)(2,1)}, bf16[1,8,16,128]{3,1,2,0:T(8,128)(2,1)S(1)}, u32[]{:S(2)}) copy-start(bf16[1,8,16,128]{3,1,2,0:T(8,128)(2,1)S(1)} %copy.390) | copy-start | bytes 98308
  192.3 21.6 %copy-start.115 = (f32[128]{0:T(128)}, f32[128]{0:T(128)S(1)}, u32[]{:S(2)}) copy-start(f32[128]{0:T(128)S(1)} %reshape.1917) | copy-start | bytes 1540
  213.6 12.7 %copy-start.29 = (f32[768,128]{1,0:T(8,128)}, f32[768,128]{1,0:T(8,128)S(1)}, u32[]{:S(2)}) copy-start(f32[768,128]{1,0:T(8,128)S(1)} %convert_reduce_fusion.6) | copy-start | bytes 1179652
  213.9 70.2 %copy-start.24 = (f32[768,128]{1,0:T(8,128)}, f32[768,128]{1,0:T(8,128)S(1)}, u32[]{:S(2)}) copy-start(f32[768,128]{1,0:T(8,128)S(1)} %get-tuple-element.209) | copy-start | bytes 1179652
  214.6 9.9 %all-to-all-start.6 = ((f32[8,1,1536]{2,1,0:T(1,128)}), f32[8,1,1536]{2,1,0:T(1,128)S(1)}, u32[]{:S(2)}, u32[]{:S(2)}) async-start(f32[8,1,1536]{2,1,0:T(1,128)} %broadcast_in_dim.196), calls=%async_computation.6 | async-start | bytes 98304 | tf_op jit(solution)/shard_map/all_to_all | solution.py:18
  226.3 23.8 %all-to-all-start.7 = ((bf16[8,768,128]{2,1,0:T(8,128)(2,1)}), bf16[8,768,128]{2,1,0:T(8,128)(2,1)}, u32[]{:S(2)}, u32[]{:S(2)}) async-start(bf16[8,768,128]{2,1,0:T(8,128)(2,1)} %broadcast_in_dim.197), calls=%async_computation.7 | async-start | bytes 3145728 | tf_op jit(solution)/shard_map/all_to_all | solution.py:18
  232.9 19.8 %copy-start.104 = (f32[2,64]{1,0:T(2,128)}, f32[2,64]{1,0:T(2,128)S(1)}, u32[]{:S(2)}) copy-start(f32[2,64]{1,0:T(2,128)S(1)} %reshape.1921) | copy-start | bytes 1540
  233.0 22.0 %copy-start.120 = (f32[2,64]{1,0:T(2,128)}, f32[2,64]{1,0:T(2,128)S(1)}, u32[]{:S(2)}) copy-start(f32[2,64]{1,0:T(2,128)S(1)} %reshape.1920) | copy-start | bytes 1540
  259.5 24.4 %all-to-all-start.8 = ((bf16[8,768,128]{2,1,0:T(8,128)(2,1)}), bf16[8,768,128]{2,1,0:T(8,128)(2,1)S(1)}, u32[]{:S(2)}, u32[]{:S(2)}) async-start(bf16[8,768,128]{2,1,0:T(8,128)(2,1)} %bitcast.459), calls=%async_computation.8 | async-start | bytes 3145728 | tf_op jit(solution)/shard_map/all_to_all | solution.py:51
  285.8 10.1 %all-to-all-start.9 = ((f32[8,1,1536]{2,1,0:T(1,128)}), f32[8,1,1536]{2,1,0:T(1,128)S(1)}, u32[]{:S(2)}, u32[]{:S(2)}) async-start(f32[8,1,1536]{2,1,0:T(1,128)} %broadcast_in_dim.198), calls=%async_computation.9 | async-start | bytes 98304 | tf_op jit(solution)/shard_map/all_to_all | solution.py:18
  290.4 74.1 %copy-start.97 = (f32[128]{0:T(128)}, f32[128]{0:T(128)S(1)}, u32[]{:S(2)}) copy-start(f32[128]{0:T(128)S(1)} %reshape.1923) | copy-start | bytes 1540
  296.0 68.5 %copy-start.67 = (f32[768]{0:T(1024)}, f32[768]{0:T(1024)S(1)}, u32[]{:S(2)}) copy-start(f32[768]{0:T(1024)S(1)} %get-tuple-element.253) | copy-start | bytes 9220
  296.0 68.5 %copy-start.68 = (f32[768]{0:T(1024)}, f32[768]{0:T(1024)S(1)}, u32[]{:S(2)}) copy-start(f32[768]{0:T(1024)S(1)} %get-tuple-element.254) | copy-start | bytes 9220
  297.7 23.8 %all-to-all-start.10 = ((bf16[8,768,128]{1,2,0:T(8,128)(2,1)}), bf16[8,768,128]{1,2,0:T(8,128)(2,1)}, u32[]{:S(2)}, u32[]{:S(2)}) async-start(bf16[8,768,128]{1,2,0:T(8,128)(2,1)} %broadcast_in_dim.199), calls=%async_computation.10 | async-start | bytes 3145728 | tf_op jit(solution)/shard_map/all_to_all | solution.py:18
  354.6 9.9 %copy-start.41 = (f32[2,1,768,128]{3,2,1,0:T(8,128)S(1)}, f32[2,1,768,128]{3,2,1,0:T(8,128)}, u32[]{:S(2)}) copy-start(f32[2,1,768,128]{3,2,1,0:T(8,128)} %param.15) | copy-start | bytes 2359300
  354.8 12.1 %copy-start.28 = (f32[768,128]{1,0:T(8,128)}, f32[768,128]{1,0:T(8,128)S(1)}, u32[]{:S(2)}) copy-start(f32[768,128]{1,0:T(8,128)S(1)} %convert_reduce_fusion.4) | copy-start | bytes 1179652
  366.9 21.7 %all-to-all-start.13 = ((bf16[8,768,128]{2,1,0:T(8,128)(2,1)}), bf16[8,768,128]{2,1,0:T(8,128)(2,1)S(1)}, u32[]{:S(2)}, u32[]{:S(2)}) async-start(bf16[8,768,128]{2,1,0:T(8,128)(2,1)} %broadcast_in_dim.201), calls=%async_computation.13 | async-start | bytes 3145728 | tf_op jit(solution)/shard_map/all_to_all | solution.py:18
  373.3 26.3 %slice-start.2 = ((s8[4718592]{0:T(1024)(128)(4,1)}), s8[524288]{0:T(1024)(128)(4,1)S(1)}, s32[]{:S(2)}) async-start(s8[4718592]{0:T(1024)(128)(4,1)} %bitcast.475), calls=%async_computation.29 | async-start | bytes 1048576
  388.6 32.4 %all-to-all-start.16 = ((bf16[8,768,128]{2,1,0:T(8,128)(2,1)}), bf16[8,768,128]{2,1,0:T(8,128)(2,1)}, u32[]{:S(2)}, u32[]{:S(2)}) async-start(bf16[8,768,128]{2,1,0:T(8,128)(2,1)} %bitcast.482), calls=%async_computation.16 | async-start | bytes 3145728 | tf_op jit(solution)/shard_map/all_to_all | solution.py:51
  421.0 25.1 %all-to-all-start.14 = ((bf16[8,768,128]{2,1,0:T(8,128)(2,1)}), bf16[8,768,128]{2,1,0:T(8,128)(2,1)S(1)}, u32[]{:S(2)}, u32[]{:S(2)}) async-start(bf16[8,768,128]{2,1,0:T(8,128)(2,1)} %bitcast.484), calls=%async_computation.14 | async-start | bytes 3145728 | tf_op jit(solution)/shard_map/all_to_all | solution.py:51
  429.8 23.0 %copy-start.3 = (f32[2,1,768,128]{3,2,1,0:T(8,128)S(1)}, f32[2,1,768,128]{3,2,1,0:T(8,128)}, u32[]{:S(2)}) copy-start(f32[2,1,768,128]{3,2,1,0:T(8,128)} %param.14) | copy-start | bytes 2359300
  446.1 9.0 %copy-start.6 = (bf16[8,768,128]{2,1,0:T(8,128)(2,1)}, bf16[8,768,128]{2,1,0:T(8,128)(2,1)S(1)}, u32[]{:S(2)}) copy-start(bf16[8,768,128]{2,1,0:T(8,128)(2,1)S(1)} %all-to-all-done.14) | copy-start | bytes 4718596
  448.9 12.1 %all-to-all-start.15 = ((f32[8,1,1536]{2,1,0:T(1,128)}), f32[8,1,1536]{2,1,0:T(1,128)}, u32[]{:S(2)}, u32[]{:S(2)}) async-start(f32[8,1,1536]{2,1,0:T(1,128)} %broadcast_in_dim.202), calls=%async_computation.15 | async-start | bytes 98304 | tf_op jit(solution)/shard_map/all_to_all | solution.py:18
  455.1 13.0 %collective-permute-start.2 = (f32[1,768,128]{2,1,0:T(8,128)}, f32[1,768,128]{2,1,0:T(8,128)S(1)}, u32[]{:S(2)}, u32[]{:S(2)}) collective-permute-start(f32[1,768,128]{2,1,0:T(8,128)} %get-tuple-element.206), channel_id=1, source_target_pairs={{0,64},{1,65},{2,66},{3,67},{4,68},{5,69},{6,70},{7,71},{8,72},{9,... | collective-permute-start | bytes 1179656 | tf_op jit(solution)/shard_map/ppermute | solution.py:504
  459.7 14.0 %collective-permute-start.1 = (f32[1,768,128]{2,1,0:T(8,128)}, f32[1,768,128]{2,1,0:T(8,128)S(1)}, u32[]{:S(2)}, u32[]{:S(2)}) collective-permute-start(f32[1,768,128]{2,1,0:T(8,128)} %get-tuple-element.207), channel_id=1, source_target_pairs={{64,0},{65,1},{66,2},{67,3},{68,4},{69,5},{70,6},{71,7},{72,8},{73... | collective-permute-start | bytes 1179656 | tf_op jit(solution)/shard_map/ppermute | solution.py:503
  474.7 24.4 %copy-start.127 = (f32[768,512]{1,0:T(8,128)S(1)}, f32[768,512]{1,0:T(8,128)}, u32[]{:S(2)}) copy-start(f32[768,512]{1,0:T(8,128)} %copy-done.126) | copy-start | bytes 4718596
  506.1 20.7 %all-to-all-start.18 = ((bf16[8,768,128]{2,1,0:T(8,128)(2,1)}), bf16[8,768,128]{2,1,0:T(8,128)(2,1)S(1)}, u32[]{:S(2)}, u32[]{:S(2)}) async-start(bf16[8,768,128]{2,1,0:T(8,128)(2,1)} %bitcast.485), calls=%async_computation.18 | async-start | bytes 3145728 | tf_op jit(solution)/shard_map/all_to_all | solution.py:51
  526.8 10.4 %copy-start.8 = (bf16[8,768,128]{2,1,0:T(8,128)(2,1)}, bf16[8,768,128]{2,1,0:T(8,128)(2,1)S(1)}, u32[]{:S(2)}) copy-start(bf16[8,768,128]{2,1,0:T(8,128)(2,1)S(1)} %all-to-all-done.18) | copy-start | bytes 4718596
  529.6 21.9 %all-to-all-start.19 = ((f32[8,1,1536]{2,1,0:T(1,128)}), f32[8,1,1536]{2,1,0:T(1,128)}, u32[]{:S(2)}, u32[]{:S(2)}) async-start(f32[8,1,1536]{2,1,0:T(1,128)} %broadcast_in_dim.204), calls=%async_computation.19 | async-start | bytes 98304 | tf_op jit(solution)/shard_map/all_to_all | solution.py:18
  554.8 41.3 %all-to-all-start.20 = ((bf16[8,768,128]{2,1,0:T(8,128)(2,1)}), bf16[8,768,128]{2,1,0:T(8,128)(2,1)}, u32[]{:S(2)}, u32[]{:S(2)}) async-start(bf16[8,768,128]{2,1,0:T(8,128)(2,1)} %broadcast_in_dim.205), calls=%async_computation.20 | async-start | bytes 3145728 | tf_op jit(solution)/shard_map/all_to_all | solution.py:18
  598.2 8.7 %slice-start = ((s8[4718592]{0:T(1024)(128)(4,1)}), s8[4194304]{0:T(1024)(128)(4,1)S(1)}, s32[]{:S(2)}) async-start(s8[4718592]{0:T(1024)(128)(4,1)} %bitcast.473), calls=%async_computation.27 | async-start | bytes 8388608
  617.5 25.3 %all-to-all-start.21 = ((bf16[8,768,128]{2,1,0:T(8,128)(2,1)}), bf16[8,768,128]{2,1,0:T(8,128)(2,1)S(1)}, u32[]{:S(2)}, u32[]{:S(2)}) async-start(bf16[8,768,128]{2,1,0:T(8,128)(2,1)} %bitcast.481), calls=%async_computation.21 | async-start | bytes 3145728 | tf_op jit(solution)/shard_map/all_to_all | solution.py:51
  643.6 8.2 %copy-start.111 = (bf16[8,16]{1,0:T(8,128)(2,1)S(1)}, bf16[8,16]{1,0:T(8,128)(2,1)}, u32[]{:S(2)}) copy-start(bf16[8,16]{1,0:T(8,128)(2,1)} %reshape.1903) | copy-start | bytes 772
  643.6 14.5 %copy-start.11 = (f32[768,128]{1,0:T(8,128)S(1)}, f32[768,128]{1,0:T(8,128)}, u32[]{:S(2)}) copy-start(f32[768,128]{1,0:T(8,128)} %copy-done.10) | copy-start | bytes 1179652
  643.6 14.5 %copy-start.72 = (f32[768]{0:T(1024)S(1)}, f32[768]{0:T(1024)}, u32[]{:S(2)}) copy-start(f32[768]{0:T(1024)} %copy-done.71) | copy-start | bytes 9220
  643.6 14.5 %copy-start.74 = (f32[768]{0:T(1024)S(1)}, f32[768]{0:T(1024)}, u32[]{:S(2)}) copy-start(f32[768]{0:T(1024)} %copy-done.73) | copy-start | bytes 9220
  643.6 14.5 %copy-start.88 = (f32[128]{0:T(128)S(1)}, f32[128]{0:T(128)}, u32[]{:S(2)}) copy-start(f32[128]{0:T(128)} %copy-done.85) | copy-start | bytes 1540
  643.6 14.5 %copy-start.90 = (f32[128]{0:T(128)S(1)}, f32[128]{0:T(128)}, u32[]{:S(2)}) copy-start(f32[128]{0:T(128)} %copy-done.89) | copy-start | bytes 1540
  644.7 16.3 %copy-start.108 = (bf16[8,16]{1,0:T(8,128)(2,1)S(1)}, bf16[8,16]{1,0:T(8,128)(2,1)}, u32[]{:S(2)}) copy-start(bf16[8,16]{1,0:T(8,128)(2,1)} %convert_element_type.684) | copy-start | bytes 772
  644.7 16.3 %copy-start.109 = (bf16[8,16]{1,0:T(8,128)(2,1)S(1)}, bf16[8,16]{1,0:T(8,128)(2,1)}, u32[]{:S(2)}) copy-start(bf16[8,16]{1,0:T(8,128)(2,1)} %convert_element_type.680) | copy-start | bytes 772
  644.7 16.3 %copy-start.112 = (bf16[8,16]{1,0:T(8,128)(2,1)S(1)}, bf16[8,16]{1,0:T(8,128)(2,1)}, u32[]{:S(2)}) copy-start(bf16[8,16]{1,0:T(8,128)(2,1)} %convert_element_type.678) | copy-start | bytes 772
  645.2 15.8 %copy-start.92 = (bf16[16,64]{1,0:T(8,128)(2,1)S(1)}, bf16[16,64]{1,0:T(8,128)(2,1)}, u32[]{:S(2)}) copy-start(bf16[16,64]{1,0:T(8,128)(2,1)} %pad_maximum_fusion.18) | copy-start | bytes 6148
  645.2 15.8 %copy-start.95 = (bf16[16,16]{1,0:T(8,128)(2,1)S(1)}, bf16[16,16]{1,0:T(8,128)(2,1)}, u32[]{:S(2)}) copy-start(bf16[16,16]{1,0:T(8,128)(2,1)} %get-tuple-element.287) | copy-start | bytes 1540
  645.2 15.8 %copy-start.96 = (bf16[16,16]{1,0:T(8,128)(2,1)S(1)}, bf16[16,16]{1,0:T(8,128)(2,1)}, u32[]{:S(2)}) copy-start(bf16[16,16]{1,0:T(8,128)(2,1)} %get-tuple-element.288) | copy-start | bytes 1540
  646.0 12.0 %all-to-all-start.22 = ((f32[8,1,1536]{2,1,0:T(1,128)}), f32[8,1,1536]{2,1,0:T(1,128)S(1)}, u32[]{:S(2)}, u32[]{:S(2)}) async-start(f32[8,1,1536]{2,1,0:T(1,128)} %broadcast_in_dim.206), calls=%async_computation.22 | async-start | bytes 98304 | tf_op jit(solution)/shard_map/all_to_all | solution.py:18
  651.7 100.4 %reduce-scatter.2.cloned.1.call-start = ((), (), s32[]{:S(2)}) async-start(), calls=%async_computation.24 | async-start | bytes 6754304 | tf_op jit(solution)/shard_map/reduce_scatter | solution.py:428
  663.2 7.6 collective-permute-start.4
  665.6 11.2 %collective-permute-start.3 = (f32[1,768,128]{2,1,0:T(8,128)S(1)}, f32[1,768,128]{2,1,0:T(8,128)S(1)}, u32[]{:S(2)}, u32[]{:S(2)}) collective-permute-start(f32[1,768,128]{2,1,0:T(8,128)S(1)} %copy-done.63), channel_id=1, source_target_pairs={{64,0},{65,1},{66,2},{67,3},{68,4},{69,5},{70,6},{71,7},{72,8},{73... | collective-permute-start | bytes 1179656 | tf_op jit(solution)/shard_map/ppermute | solution.py:511
  (97 other events, 270.8 us)
Sparse Core Ops, SparseCore 0:
  26.2 30.4 all-gather.4
  126.9 27.8 all-gather.6
  662.0 90.0 reduce-scatter.1

commit v13 on v9

--- a/solution.py
+++ b/solution.py
@@ -500,15 +500,14 @@
     grad_rows = out_grad.reshape(-1, out_grad.shape[-1]).astype(jnp.bfloat16)
     middle, kept_zero, grad_full = layer_forward(stream, weights_zero, grad_rows)
     final, kept_last, _ = layer_forward(middle, weights_last)
-    other_middle = lax.ppermute(middle, "section", [(1, 0)])
-    other_final = lax.ppermute(final, "section", [(0, 1)])
+    other_out = lax.ppermute(jnp.where(is_first, final, middle), "section", [(0, 1), (1, 0)])
     middle_grad, grads_last = layer_backward(out_grad, kept_last, weights_last, grad_full)
     other_middle_grad = lax.ppermute(middle_grad, "section", [(0, 1)])
     input_grad, grads_zero = layer_backward(middle_grad, kept_zero, weights_zero)
     other_input_grad = lax.ppermute(input_grad, "section", [(1, 0)])
     reduced = sum_at_end(grads_zero, grads_last, dims)
     section_outputs = jnp.where(
-        is_first, jnp.stack([middle, other_middle]), jnp.stack([other_final, final])
+        is_first, jnp.stack([middle, other_out]), jnp.stack([other_out, final])
     )[None]
     section_grads = jnp.where(
         is_first,

time: 713 us -> 716 us (level)
    unnamed x220 -> x222, local copies, waits for them, and re-layouts: 15 us -> 15 us
  transfers between devices with their start and end apart: 25 -> 24, of which waited for: 21 -> 19; matrix products, arithmetic and copies ran while one was open for 16% -> 16% of each run, Pallas kernels for 0% -> 0%
where the time goes in v13:
time: 716 us; the launch traced here: 702 us
  waiting for transfers between devices  253 us (35%)
  blocking collectives  113 us (16%)
  local copies, waits for them, and re-layouts  103 us (14%)
  starting transfers between devices  90 us (13%)
  matrix products  71.6 us (10%)
  other arithmetic  55.5 us (8%)
  between operations  15.8 us (2%)
    all_to_all x11, waiting for transfers between devices, sent_to_all(): return lax.all_to_all(copies, axis, split_axis=0, concat_axis=0, tiled=True)  102 us
    all_to_all x6, waiting for transfers between devices, summed_on_arrival(): lax.all_to_all(parts, axis, split_axis=0, concat_axis=0, tiled=True)  73.6 us
    all_to_all x4, blocking collectives, sent_to_all(): return lax.all_to_all(copies, axis, split_axis=0, concat_axis=0, tiled=True)  66 us
    all_to_all x11, starting transfers between devices, sent_to_all(): return lax.all_to_all(copies, axis, split_axis=0, concat_axis=0, tiled=True)  49.6 us
    all_to_all x2, blocking collectives, summed_on_arrival(): lax.all_to_all(parts, axis, split_axis=0, concat_axis=0, tiled=True)  46.6 us
    reduce_scatter x1, waiting for transfers between devices, sum_at_end(): lax.psum_scatter(rows.reshape(-1, 128), ('section', 'dp'), scatter_dimens...  36 us
    all_to_all x6, starting transfers between devices, summed_on_arrival(): lax.all_to_all(parts, axis, split_axis=0, concat_axis=0, tiled=True)  27.1 us
    all_gather x1, waiting for transfers between devices, gather_all(): lax.all_gather(jnp.where(is_first, own, other), 'dp', axis=0, tiled=False)  16.8 us
  transfers between devices with their start and end apart: 24, of which 19 were waited for; matrix products, arithmetic and copies ran while one was open for 16% of the time, Pallas kernels for 0%

profile of v13, /device:TPU:0, one launch (start us, length us, event | category | flops | bytes accessed | tf_op | source)
XLA Modules:
  0.0 702.0 jit_solution(18047361004665300734)
XLA Ops:
  12.8 3.2 collective-permute-start
  16.0 9.2 %collective-permute-done = bf16[1552,128]{1,0:T(8,128)(2,1)S(1)} collective-permute-done((bf16[1552,128]{1,0:T(8,128)(2,1)S(1)}, bf16[1552,128]{1,0:T(8,128)(2,1)S(1)}, u32[]{:S(2)}, u32[]{:S(2)}) %collective-permute-start) | collective-permute-done | bytes 397344 | tf_op jit(solution)/shard_map/ppermute | solution.py:452
  27.2 6.5 all-to-all-start
  34.7 5.3 all-to-all-done
  40.0 16.8 %all-gather.5.cloned.1.call-done = bf16[12416,128]{1,0:T(8,128)(2,1)} async-done(((bf16[1552,128]{1,0:T(8,128)(2,1)}), bf16[12416,128]{1,0:T(8,128)(2,1)}) %all-gather.5.cloned.1.call-update) | async-done | bytes 3178512 | tf_op jit(solution)/shard_map/all_gather | solution.py:453
  60.5 5.3 all-to-all-start.1
  73.3 30.3 %all-to-all-done.1 = bf16[8,2,768,128]{3,2,1,0:T(8,128)(2,1)} async-done(((bf16[8,2,768,128]{3,2,1,0:T(8,128)(2,1)}), bf16[8,2,768,128]{3,2,1,0:T(8,128)(2,1)}, u32[]{:S(2)}, u32[]{:S(2)}) %all-to-all-start.1) | async-done | bytes 3145760 | tf_op jit(solution)/shard_map/all_to_all | solution.py:18
  103.6 4.7 copy.246
  108.2 3.4 fusion.133
  119.7 3.6 all-to-all-start.2
  124.1 19.8 %all-to-all-done.2 = bf16[8,768,128]{2,1,0:T(8,128)(2,1)S(1)} async-done(((bf16[8,768,128]{2,1,0:T(8,128)(2,1)}), bf16[8,768,128]{2,1,0:T(8,128)(2,1)S(1)}, u32[]{:S(2)}, u32[]{:S(2)}) %all-to-all-start.2) | async-done | bytes 1572896 | tf_op jit(solution)/shard_map/all_to_all | solution.py:51
  145.5 3.6 all-to-all-start.3
  149.3 6.1 all-to-all-done.3
  157.2 4.6 all-to-all-start.4
  162.0 2.7 fusion.132
  168.5 12.9 %all-to-all-done.4 = bf16[8,768,128]{1,2,0:T(8,128)(2,1)} async-done(((bf16[8,768,128]{1,2,0:T(8,128)(2,1)}), bf16[8,768,128]{1,2,0:T(8,128)(2,1)}, u32[]{:S(2)}, u32[]{:S(2)}) %all-to-all-start.4) | async-done | bytes 1572896 | tf_op jit(solution)/shard_map/all_to_all | solution.py:18
  181.3 2.8 convolution_add_fusion.1
  186.8 3.6 all-to-all-start.5
  191.2 19.7 %all-to-all-done.5 = bf16[8,768,128]{2,1,0:T(8,128)(2,1)S(1)} async-done(((bf16[8,768,128]{2,1,0:T(8,128)(2,1)}), bf16[8,768,128]{2,1,0:T(8,128)(2,1)S(1)}, u32[]{:S(2)}, u32[]{:S(2)}) %all-to-all-start.5) | async-done | bytes 1572896 | tf_op jit(solution)/shard_map/all_to_all | solution.py:51
  212.3 3.6 all-to-all-start.6
  216.7 5.5 all-to-all-done.6
  223.9 4.3 all-to-all-start.7
  232.5 15.2 %all-to-all-done.7 = bf16[8,768,128]{2,1,0:T(8,128)(2,1)} async-done(((bf16[8,768,128]{2,1,0:T(8,128)(2,1)}), bf16[8,768,128]{2,1,0:T(8,128)(2,1)}, u32[]{:S(2)}, u32[]{:S(2)}) %all-to-all-start.7) | async-done | bytes 1572896 | tf_op jit(solution)/shard_map/all_to_all | solution.py:18
  256.9 3.6 all-to-all-start.8
  260.6 20.5 %all-to-all-done.8 = bf16[8,768,128]{2,1,0:T(8,128)(2,1)S(1)} async-done(((bf16[8,768,128]{2,1,0:T(8,128)(2,1)}), bf16[8,768,128]{2,1,0:T(8,128)(2,1)S(1)}, u32[]{:S(2)}, u32[]{:S(2)}) %all-to-all-start.8) | async-done | bytes 1572896 | tf_op jit(solution)/shard_map/all_to_all | solution.py:51
  282.4 3.6 all-to-all-start.9
  286.2 6.1 all-to-all-done.9
  294.2 4.3 all-to-all-start.10
  298.6 2.7 fusion.131
  305.1 12.8 %all-to-all-done.10 = bf16[8,768,128]{1,2,0:T(8,128)(2,1)} async-done(((bf16[8,768,128]{1,2,0:T(8,128)(2,1)}), bf16[8,768,128]{1,2,0:T(8,128)(2,1)}, u32[]{:S(2)}, u32[]{:S(2)}) %all-to-all-start.10) | async-done | bytes 1572896 | tf_op jit(solution)/shard_map/all_to_all | solution.py:18
  318.0 2.8 convolution_add_fusion
  320.9 2.7 fusion.122
  324.9 25.3 %all_to_all.123 = bf16[8,768,128]{2,1,0:T(8,128)(2,1)} all-to-all(bf16[8,768,128]{2,1,0:T(8,128)(2,1)S(1)} %bitcast.508), channel_id=1, replica_groups=mesh['section'=2,'dp'=8,'tensor'=8] {'tensor'}, dimensions={0} | all-to-all | bytes 3145728 | tf_op jit(solution)/shard_map/all_to_all | solution.py:51
  352.8 8.7 %all_to_all.124 = f32[8,1,1536]{2,1,0:T(1,128)S(1)} all-to-all(f32[8,1,1536]{2,1,0:T(1,128)S(1)} %broadcast_in_dim.200), channel_id=1, replica_groups=mesh['section'=2,'dp'=8,'tensor'=8] {'tensor'}, dimensions={0} | all-to-all | bytes 98304 | tf_op jit(solution)/shard_map/all_to_all | solution.py:18
  365.2 29.8 %all_to_all.125 = bf16[8,768,128]{2,1,0:T(8,128)(2,1)S(1)} all-to-all(bf16[8,768,128]{2,1,0:T(8,128)(2,1)S(1)} %broadcast_in_dim.201), channel_id=1, replica_groups=mesh['section'=2,'dp'=8,'tensor'=8] {'tensor'}, dimensions={0} | all-to-all | bytes 3145728 | tf_op jit(solution)/shard_map/all_to_all | solution.py:18
  408.5 21.3 %all_to_all.126 = bf16[8,768,128]{2,1,0:T(8,128)(2,1)S(1)} all-to-all(bf16[8,768,128]{2,1,0:T(8,128)(2,1)S(1)} %bitcast.509), channel_id=1, replica_groups=mesh['section'=2,'dp'=8,'tensor'=8] {'tensor'}, dimensions={0} | all-to-all | bytes 3145728 | tf_op jit(solution)/shard_map/all_to_all | solution.py:51
  432.3 8.8 %all_to_all.127 = f32[8,1,1536]{2,1,0:T(1,128)S(1)} all-to-all(f32[8,1,1536]{2,1,0:T(1,128)S(1)} %broadcast_in_dim.202), channel_id=1, replica_groups=mesh['section'=2,'dp'=8,'tensor'=8] {'tensor'}, dimensions={0} | all-to-all | bytes 98304 | tf_op jit(solution)/shard_map/all_to_all | solution.py:18
  443.7 18.7 %all_to_all.128 = bf16[8,768,128]{2,1,0:T(8,128)(2,1)S(1)} all-to-all(bf16[8,768,128]{2,1,0:T(8,128)(2,1)S(1)} %broadcast_in_dim.203), channel_id=1, replica_groups=mesh['section'=2,'dp'=8,'tensor'=8] {'tensor'}, dimensions={0} | all-to-all | bytes 3145728 | tf_op jit(solution)/shard_map/all_to_all | solution.py:18
  462.4 4.0 fusion.136
  469.0 4.7 all-to-all-start.18
  474.9 3.6 convolution_convert_fusion.8
  480.9 3.1 fusion.34
  493.3 5.7 all-to-all-start.19
  502.0 3.2 all-to-all-done.19
  508.2 4.4 all-to-all-start.20
  516.9 3.2 concatenate.135
  522.3 3.6 convolution_convert_fusion.9
  530.1 3.0 fusion.33
  539.0 4.0 bitcast_reduce_fusion
  543.0 4.2 multiply_reduce_fusion
  550.3 2.8 copy.294
  556.0 5.7 all-to-all-start.21
  570.6 2.7 maximum_dynamic-update-slice_fusion.2
  586.0 5.8 all-to-all-start.11
  592.0 13.6 %all-to-all-done.11 = bf16[8,768,128]{2,1,0:T(8,128)(2,1)} async-done(((bf16[8,768,128]{2,1,0:T(8,128)(2,1)}), bf16[8,768,128]{2,1,0:T(8,128)(2,1)}, u32[]{:S(2)}, u32[]{:S(2)}) %all-to-all-start.11) | async-done | bytes 1572896 | tf_op jit(solution)/shard_map/all_to_all | solution.py:51
  606.3 3.6 all-to-all-start.22
  612.3 4.1 all-to-all-done.22
  616.6 3.8 fusion.46
  620.4 2.6 collective-permute-start.1
  623.1 3.3 fusion.63
  627.7 6.1 collective-permute-start.3
  633.9 6.9 collective-permute-done.1
  641.7 8.6 %collective-permute-done.2 = f32[1,768,128]{2,1,0:T(8,128)S(1)} collective-permute-done((f32[1,768,128]{2,1,0:T(8,128)S(1)}, f32[1,768,128]{2,1,0:T(8,128)S(1)}, u32[]{:S(2)}, u32[]{:S(2)}) %collective-permute-start.2) | collective-permute-done | bytes 393248 | tf_op jit(solution)/shard_map/ppermute | solution.py:507
  651.3 36.0 %reduce-scatter.2.cloned.1.call-done = bf16[1552,128]{1,0:T(8,128)(2,1)} async-done(((bf16[24832,128]{1,0:T(8,128)(2,1)}), bf16[1552,128]{1,0:T(8,128)(2,1)}) %reduce-scatter.2.cloned.1.call-update) | async-done | bytes 397328 | tf_op jit(solution)/shard_map/reduce_scatter | solution.py:428
  (469 shorter events, 169.4 us)
Async XLA Ops:
  7.2 49.7 %all-gather.5.cloned.1.call-start = ((), (), s32[]{:S(2)}) async-start(), calls=%async_computation.25 | async-start | bytes 3575808 | tf_op jit(solution)/shard_map/all_gather | solution.py:453
  9.0 17.1 %copy-start.8 = (f32[2,1,768,128]{3,2,1,0:T(8,128)S(1)}, f32[2,1,768,128]{3,2,1,0:T(8,128)}, u32[]{:S(2)}) copy-start(f32[2,1,768,128]{3,2,1,0:T(8,128)} %param.14) | copy-start | bytes 2359300
  12.8 12.4 %collective-permute-start = (bf16[1552,128]{1,0:T(8,128)(2,1)S(1)}, bf16[1552,128]{1,0:T(8,128)(2,1)S(1)}, u32[]{:S(2)}, u32[]{:S(2)}) collective-permute-start(bf16[1552,128]{1,0:T(8,128)(2,1)S(1)} %bitcast.566), channel_id=1, source_target_pairs={{0,64},{64,0},{1,65},{65,1},{2,66},{66,2},{3,67},{67,3},{4,68},{68... | collective-permute-start | bytes 1191944 | tf_op jit(solution)/shard_map/ppermute | solution.py:452
  27.2 12.8 %all-to-all-start = ((f32[8,1,1536]{2,1,0:T(1,128)}), f32[8,1,1536]{2,1,0:T(1,128)S(1)}, u32[]{:S(2)}, u32[]{:S(2)}) async-start(f32[8,1,1536]{2,1,0:T(1,128)} %broadcast_in_dim.189), calls=%async_computation | async-start | bytes 98304 | tf_op jit(solution)/shard_map/all_to_all | solution.py:18
  60.5 43.1 %all-to-all-start.1 = ((bf16[8,2,768,128]{3,2,1,0:T(8,128)(2,1)}), bf16[8,2,768,128]{3,2,1,0:T(8,128)(2,1)}, u32[]{:S(2)}, u32[]{:S(2)}) async-start(bf16[8,2,768,128]{3,2,1,0:T(8,128)(2,1)} %broadcast_in_dim.191), calls=%async_computation.1 | async-start | bytes 6291456 | tf_op jit(solution)/shard_map/all_to_all | solution.py:18
  68.2 44.6 %copy-start.78 = (f32[2,64]{1,0:T(2,128)}, f32[2,64]{1,0:T(2,128)S(1)}, u32[]{:S(2)}) copy-start(f32[2,64]{1,0:T(2,128)S(1)} %reshape.2337) | copy-start | bytes 1540
  68.3 46.8 %copy-start.88 = (f32[2,64]{1,0:T(2,128)}, f32[2,64]{1,0:T(2,128)S(1)}, u32[]{:S(2)}) copy-start(f32[2,64]{1,0:T(2,128)S(1)} %reshape.2336) | copy-start | bytes 1540
  119.7 24.2 %all-to-all-start.2 = ((bf16[8,768,128]{2,1,0:T(8,128)(2,1)}), bf16[8,768,128]{2,1,0:T(8,128)(2,1)S(1)}, u32[]{:S(2)}, u32[]{:S(2)}) async-start(bf16[8,768,128]{2,1,0:T(8,128)(2,1)} %bitcast.489), calls=%async_computation.2 | async-start | bytes 3145728 | tf_op jit(solution)/shard_map/all_to_all | solution.py:51
  123.3 67.1 %all-gather.7.cloned.1.call-start = ((), (), s32[]{:S(2)}) async-start(), calls=%async_computation.26 | async-start | bytes 3575808 | tf_op jit(solution)/shard_map/all_gather | solution.py:454
  124.1 20.3 %copy-start.84 = (f32[128]{0:T(128)}, f32[128]{0:T(128)S(1)}, u32[]{:S(2)}) copy-start(f32[128]{0:T(128)S(1)} %reshape.2338) | copy-start | bytes 1540
  145.5 9.9 %all-to-all-start.3 = ((f32[8,1,1536]{2,1,0:T(1,128)}), f32[8,1,1536]{2,1,0:T(1,128)S(1)}, u32[]{:S(2)}, u32[]{:S(2)}) async-start(f32[8,1,1536]{2,1,0:T(1,128)} %broadcast_in_dim.194), calls=%async_computation.3 | async-start | bytes 98304 | tf_op jit(solution)/shard_map/all_to_all | solution.py:18
  149.2 8.0 %copy-start.69 = (f32[128]{0:T(128)}, f32[128]{0:T(128)S(1)}, u32[]{:S(2)}) copy-start(f32[128]{0:T(128)S(1)} %reshape.2339) | copy-start | bytes 1540
  157.2 24.1 %all-to-all-start.4 = ((bf16[8,768,128]{1,2,0:T(8,128)(2,1)}), bf16[8,768,128]{1,2,0:T(8,128)(2,1)}, u32[]{:S(2)}, u32[]{:S(2)}) async-start(bf16[8,768,128]{1,2,0:T(8,128)(2,1)} %broadcast_in_dim.195), calls=%async_computation.4 | async-start | bytes 3145728 | tf_op jit(solution)/shard_map/all_to_all | solution.py:18
  186.8 24.2 %all-to-all-start.5 = ((bf16[8,768,128]{2,1,0:T(8,128)(2,1)}), bf16[8,768,128]{2,1,0:T(8,128)(2,1)S(1)}, u32[]{:S(2)}, u32[]{:S(2)}) async-start(bf16[8,768,128]{2,1,0:T(8,128)(2,1)} %bitcast.487), calls=%async_computation.5 | async-start | bytes 3145728 | tf_op jit(solution)/shard_map/all_to_all | solution.py:51
  190.4 21.0 %copy-start.86 = (f32[128]{0:T(128)}, f32[128]{0:T(128)S(1)}, u32[]{:S(2)}) copy-start(f32[128]{0:T(128)S(1)} %reshape.2342) | copy-start | bytes 1540
  211.2 12.8 %copy-start.17 = (f32[768,128]{1,0:T(8,128)}, f32[768,128]{1,0:T(8,128)S(1)}, u32[]{:S(2)}) copy-start(f32[768,128]{1,0:T(8,128)S(1)} %convert_reduce_fusion.6) | copy-start | bytes 1179652
  211.5 69.9 %copy-start.2 = (f32[768,128]{1,0:T(8,128)}, f32[768,128]{1,0:T(8,128)S(1)}, u32[]{:S(2)}) copy-start(f32[768,128]{1,0:T(8,128)S(1)} %get-tuple-element.207) | copy-start | bytes 1179652
  212.3 9.9 %all-to-all-start.6 = ((f32[8,1,1536]{2,1,0:T(1,128)}), f32[8,1,1536]{2,1,0:T(1,128)S(1)}, u32[]{:S(2)}, u32[]{:S(2)}) async-start(f32[8,1,1536]{2,1,0:T(1,128)} %broadcast_in_dim.196), calls=%async_computation.6 | async-start | bytes 98304 | tf_op jit(solution)/shard_map/all_to_all | solution.py:18
  216.6 7.3 %copy-start.72 = (f32[128]{0:T(128)}, f32[128]{0:T(128)S(1)}, u32[]{:S(2)}) copy-start(f32[128]{0:T(128)S(1)} %reshape.2343) | copy-start | bytes 1540
  223.9 23.8 %all-to-all-start.7 = ((bf16[8,768,128]{2,1,0:T(8,128)(2,1)}), bf16[8,768,128]{2,1,0:T(8,128)(2,1)}, u32[]{:S(2)}, u32[]{:S(2)}) async-start(bf16[8,768,128]{2,1,0:T(8,128)(2,1)} %broadcast_in_dim.197), calls=%async_computation.7 | async-start | bytes 3145728 | tf_op jit(solution)/shard_map/all_to_all | solution.py:18
  229.6 20.5 %copy-start.80 = (f32[2,64]{1,0:T(2,128)}, f32[2,64]{1,0:T(2,128)S(1)}, u32[]{:S(2)}) copy-start(f32[2,64]{1,0:T(2,128)S(1)} %reshape.2346) | copy-start | bytes 1540
  229.7 22.7 %copy-start.90 = (f32[2,64]{1,0:T(2,128)}, f32[2,64]{1,0:T(2,128)S(1)}, u32[]{:S(2)}) copy-start(f32[2,64]{1,0:T(2,128)S(1)} %reshape.2345) | copy-start | bytes 1540
  232.5 17.4 %copy-start.52 = (bf16[1024,3,128]{0,2,1:T(8,128)(2,1)}, bf16[1024,3,128]{0,2,1:T(8,128)(2,1)S(1)}, u32[]{:S(2)}) copy-start(bf16[1024,3,128]{0,2,1:T(8,128)(2,1)S(1)} %copy.259) | copy-start | bytes 2359300
  256.9 24.2 %all-to-all-start.8 = ((bf16[8,768,128]{2,1,0:T(8,128)(2,1)}), bf16[8,768,128]{2,1,0:T(8,128)(2,1)S(1)}, u32[]{:S(2)}, u32[]{:S(2)}) async-start(bf16[8,768,128]{2,1,0:T(8,128)(2,1)} %bitcast.485), calls=%async_computation.8 | async-start | bytes 3145728 | tf_op jit(solution)/shard_map/all_to_all | solution.py:51
  260.6 21.0 %copy-start.65 = (f32[128]{0:T(128)}, f32[128]{0:T(128)S(1)}, u32[]{:S(2)}) copy-start(f32[128]{0:T(128)S(1)} %reshape.2347) | copy-start | bytes 1540
  281.7 12.5 %copy-start.13 = (f32[768,128]{1,0:T(8,128)}, f32[768,128]{1,0:T(8,128)S(1)}, u32[]{:S(2)}) copy-start(f32[768,128]{1,0:T(8,128)S(1)} %get-tuple-element.206) | copy-start | bytes 1179652
  282.4 9.9 %all-to-all-start.9 = ((f32[8,1,1536]{2,1,0:T(1,128)}), f32[8,1,1536]{2,1,0:T(1,128)S(1)}, u32[]{:S(2)}, u32[]{:S(2)}) async-start(f32[8,1,1536]{2,1,0:T(1,128)} %broadcast_in_dim.198), calls=%async_computation.9 | async-start | bytes 98304 | tf_op jit(solution)/shard_map/all_to_all | solution.py:18
  286.2 65.8 %copy-start.67 = (f32[128]{0:T(128)}, f32[128]{0:T(128)S(1)}, u32[]{:S(2)}) copy-start(f32[128]{0:T(128)S(1)} %reshape.2348) | copy-start | bytes 1540
  294.2 23.8 %all-to-all-start.10 = ((bf16[8,768,128]{1,2,0:T(8,128)(2,1)}), bf16[8,768,128]{1,2,0:T(8,128)(2,1)}, u32[]{:S(2)}, u32[]{:S(2)}) async-start(bf16[8,768,128]{1,2,0:T(8,128)(2,1)} %broadcast_in_dim.199), calls=%async_computation.10 | async-start | bytes 3145728 | tf_op jit(solution)/shard_map/all_to_all | solution.py:18
  324.9 72.0 %slice-start.2 = ((s8[4718592]{0:T(1024)(128)(4,1)}), s8[524288]{0:T(1024)(128)(4,1)S(1)}, s32[]{:S(2)}) async-start(s8[4718592]{0:T(1024)(128)(4,1)} %bitcast.501), calls=%async_computation.29 | async-start | bytes 1048576
  350.2 12.7 %copy-start.23 = (f32[2,1,768,128]{3,2,1,0:T(8,128)S(1)}, f32[2,1,768,128]{3,2,1,0:T(8,128)}, u32[]{:S(2)}) copy-start(f32[2,1,768,128]{3,2,1,0:T(8,128)} %param.15) | copy-start | bytes 2359300
  352.0 13.0 %copy-start.4 = (f32[768,128]{1,0:T(8,128)}, f32[768,128]{1,0:T(8,128)S(1)}, u32[]{:S(2)}) copy-start(f32[768,128]{1,0:T(8,128)S(1)} %convert_reduce_fusion.3) | copy-start | bytes 1179652
  362.9 33.9 %slice-start.3 = ((s8[4718592]{0:T(1024)(128)(4,1)}), s8[4194304]{0:T(1024)(128)(4,1)S(1)}, s32[]{:S(2)}) async-start(s8[4718592]{0:T(1024)(128)(4,1)} %bitcast.501), calls=%async_computation.30 | async-start | bytes 8388608
  443.7 18.7 %copy-start.97 = (f32[768,512]{1,0:T(8,128)S(1)}, f32[768,512]{1,0:T(8,128)}, u32[]{:S(2)}) copy-start(f32[768,512]{1,0:T(8,128)} %copy-done.96) | copy-start | bytes 4718596
  469.0 21.5 %all-to-all-start.18 = ((bf16[8,768,128]{2,1,0:T(8,128)(2,1)}), bf16[8,768,128]{2,1,0:T(8,128)(2,1)}, u32[]{:S(2)}, u32[]{:S(2)}) async-start(bf16[8,768,128]{2,1,0:T(8,128)(2,1)} %bitcast.507), calls=%async_computation.18 | async-start | bytes 3145728 | tf_op jit(solution)/shard_map/all_to_all | solution.py:51
  492.1 13.2 %copy-start.6 = (f32[768,128]{1,0:T(8,128)}, f32[768,128]{1,0:T(8,128)S(1)}, u32[]{:S(2)}) copy-start(f32[768,128]{1,0:T(8,128)S(1)} %convert_reduce_fusion.1) | copy-start | bytes 1179652
  493.3 12.0 %all-to-all-start.19 = ((f32[8,1,1536]{2,1,0:T(1,128)}), f32[8,1,1536]{2,1,0:T(1,128)S(1)}, u32[]{:S(2)}, u32[]{:S(2)}) async-start(f32[8,1,1536]{2,1,0:T(1,128)} %broadcast_in_dim.204), calls=%async_computation.19 | async-start | bytes 98304 | tf_op jit(solution)/shard_map/all_to_all | solution.py:18
  508.2 4.6 copy-start.57
  508.2 4.6 copy-start.58
  508.2 4.6 copy-start.59
  508.2 28.6 %all-to-all-start.20 = ((bf16[8,768,128]{2,1,0:T(8,128)(2,1)}), bf16[8,768,128]{2,1,0:T(8,128)(2,1)}, u32[]{:S(2)}, u32[]{:S(2)}) async-start(bf16[8,768,128]{2,1,0:T(8,128)(2,1)} %broadcast_in_dim.205), calls=%async_computation.20 | async-start | bytes 3145728 | tf_op jit(solution)/shard_map/all_to_all | solution.py:18
  534.3 4.6 copy-start.62
  539.0 4.0 copy-start.38
  539.0 8.3 %slice-start = ((s8[4718592]{0:T(1024)(128)(4,1)}), s8[4194304]{0:T(1024)(128)(4,1)S(1)}, s32[]{:S(2)}) async-start(s8[4718592]{0:T(1024)(128)(4,1)} %bitcast.499), calls=%async_computation.27 | async-start | bytes 8388608
  543.0 4.3 slice-start.1
  556.0 5.8 copy-start.54
  556.0 22.1 %all-to-all-start.21 = ((bf16[8,768,128]{2,1,0:T(8,128)(2,1)}), bf16[8,768,128]{2,1,0:T(8,128)(2,1)S(1)}, u32[]{:S(2)}, u32[]{:S(2)}) async-start(bf16[8,768,128]{2,1,0:T(8,128)(2,1)} %bitcast.506), calls=%async_computation.21 | async-start | bytes 3145728 | tf_op jit(solution)/shard_map/all_to_all | solution.py:51
  561.8 125.5 %reduce-scatter.2.cloned.1.call-start = ((), (), s32[]{:S(2)}) async-start(), calls=%async_computation.24 | async-start | bytes 6754304 | tf_op jit(solution)/shard_map/reduce_scatter | solution.py:428
  586.0 5.9 copy-start.75
  586.0 19.6 %all-to-all-start.11 = ((bf16[8,768,128]{2,1,0:T(8,128)(2,1)}), bf16[8,768,128]{2,1,0:T(8,128)(2,1)}, u32[]{:S(2)}, u32[]{:S(2)}) async-start(bf16[8,768,128]{2,1,0:T(8,128)(2,1)} %bitcast.483), calls=%async_computation.11 | async-start | bytes 3145728 | tf_op jit(solution)/shard_map/all_to_all | solution.py:51
  591.8 24.6 %copy-start.5 = (f32[768,128]{1,0:T(8,128)S(1)}, f32[768,128]{1,0:T(8,128)}, u32[]{:S(2)}) copy-start(f32[768,128]{1,0:T(8,128)} %copy-done.4) | copy-start | bytes 1179652
  591.8 24.6 %copy-start.7 = (f32[768,128]{1,0:T(8,128)S(1)}, f32[768,128]{1,0:T(8,128)}, u32[]{:S(2)}) copy-start(f32[768,128]{1,0:T(8,128)} %copy-done.6) | copy-start | bytes 1179652
  591.9 24.6 %copy-start.16 = (f32[768,128]{1,0:T(8,128)S(1)}, f32[768,128]{1,0:T(8,128)}, u32[]{:S(2)}) copy-start(f32[768,128]{1,0:T(8,128)} %copy-done.15) | copy-start | bytes 1179652
  591.9 24.6 %copy-start.18 = (f32[768,128]{1,0:T(8,128)S(1)}, f32[768,128]{1,0:T(8,128)}, u32[]{:S(2)}) copy-start(f32[768,128]{1,0:T(8,128)} %copy-done.17) | copy-start | bytes 1179652
  591.9 24.6 %copy-start.66 = (f32[128]{0:T(128)S(1)}, f32[128]{0:T(128)}, u32[]{:S(2)}) copy-start(f32[128]{0:T(128)} %copy-done.65) | copy-start | bytes 1540
  591.9 24.6 %copy-start.68 = (f32[128]{0:T(128)S(1)}, f32[128]{0:T(128)}, u32[]{:S(2)}) copy-start(f32[128]{0:T(128)} %copy-done.67) | copy-start | bytes 1540
  591.9 24.6 %copy-start.71 = (f32[128]{0:T(128)S(1)}, f32[128]{0:T(128)}, u32[]{:S(2)}) copy-start(f32[128]{0:T(128)} %copy-done.69) | copy-start | bytes 1540
  591.9 24.6 %copy-start.74 = (f32[128]{0:T(128)S(1)}, f32[128]{0:T(128)}, u32[]{:S(2)}) copy-start(f32[128]{0:T(128)} %copy-done.72) | copy-start | bytes 1540
  591.9 24.6 %copy-start.85 = (f32[128]{0:T(128)S(1)}, f32[128]{0:T(128)}, u32[]{:S(2)}) copy-start(f32[128]{0:T(128)} %copy-done.84) | copy-start | bytes 1540
  591.9 24.6 %copy-start.87 = (f32[128]{0:T(128)S(1)}, f32[128]{0:T(128)}, u32[]{:S(2)}) copy-start(f32[128]{0:T(128)} %copy-done.86) | copy-start | bytes 1540
  606.3 10.1 %all-to-all-start.22 = ((f32[8,1,1536]{2,1,0:T(1,128)}), f32[8,1,1536]{2,1,0:T(1,128)S(1)}, u32[]{:S(2)}, u32[]{:S(2)}) async-start(f32[8,1,1536]{2,1,0:T(1,128)} %broadcast_in_dim.206), calls=%async_computation.22 | async-start | bytes 98304 | tf_op jit(solution)/shard_map/all_to_all | solution.py:18
  620.4 20.3 %collective-permute-start.1 = (f32[1,768,128]{2,1,0:T(8,128)S(1)}, f32[1,768,128]{2,1,0:T(8,128)S(1)}, u32[]{:S(2)}, u32[]{:S(2)}) collective-permute-start(f32[1,768,128]{2,1,0:T(8,128)S(1)} %fusion.80), channel_id=1, source_target_pairs={{0,64},{64,0},{1,65},{65,1},{2,66},{66,2},{3,67},{67,3},{4,68},{68... | collective-permute-start | bytes 1179656 | tf_op jit(solution)/shard_map/ppermute | solution.py:503
  626.4 23.9 %collective-permute-start.2 = (f32[1,768,128]{2,1,0:T(8,128)S(1)}, f32[1,768,128]{2,1,0:T(8,128)S(1)}, u32[]{:S(2)}, u32[]{:S(2)}) collective-permute-start(f32[1,768,128]{2,1,0:T(8,128)S(1)} %get-tuple-element.203), channel_id=1, source_target_pairs={{64,0},{65,1},{66,2},{67,3},{68,4},{69,5},{70,6},{71,7},{72,8},{73... | collective-permute-start | bytes 1179656 | tf_op jit(solution)/shard_map/ppermute | solution.py:507
  627.7 22.6 %collective-permute-start.3 = (f32[1,768,128]{2,1,0:T(8,128)S(1)}, f32[1,768,128]{2,1,0:T(8,128)S(1)}, u32[]{:S(2)}, u32[]{:S(2)}) collective-permute-start(f32[1,768,128]{2,1,0:T(8,128)S(1)} %get-tuple-element.204), channel_id=1, source_target_pairs={{0,64},{1,65},{2,66},{3,67},{4,68},{5,69},{6,70},{7,71},{8,72},{9,... | collective-permute-start | bytes 1179656 | tf_op jit(solution)/shard_map/ppermute | solution.py:505
  (63 other events, 128.3 us)
Sparse Core Ops, SparseCore 0:
  26.3 30.4 all-gather.4
  126.4 27.8 all-gather.6
  580.9 106.3 reduce-scatter.1
